TPU v7x, 32 devices: a whole 2x2x4 slice. The times are simulated.
32 devices in a mesh: fsdp: 4 (over z), ctx: 4 (over x, core), tp: 2 (over y).
Axes of the slice: x: 2, y: 2, z: 4, core: 2. Of those that a mesh axis runs over, the one named last changes fastest.
Arguments:
- tokens: bfloat16 [4, 2176, 1536], P('fsdp', ('ctx', 'tp')), may hold values from -30 to 30
- segment_ids: int32 [4, 2176], P('fsdp', 'ctx'), may hold values from 0 to 7, never falling along the last dimension, each value on 1 to 1088 neighbouring positions
- wq: bfloat16 [1536, 1536], P('fsdp', 'tp'), may hold values from -0.15625 to 0.15625
- wk: bfloat16 [1536, 1536], P('fsdp', 'tp'), may hold values from -0.15625 to 0.15625
- wv: bfloat16 [1536, 1536], P('fsdp', 'tp'), may hold values from -0.15625 to 0.15625
- wo: bfloat16 [1536, 1536], P('tp', 'fsdp'), may hold values from -0.875 to 0.875
- w_gate: bfloat16 [1536, 4096], P('fsdp', 'tp'), may hold values from -0.15625 to 0.15625
- w_up: bfloat16 [1536, 4096], P('fsdp', 'tp'), may hold values from -0.15625 to 0.15625
- w_down: bfloat16 [4096, 1536], P('tp', 'fsdp'), may hold values from -0.09375 to 0.09375
- gain_attn: bfloat16 [1536], P('fsdp'), may hold values from 0.099609375 to 1.8984375
- gain_ffn: bfloat16 [1536], P('fsdp'), may hold values from 0.099609375 to 1.8984375
- cotangent: bfloat16 [4, 2176, 1536], P('fsdp', ('ctx', 'tp')), may hold values from -6 to 6
Outputs:
- layer_out: bfloat16 [4, 2176, 1536], P('fsdp', ('ctx', 'tp'))
- grad_input: float32 [4, 2176, 1536], P('fsdp', ('ctx', 'tp'))
- query_weight_gradient: float32 [1536, 1536], P('fsdp', 'tp')
- key_weight_gradient: float32 [1536, 1536], P('fsdp', 'tp')
- value_weight_gradient: float32 [1536, 1536], P('fsdp', 'tp')
- output_weight_gradient: float32 [1536, 1536], P('tp', 'fsdp')
- gate_weight_gradient: float32 [1536, 4096], P('fsdp', 'tp')
- up_weight_gradient: float32 [1536, 4096], P('fsdp', 'tp')
- down_weight_gradient: float32 [4096, 1536], P('tp', 'fsdp')
- grad_gain_attn: float32 [1536], P('fsdp')
- grad_gain_ffn: float32 [1536], P('fsdp')
Inputs may be any that keep to these rules, and one draw needn't show every extreme that they name: `segment_ids`: within each sequence the ids never fall; each document holds 1 to 1088 positions, and one document of every sequence holds exactly 1088.
All inputs are finite; a program needn't handle non-finite values.
Results may differ from a plain program's by a relative error of at most 0.024.
Values may be sent and summed in bfloat16 or wider, within the bound.
No kernel may reach another device: no remote copies, remote signals or barrier semaphores. Data moves between devices by JAX's collectives and lax.ppermute only.
A program may use at most 320 MiB of HBM per device.

v0:
```python
import jax
import jax.numpy as jnp
from jax import lax
from jax.sharding import PartitionSpec as P

HEAD_DIM = 64


epsilon = 1e-05
masked_score = -1e30


def widen_rows(values):
    return lax.all_gather(values, "tp", axis=1, tiled=True)


def narrow_rows(values):
    return lax.psum_scatter(
        values.astype(jnp.bfloat16), "tp", scatter_dimension=1, tiled=True
    ).astype(jnp.float32)


def fold_keys(fetched_keys, step_fn, start_carry):
    return step_fn(
        start_carry,
        (
            lax.all_gather(fetched_keys[0], "ctx", axis=1, tiled=True),
            lax.all_gather(fetched_keys[1], "ctx", axis=1, tiled=True),
            lax.all_gather(fetched_keys[2], "ctx", axis=1, tiled=True),
        ),
        jnp.int32(0),
    )


def rope_tables(offset, row_count, half_dim):
    where_at = (offset + jnp.arange(row_count, dtype=jnp.int32)).astype(jnp.float32)
    inv_freq = 10000.0 ** (-jnp.arange(half_dim, dtype=jnp.float32) * 2.0 / (2 * half_dim))
    angles = where_at[:, None] * inv_freq[None, :]
    return (jnp.cos(angles), jnp.sin(angles))


def rotate(values, cos_rows, sin_rows, direction):
    half_dim = values.shape[-1] // 2
    first_half = values[..., :half_dim]
    second_half = values[..., half_dim:]
    cos_part = cos_rows[None, :, None, :]
    sin_part = sin_rows[None, :, None, :] * direction
    return jnp.concatenate(
        [
            first_half * cos_part - second_half * sin_part,
            second_half * cos_part + first_half * sin_part,
        ],
        axis=-1,
    )


def split_heads(values, head_count):
    return values.reshape(
        values.shape[0], values.shape[1], head_count, values.shape[2] // head_count
    )


def normalize_back(values, inverse, gain, grad_rows):
    scaled = grad_rows * gain
    return inverse * scaled - values * inverse**3 * jnp.mean(
        scaled * values, axis=-1, keepdims=True
    )


def masked_scores(query_seq, key_seq, seg_query, seg_key, pos_query, pos_key, score_scale):
    scores = (
        jnp.einsum("qhd,khd->hqk", query_seq, key_seq, preferred_element_type=jnp.float32)
        * score_scale
    )
    allowed = (seg_query[:, None] == seg_key[None, :]) & (pos_key[None, :] <= pos_query[:, None])
    return (scores, allowed[None])


def grad_parts(
    query_seq,
    key_seq,
    value_seq,
    seg_query,
    seg_key,
    pos_query,
    pos_key,
    grad_seq,
    logsum_seq,
    delta_seq,
    score_scale,
):
    scores, allowed = masked_scores(
        query_seq, key_seq, seg_query, seg_key, pos_query, pos_key, score_scale
    )
    soft_weights = jnp.where(allowed, jnp.exp(scores - jnp.transpose(logsum_seq)[:, :, None]), 0.0)
    prob_grad = jnp.einsum("qhd,khd->hqk", grad_seq, value_seq, preferred_element_type=jnp.float32)
    score_grad = (soft_weights * (prob_grad - jnp.transpose(delta_seq)[:, :, None])).astype(
        jnp.bfloat16
    )
    query_add = (
        jnp.einsum("hqk,khd->qhd", score_grad, key_seq, preferred_element_type=jnp.float32)
        * score_scale
    )
    key_add = (
        jnp.einsum("hqk,qhd->khd", score_grad, query_seq, preferred_element_type=jnp.float32)
        * score_scale
    )
    value_add = jnp.einsum(
        "hqk,qhd->khd",
        soft_weights.astype(jnp.bfloat16),
        grad_seq,
        preferred_element_type=jnp.float32,
    )
    return (query_add, key_add, value_add)


def shards(
    tokens, segment_ids, wq, wk, wv, wo, w_gate, w_up, w_down, gain_attn, gain_ffn, cotangent
):
    (
        query_weight_whole,
        key_weight_whole,
        value_weight_whole,
        output_weight_whole,
        gate_weight_whole,
        up_weight_whole,
        down_weight_whole,
        gain_first,
        gain_second,
    ) = (
        lax.all_gather(wq, "fsdp", axis=0, tiled=True),
        lax.all_gather(wk, "fsdp", axis=0, tiled=True),
        lax.all_gather(wv, "fsdp", axis=0, tiled=True),
        lax.all_gather(wo, "fsdp", axis=1, tiled=True),
        lax.all_gather(w_gate, "fsdp", axis=0, tiled=True),
        lax.all_gather(w_up, "fsdp", axis=0, tiled=True),
        lax.all_gather(w_down, "fsdp", axis=1, tiled=True),
        lax.all_gather(gain_attn, "fsdp", axis=0, tiled=True),
        lax.all_gather(gain_ffn, "fsdp", axis=0, tiled=True),
    )
    gain_one = gain_first.astype(jnp.float32)
    gain_two = gain_second.astype(jnp.float32)
    head_count = query_weight_whole.shape[1] // HEAD_DIM
    row_width = query_weight_whole.shape[1]
    score_scale = HEAD_DIM ** (-0.5)
    seq_count = tokens.shape[0]
    ctx_rows = segment_ids.shape[1]
    ctx_count = lax.axis_size("ctx")
    first_query = lax.axis_index("ctx") * ctx_rows
    last_query = first_query + ctx_rows - 1
    pos_own = first_query + jnp.arange(ctx_rows, dtype=jnp.int32)
    cos_rows, sin_rows = rope_tables(first_query, ctx_rows, HEAD_DIM // 2)
    inputs = tokens.astype(jnp.float32)
    inv_one = lax.rsqrt(jnp.mean(inputs * inputs, axis=-1, keepdims=True) + epsilon)
    normalized_input = widen_rows((inputs * inv_one * gain_one).astype(jnp.bfloat16))
    queries = rotate(
        split_heads(
            jnp.dot(normalized_input, query_weight_whole, preferred_element_type=jnp.float32),
            head_count,
        ),
        cos_rows,
        sin_rows,
        1.0,
    ).astype(jnp.bfloat16)
    keys_rot = rotate(
        split_heads(
            jnp.dot(normalized_input, key_weight_whole, preferred_element_type=jnp.float32),
            head_count,
        ),
        cos_rows,
        sin_rows,
        1.0,
    ).astype(jnp.bfloat16)
    values_h = split_heads(
        jnp.dot(normalized_input, value_weight_whole, preferred_element_type=jnp.float32),
        head_count,
    ).astype(jnp.bfloat16)
    sent_keys = (
        keys_rot.reshape(seq_count, ctx_rows, row_width),
        values_h.reshape(seq_count, ctx_rows, row_width),
        segment_ids,
    )

    def forward_step(current, fetched, offset):
        piece_rows = fetched[0].shape[1]
        pos_keys = jnp.arange(piece_rows, dtype=jnp.int32)

        def forward_compute(running):

            def forward_per_seq(member):
                (
                    query_seq,
                    key_seq,
                    value_seq,
                    seg_query,
                    seg_key,
                    running_max,
                    running_sum,
                    weighted,
                ) = member
                scores, allowed = masked_scores(
                    query_seq, key_seq, seg_query, seg_key, pos_own, pos_keys, score_scale
                )
                scores = jnp.where(allowed, scores, masked_score)
                new_max = jnp.maximum(running_max, jnp.max(scores, axis=-1))
                factor = jnp.exp(running_max - new_max)
                exp_scores = jnp.where(allowed, jnp.exp(scores - new_max[:, :, None]), 0.0)
                new_sum = running_sum * factor + jnp.sum(exp_scores, axis=-1)
                new_weighted = weighted * factor[:, :, None] + jnp.einsum(
                    "hqk,khd->hqd",
                    exp_scores.astype(jnp.bfloat16),
                    value_seq,
                    preferred_element_type=jnp.float32,
                )
                return (new_max, new_sum, new_weighted)

            return lax.map(
                forward_per_seq,
                (
                    queries,
                    split_heads(fetched[0], head_count),
                    split_heads(fetched[1], head_count),
                    segment_ids,
                    fetched[2],
                    running[0],
                    running[1],
                    running[2],
                ),
            )

        return lax.cond(offset <= last_query, forward_compute, lambda running: running, current)

    start_max = jnp.full((seq_count, head_count, ctx_rows), masked_score, jnp.float32)
    start_sum = jnp.zeros((seq_count, head_count, ctx_rows), jnp.float32)
    start_weighted = jnp.zeros((seq_count, head_count, ctx_rows, HEAD_DIM), jnp.float32)
    final_max, final_sum, final_weighted = fold_keys(
        sent_keys, forward_step, (start_max, start_sum, start_weighted)
    )
    attended = jnp.transpose(final_weighted / final_sum[..., None], (0, 2, 1, 3))
    log_sums = jnp.transpose(final_max + jnp.log(final_sum), (0, 2, 1))
    attended_reduced = attended.astype(jnp.bfloat16).reshape(seq_count, ctx_rows, row_width)
    residual = inputs + narrow_rows(
        jnp.dot(attended_reduced, output_weight_whole, preferred_element_type=jnp.float32)
    )
    inv_two = lax.rsqrt(jnp.mean(residual * residual, axis=-1, keepdims=True) + epsilon)
    normalized_second = widen_rows((residual * inv_two * gain_two).astype(jnp.bfloat16))
    gate_pre = jnp.dot(normalized_second, gate_weight_whole, preferred_element_type=jnp.float32)
    up_pre = jnp.dot(normalized_second, up_weight_whole, preferred_element_type=jnp.float32)
    hidden_state = (jax.nn.silu(gate_pre) * up_pre).astype(jnp.bfloat16)
    layer_out = residual + narrow_rows(
        jnp.dot(hidden_state, down_weight_whole, preferred_element_type=jnp.float32)
    )
    grad_out = cotangent.astype(jnp.float32)
    feedforward_gradient = widen_rows(cotangent)
    down_weight_gradient = jnp.einsum(
        "ehu,ehx->ux", hidden_state, feedforward_gradient, preferred_element_type=jnp.float32
    )
    hidden_gradient = jnp.einsum(
        "gor,zr->goz", feedforward_gradient, down_weight_whole, preferred_element_type=jnp.float32
    )
    sigmoid_gate = jax.nn.sigmoid(gate_pre)
    gate_gradient = (
        hidden_gradient * up_pre * sigmoid_gate * (1.0 + gate_pre * (1.0 - sigmoid_gate))
    ).astype(jnp.bfloat16)
    up_gradient = (hidden_gradient * gate_pre * sigmoid_gate).astype(jnp.bfloat16)
    gate_weight_gradient = jnp.einsum(
        "vij,viz->jz", normalized_second, gate_gradient, preferred_element_type=jnp.float32
    )
    up_weight_gradient = jnp.einsum(
        "vij,viz->jz", normalized_second, up_gradient, preferred_element_type=jnp.float32
    )
    normed_two_grad = narrow_rows(
        jnp.einsum(
            "xmv,hv->xmh", gate_gradient, gate_weight_whole, preferred_element_type=jnp.float32
        )
        + jnp.einsum(
            "xmv,hv->xmh", up_gradient, up_weight_whole, preferred_element_type=jnp.float32
        )
    )
    gain_two_grad = jnp.sum(normed_two_grad * residual * inv_two, axis=(0, 1))
    resid_grad = grad_out + normalize_back(residual, inv_two, gain_two, normed_two_grad)
    attention_gradient = widen_rows(resid_grad.astype(jnp.bfloat16))
    output_weight_gradient = jnp.einsum(
        "krx,kru->xu", attended_reduced, attention_gradient, preferred_element_type=jnp.float32
    )
    out_grad = jnp.einsum(
        "fvk,hk->fvh", attention_gradient, output_weight_whole, preferred_element_type=jnp.float32
    ).astype(jnp.bfloat16)
    out_grad_h = split_heads(out_grad, head_count)
    delta_rows = jnp.sum(out_grad_h.astype(jnp.float32) * attended, axis=-1)
    zero_own = jnp.zeros((seq_count, ctx_rows, head_count, HEAD_DIM), jnp.float32)
    zero_all = jnp.zeros((seq_count, ctx_count * ctx_rows, head_count, HEAD_DIM), jnp.float32)

    def back_step(current, fetched, offset):
        piece_rows = fetched[0].shape[1]
        pos_keys = jnp.arange(piece_rows, dtype=jnp.int32)

        def back_compute(running):

            def back_per_seq(member):
                (
                    query_seq,
                    key_seq,
                    value_seq,
                    seg_query,
                    seg_key,
                    grad_seq,
                    logsum_seq,
                    delta_seq,
                ) = member
                return grad_parts(
                    query_seq,
                    key_seq,
                    value_seq,
                    seg_query,
                    seg_key,
                    pos_own,
                    pos_keys,
                    grad_seq,
                    logsum_seq,
                    delta_seq,
                    score_scale,
                )

            query_add, key_add, value_add = lax.map(
                back_per_seq,
                (
                    queries,
                    split_heads(fetched[0], head_count),
                    split_heads(fetched[1], head_count),
                    segment_ids,
                    fetched[2],
                    out_grad_h,
                    log_sums,
                    delta_rows,
                ),
            )
            key_old = running[1]
            value_old = running[2]
            return (query_add, key_add, value_add)

        return lax.cond(offset <= last_query, back_compute, lambda running: running, current)

    query_grad, key_all, value_all = fold_keys(sent_keys, back_step, (zero_own, zero_all, zero_all))
    key_grad, value_grad = (
        lax.psum_scatter(
            key_all.astype(jnp.bfloat16), "ctx", scatter_dimension=1, tiled=True
        ).astype(jnp.float32),
        lax.psum_scatter(
            value_all.astype(jnp.bfloat16), "ctx", scatter_dimension=1, tiled=True
        ).astype(jnp.float32),
    )
    query_gradient_reduced = (
        rotate(query_grad, cos_rows, sin_rows, -1.0)
        .astype(jnp.bfloat16)
        .reshape(seq_count, ctx_rows, row_width)
    )
    key_gradient_reduced = (
        rotate(key_grad, cos_rows, sin_rows, -1.0)
        .astype(jnp.bfloat16)
        .reshape(seq_count, ctx_rows, row_width)
    )
    value_gradient_reduced = value_grad.astype(jnp.bfloat16).reshape(seq_count, ctx_rows, row_width)
    query_weight_gradient = jnp.einsum(
        "zky,zkn->yn", normalized_input, query_gradient_reduced, preferred_element_type=jnp.float32
    )
    key_weight_gradient = jnp.einsum(
        "zky,zkn->yn", normalized_input, key_gradient_reduced, preferred_element_type=jnp.float32
    )
    value_weight_gradient = jnp.einsum(
        "zky,zkn->yn", normalized_input, value_gradient_reduced, preferred_element_type=jnp.float32
    )
    normed_grad = narrow_rows(
        jnp.einsum(
            "cxp,up->cxu",
            query_gradient_reduced,
            query_weight_whole,
            preferred_element_type=jnp.float32,
        )
        + jnp.einsum(
            "cxp,up->cxu",
            key_gradient_reduced,
            key_weight_whole,
            preferred_element_type=jnp.float32,
        )
        + jnp.einsum(
            "cxp,up->cxu",
            value_gradient_reduced,
            value_weight_whole,
            preferred_element_type=jnp.float32,
        )
    )
    gain_one_grad = jnp.sum(normed_grad * inputs * inv_one, axis=(0, 1))
    grad_input = resid_grad + normalize_back(inputs, inv_one, gain_one, normed_grad)
    gain_one_total, gain_two_total = lax.psum((gain_one_grad, gain_two_grad), "tp")
    share_q, share_k, share_v, share_o, share_gate, share_up, share_down, share_one, share_two = (
        lax.psum_scatter(
            query_weight_gradient.astype(jnp.bfloat16), "fsdp", scatter_dimension=0, tiled=True
        ).astype(jnp.float32),
        lax.psum_scatter(
            key_weight_gradient.astype(jnp.bfloat16), "fsdp", scatter_dimension=0, tiled=True
        ).astype(jnp.float32),
        lax.psum_scatter(
            value_weight_gradient.astype(jnp.bfloat16), "fsdp", scatter_dimension=0, tiled=True
        ).astype(jnp.float32),
        lax.psum_scatter(
            output_weight_gradient.astype(jnp.bfloat16), "fsdp", scatter_dimension=1, tiled=True
        ).astype(jnp.float32),
        lax.psum_scatter(
            gate_weight_gradient.astype(jnp.bfloat16), "fsdp", scatter_dimension=0, tiled=True
        ).astype(jnp.float32),
        lax.psum_scatter(
            up_weight_gradient.astype(jnp.bfloat16), "fsdp", scatter_dimension=0, tiled=True
        ).astype(jnp.float32),
        lax.psum_scatter(
            down_weight_gradient.astype(jnp.bfloat16), "fsdp", scatter_dimension=1, tiled=True
        ).astype(jnp.float32),
        lax.psum_scatter(
            gain_one_total.astype(jnp.bfloat16), "fsdp", scatter_dimension=0, tiled=True
        ).astype(jnp.float32),
        lax.psum_scatter(
            gain_two_total.astype(jnp.bfloat16), "fsdp", scatter_dimension=0, tiled=True
        ).astype(jnp.float32),
    )
    final_q, final_k, final_v, final_o, final_gate, final_up, final_down, final_one, final_two = (
        lax.psum(share_q.astype(jnp.bfloat16), "ctx").astype(jnp.float32),
        lax.psum(share_k.astype(jnp.bfloat16), "ctx").astype(jnp.float32),
        lax.psum(share_v.astype(jnp.bfloat16), "ctx").astype(jnp.float32),
        lax.psum(share_o.astype(jnp.bfloat16), "ctx").astype(jnp.float32),
        lax.psum(share_gate.astype(jnp.bfloat16), "ctx").astype(jnp.float32),
        lax.psum(share_up.astype(jnp.bfloat16), "ctx").astype(jnp.float32),
        lax.psum(share_down.astype(jnp.bfloat16), "ctx").astype(jnp.float32),
        lax.psum(share_one.astype(jnp.bfloat16), "ctx").astype(jnp.float32),
        lax.psum(share_two.astype(jnp.bfloat16), "ctx").astype(jnp.float32),
    )
    return (
        layer_out.astype(jnp.bfloat16),
        grad_input,
        final_q,
        final_k,
        final_v,
        final_o,
        final_gate,
        final_up,
        final_down,
        final_one,
        final_two,
    )


def solution(mesh):
    placed = (
        P("fsdp", ("ctx", "tp"), None),
        P("fsdp", "ctx"),
        P("fsdp", "tp"),
        P("fsdp", "tp"),
        P("fsdp", "tp"),
        P("tp", "fsdp"),
        P("fsdp", "tp"),
        P("fsdp", "tp"),
        P("tp", "fsdp"),
        P("fsdp"),
        P("fsdp"),
        P("fsdp", ("ctx", "tp"), None),
    )
    return jax.shard_map(
        shards,
        mesh=mesh,
        in_specs=placed,
        out_specs=(
            P("fsdp", ("ctx", "tp"), None),
            P("fsdp", ("ctx", "tp"), None),
            P("fsdp", "tp"),
            P("fsdp", "tp"),
            P("fsdp", "tp"),
            P("tp", "fsdp"),
            P("fsdp", "tp"),
            P("fsdp", "tp"),
            P("tp", "fsdp"),
            P("fsdp"),
            P("fsdp"),
        ),
        check_vma=False,
    )
```

profile of v0, /device:TPU:1, one launch (start us, length us, event | category | flops | bytes accessed | tf_op | source)
XLA Modules:
  0.0 1856.5 jit_solution(2530010445152967488)
XLA Ops:
  25.3 36.8 %all-gather.24.cloned.1.call-done = bf16[1536,768]{1,0:T(8,128)(2,1)} async-done(((bf16[384,768]{1,0:T(8,128)(2,1)}), bf16[1536,768]{1,0:T(8,128)(2,1)}) %all-gather.24.cloned.1.call-update) | async-done | bytes 2359312 | tf_op jit(solution)/shard_map/all_gather | solution.py:133
  65.0 26.5 %all-gather.16.cloned.1.call-done = bf16[1,544,1536]{2,1,0:T(8,128)(2,1)} async-done(((bf16[1,272,1536]{2,1,0:T(8,128)(2,1)}), bf16[1,544,1536]{2,1,0:T(8,128)(2,1)}) %all-gather.16.cloned.1.call-update) | async-done | bytes 1671184 | tf_op jit(solution)/shard_map/all_gather | solution.py:14
  97.3 46.2 %all-gather.20.cloned.1.call-done = bf16[1536,768]{1,0:T(8,128)(2,1)} async-done(((bf16[384,768]{1,0:T(8,128)(2,1)}), bf16[1536,768]{1,0:T(8,128)(2,1)}) %all-gather.20.cloned.1.call-update) | async-done | bytes 2359312 | tf_op jit(solution)/shard_map/all_gather | solution.py:132
  146.4 47.9 %all-gather.18.cloned.1.call-done = bf16[1536,768]{1,0:T(8,128)(2,1)} async-done(((bf16[384,768]{1,0:T(8,128)(2,1)}), bf16[1536,768]{1,0:T(8,128)(2,1)}) %all-gather.18.cloned.1.call-update) | async-done | bytes 2359312 | tf_op jit(solution)/shard_map/all_gather | solution.py:131
  225.4 31.7 %all-gather.22.cloned.1.call-done = bf16[1,2176,768]{2,1,0:T(8,128)(2,1)} async-done(((bf16[1,544,768]{2,1,0:T(8,128)(2,1)}), bf16[1,2176,768]{2,1,0:T(8,128)(2,1)}) %all-gather.22.cloned.1.call-update) | async-done | bytes 3342352 | tf_op jit(solution)/shard_map/all_gather | solution.py:27
  257.1 82.4 %conditional.2 = (f32[1,12,544]{2,1,0:T(8,128)S(1)}, f32[1,12,544]{2,1,0:T(8,128)S(1)}, f32[1,12,544,64]{2,3,1,0:T(8,128)}, f32[1,12,544]{2,1,0:T(8,128)S(1)}) conditional(s32[]{:T(128)} %convert_element_type.279, () %tuple.37, (s32[1,544]{1,0:T(1,128)S(1)}, s32[1,2176]{1,0:T(1,128)S(1)}, s32[2176]{0:T(1024)S(1)}, s32[544]{0:T(1024)}, ...), branch_computations={%region_1.0_spmd, %region_2.5_spmd} | conditional | flops 3825127424 | bytes 198137888 | solution.py:231
  293.4 25.4 %add_bitcast_fusion = f32[1,12,544,64]{2,3,1,0:T(8,128)} fusion(bf16[2176,12,64]{0,2,1:T(8,128)(2,1)} %bitcast.179, f32[12,544,2176]{2,1,0:T(8,128)} %get-tuple-element.257, f32[12,544]{1,0:T(8,128)S(1)} %get-tuple-element.255, pred[544,2176]{1,0:T(8,128)(4,1)S(1)} %compare_and_fusion, f32[12,544]{1,0:T(8,128)S(1)} %get-tuple-element.254), kind=kOutput, calls=%fused_computation.8 | convolution fusion | flops 1889673216 | bytes 63069184 | tf_op jit(solution)/shard_map/cond/branch_1_fun/while/body/eval_jaxpr/hqk,khd->hqd/dot_general | solution.py:209
  380.4 111.7 %all-gather.34.cloned.1.call-done = bf16[1536,2048]{1,0:T(8,128)(2,1)} async-done(((bf16[384,2048]{1,0:T(8,128)(2,1)}), bf16[1536,2048]{1,0:T(8,128)(2,1)}) %all-gather.34.cloned.1.call-update) | async-done | bytes 6291472 | tf_op jit(solution)/shard_map/all_gather | solution.py:136
  492.1 28.3 %all-gather.30.cloned.1.call-done = bf16[1,544,1536]{2,1,0:T(8,128)(2,1)} async-done(((bf16[1,272,1536]{2,1,0:T(8,128)(2,1)}), bf16[1,544,1536]{2,1,0:T(8,128)(2,1)}) %all-gather.30.cloned.1.call-update) | async-done | bytes 1671184 | tf_op jit(solution)/shard_map/all_gather | solution.py:14
  529.4 108.1 %all-gather.32.cloned.1.call-done = bf16[1536,2048]{1,0:T(8,128)(2,1)} async-done(((bf16[384,2048]{1,0:T(8,128)(2,1)}), bf16[1536,2048]{1,0:T(8,128)(2,1)}) %all-gather.32.cloned.1.call-update) | async-done | bytes 6291472 | tf_op jit(solution)/shard_map/all_gather | solution.py:135
  665.3 117.2 %all-gather.36.cloned.1.call-done = bf16[2048,1536]{1,0:T(8,128)(2,1)} async-done(((bf16[2048,384]{1,0:T(8,128)(2,1)}), bf16[2048,1536]{1,0:T(8,128)(2,1)}) %all-gather.36.cloned.1.call-update) | async-done | bytes 6291472 | tf_op jit(solution)/shard_map/all_gather | solution.py:137
  804.9 25.3 %reduce-scatter.26.cloned.1.call-done = bf16[1,272,1536]{2,1,0:T(8,128)(2,1)} async-done(((bf16[1,544,1536]{2,1,0:T(8,128)(2,1)}), bf16[1,272,1536]{2,1,0:T(8,128)(2,1)}) %reduce-scatter.26.cloned.1.call-update) | async-done | bytes 835600 | tf_op jit(solution)/shard_map/reduce_scatter | solution.py:18
  836.3 27.6 %all-gather.40.cloned.1.call-done = bf16[1,544,1536]{2,1,0:T(8,128)(2,1)} async-done(((bf16[1,272,1536]{2,1,0:T(8,128)(2,1)}), bf16[1,544,1536]{2,1,0:T(8,128)(2,1)}) %all-gather.40.cloned.1.call-update) | async-done | bytes 1671184 | tf_op jit(solution)/shard_map/all_gather | solution.py:14
  867.6 127.4 %conditional.3 = (bf16[1,2176,12,64]{1,3,2,0:T(8,128)(2,1)}, bf16[1,2176,12,64]{1,3,2,0:T(8,128)(2,1)}, f32[1,544,12,32]{1,3,2,0:T(8,128)}, f32[1,544,12,32]{1,3,2,0:T(8,128)}) conditional(s32[]{:T(128)} %convert_element_type.279, () %tuple.39, (s32[1,544]{1,0:T(1,128)S(1)}, s32[1,2176]{1,0:T(1,128)S(1)}, s32[2176]{0:T(1024)S(1)}, s32[544]{0:T(1024)}, ...), branch_computations={%region_10.11_spmd, %region_11.13_spmd} | conditional | flops 9241761792 | bytes 308687424 | solution.py:342
  907.3 23.5 %fusion.18 = bf16[1,2176,12,64]{1,3,2,0:T(8,128)(2,1)} fusion(bf16[544,12,64]{0,2,1:T(8,128)(2,1)S(1)} %bitcast.174, f32[12,544,2176]{2,1,0:T(8,128)} %fusion.23, f32[12,544]{1,0:T(8,128)S(1)} %bitcast.196, pred[544,2176]{1,0:T(8,128)(4,1)} %compare_and_fusion.1), kind=kOutput, calls=%fused_computation.24 | convolution fusion | flops 1875050496 | bytes 62207488 | tf_op jit(solution)/shard_map/cond/branch_1_fun/while/body/eval_jaxpr/hqk,qhd->khd/dot_general | solution.py:108
  930.8 34.0 %multiply_convert_fusion = bf16[12,544,2176]{2,1,0:T(8,128)(2,1)} fusion(f32[12,544,2176]{2,1,0:T(8,128)} %fusion.23, bf16[544,12,64]{0,2,1:T(8,128)(2,1)S(1)} %bitcast.175, bf16[2176,12,64]{0,2,1:T(8,128)(2,1)} %bitcast.180, f32[12,544]{1,0:T(8,128)S(1)} %bitcast.198, f32[12,544]{1,0:T(8,128)S(1)} %bitcast.197, pred[544,2176]{1,0:T(8,128)(4,1)} %compare_and_fusion.1), kind=kOutput, calls=%fused_computation.18 | convolution fusion | flops 1903460352 | bytes 90643456 | tf_op jit(solution)/shard_map/cond/branch_1_fun/while/body/eval_jaxpr/qhd,khd->hqk/dot_general | solution.py:96
  1151.3 110.7 %reduce-scatter.46.cloned.1.call-done = bf16[384,2048]{1,0:T(8,128)(2,1)} async-done(((bf16[1536,2048]{1,0:T(8,128)(2,1)}), bf16[384,2048]{1,0:T(8,128)(2,1)}) %reduce-scatter.46.cloned.1.call-update) | async-done | bytes 1572880
  1264.6 110.9 %reduce-scatter.38.cloned.1.call-done = bf16[384,2048]{1,0:T(8,128)(2,1)} async-done(((bf16[1536,2048]{1,0:T(8,128)(2,1)}), bf16[384,2048]{1,0:T(8,128)(2,1)}) %reduce-scatter.38.cloned.1.call-update) | async-done | bytes 1572880 | tf_op jit(solution)/shard_map/reduce_scatter | solution.py:412
  1375.5 113.6 %reduce-scatter.36.cloned.1.call-done = bf16[384,2048]{1,0:T(8,128)(2,1)} async-done(((bf16[1536,2048]{1,0:T(8,128)(2,1)}), bf16[384,2048]{1,0:T(8,128)(2,1)}) %reduce-scatter.36.cloned.1.call-update) | async-done | bytes 1572880 | tf_op jit(solution)/shard_map/reduce_scatter | solution.py:409
  1489.1 51.3 %reduce-scatter.30.cloned.1.call-done = bf16[384,768]{1,0:T(8,128)(2,1)} async-done(((bf16[1536,768]{1,0:T(8,128)(2,1)}), bf16[384,768]{1,0:T(8,128)(2,1)}) %reduce-scatter.30.cloned.1.call-update) | async-done | bytes 589840 | tf_op jit(solution)/shard_map/reduce_scatter | solution.py:397
  1540.4 50.4 %reduce-scatter.32.cloned.1.call-done = bf16[384,768]{1,0:T(8,128)(2,1)} async-done(((bf16[1536,768]{1,0:T(8,128)(2,1)}), bf16[384,768]{1,0:T(8,128)(2,1)}) %reduce-scatter.32.cloned.1.call-update) | async-done | bytes 589840 | tf_op jit(solution)/shard_map/reduce_scatter | solution.py:400
  1590.8 50.3 %reduce-scatter.34.cloned.1.call-done = bf16[384,768]{1,0:T(8,128)(2,1)} async-done(((bf16[1536,768]{1,0:T(8,128)(2,1)}), bf16[384,768]{1,0:T(8,128)(2,1)}) %reduce-scatter.34.cloned.1.call-update) | async-done | bytes 589840 | tf_op jit(solution)/shard_map/reduce_scatter | solution.py:403
  1643.0 27.8 %reduce-scatter.28.cloned.1.call-done = bf16[1,272,1536]{2,1,0:T(8,128)(2,1)} async-done(((bf16[1,544,1536]{2,1,0:T(8,128)(2,1)}), bf16[1,272,1536]{2,1,0:T(8,128)(2,1)}) %reduce-scatter.28.cloned.1.call-update) | async-done | bytes 835600 | tf_op jit(solution)/shard_map/reduce_scatter | solution.py:18
  1704.2 132.3 %all-reduce.9.cloned.1.call-done = (bf16[384,768]{1,0:T(8,128)(2,1)}, bf16[384,768]{1,0:T(8,128)(2,1)}, bf16[384,768]{1,0:T(8,128)(2,1)}, bf16[768,384]{1,0:T(8,...) async-done(((bf16[384,768]{1,0:T(8,128)(2,1)}, bf16[384,768]{1,0:T(8,128)(2,1)}, bf16[384,768]{1,0:T(8,128)(2,1)}, ...) | async-done | bytes 7077904 | tf_op jit(solution)/shard_map/psum | solution.py:426
  (281 shorter events, 502.2 us)
Async XLA Ops:
  24.0 119.5 %all-gather.20.cloned.1.call-start = ((), (), s32[]{:S(2)}) async-start(), calls=%async_computation.15 | async-start | bytes 2949120 | tf_op jit(solution)/shard_map/all_gather | solution.py:132
  24.7 169.6 %all-gather.18.cloned.1.call-start = ((), (), s32[]{:S(2)}) async-start(), calls=%async_computation.14 | async-start | bytes 2949120 | tf_op jit(solution)/shard_map/all_gather | solution.py:131
  25.3 200.1 %all-gather.26.cloned.1.call-start = ((), (), s32[]{:S(2)}) async-start(), calls=%async_computation.18 | async-start | bytes 4177920 | tf_op jit(solution)/shard_map/all_gather | solution.py:28
  96.2 160.9 %all-gather.22.cloned.1.call-start = ((), (), s32[]{:S(2)}) async-start(), calls=%async_computation.16 | async-start | bytes 4177920 | tf_op jit(solution)/shard_map/all_gather | solution.py:27
  206.2 136.5 %all-gather.28.cloned.1.call-start = ((), (), s32[]{:S(2)}) async-start(), calls=%async_computation.19 | async-start | bytes 2949120 | tf_op jit(solution)/shard_map/all_gather | solution.py:134
  207.0 167.9 %reduce-scatter.22.cloned.1.call-start = ((), (), s32[]{:S(2)}) async-start(), calls=%async_computation.20 | async-start | bytes 2506752 | tf_op jit(solution)/shard_map/reduce_scatter | solution.py:18
  348.0 144.1 %all-gather.34.cloned.1.call-start = ((), (), s32[]{:S(2)}) async-start(), calls=%async_computation.23 | async-start | bytes 7864320 | tf_op jit(solution)/shard_map/all_gather | solution.py:136
  348.7 171.7 %all-gather.30.cloned.1.call-start = ((), (), s32[]{:S(2)}) async-start(), calls=%async_computation.21 | async-start | bytes 2506752 | tf_op jit(solution)/shard_map/all_gather | solution.py:14
  378.3 259.3 %all-gather.32.cloned.1.call-start = ((), (), s32[]{:S(2)}) async-start(), calls=%async_computation.22 | async-start | bytes 7864320 | tf_op jit(solution)/shard_map/all_gather | solution.py:135
  379.0 286.3 %all-gather.38.cloned.1.call-start = ((), (), s32[]{:S(2)}) async-start(), calls=%async_computation.26 | async-start | bytes 2506752 | tf_op jit(solution)/shard_map/all_gather | solution.py:14
  379.6 402.9 %all-gather.36.cloned.1.call-start = ((), (), s32[]{:S(2)}) async-start(), calls=%async_computation.24 | async-start | bytes 7864320 | tf_op jit(solution)/shard_map/all_gather | solution.py:137
  380.3 449.8 %reduce-scatter.26.cloned.1.call-start = ((), (), s32[]{:S(2)}) async-start(), calls=%async_computation.27 | async-start | bytes 2506752 | tf_op jit(solution)/shard_map/reduce_scatter | solution.py:18
  835.4 251.8 %reduce-scatter.40.cloned.1.call-start = ((), (), s32[]{:S(2)}) async-start(), calls=%async_computation.35 | async-start | bytes 4177920
  1018.0 87.2 %reduce-scatter.42.cloned.1.call-start = ((), (), s32[]{:S(2)}) async-start(), calls=%async_computation.36 | async-start | bytes 4177920
  1041.3 107.9 %reduce-scatter.44.cloned.1.call-start = ((), (), s32[]{:S(2)}) async-start(), calls=%async_computation.37 | async-start | bytes 2949120
  1048.4 213.6 %reduce-scatter.46.cloned.1.call-start = ((), (), s32[]{:S(2)}) async-start(), calls=%async_computation.38 | async-start | bytes 7864320
  1067.7 307.8 %reduce-scatter.38.cloned.1.call-start = ((), (), s32[]{:S(2)}) async-start(), calls=%async_computation.34 | async-start | bytes 7864320 | tf_op jit(solution)/shard_map/reduce_scatter | solution.py:412
  1078.4 410.7 %reduce-scatter.36.cloned.1.call-start = ((), (), s32[]{:S(2)}) async-start(), calls=%async_computation.33 | async-start | bytes 7864320 | tf_op jit(solution)/shard_map/reduce_scatter | solution.py:409
  1087.2 453.1 %reduce-scatter.30.cloned.1.call-start = ((), (), s32[]{:S(2)}) async-start(), calls=%async_computation.30 | async-start | bytes 2949120 | tf_op jit(solution)/shard_map/reduce_scatter | solution.py:397
  1101.6 489.2 %reduce-scatter.32.cloned.1.call-start = ((), (), s32[]{:S(2)}) async-start(), calls=%async_computation.31 | async-start | bytes 2949120 | tf_op jit(solution)/shard_map/reduce_scatter | solution.py:400
  1105.1 536.0 %reduce-scatter.34.cloned.1.call-start = ((), (), s32[]{:S(2)}) async-start(), calls=%async_computation.32 | async-start | bytes 2949120 | tf_op jit(solution)/shard_map/reduce_scatter | solution.py:403
  1115.6 555.2 %reduce-scatter.28.cloned.1.call-start = ((), (), s32[]{:S(2)}) async-start(), calls=%async_computation.29 | async-start | bytes 2506752 | tf_op jit(solution)/shard_map/reduce_scatter | solution.py:18
  1125.4 574.7 %reduce-scatter.24.cloned.1.call-start = ((), (), s32[]{:S(2)}) async-start(), calls=%async_computation.25 | async-start | bytes 2506752 | tf_op jit(solution)/shard_map/reduce_scatter | solution.py:18
  1133.0 703.6 %all-reduce.9.cloned.1.call-start = ((), (), s32[]{:S(2)}) async-start(), calls=%async_computation.39 | async-start | bytes 14155776 | tf_op jit(solution)/shard_map/psum | solution.py:426
  (56 other events, 2023.1 us)
Sparse Core Ops, SparseCore 0:
  9.6 52.5 all-gather.23
  64.3 27.1 all-gather.15
  93.0 50.4 all-gather.19
  144.9 49.2 all-gather.17
  196.2 29.1 all-gather.25
  227.4 29.6 all-gather.21
  258.7 49.8 all-gather.27
  348.1 26.7 reduce-scatter.21
  376.4 115.5 all-gather.33
  522.0 115.5 all-gather.31
  666.9 115.5 all-gather.35
  835.6 28.3 all-gather.39
  1018.1 39.1 reduce-scatter.39
  1059.9 39.1 reduce-scatter.41
  1101.3 47.8 reduce-scatter.43
  1151.5 110.4 reduce-scatter.45
  1264.2 111.2 reduce-scatter.37
  1377.8 111.2 reduce-scatter.35
  1492.0 48.3 reduce-scatter.29
  1543.2 47.5 reduce-scatter.31
  1593.5 47.5 reduce-scatter.33
  1643.9 26.7 reduce-scatter.27
  1672.9 27.1 reduce-scatter.23
  1703.3 133.1 all-reduce.8
  (3 shorter events, 77.6 us)
where the time goes:
time: 1870 us; the launch traced here: 1860 us
  waiting for transfers between devices  1320 us (71%)
  matrix products  274 us (15%)
  local copies, waits for them, and re-layouts  123 us (7%)
  other arithmetic  67.9 us (4%)
  blocking collectives  55.1 us (3%)
    unnamed x31, waiting for transfers between devices  132 us
    psum x1, waiting for transfers between devices, shards(): lax.psum(share_q.astype(jnp.bfloat16), 'ctx').astype(jnp.float32)  132 us
    all_gather x1, waiting for transfers between devices, shards(): lax.all_gather(w_down, 'fsdp', axis=1, tiled=True)  117 us
    reduce_scatter x1, waiting for transfers between devices, shards(): lax.psum_scatter(gate_weight_gradient.astype(jnp.bfloat16), 'fsdp', scatt...  114 us
    all_gather x1, waiting for transfers between devices, shards(): lax.all_gather(w_up, 'fsdp', axis=0, tiled=True)  112 us
    reduce_scatter x1, waiting for transfers between devices, shards(): lax.psum_scatter(up_weight_gradient.astype(jnp.bfloat16), 'fsdp', scatter...  111 us
    all_gather x1, waiting for transfers between devices, shards(): lax.all_gather(w_gate, 'fsdp', axis=0, tiled=True)  108 us
    all_gather x4, waiting for transfers between devices, widen_rows(): return lax.all_gather(values, 'tp', axis=1, tiled=True)  101 us
  transfers between devices with their start and end apart: 27, of which 24 were waited for; matrix products, arithmetic and copies ran while one was open for 14% of the time, Pallas kernels for 0%

commit v1 on v0

v1 whole, which is shorter than its diff:
```python
import jax
import jax.numpy as jnp
from jax import lax
from jax.sharding import PartitionSpec as P

HEAD_DIM = 64
EPSILON = 1e-05
MASKED = -1e30
BF16 = jnp.bfloat16
F32 = jnp.float32


def pull_fsdp(values, step):
    count = lax.axis_size("fsdp")
    return lax.ppermute(values, "fsdp", [(i, (i - step) % count) for i in range(count)])


def push_fsdp(values, step):
    count = lax.axis_size("fsdp")
    return lax.ppermute(values, "fsdp", [(i, (i + step) % count) for i in range(count)])


def swap_chip(values):
    return lax.ppermute(values, "ctx", [(i, i ^ 2) for i in range(lax.axis_size("ctx"))])


def swap_core(values):
    return lax.ppermute(values, "ctx", [(i, i ^ 1) for i in range(lax.axis_size("ctx"))])


def widen_rows(values):
    if lax.axis_size("tp") != 2:
        return lax.all_gather(values, "tp", axis=0, tiled=True)
    other = lax.ppermute(values, "tp", [(0, 1), (1, 0)])
    first = lax.axis_index("tp") == 0
    return jnp.concatenate([jnp.where(first, values, other), jnp.where(first, other, values)], axis=0)


def narrow_rows(values):
    count = lax.axis_size("tp")
    if count != 2:
        return lax.psum_scatter(values.astype(BF16), "tp", scatter_dimension=0, tiled=True).astype(F32)
    rows = values.shape[0] // count
    me = lax.axis_index("tp")
    sent = lax.dynamic_slice_in_dim(values, (1 - me) * rows, rows, 0).astype(BF16)
    kept = lax.dynamic_slice_in_dim(values, me * rows, rows, 0)
    return kept + lax.ppermute(sent, "tp", [(0, 1), (1, 0)]).astype(F32)


def roll_columns(values, blocks):
    width = values.shape[-1]
    block = width // lax.axis_size("fsdp")
    twice = jnp.concatenate([values, values], axis=-1)
    return lax.dynamic_slice_in_dim(twice, blocks * block, width, values.ndim - 1)


def to_relative(values):
    return roll_columns(values, lax.axis_index("fsdp"))


def to_natural(values):
    count = lax.axis_size("fsdp")
    return roll_columns(values, (count - lax.axis_index("fsdp")) % count)


def after(values, earlier):
    return lax.optimization_barrier((values, earlier))[0]


def quarter(values, index, axis):
    size = values.shape[axis] // 4
    return lax.dynamic_slice_in_dim(values, index * size, size, axis)


def gather_quarters(shard, fsdp_axis, quarter_axis, earlier=None):
    count = lax.axis_size("fsdp")
    place = lax.axis_index("ctx")
    own = quarter(shard, place, quarter_axis)
    if earlier is not None:
        own = after(own, earlier)
    parts = [pull_fsdp(own, step) for step in range(1, count)]
    mine = jnp.concatenate([own] + parts, axis=fsdp_axis)
    crossed = swap_chip(jnp.concatenate(parts, axis=fsdp_axis))
    across = jnp.concatenate([quarter(shard, place ^ 2, quarter_axis), crossed], axis=fsdp_axis)
    return [mine, swap_core(mine), across, swap_core(across)], parts[-1]


def gather_plain(shard, fsdp_axis, earlier=None):
    count = lax.axis_size("fsdp")
    if earlier is not None:
        shard = after(shard, earlier)
    parts = [pull_fsdp(shard, step) for step in range(1, count)]
    return jnp.concatenate([shard] + parts, axis=fsdp_axis), parts[-1]


def add_halves(left, right):
    return (left.astype(F32) + right.astype(F32)).astype(BF16)


def fsdp_total(values, fsdp_axis):
    count = lax.axis_size("fsdp")
    pieces = jnp.split(values, count, axis=fsdp_axis)
    total = pieces[0].astype(F32)
    for step in range(1, count):
        total = total + push_fsdp(pieces[step], step).astype(F32)
    return total


def reduce_quarters(blocks, fsdp_axis, quarter_axis):
    place = lax.axis_index("ctx")
    came = swap_core(jnp.stack([blocks[1], blocks[3]]))
    near = add_halves(blocks[0], came[0])
    far = add_halves(blocks[2], came[1])
    mine = add_halves(near, swap_chip(far))
    own = fsdp_total(mine, fsdp_axis).astype(BF16)
    crossed = swap_chip(own)
    core_own, core_crossed = swap_core(own), swap_core(crossed)
    odd_core, odd_chip = place % 2 == 1, place >= 2
    pick = jnp.where
    a0, a1 = pick(odd_core, core_own, own), pick(odd_core, own, core_own)
    b0, b1 = pick(odd_core, core_crossed, crossed), pick(odd_core, crossed, core_crossed)
    order = [pick(odd_chip, b0, a0), pick(odd_chip, b1, a1), pick(odd_chip, a0, b0), pick(odd_chip, a1, b1)]
    return jnp.concatenate(order, axis=quarter_axis).astype(F32)


def reduce_plain(grad, fsdp_axis):
    return lax.psum(fsdp_total(grad, fsdp_axis).astype(BF16), "ctx").astype(F32)


def fetch_window(rows):
    count = lax.axis_size("ctx")
    even = lax.axis_index("ctx") % 2 == 0
    own = widen_rows(rows)
    far = widen_rows(lax.ppermute(rows, "ctx", [(i, i + 2) for i in range(count - 2)]))
    near = swap_core(jnp.where(even, own, far))
    return jnp.concatenate([far, near, own], axis=0)


def return_window(far, near, own):
    count = lax.axis_size("ctx")
    even = lax.axis_index("ctx") % 2 == 0
    came = swap_core(near.astype(BF16)).astype(F32)
    own = narrow_rows(own + jnp.where(even, came, 0.0))
    far = narrow_rows(far + jnp.where(even, 0.0, came)).astype(BF16)
    return own + lax.ppermute(far, "ctx", [(i, i - 2) for i in range(2, count)]).astype(F32)


def fetch_ids(ids):
    count = lax.axis_size("ctx")
    even = lax.axis_index("ctx") % 2 == 0
    far = lax.ppermute(ids, "ctx", [(i, i + 2) for i in range(count - 2)])
    return jnp.concatenate([far, swap_core(jnp.where(even, ids, far)), ids])


def rope_tables(offset, row_count, half_dim):
    where_at = (offset + jnp.arange(row_count, dtype=jnp.int32)).astype(F32)
    inv_freq = 10000.0 ** (-jnp.arange(half_dim, dtype=F32) * 2.0 / (2 * half_dim))
    angles = where_at[:, None] * inv_freq[None, :]
    return jnp.cos(angles), jnp.sin(angles)


def rotate(values, cos_rows, sin_rows, direction):
    half_dim = values.shape[-1] // 2
    first_half = values[..., :half_dim]
    second_half = values[..., half_dim:]
    cos_part = cos_rows[:, None, :]
    sin_part = sin_rows[:, None, :] * direction
    return jnp.concatenate(
        [
            first_half * cos_part - second_half * sin_part,
            second_half * cos_part + first_half * sin_part,
        ],
        axis=-1,
    )


def normalize_back(values, inverse, gain, grad_rows):
    scaled = grad_rows * gain
    return inverse * scaled - values * inverse**3 * jnp.mean(scaled * values, axis=-1, keepdims=True)


def dot(left, right):
    return jnp.dot(left, right, preferred_element_type=F32)


def dot_nt(left, right):
    return lax.dot_general(left, right, (((1,), (1,)), ((), ())), preferred_element_type=F32)


def dot_tn(left, right):
    return lax.dot_general(left, right, (((0,), (0,)), ((), ())), preferred_element_type=F32)


def shards(tokens, segment_ids, wq, wk, wv, wo, w_gate, w_up, w_down, gain_attn, gain_ffn, cotangent):
    tokens, cotangent, segment_ids = tokens[0], cotangent[0], segment_ids[0]
    ctx_rows = segment_ids.shape[0]
    head_count = wq.shape[1] // HEAD_DIM
    row_width = wq.shape[1]
    scale = HEAD_DIM ** (-0.5)
    by_heads = head_count % 4 == 0
    first_query = lax.axis_index("ctx") * ctx_rows
    cos_rows, sin_rows = rope_tables(first_query - 2 * ctx_rows, 3 * ctx_rows, HEAD_DIM // 2)

    qkv = jnp.stack([wq, wk, wv])
    if by_heads:
        qkv_parts, mark = gather_quarters(qkv, 1, 2)
        qkv_whole = jnp.concatenate(qkv_parts, axis=2)
        out_parts, mark = gather_quarters(wo, 1, 0, mark)
        out_whole = jnp.concatenate(out_parts, axis=0)
    else:
        qkv_whole, mark = gather_plain(qkv, 1)
        out_whole, mark = gather_plain(wo, 1, mark)
    wide_parts, mark = gather_quarters(jnp.stack([w_gate, w_up]), 1, 2, mark)
    wide_whole = jnp.concatenate(wide_parts, axis=2)
    gate_whole, up_whole = wide_whole[0], wide_whole[1]
    down_parts, mark = gather_quarters(w_down, 1, 0, mark)
    down_whole = jnp.concatenate(down_parts, axis=0)
    gains, _ = gather_plain(jnp.stack([gain_attn, gain_ffn]), 1)
    gain_one, gain_two = gains[0].astype(F32), gains[1].astype(F32)

    inputs = to_relative(tokens).astype(F32)
    dy_rows = to_relative(cotangent)
    inv_one = lax.rsqrt(jnp.mean(inputs * inputs, axis=-1, keepdims=True) + EPSILON)
    normed_window = fetch_window((inputs * inv_one * gain_one).astype(BF16))
    normed = normed_window[2 * ctx_rows :]
    dy_wide = widen_rows(dy_rows)

    def heads(values):
        return values.reshape(values.shape[0], head_count, HEAD_DIM)

    cos_own, sin_own = cos_rows[2 * ctx_rows :], sin_rows[2 * ctx_rows :]
    queries = rotate(heads(dot(normed, qkv_whole[0])), cos_own, sin_own, 1.0).astype(BF16)
    keys = rotate(heads(dot(normed_window, qkv_whole[1])), cos_rows, sin_rows, 1.0).astype(BF16)
    values = heads(dot(normed_window, qkv_whole[2]).astype(BF16))
    segment_window = fetch_ids(segment_ids)
    pos_query = first_query + jnp.arange(ctx_rows, dtype=jnp.int32)
    pos_key = first_query - 2 * ctx_rows + jnp.arange(3 * ctx_rows, dtype=jnp.int32)
    allowed = (
        (segment_ids[:, None] == segment_window[None, :])
        & (pos_key[None, :] <= pos_query[:, None])
        & (pos_key[None, :] >= 0)
    )[None]
    scores = jnp.einsum("qhd,khd->hqk", queries, keys, preferred_element_type=F32) * scale
    scores = jnp.where(allowed, scores, MASKED)
    top = jnp.max(scores, axis=-1, keepdims=True)
    powers = jnp.where(allowed, jnp.exp(scores - top), 0.0)
    sums = jnp.sum(powers, axis=-1, keepdims=True)
    weighted = jnp.einsum("hqk,khd->hqd", powers.astype(BF16), values, preferred_element_type=F32)
    attended = jnp.transpose(weighted / sums, (1, 0, 2))
    log_sums = top + jnp.log(sums)
    attended_low = attended.astype(BF16).reshape(ctx_rows, row_width)
    residual = inputs + narrow_rows(dot(attended_low, out_whole))

    inv_two = lax.rsqrt(jnp.mean(residual * residual, axis=-1, keepdims=True) + EPSILON)
    normed_two = widen_rows((residual * inv_two * gain_two).astype(BF16))
    gate = dot(normed_two, gate_whole)
    up = dot(normed_two, up_whole)
    sig = jax.nn.sigmoid(gate)
    silu = gate * sig
    hidden = (silu * up).astype(BF16)
    hidden_grad = dot_nt(dy_wide, down_whole)
    gate_grad = (hidden_grad * up * sig * (1.0 + gate * (1.0 - sig))).astype(BF16)
    up_grad = (hidden_grad * silu).astype(BF16)
    normed_two_grad = narrow_rows(dot_nt(gate_grad, gate_whole) + dot_nt(up_grad, up_whole))
    layer_out = residual + narrow_rows(dot(hidden, down_whole))
    down_grad = dot_tn(hidden, dy_wide).astype(BF16)
    wide_grad = jnp.stack(
        [dot_tn(normed_two, gate_grad).astype(BF16), dot_tn(normed_two, up_grad).astype(BF16)]
    )
    down_total = reduce_quarters(jnp.split(down_grad, 4, axis=0), 1, 0)
    wide_total = reduce_quarters(jnp.split(wide_grad, 4, axis=2), 1, 2)
    gain_two_grad = jnp.sum(normed_two_grad * residual * inv_two, axis=0)
    resid_grad = dy_rows.astype(F32) + normalize_back(residual, inv_two, gain_two, normed_two_grad)

    attention_grad = widen_rows(resid_grad.astype(BF16))
    out_weight_grad = dot_tn(attended_low, attention_grad).astype(BF16)
    out_grad = heads(dot_nt(attention_grad, out_whole).astype(BF16))
    delta = jnp.sum(out_grad.astype(F32) * attended, axis=-1)
    soft = jnp.where(allowed, jnp.exp(scores - log_sums), 0.0)
    prob_grad = jnp.einsum("qhd,khd->hqk", out_grad, values, preferred_element_type=F32)
    score_grad = (soft * (prob_grad - jnp.transpose(delta)[:, :, None])).astype(BF16)
    query_grad = jnp.einsum("hqk,khd->qhd", score_grad, keys, preferred_element_type=F32) * scale
    key_add = jnp.einsum("hqk,qhd->khd", score_grad, queries, preferred_element_type=F32) * scale
    value_add = jnp.einsum("hqk,qhd->khd", soft.astype(BF16), out_grad, preferred_element_type=F32)
    query_low = rotate(query_grad, cos_own, sin_own, -1.0).astype(BF16).reshape(ctx_rows, row_width)
    key_low = rotate(key_add, cos_rows, sin_rows, -1.0).astype(BF16).reshape(3 * ctx_rows, row_width)
    value_low = value_add.astype(BF16).reshape(3 * ctx_rows, row_width)
    qkv_grad = jnp.stack(
        [
            dot_tn(normed, query_low).astype(BF16),
            dot_tn(normed_window, key_low).astype(BF16),
            dot_tn(normed_window, value_low).astype(BF16),
        ]
    )
    if by_heads:
        out_total = reduce_quarters(jnp.split(out_weight_grad, 4, axis=0), 1, 0)
        qkv_total = reduce_quarters(jnp.split(qkv_grad, 4, axis=2), 1, 2)
    else:
        out_total = reduce_plain(out_weight_grad, 1)
        qkv_total = reduce_plain(qkv_grad, 1)
    normed_parts = dot_nt(key_low, qkv_whole[1]) + dot_nt(value_low, qkv_whole[2])
    far, near, own = (normed_parts[i * ctx_rows : (i + 1) * ctx_rows] for i in range(3))
    normed_grad = return_window(far, near, own + dot_nt(query_low, qkv_whole[0]))
    gain_one_grad = jnp.sum(normed_grad * inputs * inv_one, axis=0)
    grad_input = resid_grad + normalize_back(inputs, inv_one, gain_one, normed_grad)

    gain_grads = lax.psum(to_natural(jnp.stack([gain_one_grad, gain_two_grad])), ("fsdp", "ctx", "tp"))
    gain_rows = gain_attn.shape[0]
    gain_own = lax.dynamic_slice_in_dim(gain_grads, lax.axis_index("fsdp") * gain_rows, gain_rows, 1)
    return (
        to_natural(layer_out.astype(BF16))[None],
        to_natural(grad_input)[None],
        qkv_total[0],
        qkv_total[1],
        qkv_total[2],
        out_total,
        wide_total[0],
        wide_total[1],
        down_total,
        gain_own[0],
        gain_own[1],
    )


def solution(mesh):
    rows = P("fsdp", ("ctx", "tp"), None)
    into, outof, gain = P("fsdp", "tp"), P("tp", "fsdp"), P("fsdp")
    return jax.shard_map(
        shards,
        mesh=mesh,
        in_specs=(rows, P("fsdp", "ctx"), into, into, into, outof, into, into, outof, gain, gain, rows),
        out_specs=(rows, rows, into, into, into, outof, into, into, outof, gain, gain),
        check_vma=False,
    )
```

time: 1870 us -> 990 us (0.53)
  waiting for transfers between devices: 1320 us -> 232 us
  starting transfers between devices: 1.35 us -> 184 us
  blocking collectives: 55.1 us -> 136 us
  local copies, waits for them, and re-layouts: 123 us -> 46.8 us
  other arithmetic: 67.9 us -> 144 us
  matrix products: 274 us -> 237 us
    all_gather x13 -> x0, waiting for transfers between devices: 606 us -> none  [the longest x1 117 us: shards(): lax.all_gather(w_down, 'fsdp', axis=1, tiled=True)]
    reduce_scatter x9 -> x0, waiting for transfers between devices: 448 us -> none  [the longest x1 114 us: shards(): lax.psum_scatter(gate_weight_gradient.astype(jnp.bfloat16), 'fsdp', scatt...]
    ppermute x0 -> x75, waiting for transfers between devices: none -> 232 us  [the longest x12 89.4 us: push_fsdp(): lax.ppermute(values, 'fsdp', [(i, (i + step) % count) for i in range(coun...]
    ppermute x0 -> x75, starting transfers between devices: none -> 184 us  [the longest x15 72.3 us: pull_fsdp(): lax.ppermute(values, 'fsdp', [(i, (i - step) % count) for i in range(coun...]
    unnamed x31 -> x0, waiting for transfers between devices: 132 us -> none
    psum x1 -> x0, waiting for transfers between devices: 132 us -> none  [shards(): lax.psum(share_q.astype(jnp.bfloat16), 'ctx').astype(jnp.float32)]
    psum x2 -> x1, blocking collectives: 14.9 us -> 136 us  [shards(): lax.psum(to_natural(jnp.stack([gain_one_grad, gain_two_grad])), ('fsdp',...]
    unnamed x125 -> x209, local copies, waits for them, and re-layouts: 86.2 us -> 17.3 us
  transfers between devices with their start and end apart: 27 -> 75, of which waited for: 24 -> 22; matrix products, arithmetic and copies ran while one was open for 14% -> 36% of each run, Pallas kernels for 0% -> 0%
where the time goes in v1:
time: 990 us; the launch traced here: 983 us
  matrix products  237 us (24%)
  waiting for transfers between devices  232 us (23%)
  starting transfers between devices  184 us (19%)
  other arithmetic  144 us (15%)
  blocking collectives  136 us (14%)
  local copies, waits for them, and re-layouts  46.8 us (5%)
    psum x1, blocking collectives, shards(): lax.psum(to_natural(jnp.stack([gain_one_grad, gain_two_grad])), ('fsdp',...  136 us
    ppermute x12, waiting for transfers between devices, push_fsdp(): lax.ppermute(values, 'fsdp', [(i, (i + step) % count) for i in range(coun...  89.4 us
    ppermute x15, starting transfers between devices, pull_fsdp(): lax.ppermute(values, 'fsdp', [(i, (i - step) % count) for i in range(coun...  72.3 us
    ppermute x12, waiting for transfers between devices, swap_chip(): lax.ppermute(values, 'ctx', [(i, i ^ 2) for i in range(lax.axis_size('ctx...  63.1 us
    ppermute x23, starting transfers between devices, swap_core(): lax.ppermute(values, 'ctx', [(i, i ^ 1) for i in range(lax.axis_size('ctx...  54.6 us
    dot_general x7, matrix products, dot_nt(): lax.dot_general(left, right, (((1,), (1,)), ((), ())), preferred_element_...  51.7 us
    dot_general x7, matrix products, dot(): return jnp.dot(left, right, preferred_element_type=F32)  41.5 us
    dot_general x7, matrix products, dot_tn(): lax.dot_general(left, right, (((0,), (0,)), ((), ())), preferred_element_...  34.6 us
  transfers between devices with their start and end apart: 75, of which 22 were waited for; matrix products, arithmetic and copies ran while one was open for 36% of the time, Pallas kernels for 0%

profile of v1, /device:TPU:1, one launch (start us, length us, event | category | flops | bytes accessed | tf_op | source)
XLA Modules:
  0.0 983.3 jit_solution(6870542707094857288)
XLA Ops:
  63.0 19.4 %collective-permute-start.24 = (bf16[2,384,512]{2,1,0:T(8,128)(2,1)S(1)}, bf16[2,384,512]{2,1,0:T(8,128)(2,1)S(1)}, u32[]{:S(2)}, u32[]{:S(2)}) collective-permute-start(bf16[2,384,512]{2,1,0:T(8,128)(2,1)S(1)} %copy-done.34), channel_id=1, source_target_pairs={{0,16},{8,24},{16,0},{24,8},{1,17},{9,25},{17,1},{25,9},{2,18},{10... | collective-permute-start | bytes 2359304 | tf_op jit(solution)/shard_map/ppermute | solution.py:15
  101.8 13.3 %collective-permute-done.23 = bf16[2,384,512]{2,1,0:T(8,128)(2,1)S(1)} collective-permute-done((bf16[2,384,512]{2,1,0:T(8,128)(2,1)S(1)}, bf16[2,384,512]{2,1,0:T(8,128)(2,1)S(1)}, u32[]{:S(2)}, u32[]{:S(2)}) %collective-permute-start.23) | collective-permute-done | bytes 786464 | tf_op jit(solution)/shard_map/ppermute | solution.py:15
  115.1 25.5 %collective-permute-start.31 = (bf16[512,384]{1,0:T(8,128)(2,1)S(1)}, bf16[512,384]{1,0:T(8,128)(2,1)S(1)}, u32[]{:S(2)}, u32[]{:S(2)}) collective-permute-start(bf16[512,384]{1,0:T(8,128)(2,1)S(1)} %copy-done.46), channel_id=1, source_target_pairs={{0,8},{8,16},{16,24},{24,0},{1,9},{9,17},{17,25},{25,1},{2,10},{10... | collective-permute-start | bytes 1179656 | tf_op jit(solution)/shard_map/ppermute | solution.py:15
  171.5 15.6 %collective-permute-done.33 = bf16[512,1152]{1,0:T(8,128)(2,1)S(1)} collective-permute-done((bf16[512,1152]{1,0:T(8,128)(2,1)S(1)}, bf16[512,1152]{1,0:T(8,128)(2,1)S(1)}, u32[]{:S(2)}, u32[]{:S(2)}) %collective-permute-start.33) | collective-permute-done | bytes 1179680 | tf_op jit(solution)/shard_map/ppermute | solution.py:24
  195.5 11.4 %pad_maximum_fusion.1 = bf16[3,1536,768]{1,2,0:T(8,128)(2,1)S(1)} fusion(bf16[3,1536,192]{1,2,0:T(8,128)(2,1)S(1)} %collective-permute-done.11, bf16[3,1152,192]{1,2,0:T(8,128)(2,1)S(1)} %collective-permute-done.10, bf16[3,384,192]{1,2,0:T(8,128)(2,1)S(1)} %copy-done.22, bf16[3,1536,192]{1,2,0:T(8,128)(2,1)S(1)} %collective-permute-done.9, ...), kind=kLoop, calls=%fused_computation.23 | loop fusion | flops 56623104 | bytes 14155776 | tf_op jit(solution)/shard_map/concatenate | solution.py:207
  233.0 20.2 %fusion.3 = (f32[12,544]{1,0:T(8,128)S(1)}, f32[12,544,1632]{2,1,0:T(8,128)}) fusion(pred[544,1632]{1,0:T(8,128)(4,1)} %and_and_fusion, bf16[1632,12,32]{0,2,1:T(8,128)(2,1)} %get-tuple-element.85, bf16[1632,12,32]{0,2,1:T(8,128)(2,1)} %get-tuple-element.84, bf16[544,12,32]{0,2,1:T(8,128)(2,1)} %get-tuple-element.103, ...), kind=kOutput, calls=%fused_computation.7 | convolution fusion | flops 1402312320 | bytes 46871040 | tf_op jit(solution)/shard_map/qhd,khd->hqk/dot_general | solution.py:243
  253.2 23.3 %fusion = f32[12,544]{1,0:T(8,128)S(1)} fusion(f32[12,544,1632]{2,1,0:T(8,128)} %get-tuple-element.150, f32[12,544]{1,0:T(8,128)S(1)} %get-tuple-element.149, pred[544,1632]{1,0:T(8,128)(4,1)} %and_and_fusion), kind=kLoop, calls=%fused_computation.4 | loop fusion | flops 53261952 | bytes 43554816 | tf_op jit(solution)/shard_map/reduce_sum | solution.py:247
  276.6 20.9 %fusion.66 = (bf16[544,12,64]{0,2,1:T(8,128)(2,1)}, f32[12,544,64]{1,2,0:T(8,128)}) fusion(f32[544,12]{0,1:T(8,128)S(1)} %bitcast.196, bf16[1632,12,64]{0,2,1:T(8,128)(2,1)} %bitcast.182, f32[12,544,1632]{2,1,0:T(8,128)} %get-tuple-element.150, f32[12,544]{1,0:T(8,128)S(1)} %get-tuple-element.149, pred[544,1632]{1,0:T(8,128)(4,1)} %and_and_fusion), kind=kOutput, calls=%fused_computation.216 | convolution fusion | flops 1417777152 | bytes 48568320 | tf_op jit(solution)/shard_map/hqk,khd->hqd/dot_general | solution.py:248
  306.0 15.8 %collective-permute-done.21 = bf16[272,1536]{1,0:T(8,128)(2,1)S(1)} collective-permute-done((bf16[272,1536]{1,0:T(8,128)(2,1)S(1)}, bf16[272,1536]{1,0:T(8,128)(2,1)S(1)}, u32[]{:S(2)}, u32[]{:S(2)}) %collective-permute-start.21) | collective-permute-done | bytes 835616 | tf_op jit(solution)/shard_map/ppermute | solution.py:47
  323.7 11.3 %fusion.59 = f32[544,2048]{1,0:T(8,128)} fusion(bf16[272,1536]{1,0:T(8,128)(2,1)S(1)} %get-tuple-element.117, bf16[272,1536]{1,0:T(8,128)(2,1)S(1)} %get-tuple-element.116, bf16[512,1536]{1,0:T(8,128)(2,1)} %collective-permute-done.34, bf16[512,1152]{1,0:T(8,128)(2,1)S(1)} %copy-done.51, bf16[512,384]{1,0:T(8,128)(2,1)S(1)} %copy-done.45, ...), kind=kOutput, calls=%fused_computation.184 | convolution fusion | flops 3457351680 | bytes 12419072 | tf_op jit(solution)/shard_map/dot_general | solution.py:187
  342.1 28.1 %pad_maximum_fusion = bf16[2,1536,2048]{2,1,0:T(8,128)(2,1)S(1)} fusion(bf16[2,1536,512]{2,1,0:T(8,128)(2,1)S(1)} %collective-permute-done.28, bf16[2,1152,512]{2,1,0:T(8,128)(2,1)S(1)} %copy-done.7, bf16[2,384,512]{2,1,0:T(8,128)(2,1)S(1)} %copy-done.15, bf16[2,1536,512]{2,1,0:T(8,128)(2,1)} %collective-permute-done.26, ...), kind=kLoop, calls=%fused_computation.18 | loop fusion | flops 62914560 | bytes 25165824 | tf_op jit(solution)/shard_map/concatenate | solution.py:214
  437.5 10.6 %collective-permute-done.37 = bf16[272,1536]{1,0:T(8,128)(2,1)S(1)} collective-permute-done((bf16[272,1536]{1,0:T(8,128)(2,1)S(1)}, bf16[272,1536]{1,0:T(8,128)(2,1)S(1)}, u32[]{:S(2)}, u32[]{:S(2)}) %collective-permute-start.37) | collective-permute-done | bytes 835616 | tf_op jit(solution)/shard_map/ppermute | solution.py:47
  478.2 19.7 %fusion.23 = bf16[12,64,1632]{2,1,0:T(8,128)(2,1)} fusion(bf16[544,12,64]{0,2,1:T(8,128)(2,1)S(1)} %bitcast.180, f32[12,544,1632]{2,1,0:T(8,128)} %get-tuple-element.150, f32[12,544]{1,0:T(8,128)S(1)} %log_add_fusion, pred[544,1632]{1,0:T(8,128)(4,1)S(1)} %copy-done.32), kind=kOutput, calls=%fused_computation.70 | convolution fusion | flops 1418194944 | bytes 46871040 | tf_op jit(solution)/shard_map/hqk,qhd->khd/dot_general | solution.py:284
  498.0 27.7 %multiply_convert_fusion = bf16[12,544,1632]{2,1,0:T(8,128)(2,1)} fusion(f32[12,544,1632]{2,1,0:T(8,128)} %get-tuple-element.150, bf16[544,12,64]{0,2,1:T(8,128)(2,1)} %bitcast.181, bf16[1632,12,64]{0,2,1:T(8,128)(2,1)} %bitcast.183, f32[12,544]{1,0:T(8,128)S(1)} %bitcast.200, f32[12,544]{1,0:T(8,128)S(1)} %log_add_fusion, pred[544,1632]{1,0:T(8,128)(4,1)} %and_and_fusion), kind=kOutput, calls=%fused_computation | convolution fusion | flops 1438248960 | bytes 68204544 | tf_op jit(solution)/shard_map/qhd,khd->hqk/dot_general | solution.py:280
  525.7 10.9 %multiply_bitcast_fusion.1 = f32[544,12,64]{0,2,1:T(8,128)S(1)} fusion(bf16[12,544,1632]{2,1,0:T(8,128)(2,1)} %multiply_convert_fusion, bf16[1632,12,32]{0,2,1:T(8,128)(2,1)S(1)} %copy-done.20, bf16[1632,12,32]{0,2,1:T(8,128)(2,1)S(1)} %copy-done.19), kind=kOutput, calls=%fused_computation.115 | convolution fusion | flops 1369104384 | bytes 25485312 | tf_op jit(solution)/shard_map/hqk,khd->qhd/dot_general | solution.py:282
  536.6 10.1 %multiply_bitcast_fusion = f32[1632,12,64]{0,2,1:T(8,128)S(1)} fusion(bf16[12,544,1632]{2,1,0:T(8,128)(2,1)} %multiply_convert_fusion, bf16[544,12,32]{0,2,1:T(8,128)(2,1)} %get-tuple-element.103, bf16[544,12,32]{0,2,1:T(8,128)(2,1)} %get-tuple-element.102), kind=kOutput, calls=%fused_computation.41 | convolution fusion | flops 1366597632 | bytes 27156480 | tf_op jit(solution)/shard_map/hqk,qhd->khd/dot_general | solution.py:283
  605.7 12.2 %collective-permute-start.53 = (bf16[192,384]{1,0:T(8,128)(2,1)S(1)}, bf16[192,384]{1,0:T(8,128)(2,1)S(1)}, u32[]{:S(2)}, u32[]{:S(2)}) collective-permute-start(bf16[192,384]{1,0:T(8,128)(2,1)S(1)} %get-tuple-element.135), channel_id=1, source_target_pairs={{0,8},{8,16},{16,24},{24,0},{1,9},{9,17},{17,25},{25,1},{2,10},{10... | collective-permute-start | bytes 442376 | tf_op jit(solution)/shard_map/ppermute | solution.py:20
  657.7 22.3 %collective-permute-done.68 = bf16[512,1536]{1,0:T(8,128)(2,1)S(1)} collective-permute-done((bf16[512,1536]{1,0:T(8,128)(2,1)S(1)}, bf16[512,1536]{1,0:T(8,128)(2,1)S(1)}, u32[]{:S(2)}, u32[]{:S(2)}) %collective-permute-start.68) | collective-permute-done | bytes 1572896 | tf_op jit(solution)/shard_map/ppermute | solution.py:24
  686.8 11.2 %collective-permute-done.42 = bf16[272,1536]{1,0:T(8,128)(2,1)S(1)} collective-permute-done((bf16[272,1536]{1,0:T(8,128)(2,1)S(1)}, bf16[272,1536]{1,0:T(8,128)(2,1)S(1)}, u32[]{:S(2)}, u32[]{:S(2)}) %collective-permute-start.42) | collective-permute-done | bytes 835616 | tf_op jit(solution)/shard_map/ppermute | solution.py:145
  699.1 135.8 %psum.7 = f32[2,1536]{1,0:T(2,128)S(1)} all-reduce(f32[2,1536]{1,0:T(2,128)S(1)} %fusion.68), channel_id=1, replica_groups=mesh['fsdp'=4,'ctx'=4,'tp'=2] {'fsdp','ctx','tp'}, use_global_device_ids=true, to_apply=%region_9.10 | all-reduce | flops 3072 | bytes 24576 | tf_op jit(solution)/shard_map/psum | solution.py:307
  862.4 15.3 %collective-permute-start.74 = (bf16[512,384]{1,0:T(8,128)(2,1)S(1)}, bf16[512,384]{1,0:T(8,128)(2,1)S(1)}, u32[]{:S(2)}, u32[]{:S(2)}) collective-permute-start(bf16[512,384]{1,0:T(8,128)(2,1)S(1)} %add_convert_fusion.10), channel_id=1, source_target_pairs={{0,2},{2,0},{4,6},{6,4},{1,3},{3,1},{5,7},{7,5},{8,10},{10,8},{12,... | collective-permute-start | bytes 1179656 | tf_op jit(solution)/shard_map/ppermute | solution.py:28
  877.7 22.1 %collective-permute-done.46 = bf16[3,384,192]{1,2,0:T(8,128)(2,1)S(1)} collective-permute-done((bf16[3,384,192]{1,2,0:T(8,128)(2,1)S(1)}, bf16[3,384,192]{1,2,0:T(8,128)(2,1)S(1)}, u32[]{:S(2)}, u32[]{:S(2)}) %collective-permute-start.46) | collective-permute-done | bytes 442400 | tf_op jit(solution)/shard_map/ppermute | solution.py:20
  905.6 44.8 %collective-permute-done.62 = bf16[2,384,512]{2,1,0:T(8,128)(2,1)S(1)} collective-permute-done((bf16[2,384,512]{2,1,0:T(8,128)(2,1)S(1)}, bf16[2,384,512]{2,1,0:T(8,128)(2,1)S(1)}, u32[]{:S(2)}, u32[]{:S(2)}) %collective-permute-start.62) | collective-permute-done | bytes 786464 | tf_op jit(solution)/shard_map/ppermute | solution.py:20
  957.7 11.7 %collective-permute-done.64 = bf16[2,384,512]{2,1,0:T(8,128)(2,1)} collective-permute-done((bf16[2,384,512]{2,1,0:T(8,128)(2,1)}, bf16[2,384,512]{2,1,0:T(8,128)(2,1)}, u32[]{:S(2)}, u32[]{:S(2)}) %collective-permute-start.64) | collective-permute-done | bytes 786464 | tf_op jit(solution)/shard_map/ppermute | solution.py:24
  (486 shorter events, 421.3 us)
Async XLA Ops:
  35.8 52.6 %collective-permute-start.12 = (bf16[272,1536]{1,0:T(8,128)(2,1)}, bf16[272,1536]{1,0:T(8,128)(2,1)}, u32[]{:S(2)}, u32[]{:S(2)}) collective-permute-start(bf16[272,1536]{1,0:T(8,128)(2,1)} %fusion.46), channel_id=1, source_target_pairs={{0,4},{2,6},{1,5},{3,7},{8,12},{10,14},{9,13},{11,15},{16,20},{18,... | collective-permute-start | bytes 2506760 | tf_op jit(solution)/shard_map/ppermute | solution.py:134
  63.0 78.5 %collective-permute-start.24 = (bf16[2,384,512]{2,1,0:T(8,128)(2,1)S(1)}, bf16[2,384,512]{2,1,0:T(8,128)(2,1)S(1)}, u32[]{:S(2)}, u32[]{:S(2)}) collective-permute-start(bf16[2,384,512]{2,1,0:T(8,128)(2,1)S(1)} %copy-done.34), channel_id=1, source_target_pairs={{0,16},{8,24},{16,0},{24,8},{1,17},{9,25},{17,1},{25,9},{2,18},{10... | collective-permute-start | bytes 2359304 | tf_op jit(solution)/shard_map/ppermute | solution.py:15
  89.7 52.7 %collective-permute-start.13 = (bf16[272,1536]{1,0:T(8,128)(2,1)}, bf16[272,1536]{1,0:T(8,128)(2,1)S(1)}, u32[]{:S(2)}, u32[]{:S(2)}) collective-permute-start(bf16[272,1536]{1,0:T(8,128)(2,1)} %collective-permute-done.12), channel_id=1, source_target_pairs={{0,1},{1,0},{2,3},{3,2},{4,5},{5,4},{6,7},{7,6},{8,9},{9,8},{10,11... | collective-permute-start | bytes 2506760 | tf_op jit(solution)/shard_map/ppermute | solution.py:34
  98.5 204.8 %collective-permute-start.36 = (bf16[272,1536]{1,0:T(8,128)(2,1)}, bf16[272,1536]{1,0:T(8,128)(2,1)}, u32[]{:S(2)}, u32[]{:S(2)}) collective-permute-start(bf16[272,1536]{1,0:T(8,128)(2,1)} %fusion.60), channel_id=1, source_target_pairs={{0,1},{1,0},{2,3},{3,2},{4,5},{5,4},{6,7},{7,6},{8,9},{9,8},{10,11... | collective-permute-start | bytes 2506760 | tf_op jit(solution)/shard_map/ppermute | solution.py:34
  100.6 64.8 %collective-permute-start.10 = (bf16[3,1152,192]{1,2,0:T(8,128)(2,1)S(1)}, bf16[3,1152,192]{1,2,0:T(8,128)(2,1)S(1)}, u32[]{:S(2)}, u32[]{:S(2)}) collective-permute-start(bf16[3,1152,192]{1,2,0:T(8,128)(2,1)S(1)} %pad_maximum_fusion.24), channel_id=1, source_target_pairs={{0,4},{2,6},{4,0},{6,2},{1,5},{3,7},{5,1},{7,3},{8,12},{10,14},{12... | collective-permute-start | bytes 3981320 | tf_op jit(solution)/shard_map/ppermute | solution.py:24
  187.0 110.4 %collective-permute-start.18 = (bf16[192,1536]{1,0:T(8,128)(2,1)}, bf16[192,1536]{1,0:T(8,128)(2,1)}, u32[]{:S(2)}, u32[]{:S(2)}) collective-permute-start(bf16[192,1536]{1,0:T(8,128)(2,1)} %constant_dynamic-update-slice_fusion.5), channel_id=1, source_target_pairs={{0,2},{2,0},{4,6},{6,4},{1,3},{3,1},{5,7},{7,5},{8,10},{10,8},{12,... | collective-permute-start | bytes 1769480 | tf_op jit(solution)/shard_map/ppermute | solution.py:28
  192.9 104.8 %collective-permute-start.20 = (bf16[192,1536]{1,0:T(8,128)(2,1)}, bf16[192,1536]{1,0:T(8,128)(2,1)}, u32[]{:S(2)}, u32[]{:S(2)}) collective-permute-start(bf16[192,1536]{1,0:T(8,128)(2,1)} %pad_maximum_fusion.34), channel_id=1, source_target_pairs={{0,2},{2,0},{4,6},{6,4},{1,3},{3,1},{5,7},{7,5},{8,10},{10,8},{12,... | collective-permute-start | bytes 1769480 | tf_op jit(solution)/shard_map/ppermute | solution.py:28
  193.4 108.5 %collective-permute-start.27 = (bf16[2,1152,512]{2,1,0:T(8,128)(2,1)}, bf16[2,1152,512]{2,1,0:T(8,128)(2,1)S(1)}, u32[]{:S(2)}, u32[]{:S(2)}) collective-permute-start(bf16[2,1152,512]{2,1,0:T(8,128)(2,1)} %pad_maximum_fusion.11), channel_id=1, source_target_pairs={{0,4},{2,6},{4,0},{6,2},{1,5},{3,7},{5,1},{7,3},{8,12},{10,14},{12... | collective-permute-start | bytes 7077896 | tf_op jit(solution)/shard_map/ppermute | solution.py:24
  194.6 147.4 %collective-permute-start.26 = (bf16[2,1536,512]{2,1,0:T(8,128)(2,1)}, bf16[2,1536,512]{2,1,0:T(8,128)(2,1)}, u32[]{:S(2)}, u32[]{:S(2)}) collective-permute-start(bf16[2,1536,512]{2,1,0:T(8,128)(2,1)} %constant_dynamic-update-slice_fusion.9), channel_id=1, source_target_pairs={{0,2},{2,0},{4,6},{6,4},{1,3},{3,1},{5,7},{7,5},{8,10},{10,8},{12,... | collective-permute-start | bytes 9437192 | tf_op jit(solution)/shard_map/ppermute | solution.py:28
  435.1 155.2 %collective-permute-start.67 = (bf16[2,512,1536]{2,1,0:T(8,128)(2,1)}, bf16[2,512,1536]{2,1,0:T(8,128)(2,1)}, u32[]{:S(2)}, u32[]{:S(2)}) collective-permute-start(bf16[2,512,1536]{2,1,0:T(8,128)(2,1)} %pad_maximum_fusion.8), channel_id=1, source_target_pairs={{0,2},{2,0},{4,6},{6,4},{1,3},{3,1},{5,7},{7,5},{8,10},{10,8},{12,... | collective-permute-start | bytes 9437192 | tf_op jit(solution)/shard_map/ppermute | solution.py:28
  456.0 193.6 %collective-permute-start.59 = (bf16[2,2,1536,512]{3,2,1,0:T(8,128)(2,1)}, bf16[2,2,1536,512]{3,2,1,0:T(8,128)(2,1)}, u32[]{:S(2)}, u32[]{:S(2)}) collective-permute-start(bf16[2,2,1536,512]{3,2,1,0:T(8,128)(2,1)} %pad_maximum_fusion.4), channel_id=1, source_target_pairs={{0,2},{2,0},{4,6},{6,4},{1,3},{3,1},{5,7},{7,5},{8,10},{10,8},{12,... | collective-permute-start | bytes 18874376 | tf_op jit(solution)/shard_map/ppermute | solution.py:28
  587.1 68.5 %collective-permute-start.43 = (bf16[2,3,1536,192]{2,3,1,0:T(8,128)(2,1)S(1)}, bf16[2,3,1536,192]{2,3,1,0:T(8,128)(2,1)S(1)}, u32[]{:S(2)}, u32[]{:S(2)}) collective-permute-start(bf16[2,3,1536,192]{2,3,1,0:T(8,128)(2,1)S(1)} %pad_maximum_fusion.5), channel_id=1, source_target_pairs={{0,2},{2,0},{4,6},{6,4},{1,3},{3,1},{5,7},{7,5},{8,10},{10,8},{12,... | collective-permute-start | bytes 10616840 | tf_op jit(solution)/shard_map/ppermute | solution.py:28
  653.5 192.4 %collective-permute-start.60 = (bf16[2,1536,512]{2,1,0:T(8,128)(2,1)}, bf16[2,1536,512]{2,1,0:T(8,128)(2,1)}, u32[]{:S(2)}, u32[]{:S(2)}) collective-permute-start(bf16[2,1536,512]{2,1,0:T(8,128)(2,1)} %fusion.12), channel_id=1, source_target_pairs={{0,4},{2,6},{4,0},{6,2},{1,5},{3,7},{5,1},{7,3},{8,12},{10,14},{12... | collective-permute-start | bytes 9437192 | tf_op jit(solution)/shard_map/ppermute | solution.py:24
  657.6 181.6 %collective-permute-start.44 = (bf16[3,1536,192]{1,2,0:T(8,128)(2,1)}, bf16[3,1536,192]{1,2,0:T(8,128)(2,1)}, u32[]{:S(2)}, u32[]{:S(2)}) collective-permute-start(bf16[3,1536,192]{1,2,0:T(8,128)(2,1)} %fusion.21), channel_id=1, source_target_pairs={{0,4},{2,6},{4,0},{6,2},{1,5},{3,7},{5,1},{7,3},{8,12},{10,14},{12... | collective-permute-start | bytes 5308424 | tf_op jit(solution)/shard_map/ppermute | solution.py:24
  683.5 152.0 %collective-permute-start.69 = (bf16[512,384]{1,0:T(8,128)(2,1)}, bf16[512,384]{1,0:T(8,128)(2,1)}, u32[]{:S(2)}, u32[]{:S(2)}) collective-permute-start(bf16[512,384]{1,0:T(8,128)(2,1)} %get-tuple-element.126), channel_id=1, source_target_pairs={{0,8},{8,16},{16,24},{24,0},{1,9},{9,17},{17,25},{25,1},{2,10},{10... | collective-permute-start | bytes 1179656 | tf_op jit(solution)/shard_map/ppermute | solution.py:20
  683.5 152.0 %collective-permute-start.71 = (bf16[512,384]{1,0:T(8,128)(2,1)S(1)}, bf16[512,384]{1,0:T(8,128)(2,1)}, u32[]{:S(2)}, u32[]{:S(2)}) collective-permute-start(bf16[512,384]{1,0:T(8,128)(2,1)S(1)} %get-tuple-element.127), channel_id=1, source_target_pairs={{0,24},{8,0},{16,8},{24,16},{1,25},{9,1},{17,9},{25,17},{2,26},{10... | collective-permute-start | bytes 1179656 | tf_op jit(solution)/shard_map/ppermute | solution.py:20
  698.0 137.5 %collective-permute-start.70 = (bf16[512,384]{1,0:T(8,128)(2,1)S(1)}, bf16[512,384]{1,0:T(8,128)(2,1)}, u32[]{:S(2)}, u32[]{:S(2)}) collective-permute-start(bf16[512,384]{1,0:T(8,128)(2,1)S(1)} %get-tuple-element.128), channel_id=1, source_target_pairs={{0,16},{8,24},{16,0},{24,8},{1,17},{9,25},{17,1},{25,9},{2,18},{10... | collective-permute-start | bytes 1179656 | tf_op jit(solution)/shard_map/ppermute | solution.py:20
  845.9 53.9 %collective-permute-start.46 = (bf16[3,384,192]{1,2,0:T(8,128)(2,1)S(1)}, bf16[3,384,192]{1,2,0:T(8,128)(2,1)S(1)}, u32[]{:S(2)}, u32[]{:S(2)}) collective-permute-start(bf16[3,384,192]{1,2,0:T(8,128)(2,1)S(1)} %get-tuple-element.110), channel_id=1, source_target_pairs={{0,16},{8,24},{16,0},{24,8},{1,17},{9,25},{17,1},{25,9},{2,18},{10... | collective-permute-start | bytes 1327112 | tf_op jit(solution)/shard_map/ppermute | solution.py:20
  850.3 52.4 %collective-permute-start.61 = (bf16[2,384,512]{2,1,0:T(8,128)(2,1)S(1)}, bf16[2,384,512]{2,1,0:T(8,128)(2,1)S(1)}, u32[]{:S(2)}, u32[]{:S(2)}) collective-permute-start(bf16[2,384,512]{2,1,0:T(8,128)(2,1)S(1)} %get-tuple-element.93), channel_id=1, source_target_pairs={{0,8},{8,16},{16,24},{24,0},{1,9},{9,17},{17,25},{25,1},{2,10},{10... | collective-permute-start | bytes 2359304 | tf_op jit(solution)/shard_map/ppermute | solution.py:20
  850.8 54.7 %collective-permute-start.63 = (bf16[2,384,512]{2,1,0:T(8,128)(2,1)S(1)}, bf16[2,384,512]{2,1,0:T(8,128)(2,1)S(1)}, u32[]{:S(2)}, u32[]{:S(2)}) collective-permute-start(bf16[2,384,512]{2,1,0:T(8,128)(2,1)S(1)} %get-tuple-element.94), channel_id=1, source_target_pairs={{0,24},{8,0},{16,8},{24,16},{1,25},{9,1},{17,9},{25,17},{2,26},{10... | collective-permute-start | bytes 2359304 | tf_op jit(solution)/shard_map/ppermute | solution.py:20
  854.2 96.2 %collective-permute-start.62 = (bf16[2,384,512]{2,1,0:T(8,128)(2,1)S(1)}, bf16[2,384,512]{2,1,0:T(8,128)(2,1)S(1)}, u32[]{:S(2)}, u32[]{:S(2)}) collective-permute-start(bf16[2,384,512]{2,1,0:T(8,128)(2,1)S(1)} %get-tuple-element.95), channel_id=1, source_target_pairs={{0,16},{8,24},{16,0},{24,8},{1,17},{9,25},{17,1},{25,9},{2,18},{10... | collective-permute-start | bytes 2359304 | tf_op jit(solution)/shard_map/ppermute | solution.py:20
  862.4 92.7 %collective-permute-start.74 = (bf16[512,384]{1,0:T(8,128)(2,1)S(1)}, bf16[512,384]{1,0:T(8,128)(2,1)S(1)}, u32[]{:S(2)}, u32[]{:S(2)}) collective-permute-start(bf16[512,384]{1,0:T(8,128)(2,1)S(1)} %add_convert_fusion.10), channel_id=1, source_target_pairs={{0,2},{2,0},{4,6},{6,4},{1,3},{3,1},{5,7},{7,5},{8,10},{10,8},{12,... | collective-permute-start | bytes 1179656 | tf_op jit(solution)/shard_map/ppermute | solution.py:28
  899.8 55.4 %collective-permute-start.73 = (bf16[512,384]{1,0:T(8,128)(2,1)S(1)}, bf16[512,384]{1,0:T(8,128)(2,1)S(1)}, u32[]{:S(2)}, u32[]{:S(2)}) collective-permute-start(bf16[512,384]{1,0:T(8,128)(2,1)S(1)} %collective-permute-done.72), channel_id=1, source_target_pairs={{0,2},{2,0},{4,6},{6,4},{1,3},{3,1},{5,7},{7,5},{8,10},{10,8},{12,... | collective-permute-start | bytes 1179656 | tf_op jit(solution)/shard_map/ppermute | solution.py:28
  902.7 52.4 %collective-permute-start.48 = (bf16[3,384,192]{1,2,0:T(8,128)(2,1)S(1)}, bf16[3,384,192]{1,2,0:T(8,128)(2,1)S(1)}, u32[]{:S(2)}, u32[]{:S(2)}) collective-permute-start(bf16[3,384,192]{1,2,0:T(8,128)(2,1)S(1)} %add_convert_fusion.9), channel_id=1, source_target_pairs={{0,4},{2,6},{4,0},{6,2},{1,5},{3,7},{5,1},{7,3},{8,12},{10,14},{12... | collective-permute-start | bytes 1327112 | tf_op jit(solution)/shard_map/ppermute | solution.py:24
  (147 other events, 3739.3 us)

commit v2 on v1

v2 whole, which is shorter than its diff:
```python
import functools

import jax
import jax.numpy as jnp
from jax import lax
from jax.experimental import pallas as pl
from jax.experimental.pallas import tpu as pltpu
from jax.sharding import PartitionSpec as P

HEAD_DIM = 64
EPSILON = 1e-05
MASKED = -1e30
BF16 = jnp.bfloat16
F32 = jnp.float32
TILE = 256
LANES = 128
VMEM_BYTES = 60 * 1024 * 1024


def dot(left, right):
    return jnp.dot(left, right, preferred_element_type=F32)


def dot_nt(left, right):
    return lax.dot_general(left, right, (((1,), (1,)), ((), ())), preferred_element_type=F32)


def dot_tn(left, right):
    return lax.dot_general(left, right, (((0,), (0,)), ((), ())), preferred_element_type=F32)


def swap_chip(values):
    return lax.ppermute(values, "ctx", [(i, i ^ 2) for i in range(lax.axis_size("ctx"))])


def swap_core(values):
    return lax.ppermute(values, "ctx", [(i, i ^ 1) for i in range(lax.axis_size("ctx"))])


def to_later_chip(values):
    return lax.ppermute(values, "ctx", [(i, i + 2) for i in range(lax.axis_size("ctx") - 2)])


def to_earlier_chip(values):
    return lax.ppermute(values, "ctx", [(i, i - 2) for i in range(2, lax.axis_size("ctx"))])


def swap_tp(values):
    return lax.ppermute(values, "tp", [(0, 1), (1, 0)])


def in_order(mine, other, mine_first):
    return [jnp.where(mine_first, mine, other), jnp.where(mine_first, other, mine)]


def widen_chip(rows):
    if lax.axis_size("tp") == 2:
        rows = jnp.concatenate(in_order(rows, swap_tp(rows), lax.axis_index("tp") == 0), axis=0)
    else:
        rows = lax.all_gather(rows, "tp", axis=0, tiled=True)
    return in_order(rows, swap_core(rows), lax.axis_index("ctx") % 2 == 0)


def narrow_chip(partial):
    half = partial.shape[0] // 2
    core = lax.axis_index("ctx") % 2
    sent = lax.dynamic_slice_in_dim(partial, (1 - core) * half, half, 0)
    kept = lax.dynamic_slice_in_dim(partial, core * half, half, 0)
    pair = kept.astype(F32) + swap_core(sent.astype(BF16)).astype(F32)
    if lax.axis_size("tp") != 2:
        return lax.psum_scatter(pair.astype(BF16), "tp", scatter_dimension=0, tiled=True).astype(F32)
    rows = half // 2
    me = lax.axis_index("tp")
    sent = lax.dynamic_slice_in_dim(pair, (1 - me) * rows, rows, 0).astype(BF16)
    kept = lax.dynamic_slice_in_dim(pair, me * rows, rows, 0)
    return kept + swap_tp(sent).astype(F32)


def take_quarter(values, index, axis):
    size = values.shape[axis] // 4
    return lax.dynamic_slice_in_dim(values, index * size, size, axis)


def all_quarters(own):
    place = lax.axis_index("ctx")
    across = swap_chip(own)
    came = swap_core(jnp.stack([own, across]))
    low, high = in_order(jnp.stack([own, across]), came, place % 2 == 0)
    first = place < 2
    pick = jnp.where
    return [pick(first, low[0], low[1]), pick(first, high[0], high[1]), pick(first, low[1], low[0]), pick(first, high[1], high[0])]


def scatter_fsdp(values):
    return lax.psum_scatter(values, "fsdp", scatter_dimension=0, tiled=True)


def add_low(left, right):
    return (left.astype(F32) + right.astype(F32)).astype(BF16)


def call(kernel, name, flops, moved, **rest):
    return pl.pallas_call(
        kernel,
        name=name,
        cost_estimate=pl.CostEstimate(flops=flops, bytes_accessed=moved, transcendentals=0),
        compiler_params=pltpu.CompilerParams(vmem_limit_bytes=VMEM_BYTES),
        **rest,
    )


def whole():
    return pl.BlockSpec(memory_space=pltpu.VMEM)


def turn(values, cos, sin, direction):
    lane = lax.broadcasted_iota(jnp.int32, (1, LANES), 1)
    partner = jnp.where((lane // 32) % 2 == 0, pltpu.roll(values, 96, 1) * -direction, pltpu.roll(values, 32, 1) * direction)
    return values * cos + partner * sin


def project_kernel(first_query, rows_ref, weight_ref, cos_ref, sin_ref, q_ref, k_ref, v_ref):
    rows = rows_ref[...]
    cos, sin = cos_ref[...], sin_ref[...]
    width = q_ref.shape[1]

    def rotated(values, out_ref):
        for c in range(0, width, LANES):
            out_ref[:, c : c + LANES] = turn(values[:, c : c + LANES], cos, sin, 1.0).astype(BF16)

    rotated(dot_nt(rows, weight_ref[1]), k_ref)
    v_ref[...] = dot_nt(rows, weight_ref[2]).astype(BF16)

    @pl.when(pl.program_id(0) >= first_query)
    def _():
        rotated(dot_nt(rows, weight_ref[0]), q_ref)


def project(rows, weights, cos, sin, first_row):
    count, depth = rows.shape
    width = weights.shape[1]
    out = jax.ShapeDtypeStruct((count, width), BF16)
    tile = pl.BlockSpec((TILE, width), lambda i: (i, 0))
    return call(
        functools.partial(project_kernel, first_row // TILE),
        "project",
        count * depth * width * 5,
        count * depth * 2,
        grid=(count // TILE,),
        out_shape=(out, out, out),
        in_specs=[
            pl.BlockSpec((TILE, depth), lambda i: (i, 0)),
            pl.BlockSpec(weights.shape, lambda i: (0, 0, 0)),
            pl.BlockSpec((TILE, LANES), lambda i: (i, 0)),
            pl.BlockSpec((TILE, LANES), lambda i: (i, 0)),
        ],
        out_specs=[tile, tile, tile],
    )(rows, weights, cos, sin)


def lane_half(head):
    return (lax.broadcasted_iota(jnp.int32, (1, LANES), 1) // HEAD_DIM) == head % 2


def forward_kernel(rows, base, bounds, q_ref, k_ref, v_ref, start_ref, o_ref, lse_ref, q_buf, s_buf, top_buf, sum_buf, acc_buf):
    heads = q_buf.shape[0]
    zero = jnp.zeros((), BF16)
    for t in range(-(-rows // TILE)):
        low, high = bounds[0, t], bounds[1, t]
        n = min(TILE, rows - t * TILE)
        span = slice(t * TILE, (t + 1) * TILE)
        start = start_ref[:, span]
        row = base + t * TILE + lax.broadcasted_iota(jnp.int32, (1, TILE), 1)
        for h in range(heads):
            c = (h // 2) * LANES
            scaled = (q_ref[base + t * TILE : base + t * TILE + n, c : c + LANES].astype(F32) * HEAD_DIM**-0.5).astype(BF16)
            q_buf[h, :n, :] = jnp.where(lane_half(h), scaled, zero)
            if n < TILE:
                q_buf[h, n:, :] = jnp.zeros((TILE - n, LANES), BF16)
        top_buf[...] = jnp.full_like(top_buf, MASKED)
        sum_buf[...] = jnp.zeros_like(sum_buf)
        acc_buf[...] = jnp.zeros_like(acc_buf)

        @pl.loop(low, high)
        def _(i):
            at = pl.multiple_of(i * TILE, TILE)
            place = at + lax.broadcasted_iota(jnp.int32, (TILE, TILE), 0)
            allowed = (place >= start) & (place <= row)
            for h in range(heads):
                c = (h // 2) * LANES
                s = jnp.where(allowed, dot_nt(k_ref[pl.ds(at, TILE), c : c + LANES], q_buf[h]), MASKED)
                s_buf[h, pl.ds(at, TILE), :] = s
                top_buf[h] = jnp.maximum(top_buf[h], jnp.max(s.reshape(TILE // 8, 8, TILE), axis=0))

        tops = [jnp.max(top_buf[h], axis=0, keepdims=True) for h in range(heads)]

        @pl.loop(low, high)
        def _(i):
            at = pl.multiple_of(i * TILE, TILE)
            for h in range(heads):
                c = (h // 2) * LANES
                p = jnp.exp(s_buf[h, pl.ds(at, TILE), :] - tops[h])
                sum_buf[h] += jnp.sum(p.reshape(TILE // 8, 8, TILE), axis=0)
                both = dot_tn(v_ref[pl.ds(at, TILE), c : c + LANES], p.astype(BF16))
                acc_buf[h] += both[HEAD_DIM * (h % 2) : HEAD_DIM * (h % 2) + HEAD_DIM]

        for h in range(heads):
            total = jnp.sum(sum_buf[h], axis=0, keepdims=True)
            lse_ref[h : h + 1, span] = tops[h] + jnp.log(total)
            acc_buf[h] = acc_buf[h] / total
        for pair in range(heads // 2):
            o = jnp.transpose(jnp.concatenate([acc_buf[2 * pair], acc_buf[2 * pair + 1]], axis=0))
            o_ref[t * TILE : t * TILE + n, pair * LANES : (pair + 1) * LANES] = o[:n].astype(BF16)


def attend(bounds, q, k, v, start, rows, base):
    keys, width = k.shape
    heads = width // HEAD_DIM
    padded = -(-rows // TILE) * TILE
    return call(
        functools.partial(forward_kernel, rows, base),
        "attend",
        rows * rows * width * 8,
        keys * width * 8,
        out_shape=(jax.ShapeDtypeStruct((rows, width), BF16), jax.ShapeDtypeStruct((heads, padded), F32)),
        in_specs=[pl.BlockSpec(memory_space=pltpu.SMEM)] + [whole()] * 4,
        out_specs=[whole(), whole()],
        scratch_shapes=[
            pltpu.VMEM((heads, TILE, LANES), BF16),
            pltpu.VMEM((heads, keys, TILE), F32),
            pltpu.VMEM((heads, 8, TILE), F32),
            pltpu.VMEM((heads, 8, TILE), F32),
            pltpu.VMEM((heads, HEAD_DIM, TILE), F32),
        ],
    )(bounds, q, k, v, start)


def backward_kernel(
    rows, base, bounds, q_ref, k_ref, v_ref, o_ref, g_ref, lse_ref, start_ref, cos_ref, sin_ref,
    dq_ref, dk_ref, dv_ref, q_buf, g_buf, d_buf, dq_acc, dk_acc, dv_acc,
):
    heads = q_buf.shape[0]
    zero = jnp.zeros((), BF16)
    scale = HEAD_DIM**-0.5
    dk_acc[...] = jnp.zeros_like(dk_acc)
    dv_acc[...] = jnp.zeros_like(dv_acc)
    for t in range(-(-rows // TILE)):
        low, high = bounds[0, t], bounds[1, t]
        n = min(TILE, rows - t * TILE)
        span = slice(t * TILE, (t + 1) * TILE)
        here = slice(t * TILE, t * TILE + n)
        window = slice(base + t * TILE, base + t * TILE + n)
        start = start_ref[:, span]
        row = base + t * TILE + lax.broadcasted_iota(jnp.int32, (1, TILE), 1)
        for pair in range(heads // 2):
            c = pair * LANES
            scaled = (q_ref[window, c : c + LANES].astype(F32) * scale).astype(BF16)
            grad = g_ref[here, c : c + LANES]
            product = grad.astype(F32) * o_ref[here, c : c + LANES].astype(F32)
            if n < TILE:
                product = jnp.concatenate([product, jnp.zeros((TILE - n, LANES), F32)], axis=0)
            product = jnp.transpose(product)
            for h in (2 * pair, 2 * pair + 1):
                q_buf[h, :n, :] = jnp.where(lane_half(h), scaled, zero)
                g_buf[h, :n, :] = jnp.where(lane_half(h), grad, zero)
                if n < TILE:
                    q_buf[h, n:, :] = jnp.zeros((TILE - n, LANES), BF16)
                    g_buf[h, n:, :] = jnp.zeros((TILE - n, LANES), BF16)
                d_buf[h : h + 1, :] = jnp.sum(product[HEAD_DIM * (h % 2) : HEAD_DIM * (h % 2) + HEAD_DIM], axis=0, keepdims=True)
        dq_acc[...] = jnp.zeros_like(dq_acc)

        @pl.loop(low, high)
        def _(i):
            at = pl.multiple_of(i * TILE, TILE)
            place = at + lax.broadcasted_iota(jnp.int32, (TILE, TILE), 0)
            allowed = (place >= start) & (place <= row)
            for pair in range(heads // 2):
                c = pair * LANES
                k = k_ref[pl.ds(at, TILE), c : c + LANES]
                v = v_ref[pl.ds(at, TILE), c : c + LANES]
                dq = dk = dv = 0.0
                for h in (2 * pair, 2 * pair + 1):
                    p = jnp.where(allowed, jnp.exp(dot_nt(k, q_buf[h]) - lse_ref[h : h + 1, span]), 0.0)
                    ds = (p * (dot_nt(v, g_buf[h]) - d_buf[h : h + 1, :])).astype(BF16)
                    dv = dv + dot(p.astype(BF16), g_buf[h])
                    dk = dk + dot(ds, q_buf[h])
                    dq = dq + dot_tn(ds, jnp.where(lane_half(h), k, zero))
                dk_acc[pl.ds(at, TILE), c : c + LANES] += dk
                dv_acc[pl.ds(at, TILE), c : c + LANES] += dv
                dq_acc[:, c : c + LANES] += dq

        for c in range(0, heads * HEAD_DIM, LANES):
            dq = dq_acc[:n, c : c + LANES] * scale
            dq_ref[here, c : c + LANES] = turn(dq, cos_ref[window, :], sin_ref[window, :], -1.0).astype(BF16)
    for c in range(0, heads * HEAD_DIM, LANES):
        dk_ref[:, c : c + LANES] = turn(dk_acc[:, c : c + LANES], cos_ref[...], sin_ref[...], -1.0).astype(BF16)
    dv_ref[...] = dv_acc[...].astype(BF16)


def attend_back(bounds, q, k, v, o, grad, lse, start, cos, sin, rows, base):
    keys, width = k.shape
    heads = width // HEAD_DIM
    wide = jax.ShapeDtypeStruct((keys, width), BF16)
    return call(
        functools.partial(backward_kernel, rows, base),
        "attend_back",
        rows * rows * width * 20,
        keys * width * 16,
        out_shape=(jax.ShapeDtypeStruct((rows, width), BF16), wide, wide),
        in_specs=[pl.BlockSpec(memory_space=pltpu.SMEM)] + [whole()] * 9,
        out_specs=[whole()] * 3,
        scratch_shapes=[
            pltpu.VMEM((heads, TILE, LANES), BF16),
            pltpu.VMEM((heads, TILE, LANES), BF16),
            pltpu.VMEM((heads, TILE), F32),
            pltpu.VMEM((TILE, width), F32),
            pltpu.VMEM((keys, width), F32),
            pltpu.VMEM((keys, width), F32),
        ],
    )(bounds, q, k, v, o, grad, lse, start, cos, sin)


def hidden_kernel(row_tile, own_steps, n_ref, dy_ref, *refs):
    weights, (hidden_ref, gate_ref, up_ref, back_ref, acc) = refs[:6], refs[6:]
    step = pl.program_id(0)

    @pl.when(step == 0)
    def _():
        acc[...] = jnp.zeros_like(acc)

    def tile(gate_w, up_w, down_w):
        for r in range(0, n_ref.shape[0], row_tile):
            rows = slice(r, r + row_tile)
            gate = dot(n_ref[rows, :], gate_w[...])
            up = dot(n_ref[rows, :], up_w[...])
            grad = dot(dy_ref[rows, :], down_w[...])
            sig = 1.0 / (1.0 + jnp.exp(-gate))
            silu = gate * sig
            hidden_ref[rows, :] = (silu * up).astype(BF16)
            gate_grad = (grad * up * sig * (1.0 + gate * (1.0 - sig))).astype(BF16)
            up_grad = (grad * silu).astype(BF16)
            gate_ref[rows, :] = gate_grad
            up_ref[rows, :] = up_grad
            acc[rows, :] += dot_nt(gate_grad, gate_w[...]) + dot_nt(up_grad, up_w[...])

    @pl.when(step < own_steps)
    def _():
        tile(*weights[:3])

    @pl.when(step >= own_steps)
    def _():
        tile(*weights[3:])

    @pl.when(step == pl.num_programs(0) - 1)
    def _():
        back_ref[...] = acc[...].astype(BF16)


def feed(normed, dy, own, other):
    rows, depth = normed.shape
    units = own[0].shape[1]
    tile = min(TILE, units)
    steps = units // tile
    fixed = pl.BlockSpec((rows, depth), lambda i: (0, 0))
    first = pl.BlockSpec((depth, tile), lambda i: (0, jnp.minimum(i, steps - 1)))
    second = pl.BlockSpec((depth, tile), lambda i: (0, jnp.maximum(i - steps, 0)))
    out = pl.BlockSpec((rows, tile), lambda i: (0, i))
    wide = jax.ShapeDtypeStruct((rows, 2 * units), BF16)
    return call(
        functools.partial(hidden_kernel, rows // 4, steps),
        "feed",
        rows * depth * units * 20,
        depth * units * 12,
        grid=(2 * steps,),
        out_shape=(wide, wide, wide, jax.ShapeDtypeStruct((rows, depth), BF16)),
        in_specs=[fixed, fixed] + [first] * 3 + [second] * 3,
        out_specs=[out, out, out, fixed],
        scratch_shapes=[pltpu.VMEM((rows, depth), F32)],
    )(normed, dy, *own, *other)


def weights_kernel(n_ref, dy_ref, hidden_ref, gate_ref, up_ref, gate_out, up_out, down_out):
    gate_out[...] = dot_tn(n_ref[...], gate_ref[...]).astype(BF16)
    up_out[...] = dot_tn(n_ref[...], up_ref[...]).astype(BF16)
    down_out[...] = dot_tn(dy_ref[...], hidden_ref[...]).astype(BF16)


def feed_weights(normed, dy, hidden, gate_grad, up_grad, part):
    rows, depth = normed.shape
    units = hidden.shape[1] // 2
    tile = min(TILE, units)
    steps = units // tile
    fixed = pl.BlockSpec((rows, depth), lambda i: (0, 0))
    units_in = pl.BlockSpec((rows, tile), lambda i: (0, part * steps + i))
    out = pl.BlockSpec((depth, tile), lambda i: (0, i))
    shape = jax.ShapeDtypeStruct((depth, units), BF16)
    return call(
        weights_kernel,
        "feed_weights",
        rows * depth * units * 6,
        depth * units * 6,
        grid=(steps,),
        out_shape=(shape, shape, shape),
        in_specs=[fixed, fixed, units_in, units_in, units_in],
        out_specs=[out, out, out],
    )(normed, dy, hidden, gate_grad, up_grad)


def normalize_back(values, inverse, gain, grad_rows):
    scaled = grad_rows * gain
    return inverse * scaled - values * inverse**3 * jnp.mean(scaled * values, axis=-1, keepdims=True)


def inverse_rms(values):
    return lax.rsqrt(jnp.mean(values * values, axis=-1, keepdims=True) + EPSILON)


def shards(tokens, segment_ids, wq, wk, wv, wo, w_gate, w_up, w_down, gain_attn, gain_ffn, cotangent):
    tokens, cotangent, segment_ids = tokens[0], cotangent[0], segment_ids[0]
    fsdp = lax.axis_size("fsdp")
    place = lax.axis_index("ctx")
    chip, core = place // 2, place % 2
    rows = 2 * segment_ids.shape[0]
    real_width = wq.shape[1]
    shard_rows, depth = wq.shape[0], wq.shape[0] * fsdp
    width = -(-real_width // (4 * HEAD_DIM)) * 4 * HEAD_DIM
    part_width = width // 4
    keys = -(-2 * rows // TILE) * TILE

    def attention_piece():
        pad = ((0, 0), (0, width - real_width))
        pieces = [jnp.transpose(take_quarter(jnp.pad(w, pad), place, 1)) for w in (wq, wk, wv)]
        pieces.append(take_quarter(jnp.pad(wo, pad[::-1]), place, 0))
        return jnp.stack(pieces)

    attention_own = lax.all_gather(attention_piece(), "fsdp", axis=0, tiled=False)
    pieces = (take_quarter(w_gate, place, 1), take_quarter(w_up, place, 1), jnp.transpose(take_quarter(w_down, place, 0)))
    feed_own = [lax.all_gather(w, "fsdp", axis=0, tiled=True) for w in pieces]
    attention_both = jnp.stack([attention_own, swap_chip(attention_own)])
    attention_weights = jnp.transpose(attention_both, (2, 0, 3, 1, 4)).reshape(4, 2 * part_width, depth)
    feed_other = [swap_chip(w) for w in feed_own]
    gains = lax.all_gather(jnp.stack([gain_attn, gain_ffn]), "fsdp", axis=1, tiled=True).astype(F32)
    gain_one, gain_two = gains[0], gains[1]

    base = rows
    position = (chip * rows - rows + jnp.arange(keys, dtype=jnp.int32)).astype(F32)
    pair_index = (jnp.arange(LANES, dtype=jnp.int32) % (HEAD_DIM // 2)).astype(F32)
    angles = position[:, None] * (10000.0 ** (-pair_index * 2.0 / HEAD_DIM))[None, :]
    cos, sin = jnp.cos(angles), jnp.sin(angles)
    ids_own = jnp.concatenate(in_order(segment_ids, swap_core(segment_ids), core == 0))
    ids_before = jnp.where(chip > 0, to_later_chip(ids_own), -1)
    ids = jnp.concatenate([ids_before, ids_own])
    start = jnp.sum((ids[None, :] < ids_own[:, None]).astype(jnp.int32), axis=1)
    tiles = -(-rows // TILE)
    low = start[::TILE] // TILE
    ends = [-(-min(base + (t + 1) * TILE, base + rows) // TILE) for t in range(tiles)]
    bounds = jnp.stack([low, jnp.array(ends, jnp.int32)])
    start = jnp.pad(start, (0, tiles * TILE - rows), constant_values=2 * keys)[None]

    inputs = tokens.astype(F32)
    inv_one = inverse_rms(inputs)
    normed = (inputs * inv_one * gain_one).astype(BF16)
    before = widen_chip(to_later_chip(normed))
    window = jnp.concatenate(before + widen_chip(normed) + [jnp.zeros((keys - 2 * rows, depth), BF16)], axis=0)
    dy = jnp.concatenate(widen_chip(cotangent), axis=0)
    q, k, v = project(window, attention_weights, cos, sin, base)
    attended, lse = attend(bounds, q, k, v, start, rows, base)
    residual = inputs + narrow_chip(dot(attended, attention_weights[3]))

    inv_two = inverse_rms(residual)
    normed_two = jnp.concatenate(widen_chip((residual * inv_two * gain_two).astype(BF16)), axis=0)
    hidden, gate_grad, up_grad, back_two = feed(normed_two, dy, feed_own, feed_other)
    normed_two_grad = narrow_chip(back_two)
    grads_other = feed_weights(normed_two, dy, hidden, gate_grad, up_grad, 1)
    grads_own = feed_weights(normed_two, dy, hidden, gate_grad, up_grad, 0)
    feed_sums = [scatter_fsdp(add_low(own, swap_chip(other))) for own, other in zip(grads_own, grads_other)]
    units = feed_own[2].shape[1]
    out_partial = dot_nt(hidden[:, :units], feed_own[2]) + dot_nt(hidden[:, units:], feed_other[2])
    layer_out = residual + narrow_chip(out_partial)
    gain_two_grad = jnp.sum(normed_two_grad * residual * inv_two, axis=0)
    resid_grad = cotangent.astype(F32) + normalize_back(residual, inv_two, gain_two, normed_two_grad)

    grad = jnp.concatenate(widen_chip(resid_grad.astype(BF16)), axis=0)
    out_grad = dot_nt(grad, attention_weights[3]).astype(BF16)
    dq, dk, dv = attend_back(bounds, q, k, v, attended, out_grad, lse, start, cos, sin, rows, base)
    chip_rows = window[base : base + rows]
    weight_grads = jnp.stack(
        [
            dot_tn(dq, chip_rows).astype(BF16),
            dot_tn(dk, window).astype(BF16),
            dot_tn(dv, window).astype(BF16),
            dot_tn(attended, grad).astype(BF16),
        ]
    ).reshape(4, 2, part_width, fsdp, shard_rows)
    weight_grads = jnp.transpose(weight_grads, (1, 3, 0, 2, 4))
    attention_sum = scatter_fsdp(add_low(weight_grads[0], swap_chip(weight_grads[1])))[0]
    window_back = dot(dk, attention_weights[1]) + dot(dv, attention_weights[2])
    own_back = window_back[base : base + rows] + dot(dq, attention_weights[0])
    earlier_back = to_earlier_chip(narrow_chip(window_back[:base]).astype(BF16)).astype(F32)
    normed_grad = narrow_chip(own_back) + earlier_back
    gain_one_grad = jnp.sum(normed_grad * inputs * inv_one, axis=0)
    grad_input = resid_grad + normalize_back(inputs, inv_one, gain_one, normed_grad)

    attention_all = jnp.stack(all_quarters(attention_sum), axis=1).reshape(4, width, shard_rows)
    attention_all = attention_all[:, :real_width].astype(F32)
    feed_all = [all_quarters(total) for total in feed_sums]
    gain_grads = lax.psum(jnp.stack([gain_one_grad, gain_two_grad]), ("fsdp", "ctx", "tp"))
    gain_rows = gain_attn.shape[0]
    gain_own = lax.dynamic_slice_in_dim(gain_grads, lax.axis_index("fsdp") * gain_rows, gain_rows, 1)
    return (
        layer_out.astype(BF16)[None],
        grad_input[None],
        jnp.transpose(attention_all[0]),
        jnp.transpose(attention_all[1]),
        jnp.transpose(attention_all[2]),
        attention_all[3],
        jnp.concatenate(feed_all[0], axis=1).astype(F32),
        jnp.concatenate(feed_all[1], axis=1).astype(F32),
        jnp.transpose(jnp.concatenate(feed_all[2], axis=1)).astype(F32),
        gain_own[0],
        gain_own[1],
    )


def solution(mesh):
    rows = P("fsdp", ("ctx", "tp"), None)
    into, outof, gain = P("fsdp", "tp"), P("tp", "fsdp"), P("fsdp")
    return jax.shard_map(
        shards,
        mesh=mesh,
        in_specs=(rows, P("fsdp", "ctx"), into, into, into, outof, into, into, outof, gain, gain, rows),
        out_specs=(rows, rows, into, into, into, outof, into, into, outof, gain, gain),
        check_vma=False,
    )
```

time: 990 us -> 868 us (0.88)
  matrix products: 237 us -> 50.3 us
  waiting for transfers between devices: 232 us -> 369 us
  starting transfers between devices: 184 us -> 69 us
  Pallas kernels: 0 us -> 110 us
  blocking collectives: 136 us -> 49.3 us
  local copies, waits for them, and re-layouts: 46.8 us -> 82.7 us
  other arithmetic: 144 us -> 112 us
  between operations: 2.75 us -> 15.4 us
    ppermute x12, waiting for transfers between devices: 63.1 us -> 197 us  [swap_chip(): lax.ppermute(values, 'ctx', [(i, i ^ 2) for i in range(lax.axis_size('ctx...]
    pallas_call x0 -> x6, Pallas kernels: none -> 110 us  [the longest x1 30.8 us: feed(): call(functools.partial(hidden_kernel, rows // 4, steps), 'feed', rows * d...]
    dot_general x6 -> x0, matrix products: 110 us -> none  [the longest x1 27.7 us: shards(): jnp.einsum('qhd,khd->hqk', out_grad, values, preferred_element_type=F32)]
    ppermute x40 -> x13, starting transfers between devices: 118 us -> 17.2 us  [the longest x10 10.7 us: swap_tp(): return lax.ppermute(values, 'tp', [(0, 1), (1, 0)])]
    psum x1, blocking collectives: 136 us -> 38.9 us  [shards(): lax.psum(jnp.stack([gain_one_grad, gain_two_grad]), ('fsdp', 'ctx', 'tp'))]
    dot_general x7 -> x3, matrix products: 51.7 us -> 9.5 us  [dot_nt(): lax.dot_general(left, right, (((1,), (1,)), ((), ())), preferred_element_...]
    ppermute x40 -> x13, waiting for transfers between devices: 169 us -> 131 us  [the longest x10 125 us: swap_tp(): return lax.ppermute(values, 'tp', [(0, 1), (1, 0)])]
    concatenate x14 -> x8, other arithmetic: 45.3 us -> 12.6 us  [the longest x5 6.67 us: widen_chip(): jnp.concatenate(in_order(rows, swap_tp(rows), lax.axis_index('tp') == 0),...]
  transfers between devices with their start and end apart: 75 -> 48, of which waited for: 22 -> 20; matrix products, arithmetic and copies ran while one was open for 36% -> 25% of each run, Pallas kernels for 0% -> 8%
where the time goes in v2:
time: 868 us; the launch traced here: 857 us
  waiting for transfers between devices  369 us (43%)
  other arithmetic  112 us (13%)
  Pallas kernels  110 us (13%)
  local copies, waits for them, and re-layouts  82.7 us (10%)
  starting transfers between devices  69 us (8%)
  matrix products  50.3 us (6%)
  blocking collectives  49.3 us (6%)
  between operations  15.4 us (2%)
    ppermute x12, waiting for transfers between devices, swap_chip(): lax.ppermute(values, 'ctx', [(i, i ^ 2) for i in range(lax.axis_size('ctx...  197 us
    ppermute x10, waiting for transfers between devices, swap_tp(): return lax.ppermute(values, 'tp', [(0, 1), (1, 0)])  125 us
    psum x1, blocking collectives, shards(): lax.psum(jnp.stack([gain_one_grad, gain_two_grad]), ('fsdp', 'ctx', 'tp'))  38.9 us
    pallas_call x1, Pallas kernels, feed(): call(functools.partial(hidden_kernel, rows // 4, steps), 'feed', rows * d...  30.8 us
    ppermute x12, starting transfers between devices, swap_chip(): lax.ppermute(values, 'ctx', [(i, i ^ 2) for i in range(lax.axis_size('ctx...  28.5 us
    unnamed x154, local copies, waits for them, and re-layouts  28.1 us
    pallas_call x1, Pallas kernels, attend_back(): call(functools.partial(backward_kernel, rows, base), 'attend_back', rows...  25.1 us
    pallas_call x2, Pallas kernels, feed_weights(): call(weights_kernel, 'feed_weights', rows * depth * units * 6, depth * un...  23.4 us
  transfers between devices with their start and end apart: 48, of which 20 were waited for; matrix products, arithmetic and copies ran while one was open for 25% of the time, Pallas kernels for 8%

profile of v2, /device:TPU:1, one launch (start us, length us, event | category | flops | bytes accessed | tf_op | source)
XLA Modules:
  0.0 857.3 jit_solution(10959010566301482397)
XLA Ops:
  12.2 10.3 %all_gather.18 = bf16[2,1536]{1,0:T(2,128)(2,1)S(1)} all-gather(bf16[2,384]{1,0:T(2,128)(2,1)S(1)} %pad_maximum_fusion.16), channel_id=1, replica_groups=mesh['fsdp'=4,'ctx'=4,'tp'=2] {'fsdp'}, dimensions={1}, use_global_device_ids=true | all-gather | bytes 7680 | tf_op jit(solution)/shard_map/all_gather | solution.py:442
  52.4 28.8 %collective-permute-done.3 = bf16[272,1536]{1,0:T(8,128)(2,1)} collective-permute-done((bf16[272,1536]{1,0:T(8,128)(2,1)}, bf16[272,1536]{1,0:T(8,128)(2,1)}, u32[]{:S(2)}, u32[]{:S(2)}) %collective-permute-start.3) | collective-permute-done | bytes 835616 | tf_op jit(solution)/shard_map/ppermute | solution.py:49
  112.1 39.6 %collective-permute-done.7 = bf16[4,4,192,384]{3,0,2,1:T(4,128)(2,1)S(1)} collective-permute-done((bf16[4,4,192,384]{3,0,2,1:T(4,128)(2,1)S(1)}, bf16[4,4,192,384]{3,0,2,1:T(4,128)(2,1)S(1)}, u32[]{:S(2)}, u32[]{:S(2)}) %collective-permute-start.7) | collective-permute-done | bytes 2359328 | tf_op jit(solution)/shard_map/ppermute | solution.py:33
  170.5 17.9 %project.1 = (bf16[2304,384]{1,0:T(8,128)(2,1)}, bf16[2304,384]{1,0:T(8,128)(2,1)}, bf16[2304,384]{1,0:T(8,128)(2,1)}) custom-call(bf16[2304,1536]{1,0:T(8,128)(2,1)} %copy-done.57, bf16[4,384,1536]{2,1,0:T(8,128)(2,1)} %reshape.212.weight_ref, f32[2304,128]{1,0:T(8,128)} %get-tuple-element.158.cos_ref, f32[2304,128]{1,0:T(8,128)} %get-tuple-element.157.sin_ref), custom_call_target="tpu_custom_call" | custom-call | flops 6794772480 | bytes 7077888 | tf_op jit(solution)/shard_map/project/pallas_call | solution.py:144
  188.5 12.5 %attend.1 = (bf16[1088,384]{1,0:T(8,128)(2,1)}, f32[6,1280]{1,0:T(8,128)}) custom-call(s32[2,5]{1,0:T(2,128)} %pad_add_fusion.1.bounds, bf16[2304,384]{1,0:T(8,128)(2,1)} %get-tuple-element.29.q_ref, bf16[2304,384]{1,0:T(8,128)(2,1)} %get-tuple-element.30.k_ref, bf16[2304,384]{1,0:T(8,128)(2,1)} %get-tuple-element.31.v_ref, s32[1,1280]{1,0:T(1,128)} %broadcast_in_dim.26.start_ref), custom_call_target="tpu_custom_call" | custom-call | flops 3636461568 | bytes 7077888 | tf_op jit(solution)/shard_map/attend/pallas_call | solution.py:220
  217.2 18.7 %collective-permute-done.9 = bf16[272,1536]{1,0:T(8,128)(2,1)} collective-permute-done((bf16[272,1536]{1,0:T(8,128)(2,1)S(1)}, bf16[272,1536]{1,0:T(8,128)(2,1)}, u32[]{:S(2)}, u32[]{:S(2)}) %collective-permute-start.9) | collective-permute-done | bytes 835616 | tf_op jit(solution)/shard_map/ppermute | solution.py:49
  241.4 15.9 %collective-permute-done.10 = bf16[272,1536]{1,0:T(8,128)(2,1)} collective-permute-done((bf16[272,1536]{1,0:T(8,128)(2,1)S(1)}, bf16[272,1536]{1,0:T(8,128)(2,1)}, u32[]{:S(2)}, u32[]{:S(2)}) %collective-permute-start.10) | collective-permute-done | bytes 835616 | tf_op jit(solution)/shard_map/ppermute | solution.py:49
  269.4 20.9 %all-gather.6.cloned.1.call-done.refs_0_ = bf16[1536,512]{1,0:T(8,128)(2,1)} async-done(((bf16[384,512]{1,0:T(8,128)(2,1)}), bf16[1536,512]{1,0:T(8,128)(2,1)}) %all-gather.6.cloned.1.call-update) | async-done | bytes 1572880 | tf_op jit(solution)/shard_map/all_gather | solution.py:438
  304.4 33.7 %collective-permute-done.15.refs_4_ = bf16[1536,512]{1,0:T(8,128)(2,1)} collective-permute-done((bf16[1536,512]{1,0:T(8,128)(2,1)}, bf16[1536,512]{1,0:T(8,128)(2,1)}, u32[]{:S(2)}, u32[]{:S(2)}) %collective-permute-start.15) | collective-permute-done | bytes 1572896 | tf_op jit(solution)/shard_map/ppermute | solution.py:33
  338.1 33.7 %collective-permute-done.14.refs_3_ = bf16[1536,512]{1,0:T(8,128)(2,1)} collective-permute-done((bf16[1536,512]{1,0:T(8,128)(2,1)}, bf16[1536,512]{1,0:T(8,128)(2,1)}, u32[]{:S(2)}, u32[]{:S(2)}) %collective-permute-start.14) | collective-permute-done | bytes 1572896 | tf_op jit(solution)/shard_map/ppermute | solution.py:33
  371.9 30.8 %feed.1 = (bf16[1088,1024]{1,0:T(8,128)(2,1)}, bf16[1088,1024]{1,0:T(8,128)(2,1)}, bf16[1088,1024]{1,0:T(8,128)(2,1)}, bf16[1088,1536]{1,0:T(8,128)(2,1)}) custom-call(bf16[1088,1536]{1,0:T(8,128)(2,1)} %pad_maximum_fusion.n_ref, bf16[1088,1536]{1,0:T(8,128)(2,1)} %pad_maximum_fusion.1.dy_ref, bf16[1536,512]{1,0:T(8,128)(2,1)} %all-gather.6.cloned.1.call-done.refs_0_, ...), custom_call_target="tpu_custom_call" | custom-call | flops 17112760320 | bytes 9437184 | tf_op jit(solution)/shard_map/feed/pallas_call | solution.py:369
  402.6 11.9 %feed_weights.3 = (bf16[1536,512]{1,0:T(8,128)(2,1)}, bf16[1536,512]{1,0:T(8,128)(2,1)}, bf16[1536,512]{1,0:T(8,128)(2,1)}) custom-call(bf16[1088,1536]{1,0:T(8,128)(2,1)} %pad_maximum_fusion.n_ref, bf16[1088,1536]{1,0:T(8,128)(2,1)} %pad_maximum_fusion.1.dy_ref, bf16[1088,1024]{1,0:T(8,128)(2,1)} %get-tuple-element.33.hidden_ref, ...), custom_call_target="tpu_custom_call" | custom-call | flops 5133828096 | bytes 4718592 | tf_op jit(solution)/shard_map/feed_weights/pallas_call | solution.py:397
  415.9 11.4 %feed_weights.2 = (bf16[1536,512]{1,0:T(8,128)(2,1)}, bf16[1536,512]{1,0:T(8,128)(2,1)}, bf16[1536,512]{1,0:T(8,128)(2,1)}) custom-call(bf16[1088,1536]{1,0:T(8,128)(2,1)} %pad_maximum_fusion.n_ref, bf16[1088,1536]{1,0:T(8,128)(2,1)} %pad_maximum_fusion.1.dy_ref, bf16[1088,1024]{1,0:T(8,128)(2,1)} %get-tuple-element.33.hidden_ref, ...), custom_call_target="tpu_custom_call" | custom-call | flops 5133828096 | bytes 4718592 | tf_op jit(solution)/shard_map/feed_weights/pallas_call | solution.py:397
  427.3 22.8 %collective-permute-done.31 = bf16[1536,512]{1,0:T(8,128)(2,1)S(1)} collective-permute-done((bf16[1536,512]{1,0:T(8,128)(2,1)}, bf16[1536,512]{1,0:T(8,128)(2,1)S(1)}, u32[]{:S(2)}, u32[]{:S(2)}) %collective-permute-start.31) | collective-permute-done | bytes 1572896 | tf_op jit(solution)/shard_map/ppermute | solution.py:33
  468.8 24.9 %collective-permute-done.34 = bf16[1536,512]{1,0:T(8,128)(2,1)S(1)} collective-permute-done((bf16[1536,512]{1,0:T(8,128)(2,1)}, bf16[1536,512]{1,0:T(8,128)(2,1)S(1)}, u32[]{:S(2)}, u32[]{:S(2)}) %collective-permute-start.34) | collective-permute-done | bytes 1572896 | tf_op jit(solution)/shard_map/ppermute | solution.py:33
  502.9 14.5 %collective-permute-done.20 = bf16[272,1536]{1,0:T(8,128)(2,1)S(1)} collective-permute-done((bf16[272,1536]{1,0:T(8,128)(2,1)S(1)}, bf16[272,1536]{1,0:T(8,128)(2,1)S(1)}, u32[]{:S(2)}, u32[]{:S(2)}) %collective-permute-start.20) | collective-permute-done | bytes 835616 | tf_op jit(solution)/shard_map/ppermute | solution.py:49
  518.1 17.1 %collective-permute-done.18 = bf16[272,1536]{1,0:T(8,128)(2,1)S(1)} collective-permute-done((bf16[272,1536]{1,0:T(8,128)(2,1)S(1)}, bf16[272,1536]{1,0:T(8,128)(2,1)S(1)}, u32[]{:S(2)}, u32[]{:S(2)}) %collective-permute-start.18) | collective-permute-done | bytes 835616 | tf_op jit(solution)/shard_map/ppermute | solution.py:49
  543.3 14.0 %collective-permute-done.21 = bf16[272,1536]{1,0:T(8,128)(2,1)S(1)} collective-permute-done((bf16[272,1536]{1,0:T(8,128)(2,1)}, bf16[272,1536]{1,0:T(8,128)(2,1)S(1)}, u32[]{:S(2)}, u32[]{:S(2)}) %collective-permute-start.21) | collective-permute-done | bytes 835616 | tf_op jit(solution)/shard_map/ppermute | solution.py:49
  589.8 25.1 %attend_back.1 = (bf16[1088,384]{1,0:T(8,128)(2,1)}, bf16[2304,384]{1,0:T(8,128)(2,1)}, bf16[2304,384]{1,0:T(8,128)(2,1)}) custom-call(s32[2,5]{1,0:T(2,128)} %pad_add_fusion.1.bounds, bf16[2304,384]{1,0:T(8,128)(2,1)} %get-tuple-element.29.q_ref, bf16[2304,384]{1,0:T(8,128)(2,1)} %get-tuple-element.30.k_ref, bf16[2304,384]{1,0:T(8,128)(2,1)} %get-tuple-element.31.v_ref, ...), custom_call_target="tpu_custom_call" | custom-call | flops 9091153920 | bytes 14155776 | tf_op jit(solution)/shard_map/attend_back/pallas_call | solution.py:304
  653.1 13.5 %collective-permute-start.28 = (bf16[4,4,192,384]{3,2,1,0:T(8,128)(2,1)}, bf16[4,4,192,384]{3,2,1,0:T(8,128)(2,1)}, u32[]{:S(2)}, u32[]{:S(2)}) collective-permute-start(bf16[4,4,192,384]{3,2,1,0:T(8,128)(2,1)} %slice_bitcast_fusion), channel_id=1, source_target_pairs={{0,4},{2,6},{4,0},{6,2},{1,5},{3,7},{5,1},{7,3},{8,12},{10,14},{12... | collective-permute-start | bytes 7077896 | tf_op jit(solution)/shard_map/ppermute | solution.py:33
  694.1 23.3 %collective-permute-done.28 = bf16[4,4,192,384]{3,2,1,0:T(8,128)(2,1)} collective-permute-done((bf16[4,4,192,384]{3,2,1,0:T(8,128)(2,1)}, bf16[4,4,192,384]{3,2,1,0:T(8,128)(2,1)}, u32[]{:S(2)}, u32[]{:S(2)}) %collective-permute-start.28) | collective-permute-done | bytes 2359328 | tf_op jit(solution)/shard_map/ppermute | solution.py:33
  740.7 15.8 %collective-permute-done.26 = bf16[272,1536]{1,0:T(8,128)(2,1)S(1)} collective-permute-done((bf16[272,1536]{1,0:T(8,128)(2,1)S(1)}, bf16[272,1536]{1,0:T(8,128)(2,1)S(1)}, u32[]{:S(2)}, u32[]{:S(2)}) %collective-permute-start.26) | collective-permute-done | bytes 835616 | tf_op jit(solution)/shard_map/ppermute | solution.py:49
  777.5 13.8 %collective-permute-done.29 = bf16[4,192,384]{2,1,0:T(8,128)(2,1)S(1)} collective-permute-done((bf16[4,192,384]{2,1,0:T(8,128)(2,1)}, bf16[4,192,384]{2,1,0:T(8,128)(2,1)S(1)}, u32[]{:S(2)}, u32[]{:S(2)}) %collective-permute-start.29) | collective-permute-done | bytes 589856 | tf_op jit(solution)/shard_map/ppermute | solution.py:33
  797.8 38.9 %psum.7 = f32[2,1536]{1,0:T(2,128)S(1)} all-reduce(f32[2,1536]{1,0:T(2,128)S(1)} %pad_maximum_fusion.15), channel_id=1, replica_groups=mesh['fsdp'=4,'ctx'=4,'tp'=2] {'fsdp','ctx','tp'}, use_global_device_ids=true, to_apply=%region_11.12 | all-reduce | flops 3072 | bytes 24576 | tf_op jit(solution)/shard_map/psum | solution.py:507
  (373 shorter events, 331.9 us)
Async XLA Ops:
  7.2 88.2 %all-gather.12.cloned.1.call-start = ((), (), s32[]{:S(2)}) async-start(), calls=%async_computation.11 | async-start | bytes 2949120 | tf_op jit(solution)/shard_map/all_gather | solution.py:436
  12.1 250.4 %all-gather.10.cloned.1.call-start = ((), (), s32[]{:S(2)}) async-start(), calls=%async_computation.6 | async-start | bytes 1966080 | tf_op jit(solution)/shard_map/all_gather | solution.py:438
  28.6 59.9 %collective-permute-start.5 = (bf16[272,1536]{1,0:T(8,128)(2,1)}, bf16[272,1536]{1,0:T(8,128)(2,1)}, u32[]{:S(2)}, u32[]{:S(2)}) collective-permute-start(bf16[272,1536]{1,0:T(8,128)(2,1)} %fusion.10), channel_id=1, source_target_pairs={{0,1},{1,0},{2,3},{3,2},{4,5},{5,4},{6,7},{7,6},{8,9},{9,8},{10,11... | collective-permute-start | bytes 2506760 | tf_op jit(solution)/shard_map/ppermute | solution.py:49
  33.8 58.1 %collective-permute-start.12 = (bf16[272,1536]{1,0:T(8,128)(2,1)}, bf16[272,1536]{1,0:T(8,128)(2,1)}, u32[]{:S(2)}, u32[]{:S(2)}) collective-permute-start(bf16[272,1536]{1,0:T(8,128)(2,1)} %bitcast.14), channel_id=1, source_target_pairs={{0,1},{1,0},{2,3},{3,2},{4,5},{5,4},{6,7},{7,6},{8,9},{9,8},{10,11... | collective-permute-start | bytes 2506760 | tf_op jit(solution)/shard_map/ppermute | solution.py:49
  35.1 234.3 %all-gather.8.cloned.1.call-start = ((), (), s32[]{:S(2)}) async-start(), calls=%async_computation.5 | async-start | bytes 1966080 | tf_op jit(solution)/shard_map/all_gather | solution.py:438
  98.9 52.9 %collective-permute-start.7 = (bf16[4,4,192,384]{3,0,2,1:T(4,128)(2,1)S(1)}, bf16[4,4,192,384]{3,0,2,1:T(4,128)(2,1)S(1)}, u32[]{:S(2)}, u32[]{:S(2)}) collective-permute-start(bf16[4,4,192,384]{3,0,2,1:T(4,128)(2,1)S(1)} %copy.71), channel_id=1, source_target_pairs={{0,4},{2,6},{4,0},{6,2},{1,5},{3,7},{5,1},{7,3},{8,12},{10,14},{12... | collective-permute-start | bytes 7077896 | tf_op jit(solution)/shard_map/ppermute | solution.py:33
  209.7 80.6 %all-gather.6.cloned.1.call-start = ((), (), s32[]{:S(2)}) async-start(), calls=%async_computation.4 | async-start | bytes 1966080 | tf_op jit(solution)/shard_map/all_gather | solution.py:438
  241.3 327.7 %reduce-scatter.7.cloned.1.call-start = ((), (), s32[]{:S(2)}) async-start(), calls=%async_computation.8 | async-start | bytes 1966080 | tf_op jit(solution)/shard_map/reduce_scatter | solution.py:95
  262.5 42.0 %collective-permute-start.16 = (bf16[1536,512]{1,0:T(8,128)(2,1)}, bf16[1536,512]{1,0:T(8,128)(2,1)}, u32[]{:S(2)}, u32[]{:S(2)}) collective-permute-start(bf16[1536,512]{1,0:T(8,128)(2,1)} %all-gather.10.cloned.1.call-done.refs_2_), channel_id=1, source_target_pairs={{0,4},{2,6},{4,0},{6,2},{1,5},{3,7},{5,1},{7,3},{8,12},{10,14},{12... | collective-permute-start | bytes 4718600 | tf_op jit(solution)/shard_map/ppermute | solution.py:33
  269.4 68.8 %collective-permute-start.15 = (bf16[1536,512]{1,0:T(8,128)(2,1)}, bf16[1536,512]{1,0:T(8,128)(2,1)}, u32[]{:S(2)}, u32[]{:S(2)}) collective-permute-start(bf16[1536,512]{1,0:T(8,128)(2,1)} %all-gather.8.cloned.1.call-done.refs_1_), channel_id=1, source_target_pairs={{0,4},{2,6},{4,0},{6,2},{1,5},{3,7},{5,1},{7,3},{8,12},{10,14},{12... | collective-permute-start | bytes 4718600 | tf_op jit(solution)/shard_map/ppermute | solution.py:33
  290.3 81.5 %collective-permute-start.14 = (bf16[1536,512]{1,0:T(8,128)(2,1)}, bf16[1536,512]{1,0:T(8,128)(2,1)}, u32[]{:S(2)}, u32[]{:S(2)}) collective-permute-start(bf16[1536,512]{1,0:T(8,128)(2,1)} %all-gather.6.cloned.1.call-done.refs_0_), channel_id=1, source_target_pairs={{0,4},{2,6},{4,0},{6,2},{1,5},{3,7},{5,1},{7,3},{8,12},{10,14},{12... | collective-permute-start | bytes 4718600 | tf_op jit(solution)/shard_map/ppermute | solution.py:33
  453.1 117.3 %reduce-scatter.9.cloned.1.call-start = ((), (), s32[]{:S(2)}) async-start(), calls=%async_computation.9 | async-start | bytes 1966080 | tf_op jit(solution)/shard_map/reduce_scatter | solution.py:95
  456.0 39.6 %collective-permute-start.19 = (bf16[544,1536]{1,0:T(8,128)(2,1)}, bf16[544,1536]{1,0:T(8,128)(2,1)}, u32[]{:S(2)}, u32[]{:S(2)}) collective-permute-start(bf16[544,1536]{1,0:T(8,128)(2,1)} %constant_dynamic-slice_fusion.1), channel_id=1, source_target_pairs={{0,2},{2,0},{4,6},{6,4},{1,3},{3,1},{5,7},{7,5},{8,10},{10,8},{12,... | collective-permute-start | bytes 5013512 | tf_op jit(solution)/shard_map/ppermute | solution.py:37
  468.6 71.6 %collective-permute-start.37 = (bf16[1536,512]{1,0:T(8,128)(2,1)}, bf16[1536,512]{1,0:T(8,128)(2,1)}, u32[]{:S(2)}, u32[]{:S(2)}) collective-permute-start(bf16[1536,512]{1,0:T(8,128)(2,1)} %get-tuple-element.46), channel_id=1, source_target_pairs={{0,4},{2,6},{4,0},{6,2},{1,5},{3,7},{5,1},{7,3},{8,12},{10,14},{12... | collective-permute-start | bytes 4718600 | tf_op jit(solution)/shard_map/ppermute | solution.py:33
  495.4 84.3 %reduce-scatter.11.cloned.1.call-start = ((), (), s32[]{:S(2)}) async-start(), calls=%async_computation.10 | async-start | bytes 1966080 | tf_op jit(solution)/shard_map/reduce_scatter | solution.py:95
  543.2 228.9 %reduce-scatter.5.cloned.1.call-start = ((), (), s32[]{:S(2)}) async-start(), calls=%async_computation.7 | async-start | bytes 2949120 | tf_op jit(solution)/shard_map/reduce_scatter | solution.py:95
  569.0 117.2 %collective-permute-start.32 = (bf16[384,512]{1,0:T(8,128)(2,1)}, bf16[384,512]{1,0:T(8,128)(2,1)}, u32[]{:S(2)}, u32[]{:S(2)}) collective-permute-start(bf16[384,512]{1,0:T(8,128)(2,1)} %reduce-scatter.7.cloned.1.call-done), channel_id=1, source_target_pairs={{0,4},{2,6},{4,0},{6,2},{1,5},{3,7},{5,1},{7,3},{8,12},{10,14},{12... | collective-permute-start | bytes 1179656 | tf_op jit(solution)/shard_map/ppermute | solution.py:33
  570.4 119.8 %collective-permute-start.35 = (bf16[384,512]{1,0:T(8,128)(2,1)}, bf16[384,512]{1,0:T(8,128)(2,1)}, u32[]{:S(2)}, u32[]{:S(2)}) collective-permute-start(bf16[384,512]{1,0:T(8,128)(2,1)} %reduce-scatter.9.cloned.1.call-done), channel_id=1, source_target_pairs={{0,4},{2,6},{4,0},{6,2},{1,5},{3,7},{5,1},{7,3},{8,12},{10,14},{12... | collective-permute-start | bytes 1179656 | tf_op jit(solution)/shard_map/ppermute | solution.py:33
  579.7 113.0 %collective-permute-start.38 = (bf16[384,512]{1,0:T(8,128)(2,1)}, bf16[384,512]{1,0:T(8,128)(2,1)S(1)}, u32[]{:S(2)}, u32[]{:S(2)}) collective-permute-start(bf16[384,512]{1,0:T(8,128)(2,1)} %reduce-scatter.11.cloned.1.call-done), channel_id=1, source_target_pairs={{0,4},{2,6},{4,0},{6,2},{1,5},{3,7},{5,1},{7,3},{8,12},{10,14},{12... | collective-permute-start | bytes 1179656 | tf_op jit(solution)/shard_map/ppermute | solution.py:33
  653.1 64.3 %collective-permute-start.28 = (bf16[4,4,192,384]{3,2,1,0:T(8,128)(2,1)}, bf16[4,4,192,384]{3,2,1,0:T(8,128)(2,1)}, u32[]{:S(2)}, u32[]{:S(2)}) collective-permute-start(bf16[4,4,192,384]{3,2,1,0:T(8,128)(2,1)} %slice_bitcast_fusion), channel_id=1, source_target_pairs={{0,4},{2,6},{4,0},{6,2},{1,5},{3,7},{5,1},{7,3},{8,12},{10,14},{12... | collective-permute-start | bytes 7077896 | tf_op jit(solution)/shard_map/ppermute | solution.py:33
  690.1 47.2 %collective-permute-start.23 = (bf16[544,1536]{1,0:T(8,128)(2,1)S(1)}, bf16[544,1536]{1,0:T(8,128)(2,1)}, u32[]{:S(2)}, u32[]{:S(2)}) collective-permute-start(bf16[544,1536]{1,0:T(8,128)(2,1)S(1)} %dynamic-slice_convert_fusion.1), channel_id=1, source_target_pairs={{0,2},{2,0},{4,6},{6,4},{1,3},{3,1},{5,7},{7,5},{8,10},{10,8},{12,... | collective-permute-start | bytes 5013512 | tf_op jit(solution)/shard_map/ppermute | solution.py:37
  690.2 43.0 %collective-permute-start.25 = (bf16[544,1536]{1,0:T(8,128)(2,1)}, bf16[544,1536]{1,0:T(8,128)(2,1)}, u32[]{:S(2)}, u32[]{:S(2)}) collective-permute-start(bf16[544,1536]{1,0:T(8,128)(2,1)} %dynamic-slice_convert_fusion), channel_id=1, source_target_pairs={{0,2},{2,0},{4,6},{6,4},{1,3},{3,1},{5,7},{7,5},{8,10},{10,8},{12,... | collective-permute-start | bytes 5013512 | tf_op jit(solution)/shard_map/ppermute | solution.py:37
  740.4 54.1 %collective-permute-start.24 = (bf16[272,1536]{1,0:T(8,128)(2,1)}, bf16[272,1536]{1,0:T(8,128)(2,1)}, u32[]{:S(2)}, u32[]{:S(2)}) collective-permute-start(bf16[272,1536]{1,0:T(8,128)(2,1)} %dynamic-slice_convert_fusion.5), channel_id=1, source_target_pairs={{0,1},{1,0},{2,3},{3,2},{4,5},{5,4},{6,7},{7,6},{8,9},{9,8},{10,11... | collective-permute-start | bytes 2506760 | tf_op jit(solution)/shard_map/ppermute | solution.py:49
  792.5 48.1 %collective-permute-start.30 = (bf16[2,4,192,384]{3,2,1,0:T(8,128)(2,1)}, bf16[2,4,192,384]{3,2,1,0:T(8,128)(2,1)}, u32[]{:S(2)}, u32[]{:S(2)}) collective-permute-start(bf16[2,4,192,384]{3,2,1,0:T(8,128)(2,1)} %pad_maximum_fusion.10), channel_id=1, source_target_pairs={{0,2},{2,0},{4,6},{6,4},{1,3},{3,1},{5,7},{7,5},{8,10},{10,8},{12,... | collective-permute-start | bytes 3538952 | tf_op jit(solution)/shard_map/ppermute | solution.py:37
  (95 other events, 1375.1 us)
Sparse Core Ops, SparseCore 0:
  12.2 52.5 all-gather.11
  66.4 35.8 all-gather.9
  209.8 42.4 all-gather.7
  254.3 35.9 all-gather.5
  453.2 36.3 reduce-scatter.6
  495.5 36.0 reduce-scatter.8
  543.4 36.2 reduce-scatter.10
  723.8 48.3 reduce-scatter.4

commit v3 on v2

--- a/solution.py
+++ b/solution.py
@@ -53,27 +53,40 @@
     return [jnp.where(mine_first, mine, other), jnp.where(mine_first, other, mine)]
 
 
+def after(values, *earlier):
+    return lax.optimization_barrier((values, earlier))[0]
+
+
+def widen_tp(rows):
+    if lax.axis_size("tp") == 2:
+        return [rows, swap_tp(rows)]
+    return [lax.all_gather(rows, "tp", axis=0, tiled=True)]
+
+
 def widen_chip(rows):
-    if lax.axis_size("tp") == 2:
-        rows = jnp.concatenate(in_order(rows, swap_tp(rows), lax.axis_index("tp") == 0), axis=0)
-    else:
-        rows = lax.all_gather(rows, "tp", axis=0, tiled=True)
-    return in_order(rows, swap_core(rows), lax.axis_index("ctx") % 2 == 0)
-
-
-def narrow_chip(partial):
-    half = partial.shape[0] // 2
+    mine = widen_tp(rows)
+    return mine + [swap_core(block) for block in mine]
+
+
+def block_offset(index, half):
     core = lax.axis_index("ctx") % 2
-    sent = lax.dynamic_slice_in_dim(partial, (1 - core) * half, half, 0)
-    kept = lax.dynamic_slice_in_dim(partial, core * half, half, 0)
-    pair = kept.astype(F32) + swap_core(sent.astype(BF16)).astype(F32)
+    if lax.axis_size("tp") != 2:
+        return jnp.where(index == 0, core, 1 - core) * half
+    place = lax.axis_index("tp")
+    core = core if index < 2 else 1 - core
+    place = place if index % 2 == 0 else 1 - place
+    return core * half + place * (half // 2)
+
+
+def narrow_core(kept, sent):
+    return kept.astype(F32) + swap_core(sent).astype(F32)
+
+
+def narrow_tp(pair):
     if lax.axis_size("tp") != 2:
         return lax.psum_scatter(pair.astype(BF16), "tp", scatter_dimension=0, tiled=True).astype(F32)
-    rows = half // 2
-    me = lax.axis_index("tp")
-    sent = lax.dynamic_slice_in_dim(pair, (1 - me) * rows, rows, 0).astype(BF16)
-    kept = lax.dynamic_slice_in_dim(pair, me * rows, rows, 0)
-    return kept + swap_tp(sent).astype(F32)
+    rows = pair.shape[0] // 2
+    return pair[:rows] + swap_tp(pair[rows:].astype(BF16)).astype(F32)
 
 
 def take_quarter(values, index, axis):
@@ -91,10 +104,6 @@
     return [pick(first, low[0], low[1]), pick(first, high[0], high[1]), pick(first, low[1], low[0]), pick(first, high[1], high[0])]
 
 
-def scatter_fsdp(values):
-    return lax.psum_scatter(values, "fsdp", scatter_dimension=0, tiled=True)
-
-
 def add_low(left, right):
     return (left.astype(F32) + right.astype(F32)).astype(BF16)
 
@@ -119,43 +128,199 @@
     return values * cos + partner * sin
 
 
-def project_kernel(first_query, rows_ref, weight_ref, cos_ref, sin_ref, q_ref, k_ref, v_ref):
-    rows = rows_ref[...]
-    cos, sin = cos_ref[...], sin_ref[...]
+def block_spans(count, half, base):
+    block = 2 * half // count
+    offsets = [pl.multiple_of(block_offset(i, half), 16) for i in range(count)]
+    return [pl.ds(at, block) for at in offsets] + [pl.ds(pl.multiple_of(base + at, 16), block) for at in offsets]
+
+
+def project_kernel(count, half, base, *refs):
+    blocks = refs[: 2 * count]
+    weight_ref, cos_ref, sin_ref, q_ref, k_ref, v_ref = refs[2 * count :]
     width = q_ref.shape[1]
-
-    def rotated(values, out_ref):
-        for c in range(0, width, LANES):
-            out_ref[:, c : c + LANES] = turn(values[:, c : c + LANES], cos, sin, 1.0).astype(BF16)
-
-    rotated(dot_nt(rows, weight_ref[1]), k_ref)
-    v_ref[...] = dot_nt(rows, weight_ref[2]).astype(BF16)
-
-    @pl.when(pl.program_id(0) >= first_query)
-    def _():
-        rotated(dot_nt(rows, weight_ref[0]), q_ref)
-
-
-def project(rows, weights, cos, sin, first_row):
-    count, depth = rows.shape
+    tail = k_ref.shape[0] - 2 * base
+    block = 2 * half // count
+    k_ref[2 * base :, :] = jnp.zeros((tail, width), BF16)
+    v_ref[2 * base :, :] = jnp.zeros((tail, width), BF16)
+    for i, span in enumerate(block_spans(count, half, base)):
+        rows = blocks[i][...]
+        cos, sin = cos_ref[span, :], sin_ref[span, :]
+
+        def rotated(values, out_ref, where):
+            for c in range(0, width, LANES):
+                out_ref[where, c : c + LANES] = turn(values[:, c : c + LANES], cos, sin, 1.0).astype(BF16)
+
+        rotated(dot_nt(rows, weight_ref[1]), k_ref, span)
+        v_ref[span, :] = dot_nt(rows, weight_ref[2]).astype(BF16)
+        if i >= count:
+            own = pl.ds(pl.multiple_of(block_offset(i - count, half), 16), block)
+            rotated(dot_nt(rows, weight_ref[0]), q_ref, own)
+
+
+def project(blocks, weights, cos, sin, keys):
+    count = len(blocks) // 2
+    block, depth = blocks[0].shape
+    rows = count * block
     width = weights.shape[1]
-    out = jax.ShapeDtypeStruct((count, width), BF16)
-    tile = pl.BlockSpec((TILE, width), lambda i: (i, 0))
-    return call(
-        functools.partial(project_kernel, first_row // TILE),
+    wide = jax.ShapeDtypeStruct((keys, width), BF16)
+    return call(
+        functools.partial(project_kernel, count, rows // 2, rows),
         "project",
-        count * depth * width * 5,
-        count * depth * 2,
-        grid=(count // TILE,),
-        out_shape=(out, out, out),
-        in_specs=[
-            pl.BlockSpec((TILE, depth), lambda i: (i, 0)),
-            pl.BlockSpec(weights.shape, lambda i: (0, 0, 0)),
-            pl.BlockSpec((TILE, LANES), lambda i: (i, 0)),
-            pl.BlockSpec((TILE, LANES), lambda i: (i, 0)),
-        ],
-        out_specs=[tile, tile, tile],
-    )(rows, weights, cos, sin)
+        keys * depth * width * 5,
+        keys * depth * 2,
+        out_shape=(jax.ShapeDtypeStruct((rows, width), BF16), wide, wide),
+        in_specs=[whole()] * (2 * count + 3),
+        out_specs=[whole()] * 3,
+    )(*blocks, weights, cos, sin)
+
+
+def place_kernel(fsdp, *refs):
+    blocks, out_ref = refs[:-1], refs[-1]
+    part, columns = blocks[0].shape[1:]
+    me = lax.axis_index("fsdp")
+    for i, block in enumerate(blocks):
+        at = pl.multiple_of((me + i % fsdp) % fsdp * columns, LANES)
+        first = i // fsdp * part
+        out_ref[:, first : first + part, pl.ds(at, columns)] = block[...]
+
+
+def place_weights(blocks, fsdp):
+    kinds, part, columns = blocks[0].shape
+    shape = (kinds, 2 * part, fsdp * columns)
+    return call(
+        functools.partial(place_kernel, fsdp),
+        "place_weights",
+        0,
+        kinds * part * fsdp * columns * 8,
+        out_shape=jax.ShapeDtypeStruct(shape, BF16),
+        in_specs=[whole()] * len(blocks),
+        out_specs=whole(),
+    )(*blocks)
+
+
+def out_kernel(half, count, o_ref, weight_ref, kept_ref, sent_ref):
+    block = 2 * half // count
+    for i in range(count):
+        at = pl.multiple_of(block_offset(i, half), 16)
+        part = dot(o_ref[pl.ds(at, block), :], weight_ref[3])
+        if i < count // 2:
+            kept_ref[i * block : (i + 1) * block, :] = part
+        else:
+            sent_ref[i * block - half : (i + 1) * block - half, :] = part.astype(BF16)
+
+
+def out_project(attended, weights, count):
+    rows, width = attended.shape
+    depth = weights.shape[2]
+    half = rows // 2
+    return call(
+        functools.partial(out_kernel, half, count),
+        "out_project",
+        rows * width * depth * 2,
+        rows * depth * 3,
+        out_shape=(jax.ShapeDtypeStruct((half, depth), F32), jax.ShapeDtypeStruct((half, depth), BF16)),
+        in_specs=[whole(), whole()],
+        out_specs=[whole(), whole()],
+    )(attended, weights)
+
+
+def out_back_kernel(half, count, fsdp, o_ref, weight_ref, *refs):
+    blocks, (grad_ref, own_ref, other_ref, chip_rows) = refs[:count], refs[count:]
+    block = 2 * half // count
+    for i in range(count):
+        at = pl.multiple_of(block_offset(i, half), 16)
+        grad = blocks[i][...]
+        grad_ref[pl.ds(at, block), :] = dot_nt(grad, weight_ref[3]).astype(BF16)
+        chip_rows[pl.ds(at, block), :] = grad
+    total = dot_tn(o_ref[...], chip_rows[...])
+    part, columns = own_ref.shape[1], own_ref.shape[2]
+    for z in range(fsdp):
+        own_ref[z] = total[:part, z * columns : (z + 1) * columns].astype(BF16)
+        other_ref[z] = total[part:, z * columns : (z + 1) * columns].astype(BF16)
+
+
+def out_back(attended, weights, blocks, fsdp):
+    rows, width = attended.shape
+    depth = weights.shape[2]
+    grads = jax.ShapeDtypeStruct((fsdp, width // 2, depth // fsdp), BF16)
+    return call(
+        functools.partial(out_back_kernel, rows // 2, len(blocks), fsdp),
+        "out_back",
+        rows * width * depth * 4,
+        rows * depth * 3,
+        out_shape=(jax.ShapeDtypeStruct((rows, width), BF16), grads, grads),
+        in_specs=[whole()] * (2 + len(blocks)),
+        out_specs=[whole()] * 3,
+        scratch_shapes=[pltpu.VMEM((rows, depth), BF16)],
+    )(attended, weights, *blocks)
+
+
+def project_weights_kernel(count, half, base, dq_ref, dk_ref, dv_ref, *refs):
+    blocks, out_refs, window = refs[: 2 * count], refs[2 * count : -1], refs[-1]
+    window[2 * base :, :] = jnp.zeros((window.shape[0] - 2 * base, window.shape[1]), BF16)
+    for block, span in zip(blocks, block_spans(count, half, base)):
+        window[span, :] = block[...]
+    part = out_refs[0].shape[1]
+    results = (
+        dot_tn(dv_ref[...], window[...]),
+        dot_tn(dk_ref[...], window[...]),
+        dot_tn(dq_ref[...], window[base : 2 * base, :]),
+    )
+    for i, result in enumerate(results):
+        out_refs[2 * i][0] = result[:part].astype(BF16)
+        out_refs[2 * i + 1][0] = result[part:].astype(BF16)
+
+
+def project_weights(dq, dk, dv, blocks, fsdp):
+    keys, width = dk.shape
+    rows = dq.shape[0]
+    block, depth = blocks[0].shape
+    count = len(blocks) // 2
+    columns = depth // fsdp
+    fixed = lambda array: pl.BlockSpec(array.shape, lambda z: (0, 0))
+    return call(
+        functools.partial(project_weights_kernel, count, rows // 2, rows),
+        "project_weights",
+        keys * width * depth * 5,
+        keys * depth * 2,
+        grid=(fsdp,),
+        out_shape=[jax.ShapeDtypeStruct((fsdp, width // 2, columns), BF16)] * 6,
+        in_specs=[fixed(dq), fixed(dk), fixed(dv)] + [pl.BlockSpec((block, columns), lambda z: (0, z))] * (2 * count),
+        out_specs=[pl.BlockSpec((1, width // 2, columns), lambda z: (z, 0, 0))] * 6,
+        scratch_shapes=[pltpu.VMEM((keys, columns), BF16)],
+    )(dq, dk, dv, *blocks)
+
+
+def project_back_kernel(half, count, base, dq_ref, dk_ref, dv_ref, weight_ref, *out_refs):
+    block = 2 * half // count
+    for part in range(2):
+        kept_ref, sent_ref = out_refs[2 * part : 2 * part + 2]
+        for i in range(count):
+            at = pl.multiple_of(block_offset(i, half), 16)
+            where = pl.ds(part * base + at, block)
+            total = dot(dk_ref[where, :], weight_ref[1]) + dot(dv_ref[where, :], weight_ref[2])
+            if part == 1:
+                total = total + dot(dq_ref[pl.ds(at, block), :], weight_ref[0])
+            if i < count // 2:
+                kept_ref[i * block : (i + 1) * block, :] = total
+            else:
+                sent_ref[i * block - half : (i + 1) * block - half, :] = total.astype(BF16)
+
+
+def project_back(dq, dk, dv, weights, base, count):
+    rows, width = dq.shape
+    depth = weights.shape[2]
+    half = rows // 2
+    kept, sent = jax.ShapeDtypeStruct((half, depth), F32), jax.ShapeDtypeStruct((half, depth), BF16)
+    return call(
+        functools.partial(project_back_kernel, half, count, base),
+        "project_back",
+        rows * width * depth * 10,
+        rows * depth * 6,
+        out_shape=(kept, sent, kept, sent),
+        in_specs=[whole()] * 4,
+        out_specs=[whole()] * 4,
+    )(dq, dk, dv, weights)
 
 
 def lane_half(head):
@@ -173,7 +338,7 @@
         row = base + t * TILE + lax.broadcasted_iota(jnp.int32, (1, TILE), 1)
         for h in range(heads):
             c = (h // 2) * LANES
-            scaled = (q_ref[base + t * TILE : base + t * TILE + n, c : c + LANES].astype(F32) * HEAD_DIM**-0.5).astype(BF16)
+            scaled = (q_ref[t * TILE : t * TILE + n, c : c + LANES].astype(F32) * HEAD_DIM**-0.5).astype(BF16)
             q_buf[h, :n, :] = jnp.where(lane_half(h), scaled, zero)
             if n < TILE:
                 q_buf[h, n:, :] = jnp.zeros((TILE - n, LANES), BF16)
@@ -254,7 +419,7 @@
         row = base + t * TILE + lax.broadcasted_iota(jnp.int32, (1, TILE), 1)
         for pair in range(heads // 2):
             c = pair * LANES
-            scaled = (q_ref[window, c : c + LANES].astype(F32) * scale).astype(BF16)
+            scaled = (q_ref[here, c : c + LANES].astype(F32) * scale).astype(BF16)
             grad = g_ref[here, c : c + LANES]
             product = grad.astype(F32) * o_ref[here, c : c + LANES].astype(F32)
             if n < TILE:
@@ -320,20 +485,24 @@
     )(bounds, q, k, v, o, grad, lse, start, cos, sin)
 
 
-def hidden_kernel(row_tile, own_steps, n_ref, dy_ref, *refs):
-    weights, (hidden_ref, gate_ref, up_ref, back_ref, acc) = refs[:6], refs[6:]
+def feed_kernel(count, own_steps, *refs):
+    n_refs, dy_refs, weights = refs[:count], refs[count : 2 * count], refs[2 * count : 2 * count + 6]
+    hidden_ref, gate_ref, up_ref, kept_ref, sent_ref, acc = refs[2 * count + 6 :]
     step = pl.program_id(0)
+    block = n_refs[0].shape[0]
+    half = kept_ref.shape[0]
 
     @pl.when(step == 0)
     def _():
         acc[...] = jnp.zeros_like(acc)
 
     def tile(gate_w, up_w, down_w):
-        for r in range(0, n_ref.shape[0], row_tile):
-            rows = slice(r, r + row_tile)
-            gate = dot(n_ref[rows, :], gate_w[...])
-            up = dot(n_ref[rows, :], up_w[...])
-            grad = dot(dy_ref[rows, :], down_w[...])
+        for i in range(count):
+            rows = slice(i * block, (i + 1) * block)
+            normed = n_refs[i][...]
+            gate = dot(normed, gate_w[...])
+            up = dot(normed, up_w[...])
+            grad = dot(dy_refs[i][...], down_w[...])
             sig = 1.0 / (1.0 + jnp.exp(-gate))
             silu = gate * sig
             hidden_ref[rows, :] = (silu * up).astype(BF16)
@@ -353,57 +522,100 @@
 
     @pl.when(step == pl.num_programs(0) - 1)
     def _():
-        back_ref[...] = acc[...].astype(BF16)
+        kept_ref[...] = acc[:half, :]
+        sent_ref[...] = acc[half:, :].astype(BF16)
 
 
 def feed(normed, dy, own, other):
-    rows, depth = normed.shape
+    count = len(normed)
+    block, depth = normed[0].shape
+    rows = count * block
     units = own[0].shape[1]
     tile = min(TILE, units)
     steps = units // tile
-    fixed = pl.BlockSpec((rows, depth), lambda i: (0, 0))
+    fixed = pl.BlockSpec((block, depth), lambda i: (0, 0))
+    kept = pl.BlockSpec((rows // 2, depth), lambda i: (0, 0))
     first = pl.BlockSpec((depth, tile), lambda i: (0, jnp.minimum(i, steps - 1)))
     second = pl.BlockSpec((depth, tile), lambda i: (0, jnp.maximum(i - steps, 0)))
     out = pl.BlockSpec((rows, tile), lambda i: (0, i))
     wide = jax.ShapeDtypeStruct((rows, 2 * units), BF16)
     return call(
-        functools.partial(hidden_kernel, rows // 4, steps),
+        functools.partial(feed_kernel, count, steps),
         "feed",
         rows * depth * units * 20,
         depth * units * 12,
         grid=(2 * steps,),
-        out_shape=(wide, wide, wide, jax.ShapeDtypeStruct((rows, depth), BF16)),
-        in_specs=[fixed, fixed] + [first] * 3 + [second] * 3,
-        out_specs=[out, out, out, fixed],
+        out_shape=(wide, wide, wide, jax.ShapeDtypeStruct((rows // 2, depth), F32), jax.ShapeDtypeStruct((rows // 2, depth), BF16)),
+        in_specs=[fixed] * (2 * count) + [first] * 3 + [second] * 3,
+        out_specs=[out, out, out, kept, kept],
         scratch_shapes=[pltpu.VMEM((rows, depth), F32)],
-    )(normed, dy, *own, *other)
-
-
-def weights_kernel(n_ref, dy_ref, hidden_ref, gate_ref, up_ref, gate_out, up_out, down_out):
-    gate_out[...] = dot_tn(n_ref[...], gate_ref[...]).astype(BF16)
-    up_out[...] = dot_tn(n_ref[...], up_ref[...]).astype(BF16)
-    down_out[...] = dot_tn(dy_ref[...], hidden_ref[...]).astype(BF16)
+    )(*normed, *dy, *own, *other)
+
+
+def feed_weights_kernel(count, *refs):
+    blocks = refs[: 2 * count]
+    hidden_ref, gate_ref, up_ref, gate_out, up_out, down_out, normed, dy = refs[2 * count :]
+    block = blocks[0].shape[0]
+
+    @pl.when(pl.program_id(0) == 0)
+    def _():
+        for i in range(count):
+            normed[i * block : (i + 1) * block, :] = blocks[i][...]
+            dy[i * block : (i + 1) * block, :] = blocks[count + i][...]
+
+    gate_out[...] = dot_tn(normed[...], gate_ref[...]).astype(BF16)
+    up_out[...] = dot_tn(normed[...], up_ref[...]).astype(BF16)
+    down_out[...] = dot_tn(dy[...], hidden_ref[...]).astype(BF16)
 
 
 def feed_weights(normed, dy, hidden, gate_grad, up_grad, part):
-    rows, depth = normed.shape
+    count = len(normed)
+    block, depth = normed[0].shape
+    rows = count * block
     units = hidden.shape[1] // 2
     tile = min(TILE, units)
     steps = units // tile
-    fixed = pl.BlockSpec((rows, depth), lambda i: (0, 0))
+    fixed = pl.BlockSpec((block, depth), lambda i: (0, 0))
     units_in = pl.BlockSpec((rows, tile), lambda i: (0, part * steps + i))
     out = pl.BlockSpec((depth, tile), lambda i: (0, i))
     shape = jax.ShapeDtypeStruct((depth, units), BF16)
     return call(
-        weights_kernel,
+        functools.partial(feed_weights_kernel, count),
         "feed_weights",
         rows * depth * units * 6,
         depth * units * 6,
         grid=(steps,),
         out_shape=(shape, shape, shape),
-        in_specs=[fixed, fixed, units_in, units_in, units_in],
+        in_specs=[fixed] * (2 * count) + [units_in] * 3,
         out_specs=[out, out, out],
-    )(normed, dy, hidden, gate_grad, up_grad)
+        scratch_shapes=[pltpu.VMEM((rows, depth), BF16)] * 2,
+    )(*normed, *dy, hidden, gate_grad, up_grad)
+
+
+def feed_out_kernel(half, hidden_ref, own_ref, other_ref, kept_ref, sent_ref):
+    units = own_ref.shape[1]
+    tile = half // 2
+    for r in range(0, 2 * half, tile):
+        total = dot_nt(hidden_ref[r : r + tile, :units], own_ref[...]) + dot_nt(hidden_ref[r : r + tile, units:], other_ref[...])
+        if r < half:
+            kept_ref[r : r + tile, :] = total
+        else:
+            sent_ref[r - half : r - half + tile, :] = total.astype(BF16)
+
+
+def feed_out(hidden, own, other):
+    rows = hidden.shape[0]
+    depth, units = own.shape
+    half = rows // 2
+    return call(
+        functools.partial(feed_out_kernel, half),
+        "feed_out",
+        rows * depth * units * 4,
+        rows * depth * 3,
+        out_shape=(jax.ShapeDtypeStruct((half, depth), F32), jax.ShapeDtypeStruct((half, depth), BF16)),
+        in_specs=[whole()] * 3,
+        out_specs=[whole()] * 2,
+    )(hidden, own, other)
 
 
 def normalize_back(values, inverse, gain, grad_rows):
@@ -413,6 +625,36 @@
 
 def inverse_rms(values):
     return lax.rsqrt(jnp.mean(values * values, axis=-1, keepdims=True) + EPSILON)
+
+
+def pull_fsdp(values, step):
+    count = lax.axis_size("fsdp")
+    return lax.ppermute(values, "fsdp", [(i, (i - step) % count) for i in range(count)])
+
+
+def gather_gains(gains):
+    count = lax.axis_size("fsdp")
+    rolled = jnp.concatenate([gains] + [pull_fsdp(gains, step) for step in range(1, count)], axis=1).astype(F32)
+    twice = jnp.concatenate([rolled, rolled], axis=1)
+    at = (count - lax.axis_index("fsdp")) % count * gains.shape[1]
+    return lax.dynamic_slice_in_dim(twice, at, rolled.shape[1], 1)
+
+
+def gain_totals(gains):
+    if lax.axis_size("tp") == 2:
+        gains = gains + swap_tp(gains)
+    else:
+        gains = lax.psum(gains, "tp")
+    gains = gains + swap_core(gains)
+    gains = gains + swap_chip(gains)
+    count = lax.axis_size("fsdp")
+    blocks = jnp.stack(jnp.split(gains, count, axis=1))
+    return jnp.sum(lax.all_to_all(blocks, "fsdp", 0, 0, tiled=True), axis=0)
+
+
+def sum_over_chips_and_fsdp(own, other):
+    mine = add_low(own, swap_chip(other))
+    return jnp.sum(lax.all_to_all(mine, "fsdp", 0, 0, tiled=True).astype(F32), axis=0).astype(BF16)
 
 
 def shards(tokens, segment_ids, wq, wk, wv, wo, w_gate, w_up, w_down, gain_attn, gain_ffn, cotangent):
@@ -420,29 +662,42 @@
     fsdp = lax.axis_size("fsdp")
     place = lax.axis_index("ctx")
     chip, core = place // 2, place % 2
-    rows = 2 * segment_ids.shape[0]
+    half = segment_ids.shape[0]
+    rows = 2 * half
     real_width = wq.shape[1]
-    shard_rows, depth = wq.shape[0], wq.shape[0] * fsdp
+    columns, depth = wq.shape[0], wq.shape[0] * fsdp
     width = -(-real_width // (4 * HEAD_DIM)) * 4 * HEAD_DIM
-    part_width = width // 4
+    part = width // 4
     keys = -(-2 * rows // TILE) * TILE
-
-    def attention_piece():
-        pad = ((0, 0), (0, width - real_width))
-        pieces = [jnp.transpose(take_quarter(jnp.pad(w, pad), place, 1)) for w in (wq, wk, wv)]
-        pieces.append(take_quarter(jnp.pad(wo, pad[::-1]), place, 0))
-        return jnp.stack(pieces)
-
-    attention_own = lax.all_gather(attention_piece(), "fsdp", axis=0, tiled=False)
+    base = rows
+
+    pad = ((0, 0), (0, width - real_width))
+    wide = [jnp.pad(w, pad) for w in (wq, wk, wv)] + [jnp.pad(wo, pad[::-1])]
+
+    def attention_piece(index):
+        pieces = [jnp.transpose(take_quarter(w, index, 1)) for w in wide[:3]]
+        return jnp.stack(pieces + [take_quarter(wide[3], index, 0)])
+
+    gain_one, gain_two = gather_gains(jnp.stack([gain_attn, gain_ffn]))
+    inputs = tokens.astype(F32)
+    inv_one = inverse_rms(inputs)
+    normed = (inputs * inv_one * gain_one).astype(BF16)
+    before = to_later_chip(normed)
+    own_blocks = widen_chip(normed)
+    before_blocks = widen_chip(before)
+    count = len(own_blocks)
+    blocks = before_blocks + own_blocks
+    ring = [attention_piece(place)]
+    ring.append(pull_fsdp(ring[0], 1))
+    for step in range(2, fsdp):
+        ring.append(pull_fsdp(after(ring[-1], normed if step == 2 else own_blocks[1]), 1))
+    crossed = [attention_piece(place ^ 2)] + [swap_chip(block) for block in ring[1:]]
+    weights = place_weights(ring + crossed, fsdp)
+
     pieces = (take_quarter(w_gate, place, 1), take_quarter(w_up, place, 1), jnp.transpose(take_quarter(w_down, place, 0)))
-    feed_own = [lax.all_gather(w, "fsdp", axis=0, tiled=True) for w in pieces]
-    attention_both = jnp.stack([attention_own, swap_chip(attention_own)])
-    attention_weights = jnp.transpose(attention_both, (2, 0, 3, 1, 4)).reshape(4, 2 * part_width, depth)
+    feed_own = [lax.all_gather(after(w, ring[-2]), "fsdp", axis=0, tiled=True) for w in pieces]
     feed_other = [swap_chip(w) for w in feed_own]
-    gains = lax.all_gather(jnp.stack([gain_attn, gain_ffn]), "fsdp", axis=1, tiled=True).astype(F32)
-    gain_one, gain_two = gains[0], gains[1]
-
-    base = rows
+
     position = (chip * rows - rows + jnp.arange(keys, dtype=jnp.int32)).astype(F32)
     pair_index = (jnp.arange(LANES, dtype=jnp.int32) % (HEAD_DIM // 2)).astype(F32)
     angles = position[:, None] * (10000.0 ** (-pair_index * 2.0 / HEAD_DIM))[None, :]
@@ -452,61 +707,49 @@
     ids = jnp.concatenate([ids_before, ids_own])
     start = jnp.sum((ids[None, :] < ids_own[:, None]).astype(jnp.int32), axis=1)
     tiles = -(-rows // TILE)
-    low = start[::TILE] // TILE
     ends = [-(-min(base + (t + 1) * TILE, base + rows) // TILE) for t in range(tiles)]
-    bounds = jnp.stack([low, jnp.array(ends, jnp.int32)])
+    bounds = jnp.stack([start[::TILE] // TILE, jnp.array(ends, jnp.int32)])
     start = jnp.pad(start, (0, tiles * TILE - rows), constant_values=2 * keys)[None]
 
-    inputs = tokens.astype(F32)
-    inv_one = inverse_rms(inputs)
-    normed = (inputs * inv_one * gain_one).astype(BF16)
-    before = widen_chip(to_later_chip(normed))
-    window = jnp.concatenate(before + widen_chip(normed) + [jnp.zeros((keys - 2 * rows, depth), BF16)], axis=0)
-    dy = jnp.concatenate(widen_chip(cotangent), axis=0)
-    q, k, v = project(window, attention_weights, cos, sin, base)
-    attended, lse = attend(bounds, q, k, v, start, rows, base)
-    residual = inputs + narrow_chip(dot(attended, attention_weights[3]))
+    q, k, v = project(blocks, weights, cos, sin, keys)
+    dy = widen_chip(after(cotangent, before_blocks[1]))
+    attended, lse = attend(bounds, after(q, feed_own[0]), after(k, *dy), v, start, rows, base)
+    kept, sent = out_project(after(attended, feed_own[1], feed_other[0]), weights, count)
+    residual = inputs + narrow_tp(narrow_core(kept, sent))
 
     inv_two = inverse_rms(residual)
-    normed_two = jnp.concatenate(widen_chip((residual * inv_two * gain_two).astype(BF16)), axis=0)
-    hidden, gate_grad, up_grad, back_two = feed(normed_two, dy, feed_own, feed_other)
-    normed_two_grad = narrow_chip(back_two)
-    grads_other = feed_weights(normed_two, dy, hidden, gate_grad, up_grad, 1)
-    grads_own = feed_weights(normed_two, dy, hidden, gate_grad, up_grad, 0)
-    feed_sums = [scatter_fsdp(add_low(own, swap_chip(other))) for own, other in zip(grads_own, grads_other)]
-    units = feed_own[2].shape[1]
-    out_partial = dot_nt(hidden[:, :units], feed_own[2]) + dot_nt(hidden[:, units:], feed_other[2])
-    layer_out = residual + narrow_chip(out_partial)
+    normed_two = widen_chip(after((residual * inv_two * gain_two).astype(BF16), feed_own[2], feed_other[1]))
+    hidden, gate_grad, up_grad, kept, sent = feed(normed_two, dy, feed_own, feed_other)
+    pair = narrow_core(kept, sent)
+    normed_two_grad = narrow_tp(pair)
+    grads_other = feed_weights(normed_two, dy, after(hidden, pair), gate_grad, up_grad, 1)
     gain_two_grad = jnp.sum(normed_two_grad * residual * inv_two, axis=0)
     resid_grad = cotangent.astype(F32) + normalize_back(residual, inv_two, gain_two, normed_two_grad)
-
-    grad = jnp.concatenate(widen_chip(resid_grad.astype(BF16)), axis=0)
-    out_grad = dot_nt(grad, attention_weights[3]).astype(BF16)
-    dq, dk, dv = attend_back(bounds, q, k, v, attended, out_grad, lse, start, cos, sin, rows, base)
-    chip_rows = window[base : base + rows]
-    weight_grads = jnp.stack(
-        [
-            dot_tn(dq, chip_rows).astype(BF16),
-            dot_tn(dk, window).astype(BF16),
-            dot_tn(dv, window).astype(BF16),
-            dot_tn(attended, grad).astype(BF16),
-        ]
-    ).reshape(4, 2, part_width, fsdp, shard_rows)
-    weight_grads = jnp.transpose(weight_grads, (1, 3, 0, 2, 4))
-    attention_sum = scatter_fsdp(add_low(weight_grads[0], swap_chip(weight_grads[1])))[0]
-    window_back = dot(dk, attention_weights[1]) + dot(dv, attention_weights[2])
-    own_back = window_back[base : base + rows] + dot(dq, attention_weights[0])
-    earlier_back = to_earlier_chip(narrow_chip(window_back[:base]).astype(BF16)).astype(F32)
-    normed_grad = narrow_chip(own_back) + earlier_back
+    resid_low = resid_grad.astype(BF16)
+    grads_own = feed_weights(normed_two, dy, after(hidden, resid_low), gate_grad, up_grad, 0)
+    feed_mine = [add_low(own, swap_chip(other)) for own, other in zip(grads_own, grads_other)]
+    feed_sums = [lax.psum_scatter(mine, "fsdp", scatter_dimension=0, tiled=True) for mine in feed_mine]
+    kept, sent = feed_out(after(hidden, grads_own[0]), feed_own[2], feed_other[2])
+    layer_out = residual + narrow_tp(narrow_core(kept, sent))
+
+    grad_blocks = widen_chip(resid_low)
+    out_grad, out_own, out_other = out_back(attended, weights, grad_blocks, fsdp)
+    dq, dk, dv = attend_back(bounds, q, k, v, attended, after(out_grad, feed_mine[0]), lse, start, cos, sin, rows, base)
+    out_sum = sum_over_chips_and_fsdp(out_own, out_other)
+    v_own, v_other, k_own, k_other, q_own, q_other = project_weights(after(dq, feed_sums[0]), dk, dv, blocks, fsdp)
+    v_sum, k_sum, q_sum = (
+        sum_over_chips_and_fsdp(*pair) for pair in ((v_own, v_other), (k_own, k_other), (q_own, q_other))
+    )
+    early_kept, early_sent, kept, sent = project_back(after(dq, feed_sums[1], feed_mine[2]), dk, dv, weights, base, count)
+    earlier_back = to_earlier_chip(narrow_tp(narrow_core(early_kept, early_sent)).astype(BF16)).astype(F32)
+    normed_grad = narrow_tp(narrow_core(kept, sent)) + earlier_back
     gain_one_grad = jnp.sum(normed_grad * inputs * inv_one, axis=0)
     grad_input = resid_grad + normalize_back(inputs, inv_one, gain_one, normed_grad)
 
-    attention_all = jnp.stack(all_quarters(attention_sum), axis=1).reshape(4, width, shard_rows)
+    attention_all = jnp.stack(all_quarters(jnp.stack([q_sum, k_sum, v_sum, out_sum])), axis=1).reshape(4, width, columns)
     attention_all = attention_all[:, :real_width].astype(F32)
     feed_all = [all_quarters(total) for total in feed_sums]
-    gain_grads = lax.psum(jnp.stack([gain_one_grad, gain_two_grad]), ("fsdp", "ctx", "tp"))
-    gain_rows = gain_attn.shape[0]
-    gain_own = lax.dynamic_slice_in_dim(gain_grads, lax.axis_index("fsdp") * gain_rows, gain_rows, 1)
+    gain_own = gain_totals(jnp.stack([gain_one_grad, gain_two_grad]))
     return (
         layer_out.astype(BF16)[None],
         grad_input[None],

time: 868 us -> 716 us (0.82)
  waiting for transfers between devices: 369 us -> 266 us
  starting transfers between devices: 69 us -> 143 us
  Pallas kernels: 110 us -> 168 us
  matrix products: 50.3 us -> 0 us
  blocking collectives: 49.3 us -> 0 us
  local copies, waits for them, and re-layouts: 82.7 us -> 36.6 us
  other arithmetic: 112 us -> 82.4 us
    ppermute x12 -> x18, waiting for transfers between devices: 197 us -> 125 us  [swap_chip(): lax.ppermute(values, 'ctx', [(i, i ^ 2) for i in range(lax.axis_size('ctx...]
    ppermute x10 -> x11, waiting for transfers between devices: 125 us -> 62.6 us  [swap_tp(): return lax.ppermute(values, 'tp', [(0, 1), (1, 0)])]
    pallas_call x4 -> x10, Pallas kernels: 72.1 us -> 126 us  [the longest x1 31.1 us: feed(): call(functools.partial(feed_kernel, count, steps), 'feed', rows * depth *...]
    dot_general x11 -> x0, matrix products: 50.3 us -> none  [the longest x4 20.6 us: dot(): return jnp.dot(left, right, preferred_element_type=F32)]
    psum x1 -> x0, blocking collectives: 38.9 us -> none  [shards(): lax.psum(jnp.stack([gain_one_grad, gain_two_grad]), ('fsdp', 'ctx', 'tp'))]
    ppermute x15 -> x21, starting transfers between devices: 22.9 us -> 55.2 us  [swap_core(): lax.ppermute(values, 'ctx', [(i, i ^ 1) for i in range(lax.axis_size('ctx...]
    ppermute x0 -> x6, waiting for transfers between devices: none -> 30.3 us  [pull_fsdp(): lax.ppermute(values, 'fsdp', [(i, (i - step) % count) for i in range(coun...]
    all_to_all x0 -> x5, starting transfers between devices: none -> 18.9 us  [the longest x4 15.6 us: sum_over_chips_and_fsdp(): lax.all_to_all(mine, 'fsdp', 0, 0, tiled=True).astype(F32)]
  transfers between devices with their start and end apart: 48 -> 70, of which waited for: 20 -> 31; matrix products, arithmetic and copies ran while one was open for 25% -> 14% of each run, Pallas kernels for 8% -> 18%
where the time goes in v3:
time: 716 us; the launch traced here: 710 us
  waiting for transfers between devices  266 us (37%)
  Pallas kernels  168 us (23%)
  starting transfers between devices  143 us (20%)
  other arithmetic  82.4 us (12%)
  local copies, waits for them, and re-layouts  36.6 us (5%)
  between operations  15.1 us (2%)
    ppermute x18, waiting for transfers between devices, swap_chip(): lax.ppermute(values, 'ctx', [(i, i ^ 2) for i in range(lax.axis_size('ctx...  125 us
    ppermute x11, waiting for transfers between devices, swap_tp(): return lax.ppermute(values, 'tp', [(0, 1), (1, 0)])  62.6 us
    ppermute x21, starting transfers between devices, swap_core(): lax.ppermute(values, 'ctx', [(i, i ^ 1) for i in range(lax.axis_size('ctx...  55.2 us
    ppermute x18, starting transfers between devices, swap_chip(): lax.ppermute(values, 'ctx', [(i, i ^ 2) for i in range(lax.axis_size('ctx...  34.2 us
    pallas_call x1, Pallas kernels, feed(): call(functools.partial(feed_kernel, count, steps), 'feed', rows * depth *...  31.1 us
    ppermute x6, waiting for transfers between devices, pull_fsdp(): lax.ppermute(values, 'fsdp', [(i, (i - step) % count) for i in range(coun...  30.3 us
    pallas_call x1, Pallas kernels, attend_back(): call(functools.partial(backward_kernel, rows, base), 'attend_back', rows...  27.7 us
    pallas_call x2, Pallas kernels, feed_weights(): call(functools.partial(feed_weights_kernel, count), 'feed_weights', rows...  23.9 us
  transfers between devices with their start and end apart: 70, of which 31 were waited for; matrix products, arithmetic and copies ran while one was open for 14% of the time, Pallas kernels for 18%

profile of v3, /device:TPU:1, one launch (start us, length us, event | category | flops | bytes accessed | tf_op | source)
XLA Modules:
  0.0 710.2 jit_solution(8302952672823285851)
XLA Ops:
  27.5 10.0 %collective-permute-done.12.refs_1_ = bf16[4,192,384]{2,1,0:T(8,128)(2,1)} collective-permute-done((bf16[4,192,384]{2,1,0:T(8,128)(2,1)S(1)}, bf16[4,192,384]{2,1,0:T(8,128)(2,1)}, u32[]{:S(2)}, u32[]{:S(2)}) %collective-permute-start.12) | collective-permute-done | bytes 589856 | tf_op jit(solution)/shard_map/ppermute | solution.py:632
  42.2 10.1 %collective-permute-done.13.refs_2_ = bf16[4,192,384]{2,1,0:T(8,128)(2,1)} collective-permute-done((bf16[4,192,384]{2,1,0:T(8,128)(2,1)}, bf16[4,192,384]{2,1,0:T(8,128)(2,1)}, u32[]{:S(2)}, u32[]{:S(2)}) %collective-permute-start.13) | collective-permute-done | bytes 589856 | tf_op jit(solution)/shard_map/ppermute | solution.py:632
  57.2 12.8 %collective-permute-done.5.refs_0_ = bf16[272,1536]{1,0:T(8,128)(2,1)} collective-permute-done((bf16[272,1536]{1,0:T(8,128)(2,1)}, bf16[272,1536]{1,0:T(8,128)(2,1)}, u32[]{:S(2)}, u32[]{:S(2)}) %collective-permute-start.5) | collective-permute-done | bytes 835616 | tf_op jit(solution)/shard_map/ppermute | solution.py:41
  93.7 10.2 %collective-permute-done.14.refs_3_ = bf16[4,192,384]{2,1,0:T(8,128)(2,1)S(1)} collective-permute-done((bf16[4,192,384]{2,1,0:T(8,128)(2,1)}, bf16[4,192,384]{2,1,0:T(8,128)(2,1)S(1)}, u32[]{:S(2)}, u32[]{:S(2)}) %collective-permute-start.14) | collective-permute-done | bytes 589856 | tf_op jit(solution)/shard_map/ppermute | solution.py:632
  116.1 11.1 %collective-permute-done.17.refs_7_ = bf16[4,192,384]{2,1,0:T(8,128)(2,1)} collective-permute-done((bf16[4,192,384]{2,1,0:T(8,128)(2,1)S(1)}, bf16[4,192,384]{2,1,0:T(8,128)(2,1)}, u32[]{:S(2)}, u32[]{:S(2)}) %collective-permute-start.17) | collective-permute-done | bytes 589856 | tf_op jit(solution)/shard_map/ppermute | solution.py:33
  143.2 15.9 %project.1 = (bf16[1088,384]{1,0:T(8,128)(2,1)}, bf16[2304,384]{1,0:T(8,128)(2,1)}, bf16[2304,384]{1,0:T(8,128)(2,1)}) custom-call(bf16[272,1536]{1,0:T(8,128)(2,1)} %collective-permute-done.5.refs_0_, bf16[272,1536]{1,0:T(8,128)(2,1)} %collective-permute-done.6.refs_1_, bf16[272,1536]{1,0:T(8,128)(2,1)} %collective-permute-done.7.refs_2_, ...), custom_call_target="tpu_custom_call" | custom-call | flops 6794772480 | bytes 7077888 | tf_op jit(solution)/shard_map/project/pallas_call | solution.py:166
  159.2 14.2 %attend.1 = (bf16[1088,384]{1,0:T(8,128)(2,1)}, f32[6,1280]{1,0:T(8,128)}) custom-call(s32[2,5]{1,0:T(2,128)} %pad_add_fusion.1.bounds, bf16[1088,384]{1,0:T(8,128)(2,1)} %get-tuple-element.67.q_ref, bf16[2304,384]{1,0:T(8,128)(2,1)} %get-tuple-element.70.k_ref, bf16[2304,384]{1,0:T(8,128)(2,1)} %get-tuple-element.71.v_ref, s32[1,1280]{1,0:T(1,128)} %broadcast_in_dim.11.start_ref), custom_call_target="tpu_custom_call" | custom-call | flops 3636461568 | bytes 7077888 | tf_op jit(solution)/shard_map/attend/pallas_call | solution.py:385
  192.8 12.9 %collective-permute-done.23 = bf16[272,1536]{1,0:T(8,128)(2,1)S(1)} collective-permute-done((bf16[272,1536]{1,0:T(8,128)(2,1)S(1)}, bf16[272,1536]{1,0:T(8,128)(2,1)S(1)}, u32[]{:S(2)}, u32[]{:S(2)}) %collective-permute-start.23) | collective-permute-done | bytes 835616 | tf_op jit(solution)/shard_map/ppermute | solution.py:49
  206.4 15.9 %all-gather.8.cloned.1.call-done.refs_10_.own_ref = bf16[1536,512]{1,0:T(8,128)(2,1)} async-done(((bf16[384,512]{1,0:T(8,128)(2,1)}), bf16[1536,512]{1,0:T(8,128)(2,1)}) %all-gather.8.cloned.1.call-update) | async-done | bytes 1572880 | tf_op jit(solution)/shard_map/all_gather | solution.py:698
  230.8 15.4 %collective-permute-done.25.refs_1_ = bf16[272,1536]{1,0:T(8,128)(2,1)S(1)} collective-permute-done((bf16[272,1536]{1,0:T(8,128)(2,1)S(1)}, bf16[272,1536]{1,0:T(8,128)(2,1)S(1)}, u32[]{:S(2)}, u32[]{:S(2)}) %collective-permute-start.25) | collective-permute-done | bytes 835616 | tf_op jit(solution)/shard_map/ppermute | solution.py:49
  248.3 13.8 %collective-permute-done.28.refs_13_.other_ref = bf16[1536,512]{1,0:T(8,128)(2,1)S(1)} collective-permute-done((bf16[1536,512]{1,0:T(8,128)(2,1)}, bf16[1536,512]{1,0:T(8,128)(2,1)S(1)}, u32[]{:S(2)}, u32[]{:S(2)}) %collective-permute-start.28) | collective-permute-done | bytes 1572896 | tf_op jit(solution)/shard_map/ppermute | solution.py:33
  264.2 31.1 %feed.1 = (bf16[1088,1024]{1,0:T(8,128)(2,1)}, bf16[1088,1024]{1,0:T(8,128)(2,1)}, bf16[1088,1024]{1,0:T(8,128)(2,1)}, f32[544,1536]{1,0:T(8,128)}, bf16[544,1536]{1,0:T(8,128)(2,1)}) custom-call(bf16[272,1536]{1,0:T(8,128)(2,1)} %copy-done.31, bf16[272,1536]{1,0:T(8,128)(2,1)} %copy-done.44, bf16[272,1536]{1,0:T(8,128)(2,1)} %copy-done.45, ...), custom_call_target="tpu_custom_call" | custom-call | flops 17112760320 | bytes 9437184 | tf_op jit(solution)/shard_map/feed/pallas_call | solution.py:542
  309.0 12.1 %feed_weights.3 = (bf16[1536,512]{1,0:T(8,128)(2,1)}, bf16[1536,512]{1,0:T(8,128)(2,1)}, bf16[1536,512]{1,0:T(8,128)(2,1)}) custom-call(bf16[272,1536]{1,0:T(8,128)(2,1)} %copy-done.31, bf16[272,1536]{1,0:T(8,128)(2,1)} %copy-done.44, bf16[272,1536]{1,0:T(8,128)(2,1)} %copy-done.45, bf16[272,1536]{1,0:T(8,128)(2,1)} %collective-permute-done.27.refs_3_, ...), custom_call_target="tpu_custom_call" | custom-call | flops 5133828096 | bytes 4718592 | tf_op jit(solution)/shard_map/feed_weights/pallas_call | solution.py:582
  333.4 11.9 %feed_weights.2 = (bf16[1536,512]{1,0:T(8,128)(2,1)}, bf16[1536,512]{1,0:T(8,128)(2,1)}, bf16[1536,512]{1,0:T(8,128)(2,1)}) custom-call(bf16[272,1536]{1,0:T(8,128)(2,1)} %copy-done.31, bf16[272,1536]{1,0:T(8,128)(2,1)} %copy-done.44, bf16[272,1536]{1,0:T(8,128)(2,1)} %copy-done.45, bf16[272,1536]{1,0:T(8,128)(2,1)} %collective-permute-done.27.refs_3_, ...), custom_call_target="tpu_custom_call" | custom-call | flops 5133828096 | bytes 4718592 | tf_op jit(solution)/shard_map/feed_weights/pallas_call | solution.py:582
  345.3 11.4 %collective-permute-done.37 = bf16[1536,512]{1,0:T(8,128)(2,1)} collective-permute-done((bf16[1536,512]{1,0:T(8,128)(2,1)}, bf16[1536,512]{1,0:T(8,128)(2,1)}, u32[]{:S(2)}, u32[]{:S(2)}) %collective-permute-start.37) | collective-permute-done | bytes 1572896 | tf_op jit(solution)/shard_map/ppermute | solution.py:33
  361.5 33.4 %collective-permute-done.36 = bf16[1536,512]{1,0:T(8,128)(2,1)S(1)} collective-permute-done((bf16[1536,512]{1,0:T(8,128)(2,1)}, bf16[1536,512]{1,0:T(8,128)(2,1)S(1)}, u32[]{:S(2)}, u32[]{:S(2)}) %collective-permute-start.36) | collective-permute-done | bytes 1572896 | tf_op jit(solution)/shard_map/ppermute | solution.py:33
  420.8 11.5 %collective-permute-done.38 = bf16[1536,512]{1,0:T(8,128)(2,1)} collective-permute-done((bf16[1536,512]{1,0:T(8,128)(2,1)}, bf16[1536,512]{1,0:T(8,128)(2,1)}, u32[]{:S(2)}, u32[]{:S(2)}) %collective-permute-start.38) | collective-permute-done | bytes 1572896 | tf_op jit(solution)/shard_map/ppermute | solution.py:33
  460.3 27.7 %attend_back.1 = (bf16[1088,384]{1,0:T(8,128)(2,1)}, bf16[2304,384]{1,0:T(8,128)(2,1)}, bf16[2304,384]{1,0:T(8,128)(2,1)}) custom-call(s32[2,5]{1,0:T(2,128)} %pad_add_fusion.1.bounds, bf16[1088,384]{1,0:T(8,128)(2,1)} %get-tuple-element.67.q_ref, bf16[2304,384]{1,0:T(8,128)(2,1)} %get-tuple-element.70.k_ref, bf16[2304,384]{1,0:T(8,128)(2,1)} %get-tuple-element.71.v_ref, ...), custom_call_target="tpu_custom_call" | custom-call | flops 9091153920 | bytes 14155776 | tf_op jit(solution)/shard_map/attend_back/pallas_call | solution.py:469
  491.7 14.7 %project_weights.1 = (bf16[4,192,384]{2,1,0:T(8,128)(2,1)}, bf16[4,192,384]{2,1,0:T(8,128)(2,1)}, bf16[4,192,384]{2,1,0:T(8,128)(2,1)}, bf16[4,192,384]{2,1,0:T(...) custom-call(bf16[1088,384]{1,0:T(8,128)(2,1)} %get-tuple-element.106.dq_ref, ...), custom_call_target="tpu_custom_call" | custom-call | flops 6794772480 | bytes 7077888 | tf_op jit(solution)/shard_map/project_weights/pallas_call | solution.py:281
  506.4 13.0 %collective-permute-start.44 = (bf16[4,192,384]{2,1,0:T(8,128)(2,1)}, bf16[4,192,384]{2,1,0:T(8,128)(2,1)}, u32[]{:S(2)}, u32[]{:S(2)}) collective-permute-start(bf16[4,192,384]{2,1,0:T(8,128)(2,1)} %get-tuple-element.108), channel_id=1, source_target_pairs={{0,4},{2,6},{4,0},{6,2},{1,5},{3,7},{5,1},{7,3},{8,12},{10,14},{12... | collective-permute-start | bytes 1769480 | tf_op jit(solution)/shard_map/ppermute | solution.py:33
  520.9 13.7 %project_back.1 = (f32[544,1536]{1,0:T(8,128)}, bf16[544,1536]{1,0:T(8,128)(2,1)}, f32[544,1536]{1,0:T(8,128)}, bf16[544,1536]{1,0:T(8,128)(2,1)}) custom-call(bf16[1088,384]{1,0:T(8,128)(2,1)} %get-tuple-element.106.dq_ref, bf16[2304,384]{1,0:T(8,128)(2,1)} %get-tuple-element.100.dk_ref, bf16[2304,384]{1,0:T(8,128)(2,1)} %get-tuple-element.101.dv_ref, ...), custom_call_target="tpu_custom_call" | custom-call | flops 6417285120 | bytes 10027008 | tf_op jit(solution)/shard_map/project_back/pallas_call | solution.py:315
  562.7 17.0 %collective-permute-done.50 = bf16[384,512]{1,0:T(8,128)(2,1)S(1)} collective-permute-done((bf16[384,512]{1,0:T(8,128)(2,1)S(1)}, bf16[384,512]{1,0:T(8,128)(2,1)S(1)}, u32[]{:S(2)}, u32[]{:S(2)}) %collective-permute-start.50) | collective-permute-done | bytes 393248 | tf_op jit(solution)/shard_map/ppermute | solution.py:33
  602.8 10.2 %all-to-all-done.1 = bf16[4,192,384]{2,1,0:T(8,128)(2,1)} async-done(((bf16[4,192,384]{2,1,0:T(8,128)(2,1)}), bf16[4,192,384]{2,1,0:T(8,128)(2,1)}, u32[]{:S(2)}, u32[]{:S(2)}) %all-to-all-start.1) | async-done | bytes 589856 | tf_op jit(solution)/shard_map/all_to_all | solution.py:657
  659.2 13.8 %collective-permute-done.40 = bf16[272,1536]{1,0:T(8,128)(2,1)S(1)} collective-permute-done((bf16[272,1536]{1,0:T(8,128)(2,1)S(1)}, bf16[272,1536]{1,0:T(8,128)(2,1)S(1)}, u32[]{:S(2)}, u32[]{:S(2)}) %collective-permute-start.40) | collective-permute-done | bytes 835616 | tf_op jit(solution)/shard_map/ppermute | solution.py:49
  (336 shorter events, 331.3 us)
Async XLA Ops:
  7.2 107.4 %all-gather.4.cloned.1.call-start = ((), (), s32[]{:S(2)}) async-start(), calls=%async_computation.8 | async-start | bytes 1966080 | tf_op jit(solution)/shard_map/all_gather | solution.py:698
  52.3 121.1 %all-gather.6.cloned.1.call-start = ((), (), s32[]{:S(2)}) async-start(), calls=%async_computation.9 | async-start | bytes 1966080 | tf_op jit(solution)/shard_map/all_gather | solution.py:698
  88.6 133.6 %all-gather.8.cloned.1.call-start = ((), (), s32[]{:S(2)}) async-start(), calls=%async_computation.10 | async-start | bytes 1966080 | tf_op jit(solution)/shard_map/all_gather | solution.py:698
  92.5 44.6 %collective-permute-start.18 = (bf16[272,1536]{1,0:T(8,128)(2,1)S(1)}, bf16[272,1536]{1,0:T(8,128)(2,1)}, u32[]{:S(2)}, u32[]{:S(2)}) collective-permute-start(bf16[272,1536]{1,0:T(8,128)(2,1)S(1)} %bitcast.134), channel_id=1, source_target_pairs={{0,1},{1,0},{2,3},{3,2},{4,5},{5,4},{6,7},{7,6},{8,9},{9,8},{10,11... | collective-permute-start | bytes 2506760 | tf_op jit(solution)/shard_map/ppermute | solution.py:49
  114.6 58.8 %collective-permute-start.21 = (bf16[1536,512]{1,0:T(8,128)(2,1)}, bf16[1536,512]{1,0:T(8,128)(2,1)}, u32[]{:S(2)}, u32[]{:S(2)}) collective-permute-start(bf16[1536,512]{1,0:T(8,128)(2,1)} %all-gather.4.cloned.1.call-done.refs_8_), channel_id=1, source_target_pairs={{0,4},{2,6},{4,0},{6,2},{1,5},{3,7},{5,1},{7,3},{8,12},{10,14},{12... | collective-permute-start | bytes 4718600 | tf_op jit(solution)/shard_map/ppermute | solution.py:33
  181.8 309.9 %reduce-scatter.4.cloned.1.call-start = ((), (), s32[]{:S(2)}) async-start(), calls=%async_computation.11 | async-start | bytes 1966080 | tf_op jit(solution)/shard_map/reduce_scatter | solution.py:731
  187.0 40.3 %collective-permute-start.24 = (bf16[1536,512]{1,0:T(8,128)(2,1)}, bf16[1536,512]{1,0:T(8,128)(2,1)}, u32[]{:S(2)}, u32[]{:S(2)}) collective-permute-start(bf16[1536,512]{1,0:T(8,128)(2,1)} %all-gather.6.cloned.1.call-done.refs_9_), channel_id=1, source_target_pairs={{0,4},{2,6},{4,0},{6,2},{1,5},{3,7},{5,1},{7,3},{8,12},{10,14},{12... | collective-permute-start | bytes 4718600 | tf_op jit(solution)/shard_map/ppermute | solution.py:33
  227.5 34.6 %collective-permute-start.28 = (bf16[1536,512]{1,0:T(8,128)(2,1)}, bf16[1536,512]{1,0:T(8,128)(2,1)S(1)}, u32[]{:S(2)}, u32[]{:S(2)}) collective-permute-start(bf16[1536,512]{1,0:T(8,128)(2,1)} %all-gather.8.cloned.1.call-done.refs_10_.own_ref), channel_id=1, source_target_pairs={{0,4},{2,6},{4,0},{6,2},{1,5},{3,7},{5,1},{7,3},{8,12},{10,14},{12... | collective-permute-start | bytes 4718600 | tf_op jit(solution)/shard_map/ppermute | solution.py:33
  321.1 35.7 %collective-permute-start.37 = (bf16[1536,512]{1,0:T(8,128)(2,1)}, bf16[1536,512]{1,0:T(8,128)(2,1)}, u32[]{:S(2)}, u32[]{:S(2)}) collective-permute-start(bf16[1536,512]{1,0:T(8,128)(2,1)} %get-tuple-element.96), channel_id=1, source_target_pairs={{0,4},{2,6},{4,0},{6,2},{1,5},{3,7},{5,1},{7,3},{8,12},{10,14},{12... | collective-permute-start | bytes 4718600 | tf_op jit(solution)/shard_map/ppermute | solution.py:33
  360.2 131.5 %reduce-scatter.6.cloned.1.call-start = ((), (), s32[]{:S(2)}) async-start(), calls=%async_computation.12 | async-start | bytes 1966080 | tf_op jit(solution)/shard_map/reduce_scatter | solution.py:731
  360.3 34.6 %collective-permute-start.36 = (bf16[1536,512]{1,0:T(8,128)(2,1)}, bf16[1536,512]{1,0:T(8,128)(2,1)S(1)}, u32[]{:S(2)}, u32[]{:S(2)}) collective-permute-start(bf16[1536,512]{1,0:T(8,128)(2,1)} %get-tuple-element.91), channel_id=1, source_target_pairs={{0,4},{2,6},{4,0},{6,2},{1,5},{3,7},{5,1},{7,3},{8,12},{10,14},{12... | collective-permute-start | bytes 4718600 | tf_op jit(solution)/shard_map/ppermute | solution.py:33
  398.0 121.5 %reduce-scatter.8.cloned.1.call-start = ((), (), s32[]{:S(2)}) async-start(), calls=%async_computation.13 | async-start | bytes 1966080 | tf_op jit(solution)/shard_map/reduce_scatter | solution.py:731
  407.4 37.7 %collective-permute-start.31 = (bf16[544,1536]{1,0:T(8,128)(2,1)}, bf16[544,1536]{1,0:T(8,128)(2,1)}, u32[]{:S(2)}, u32[]{:S(2)}) collective-permute-start(bf16[544,1536]{1,0:T(8,128)(2,1)} %get-tuple-element.88), channel_id=1, source_target_pairs={{0,2},{2,0},{4,6},{6,4},{1,3},{3,1},{5,7},{7,5},{8,10},{10,8},{12,... | collective-permute-start | bytes 5013512 | tf_op jit(solution)/shard_map/ppermute | solution.py:37
  452.3 35.6 %collective-permute-start.32 = (bf16[272,1536]{1,0:T(8,128)(2,1)}, bf16[272,1536]{1,0:T(8,128)(2,1)}, u32[]{:S(2)}, u32[]{:S(2)}) collective-permute-start(bf16[272,1536]{1,0:T(8,128)(2,1)} %slice.259), channel_id=1, source_target_pairs={{0,1},{1,0},{2,3},{3,2},{4,5},{5,4},{6,7},{7,6},{8,9},{9,8},{10,11... | collective-permute-start | bytes 2506760 | tf_op jit(solution)/shard_map/ppermute | solution.py:49
  456.8 34.2 %all-to-all-start.3 = ((bf16[4,192,384]{2,1,0:T(8,128)(2,1)}), bf16[4,192,384]{2,1,0:T(8,128)(2,1)S(1)}, u32[]{:S(2)}, u32[]{:S(2)}) async-start(bf16[4,192,384]{2,1,0:T(8,128)(2,1)} %add_convert_fusion.3), calls=%async_computation.5 | async-start | bytes 1179648 | tf_op jit(solution)/shard_map/all_to_all | solution.py:657
  506.4 49.7 %collective-permute-start.44 = (bf16[4,192,384]{2,1,0:T(8,128)(2,1)}, bf16[4,192,384]{2,1,0:T(8,128)(2,1)}, u32[]{:S(2)}, u32[]{:S(2)}) collective-permute-start(bf16[4,192,384]{2,1,0:T(8,128)(2,1)} %get-tuple-element.108), channel_id=1, source_target_pairs={{0,4},{2,6},{4,0},{6,2},{1,5},{3,7},{5,1},{7,3},{8,12},{10,14},{12... | collective-permute-start | bytes 1769480 | tf_op jit(solution)/shard_map/ppermute | solution.py:33
  534.6 50.8 %collective-permute-start.45 = (bf16[4,192,384]{2,1,0:T(8,128)(2,1)}, bf16[4,192,384]{2,1,0:T(8,128)(2,1)}, u32[]{:S(2)}, u32[]{:S(2)}) collective-permute-start(bf16[4,192,384]{2,1,0:T(8,128)(2,1)} %get-tuple-element.110), channel_id=1, source_target_pairs={{0,4},{2,6},{4,0},{6,2},{1,5},{3,7},{5,1},{7,3},{8,12},{10,14},{12... | collective-permute-start | bytes 1769480 | tf_op jit(solution)/shard_map/ppermute | solution.py:33
  534.7 52.9 %collective-permute-start.46 = (bf16[4,192,384]{2,1,0:T(8,128)(2,1)}, bf16[4,192,384]{2,1,0:T(8,128)(2,1)}, u32[]{:S(2)}, u32[]{:S(2)}) collective-permute-start(bf16[4,192,384]{2,1,0:T(8,128)(2,1)} %get-tuple-element.112), channel_id=1, source_target_pairs={{0,4},{2,6},{4,0},{6,2},{1,5},{3,7},{5,1},{7,3},{8,12},{10,14},{12... | collective-permute-start | bytes 1769480 | tf_op jit(solution)/shard_map/ppermute | solution.py:33
  537.6 42.1 %collective-permute-start.50 = (bf16[384,512]{1,0:T(8,128)(2,1)S(1)}, bf16[384,512]{1,0:T(8,128)(2,1)S(1)}, u32[]{:S(2)}, u32[]{:S(2)}) collective-permute-start(bf16[384,512]{1,0:T(8,128)(2,1)S(1)} %copy-done.24), channel_id=1, source_target_pairs={{0,4},{2,6},{4,0},{6,2},{1,5},{3,7},{5,1},{7,3},{8,12},{10,14},{12... | collective-permute-start | bytes 1179656 | tf_op jit(solution)/shard_map/ppermute | solution.py:33
  546.0 44.2 %collective-permute-start.53 = (bf16[2,384,512]{2,1,0:T(8,128)(2,1)}, bf16[2,384,512]{2,1,0:T(8,128)(2,1)}, u32[]{:S(2)}, u32[]{:S(2)}) collective-permute-start(bf16[2,384,512]{2,1,0:T(8,128)(2,1)} %pad_maximum_fusion.2), channel_id=1, source_target_pairs={{0,2},{2,0},{4,6},{6,4},{1,3},{3,1},{5,7},{7,5},{8,10},{10,8},{12,... | collective-permute-start | bytes 2359304 | tf_op jit(solution)/shard_map/ppermute | solution.py:37
  556.1 34.0 %collective-permute-start.55 = (bf16[2,384,512]{2,1,0:T(8,128)(2,1)}, bf16[2,384,512]{2,1,0:T(8,128)(2,1)}, u32[]{:S(2)}, u32[]{:S(2)}) collective-permute-start(bf16[2,384,512]{2,1,0:T(8,128)(2,1)} %pad_maximum_fusion.3), channel_id=1, source_target_pairs={{0,2},{2,0},{4,6},{6,4},{1,3},{3,1},{5,7},{7,5},{8,10},{10,8},{12,... | collective-permute-start | bytes 2359304 | tf_op jit(solution)/shard_map/ppermute | solution.py:37
  558.2 34.5 %all-to-all-start = ((bf16[4,192,384]{2,1,0:T(8,128)(2,1)}), bf16[4,192,384]{2,1,0:T(8,128)(2,1)}, u32[]{:S(2)}, u32[]{:S(2)}) async-start(bf16[4,192,384]{2,1,0:T(8,128)(2,1)} %add_convert_fusion.6), calls=%async_computation.2 | async-start | bytes 1179648 | tf_op jit(solution)/shard_map/all_to_all | solution.py:657
  579.8 68.3 %collective-permute-start.39 = (bf16[544,1536]{1,0:T(8,128)(2,1)}, bf16[544,1536]{1,0:T(8,128)(2,1)}, u32[]{:S(2)}, u32[]{:S(2)}) collective-permute-start(bf16[544,1536]{1,0:T(8,128)(2,1)} %get-tuple-element.103), channel_id=1, source_target_pairs={{0,2},{2,0},{4,6},{6,4},{1,3},{3,1},{5,7},{7,5},{8,10},{10,8},{12,... | collective-permute-start | bytes 5013512 | tf_op jit(solution)/shard_map/ppermute | solution.py:37
  585.4 48.2 %collective-permute-start.41 = (bf16[544,1536]{1,0:T(8,128)(2,1)}, bf16[544,1536]{1,0:T(8,128)(2,1)}, u32[]{:S(2)}, u32[]{:S(2)}) collective-permute-start(bf16[544,1536]{1,0:T(8,128)(2,1)} %get-tuple-element.105), channel_id=1, source_target_pairs={{0,2},{2,0},{4,6},{6,4},{1,3},{3,1},{5,7},{7,5},{8,10},{10,8},{12,... | collective-permute-start | bytes 5013512 | tf_op jit(solution)/shard_map/ppermute | solution.py:37
  (92 other events, 1472.9 us)
Sparse Core Ops, SparseCore 0:
  52.4 45.6 all-gather.3
  100.2 43.0 all-gather.5
  181.9 40.3 all-gather.7
  360.3 34.1 reduce-scatter.3
  398.1 35.1 reduce-scatter.5
  435.9 40.2 reduce-scatter.7

commit v4 on v3

--- a/solution.py
+++ b/solution.py
@@ -30,19 +30,19 @@
 
 
 def swap_chip(values):
-    return lax.ppermute(values, "ctx", [(i, i ^ 2) for i in range(lax.axis_size("ctx"))])
+    return lax.ppermute(values, "chip", [(0, 1), (1, 0)])
 
 
 def swap_core(values):
-    return lax.ppermute(values, "ctx", [(i, i ^ 1) for i in range(lax.axis_size("ctx"))])
+    return lax.ppermute(values, "core", [(0, 1), (1, 0)])
 
 
 def to_later_chip(values):
-    return lax.ppermute(values, "ctx", [(i, i + 2) for i in range(lax.axis_size("ctx") - 2)])
+    return lax.ppermute(values, "chip", [(0, 1)])
 
 
 def to_earlier_chip(values):
-    return lax.ppermute(values, "ctx", [(i, i - 2) for i in range(2, lax.axis_size("ctx"))])
+    return lax.ppermute(values, "chip", [(1, 0)])
 
 
 def swap_tp(values):
@@ -63,13 +63,16 @@
     return [lax.all_gather(rows, "tp", axis=0, tiled=True)]
 
 
+def widen_core(blocks):
+    return blocks + [swap_core(block) for block in blocks]
+
+
 def widen_chip(rows):
-    mine = widen_tp(rows)
-    return mine + [swap_core(block) for block in mine]
+    return widen_core(widen_tp(rows))
 
 
 def block_offset(index, half):
-    core = lax.axis_index("ctx") % 2
+    core = lax.axis_index("core")
     if lax.axis_size("tp") != 2:
         return jnp.where(index == 0, core, 1 - core) * half
     place = lax.axis_index("tp")
@@ -78,15 +81,14 @@
     return core * half + place * (half // 2)
 
 
-def narrow_core(kept, sent):
-    return kept.astype(F32) + swap_core(sent).astype(F32)
-
-
-def narrow_tp(pair):
+def narrow_chip(kept, sent):
+    came = swap_core(sent)
     if lax.axis_size("tp") != 2:
-        return lax.psum_scatter(pair.astype(BF16), "tp", scatter_dimension=0, tiled=True).astype(F32)
-    rows = pair.shape[0] // 2
-    return pair[:rows] + swap_tp(pair[rows:].astype(BF16)).astype(F32)
+        pair = (kept + came.astype(F32)).astype(BF16)
+        return lax.psum_scatter(pair, "tp", scatter_dimension=0, tiled=True).astype(F32), came
+    rows = kept.shape[0] // 2
+    other = swap_tp((kept[rows:] + came[rows:].astype(F32)).astype(BF16))
+    return kept[:rows] + came[:rows].astype(F32) + other.astype(F32), came
 
 
 def take_quarter(values, index, axis):
@@ -95,13 +97,8 @@
 
 
 def all_quarters(own):
-    place = lax.axis_index("ctx")
     across = swap_chip(own)
-    came = swap_core(jnp.stack([own, across]))
-    low, high = in_order(jnp.stack([own, across]), came, place % 2 == 0)
-    first = place < 2
-    pick = jnp.where
-    return [pick(first, low[0], low[1]), pick(first, high[0], high[1]), pick(first, low[1], low[0]), pick(first, high[1], high[0])]
+    return own, across, swap_core(jnp.stack([own, across]))
 
 
 def add_low(left, right):
@@ -485,9 +482,14 @@
     )(bounds, q, k, v, o, grad, lse, start, cos, sin)
 
 
-def feed_kernel(count, own_steps, *refs):
-    n_refs, dy_refs, weights = refs[:count], refs[count : 2 * count], refs[2 * count : 2 * count + 6]
-    hidden_ref, gate_ref, up_ref, kept_ref, sent_ref, acc = refs[2 * count + 6 :]
+def joined(ref):
+    shape = ref.shape
+    return ref[...].reshape(shape[0] * shape[3], shape[4])
+
+
+def feed_kernel(count, *refs):
+    n_refs, dy_refs, weights = refs[:count], refs[count : 2 * count], refs[2 * count : 2 * count + 3]
+    hidden_ref, gate_ref, up_ref, kept_ref, sent_ref, acc = refs[2 * count + 3 :]
     step = pl.program_id(0)
     block = n_refs[0].shape[0]
     half = kept_ref.shape[0]
@@ -496,29 +498,21 @@
     def _():
         acc[...] = jnp.zeros_like(acc)
 
-    def tile(gate_w, up_w, down_w):
-        for i in range(count):
-            rows = slice(i * block, (i + 1) * block)
-            normed = n_refs[i][...]
-            gate = dot(normed, gate_w[...])
-            up = dot(normed, up_w[...])
-            grad = dot(dy_refs[i][...], down_w[...])
-            sig = 1.0 / (1.0 + jnp.exp(-gate))
-            silu = gate * sig
-            hidden_ref[rows, :] = (silu * up).astype(BF16)
-            gate_grad = (grad * up * sig * (1.0 + gate * (1.0 - sig))).astype(BF16)
-            up_grad = (grad * silu).astype(BF16)
-            gate_ref[rows, :] = gate_grad
-            up_ref[rows, :] = up_grad
-            acc[rows, :] += dot_nt(gate_grad, gate_w[...]) + dot_nt(up_grad, up_w[...])
-
-    @pl.when(step < own_steps)
-    def _():
-        tile(*weights[:3])
-
-    @pl.when(step >= own_steps)
-    def _():
-        tile(*weights[3:])
+    gate_w, up_w, down_w = (joined(ref) for ref in weights)
+    for i in range(count):
+        rows = slice(i * block, (i + 1) * block)
+        normed = n_refs[i][...]
+        gate = dot(normed, gate_w)
+        up = dot(normed, up_w)
+        grad = dot(dy_refs[i][...], down_w)
+        sig = 1.0 / (1.0 + jnp.exp(-gate))
+        silu = gate * sig
+        hidden_ref[rows, :] = (silu * up).astype(BF16)
+        gate_grad = (grad * up * sig * (1.0 + gate * (1.0 - sig))).astype(BF16)
+        up_grad = (grad * silu).astype(BF16)
+        gate_ref[rows, :] = gate_grad
+        up_ref[rows, :] = up_grad
+        acc[rows, :] += dot_nt(gate_grad, gate_w) + dot_nt(up_grad, up_w)
 
     @pl.when(step == pl.num_programs(0) - 1)
     def _():
@@ -526,36 +520,36 @@
         sent_ref[...] = acc[half:, :].astype(BF16)
 
 
-def feed(normed, dy, own, other):
+def feed(normed, dy, weights):
     count = len(normed)
     block, depth = normed[0].shape
     rows = count * block
-    units = own[0].shape[1]
+    fsdp, chips, _, columns, units = weights.shape
     tile = min(TILE, units)
     steps = units // tile
     fixed = pl.BlockSpec((block, depth), lambda i: (0, 0))
     kept = pl.BlockSpec((rows // 2, depth), lambda i: (0, 0))
-    first = pl.BlockSpec((depth, tile), lambda i: (0, jnp.minimum(i, steps - 1)))
-    second = pl.BlockSpec((depth, tile), lambda i: (0, jnp.maximum(i - steps, 0)))
+    kind = lambda k: pl.BlockSpec((fsdp, 1, 1, columns, tile), lambda i: (0, i // steps, k, 0, i % steps))
     out = pl.BlockSpec((rows, tile), lambda i: (0, i))
-    wide = jax.ShapeDtypeStruct((rows, 2 * units), BF16)
-    return call(
-        functools.partial(feed_kernel, count, steps),
+    wide = jax.ShapeDtypeStruct((rows, chips * units), BF16)
+    return call(
+        functools.partial(feed_kernel, count),
         "feed",
         rows * depth * units * 20,
         depth * units * 12,
-        grid=(2 * steps,),
+        grid=(chips * steps,),
         out_shape=(wide, wide, wide, jax.ShapeDtypeStruct((rows // 2, depth), F32), jax.ShapeDtypeStruct((rows // 2, depth), BF16)),
-        in_specs=[fixed] * (2 * count) + [first] * 3 + [second] * 3,
+        in_specs=[fixed] * (2 * count) + [kind(0), kind(1), kind(2)],
         out_specs=[out, out, out, kept, kept],
         scratch_shapes=[pltpu.VMEM((rows, depth), F32)],
-    )(*normed, *dy, *own, *other)
+    )(*normed, *dy, weights, weights, weights)
 
 
 def feed_weights_kernel(count, *refs):
     blocks = refs[: 2 * count]
-    hidden_ref, gate_ref, up_ref, gate_out, up_out, down_out, normed, dy = refs[2 * count :]
+    hidden_ref, gate_ref, up_ref, out_ref, normed, dy = refs[2 * count :]
     block = blocks[0].shape[0]
+    fsdp, _, _, columns, tile = out_ref.shape
 
     @pl.when(pl.program_id(0) == 0)
     def _():
@@ -563,59 +557,124 @@
             normed[i * block : (i + 1) * block, :] = blocks[i][...]
             dy[i * block : (i + 1) * block, :] = blocks[count + i][...]
 
-    gate_out[...] = dot_tn(normed[...], gate_ref[...]).astype(BF16)
-    up_out[...] = dot_tn(normed[...], up_ref[...]).astype(BF16)
-    down_out[...] = dot_tn(dy[...], hidden_ref[...]).astype(BF16)
-
-
-def feed_weights(normed, dy, hidden, gate_grad, up_grad, part):
+    for k, (left, right) in enumerate(((normed, gate_ref), (normed, up_ref), (dy, hidden_ref))):
+        out_ref[:, 0, k] = dot_tn(left[...], right[...]).astype(BF16).reshape(fsdp, columns, tile)
+
+
+def feed_weights(normed, dy, hidden, gate_grad, up_grad, fsdp, chips):
     count = len(normed)
     block, depth = normed[0].shape
     rows = count * block
-    units = hidden.shape[1] // 2
+    units = hidden.shape[1] // chips
+    columns = depth // fsdp
     tile = min(TILE, units)
     steps = units // tile
     fixed = pl.BlockSpec((block, depth), lambda i: (0, 0))
-    units_in = pl.BlockSpec((rows, tile), lambda i: (0, part * steps + i))
-    out = pl.BlockSpec((depth, tile), lambda i: (0, i))
-    shape = jax.ShapeDtypeStruct((depth, units), BF16)
+    units_in = pl.BlockSpec((rows, tile), lambda i: (0, i))
     return call(
         functools.partial(feed_weights_kernel, count),
         "feed_weights",
-        rows * depth * units * 6,
-        depth * units * 6,
-        grid=(steps,),
-        out_shape=(shape, shape, shape),
+        rows * depth * units * 12,
+        depth * units * 12,
+        grid=(chips * steps,),
+        out_shape=jax.ShapeDtypeStruct((fsdp, chips, 3, columns, units), BF16),
         in_specs=[fixed] * (2 * count) + [units_in] * 3,
-        out_specs=[out, out, out],
+        out_specs=pl.BlockSpec((fsdp, 1, 3, columns, tile), lambda i: (0, i // steps, 0, 0, i % steps)),
         scratch_shapes=[pltpu.VMEM((rows, depth), BF16)] * 2,
     )(*normed, *dy, hidden, gate_grad, up_grad)
 
 
-def feed_out_kernel(half, hidden_ref, own_ref, other_ref, kept_ref, sent_ref):
-    units = own_ref.shape[1]
-    tile = half // 2
-    for r in range(0, 2 * half, tile):
-        total = dot_nt(hidden_ref[r : r + tile, :units], own_ref[...]) + dot_nt(hidden_ref[r : r + tile, units:], other_ref[...])
-        if r < half:
-            kept_ref[r : r + tile, :] = total
-        else:
-            sent_ref[r - half : r - half + tile, :] = total.astype(BF16)
-
-
-def feed_out(hidden, own, other):
+def feed_out_kernel(hidden_ref, weight_ref, kept_ref, sent_ref, acc):
+    step = pl.program_id(0)
+    half = kept_ref.shape[0]
+    weight = joined(weight_ref)
+
+    @pl.when(step == 0)
+    def _():
+        acc[...] = dot_nt(hidden_ref[...], weight)
+
+    @pl.when(step > 0)
+    def _():
+        acc[...] += dot_nt(hidden_ref[...], weight)
+
+    @pl.when(step == pl.num_programs(0) - 1)
+    def _():
+        kept_ref[...] = acc[:half, :]
+        sent_ref[...] = acc[half:, :].astype(BF16)
+
+
+def feed_out(hidden, weights):
     rows = hidden.shape[0]
-    depth, units = own.shape
+    fsdp, chips, _, columns, units = weights.shape
+    depth = fsdp * columns
     half = rows // 2
-    return call(
-        functools.partial(feed_out_kernel, half),
+    out = pl.BlockSpec((half, depth), lambda i: (0, 0))
+    return call(
+        feed_out_kernel,
         "feed_out",
         rows * depth * units * 4,
         rows * depth * 3,
+        grid=(chips,),
         out_shape=(jax.ShapeDtypeStruct((half, depth), F32), jax.ShapeDtypeStruct((half, depth), BF16)),
+        in_specs=[
+            pl.BlockSpec((rows, units), lambda i: (0, i)),
+            pl.BlockSpec((fsdp, 1, 1, columns, units), lambda i: (0, i, 2, 0, 0)),
+        ],
+        out_specs=[out, out],
+        scratch_shapes=[pltpu.VMEM((rows, depth), F32)],
+    )(hidden, weights)
+
+
+def quarter_places():
+    place = 2 * lax.axis_index("chip") + lax.axis_index("core")
+    return place, place ^ 2, place ^ 1, place ^ 3
+
+
+def finish_feed_kernel(own_ref, across_ref, came_ref, gate_ref, up_ref, down_ref):
+    units = own_ref.shape[2]
+    for place, piece in zip(quarter_places(), (own_ref, across_ref, came_ref.at[0], came_ref.at[1])):
+        span = pl.ds(pl.multiple_of(place * units, LANES), units)
+        gate_ref[:, span] = piece[0].astype(F32)
+        up_ref[:, span] = piece[1].astype(F32)
+        down_ref[span, :] = jnp.transpose(piece[2].astype(F32))
+
+
+def finish_feed(own, across, came):
+    _, columns, units = own.shape
+    wide = jax.ShapeDtypeStruct((columns, 4 * units), F32)
+    return call(
+        finish_feed_kernel,
+        "finish_feed",
+        0,
+        own.size * 24,
+        out_shape=(wide, wide, jax.ShapeDtypeStruct((4 * units, columns), F32)),
         in_specs=[whole()] * 3,
-        out_specs=[whole()] * 2,
-    )(hidden, own, other)
+        out_specs=[whole()] * 3,
+    )(own, across, came)
+
+
+def finish_attention_kernel(real, own_ref, across_ref, came_ref, q_ref, k_ref, v_ref, out_ref, buf):
+    part = own_ref.shape[1]
+    pieces = (own_ref, across_ref, came_ref.at[0], came_ref.at[1])
+    for kind, ref in enumerate((q_ref, k_ref, v_ref, out_ref)):
+        for place, piece in zip(quarter_places(), pieces):
+            buf[pl.ds(pl.multiple_of(place * part, 16), part), :] = piece[kind].astype(F32)
+        ref[...] = buf[:real, :] if kind == 3 else jnp.transpose(buf[...])[:, :real]
+
+
+def finish_attention(own, across, came, real):
+    _, part, columns = own.shape
+    into = jax.ShapeDtypeStruct((columns, real), F32)
+    return call(
+        functools.partial(finish_attention_kernel, real),
+        "finish_attention",
+        0,
+        own.size * 24,
+        out_shape=(into, into, into, jax.ShapeDtypeStruct((real, columns), F32)),
+        in_specs=[whole()] * 3,
+        out_specs=[whole()] * 4,
+        scratch_shapes=[pltpu.VMEM((4 * part, columns), F32)],
+    )(own, across, came)
 
 
 def normalize_back(values, inverse, gain, grad_rows):
@@ -657,11 +716,16 @@
     return jnp.sum(lax.all_to_all(mine, "fsdp", 0, 0, tiled=True).astype(F32), axis=0).astype(BF16)
 
 
+def together(*values):
+    return lax.optimization_barrier(values)
+
+
 def shards(tokens, segment_ids, wq, wk, wv, wo, w_gate, w_up, w_down, gain_attn, gain_ffn, cotangent):
     tokens, cotangent, segment_ids = tokens[0], cotangent[0], segment_ids[0]
     fsdp = lax.axis_size("fsdp")
-    place = lax.axis_index("ctx")
-    chip, core = place // 2, place % 2
+    chips = lax.axis_size("chip")
+    chip, core = lax.axis_index("chip"), lax.axis_index("core")
+    place = 2 * chip + core
     half = segment_ids.shape[0]
     rows = 2 * half
     real_width = wq.shape[1]
@@ -678,32 +742,44 @@
         pieces = [jnp.transpose(take_quarter(w, index, 1)) for w in wide[:3]]
         return jnp.stack(pieces + [take_quarter(wide[3], index, 0)])
 
+    feed_piece = jnp.stack([take_quarter(w_gate, place, 1), take_quarter(w_up, place, 1), jnp.transpose(take_quarter(w_down, place, 0))])
+
+    ring, crossed = [attention_piece(place)], [attention_piece(place ^ 2)]
     gain_one, gain_two = gather_gains(jnp.stack([gain_attn, gain_ffn]))
-    inputs = tokens.astype(F32)
-    inv_one = inverse_rms(inputs)
-    normed = (inputs * inv_one * gain_one).astype(BF16)
-    before = to_later_chip(normed)
-    own_blocks = widen_chip(normed)
-    before_blocks = widen_chip(before)
-    count = len(own_blocks)
-    blocks = before_blocks + own_blocks
-    ring = [attention_piece(place)]
-    ring.append(pull_fsdp(ring[0], 1))
-    for step in range(2, fsdp):
-        ring.append(pull_fsdp(after(ring[-1], normed if step == 2 else own_blocks[1]), 1))
-    crossed = [attention_piece(place ^ 2)] + [swap_chip(block) for block in ring[1:]]
+    ids_other = swap_core(segment_ids)
+    block, own, before = together(pull_fsdp(ring[0], 1), widen_tp(tokens), to_later_chip(tokens))
+    ring.append(block)
+    ids_own = jnp.concatenate(in_order(segment_ids, ids_other, core == 0))
+    ids_before = jnp.where(chip > 0, to_later_chip(ids_own), -1)
+    block, over, before, own = together(pull_fsdp(ring[-1], 1), swap_chip(ring[-1]), widen_tp(before), widen_core(own))
+    ring.append(block)
+    crossed.append(over)
+    feed_weight = lax.all_gather(after(feed_piece, block), ("fsdp", "chip"), axis=0, tiled=False)
+    feed_weight = feed_weight.reshape((fsdp, chips) + feed_piece.shape)
+    dy = cotangent
+    for step in range(2, fsdp - 1):
+        moves = [pull_fsdp(ring[-1], 1), swap_chip(ring[-1])]
+        if step == 2:
+            moves += [widen_core(before), widen_tp(after(cotangent, block))]
+        moves = together(*moves)
+        ring.append(moves[0])
+        crossed.append(moves[1])
+        if step == 2:
+            before, dy = moves[2], moves[3]
+    crossed.append(swap_chip(ring[-1]))
+    dy = widen_core(dy)
     weights = place_weights(ring + crossed, fsdp)
 
-    pieces = (take_quarter(w_gate, place, 1), take_quarter(w_up, place, 1), jnp.transpose(take_quarter(w_down, place, 0)))
-    feed_own = [lax.all_gather(after(w, ring[-2]), "fsdp", axis=0, tiled=True) for w in pieces]
-    feed_other = [swap_chip(w) for w in feed_own]
-
+    def normed(values):
+        values = values.astype(F32)
+        return (values * inverse_rms(values) * gain_one).astype(BF16)
+
+    blocks = [normed(values) for values in before + own]
+    count = len(own)
     position = (chip * rows - rows + jnp.arange(keys, dtype=jnp.int32)).astype(F32)
     pair_index = (jnp.arange(LANES, dtype=jnp.int32) % (HEAD_DIM // 2)).astype(F32)
     angles = position[:, None] * (10000.0 ** (-pair_index * 2.0 / HEAD_DIM))[None, :]
     cos, sin = jnp.cos(angles), jnp.sin(angles)
-    ids_own = jnp.concatenate(in_order(segment_ids, swap_core(segment_ids), core == 0))
-    ids_before = jnp.where(chip > 0, to_later_chip(ids_own), -1)
     ids = jnp.concatenate([ids_before, ids_own])
     start = jnp.sum((ids[None, :] < ids_own[:, None]).astype(jnp.int32), axis=1)
     tiles = -(-rows // TILE)
@@ -711,67 +787,68 @@
     bounds = jnp.stack([start[::TILE] // TILE, jnp.array(ends, jnp.int32)])
     start = jnp.pad(start, (0, tiles * TILE - rows), constant_values=2 * keys)[None]
 
+    inputs = tokens.astype(F32)
+    inv_one = inverse_rms(inputs)
     q, k, v = project(blocks, weights, cos, sin, keys)
-    dy = widen_chip(after(cotangent, before_blocks[1]))
-    attended, lse = attend(bounds, after(q, feed_own[0]), after(k, *dy), v, start, rows, base)
-    kept, sent = out_project(after(attended, feed_own[1], feed_other[0]), weights, count)
-    residual = inputs + narrow_tp(narrow_core(kept, sent))
+    attended, lse = attend(bounds, q, after(k, *dy), v, start, rows, base)
+    attn_out, _ = narrow_chip(*out_project(attended, weights, count))
+    residual = inputs + attn_out
 
     inv_two = inverse_rms(residual)
-    normed_two = widen_chip(after((residual * inv_two * gain_two).astype(BF16), feed_own[2], feed_other[1]))
-    hidden, gate_grad, up_grad, kept, sent = feed(normed_two, dy, feed_own, feed_other)
-    pair = narrow_core(kept, sent)
-    normed_two_grad = narrow_tp(pair)
-    grads_other = feed_weights(normed_two, dy, after(hidden, pair), gate_grad, up_grad, 1)
+    normed_two = widen_chip((residual * inv_two * gain_two).astype(BF16))
+    hidden, gate_grad, up_grad, kept, sent = feed(normed_two, dy, feed_weight)
+    normed_two_grad, came = narrow_chip(kept, sent)
+    feed_grads = feed_weights(normed_two, dy, after(hidden, came), gate_grad, up_grad, fsdp, chips)
+    feed_sums = lax.psum_scatter(
+        feed_grads.reshape((fsdp * chips,) + feed_piece.shape), ("fsdp", "chip"), scatter_dimension=0, tiled=True
+    )[0]
     gain_two_grad = jnp.sum(normed_two_grad * residual * inv_two, axis=0)
     resid_grad = cotangent.astype(F32) + normalize_back(residual, inv_two, gain_two, normed_two_grad)
     resid_low = resid_grad.astype(BF16)
-    grads_own = feed_weights(normed_two, dy, after(hidden, resid_low), gate_grad, up_grad, 0)
-    feed_mine = [add_low(own, swap_chip(other)) for own, other in zip(grads_own, grads_other)]
-    feed_sums = [lax.psum_scatter(mine, "fsdp", scatter_dimension=0, tiled=True) for mine in feed_mine]
-    kept, sent = feed_out(after(hidden, grads_own[0]), feed_own[2], feed_other[2])
-    layer_out = residual + narrow_tp(narrow_core(kept, sent))
 
     grad_blocks = widen_chip(resid_low)
     out_grad, out_own, out_other = out_back(attended, weights, grad_blocks, fsdp)
-    dq, dk, dv = attend_back(bounds, q, k, v, attended, after(out_grad, feed_mine[0]), lse, start, cos, sin, rows, base)
+    dq, dk, dv = attend_back(bounds, q, k, v, attended, out_grad, lse, start, cos, sin, rows, base)
     out_sum = sum_over_chips_and_fsdp(out_own, out_other)
-    v_own, v_other, k_own, k_other, q_own, q_other = project_weights(after(dq, feed_sums[0]), dk, dv, blocks, fsdp)
+    v_own, v_other, k_own, k_other, q_own, q_other = project_weights(dq, dk, dv, blocks, fsdp)
     v_sum, k_sum, q_sum = (
         sum_over_chips_and_fsdp(*pair) for pair in ((v_own, v_other), (k_own, k_other), (q_own, q_other))
     )
-    early_kept, early_sent, kept, sent = project_back(after(dq, feed_sums[1], feed_mine[2]), dk, dv, weights, base, count)
-    earlier_back = to_earlier_chip(narrow_tp(narrow_core(early_kept, early_sent)).astype(BF16)).astype(F32)
-    normed_grad = narrow_tp(narrow_core(kept, sent)) + earlier_back
+    early_kept, early_sent, kept, sent = project_back(dq, dk, dv, weights, base, count)
+    earlier_back = to_earlier_chip(narrow_chip(early_kept, early_sent)[0].astype(BF16)).astype(F32)
+    normed_grad = narrow_chip(kept, sent)[0] + earlier_back
     gain_one_grad = jnp.sum(normed_grad * inputs * inv_one, axis=0)
     grad_input = resid_grad + normalize_back(inputs, inv_one, gain_one, normed_grad)
-
-    attention_all = jnp.stack(all_quarters(jnp.stack([q_sum, k_sum, v_sum, out_sum])), axis=1).reshape(4, width, columns)
-    attention_all = attention_all[:, :real_width].astype(F32)
-    feed_all = [all_quarters(total) for total in feed_sums]
+    kept, sent = feed_out(after(hidden, came), feed_weight)
+    layer_out = residual + narrow_chip(kept, sent)[0]
+
+    gate_all, up_all, down_all = finish_feed(*all_quarters(feed_sums))
+    q_all, k_all, v_all, out_all = finish_attention(*all_quarters(jnp.stack([q_sum, k_sum, v_sum, out_sum])), real_width)
     gain_own = gain_totals(jnp.stack([gain_one_grad, gain_two_grad]))
     return (
         layer_out.astype(BF16)[None],
         grad_input[None],
-        jnp.transpose(attention_all[0]),
-        jnp.transpose(attention_all[1]),
-        jnp.transpose(attention_all[2]),
-        attention_all[3],
-        jnp.concatenate(feed_all[0], axis=1).astype(F32),
-        jnp.concatenate(feed_all[1], axis=1).astype(F32),
-        jnp.transpose(jnp.concatenate(feed_all[2], axis=1)).astype(F32),
+        q_all,
+        k_all,
+        v_all,
+        out_all,
+        gate_all,
+        up_all,
+        down_all,
         gain_own[0],
         gain_own[1],
     )
 
 
 def solution(mesh):
-    rows = P("fsdp", ("ctx", "tp"), None)
+    devices = mesh.devices.reshape(mesh.shape["fsdp"], mesh.shape["ctx"] // 2, 2, mesh.shape["tp"])
+    split = jax.sharding.Mesh(devices, ("fsdp", "chip", "core", "tp"))
+    rows = P("fsdp", ("chip", "core", "tp"), None)
     into, outof, gain = P("fsdp", "tp"), P("tp", "fsdp"), P("fsdp")
     return jax.shard_map(
         shards,
-        mesh=mesh,
-        in_specs=(rows, P("fsdp", "ctx"), into, into, into, outof, into, into, outof, gain, gain, rows),
+        mesh=split,
+        in_specs=(rows, P("fsdp", ("chip", "core")), into, into, into, outof, into, into, outof, gain, gain, rows),
         out_specs=(rows, rows, into, into, into, outof, into, into, outof, gain, gain),
         check_vma=False,
     )

time: 716 us -> 654 us (0.913)
  starting transfers between devices: 143 us -> 105 us
  other arithmetic: 82.4 us -> 60.5 us
  local copies, waits for them, and re-layouts: 36.6 us -> 16.1 us
  Pallas kernels: 168 us -> 179 us
    ppermute x42 -> x32, starting transfers between devices: 98.5 us -> 62.8 us  [the longest x19 28.1 us: swap_core(): return lax.ppermute(values, 'core', [(0, 1), (1, 0)])]
    ppermute x11, waiting for transfers between devices: 62.6 us -> 91.4 us  [swap_tp(): return lax.ppermute(values, 'tp', [(0, 1), (1, 0)])]
    ppermute x42 -> x32, waiting for transfers between devices: 143 us -> 115 us  [the longest x10 103 us: swap_chip(): return lax.ppermute(values, 'chip', [(0, 1), (1, 0)])]
    ppermute x6, waiting for transfers between devices: 30.3 us -> 52.4 us  [pull_fsdp(): lax.ppermute(values, 'fsdp', [(i, (i - step) % count) for i in range(coun...]
    add x5 -> x0, other arithmetic: 16.1 us -> none  [narrow_core(): return kept.astype(F32) + swap_core(sent).astype(F32)]
    all_gather x3 -> x1, waiting for transfers between devices: 15.9 us -> 0.01 us  [shards(): lax.all_gather(after(feed_piece, block), ('fsdp', 'chip'), axis=0, tiled=...]
    pallas_call x2 -> x4, Pallas kernels: 38.5 us -> 50 us  [the longest x1 30.2 us: feed(): call(functools.partial(feed_kernel, count), 'feed', rows * depth * units...]
    convert_element_type x7 -> x4, other arithmetic: 17.2 us -> 7.04 us  [add_low(): return (left.astype(F32) + right.astype(F32)).astype(BF16)]
  transfers between devices with their start and end apart: 70 -> 56, of which waited for: 31 -> 26; matrix products, arithmetic and copies ran while one was open for 14% -> 12% of each run, Pallas kernels for 18% -> 19%
where the time goes in v4:
time: 654 us; the launch traced here: 648 us
  waiting for transfers between devices  272 us (42%)
  Pallas kernels  179 us (27%)
  starting transfers between devices  105 us (16%)
  other arithmetic  60.5 us (9%)
  local copies, waits for them, and re-layouts  16.1 us (2%)
  between operations  15.1 us (2%)
    ppermute x10, waiting for transfers between devices, swap_chip(): return lax.ppermute(values, 'chip', [(0, 1), (1, 0)])  103 us
    ppermute x11, waiting for transfers between devices, swap_tp(): return lax.ppermute(values, 'tp', [(0, 1), (1, 0)])  91.4 us
    ppermute x6, waiting for transfers between devices, pull_fsdp(): lax.ppermute(values, 'fsdp', [(i, (i - step) % count) for i in range(coun...  52.4 us
    pallas_call x1, Pallas kernels, attend_back(): call(functools.partial(backward_kernel, rows, base), 'attend_back', rows...  30.8 us
    pallas_call x1, Pallas kernels, feed(): call(functools.partial(feed_kernel, count), 'feed', rows * depth * units...  30.2 us
    ppermute x19, starting transfers between devices, swap_core(): return lax.ppermute(values, 'core', [(0, 1), (1, 0)])  28.1 us
    ppermute x10, starting transfers between devices, swap_chip(): return lax.ppermute(values, 'chip', [(0, 1), (1, 0)])  28.1 us
    pallas_call x1, Pallas kernels, feed_weights(): call(functools.partial(feed_weights_kernel, count), 'feed_weights', rows...  18.9 us
  transfers between devices with their start and end apart: 56, of which 26 were waited for; matrix products, arithmetic and copies ran while one was open for 12% of the time, Pallas kernels for 19%

profile of v4, /device:TPU:1, one launch (start us, length us, event | category | flops | bytes accessed | tf_op | source)
XLA Modules:
  0.0 647.6 jit_solution(1541015236682952922)
XLA Ops:
  27.1 11.4 %collective-permute-done.2.refs_1_ = bf16[4,192,384]{2,1,0:T(8,128)(2,1)} collective-permute-done((bf16[4,192,384]{2,1,0:T(8,128)(2,1)S(1)}, bf16[4,192,384]{2,1,0:T(8,128)(2,1)}, u32[]{:S(2)}, u32[]{:S(2)}) %collective-permute-start.2) | collective-permute-done | bytes 589856 | tf_op jit(solution)/shard_map/ppermute | solution.py:691
  49.8 8.2 %collective-permute-done.5.refs_2_ = bf16[4,192,384]{2,1,0:T(8,128)(2,1)} collective-permute-done((bf16[4,192,384]{2,1,0:T(8,128)(2,1)}, bf16[4,192,384]{2,1,0:T(8,128)(2,1)}, u32[]{:S(2)}, u32[]{:S(2)}) %collective-permute-start.5) | collective-permute-done | bytes 589856 | tf_op jit(solution)/shard_map/ppermute | solution.py:691
  88.1 32.8 %collective-permute-done.10.refs_3_ = bf16[4,192,384]{2,1,0:T(8,128)(2,1)S(1)} collective-permute-done((bf16[4,192,384]{2,1,0:T(8,128)(2,1)}, bf16[4,192,384]{2,1,0:T(8,128)(2,1)S(1)}, u32[]{:S(2)}, u32[]{:S(2)}) %collective-permute-start.10) | collective-permute-done | bytes 589856 | tf_op jit(solution)/shard_map/ppermute | solution.py:691
  131.7 9.7 %collective-permute-done.18.refs_7_ = bf16[4,192,384]{2,1,0:T(8,128)(2,1)} collective-permute-done((bf16[4,192,384]{2,1,0:T(8,128)(2,1)S(1)}, bf16[4,192,384]{2,1,0:T(8,128)(2,1)}, u32[]{:S(2)}, u32[]{:S(2)}) %collective-permute-start.18) | collective-permute-done | bytes 589856 | tf_op jit(solution)/shard_map/ppermute | solution.py:33
  146.3 16.0 %project.1 = (bf16[1088,384]{1,0:T(8,128)(2,1)}, bf16[2304,384]{1,0:T(8,128)(2,1)}, bf16[2304,384]{1,0:T(8,128)(2,1)}) custom-call(bf16[272,1536]{1,0:T(8,128)(2,1)} %get-tuple-element.173.refs_0_, bf16[272,1536]{1,0:T(8,128)(2,1)} %get-tuple-element.167.refs_1_, bf16[272,1536]{1,0:T(8,128)(2,1)} %get-tuple-element.168.refs_2_, ...), custom_call_target="tpu_custom_call" | custom-call | flops 6794772480 | bytes 7077888 | tf_op jit(solution)/shard_map/project/pallas_call | solution.py:163
  162.3 15.6 %attend.1 = (bf16[1088,384]{1,0:T(8,128)(2,1)}, f32[6,1280]{1,0:T(8,128)}) custom-call(s32[2,5]{1,0:T(2,128)} %pad_add_fusion.1.bounds, bf16[1088,384]{1,0:T(8,128)(2,1)} %get-tuple-element.91.q_ref, bf16[2304,384]{1,0:T(8,128)(2,1)} %get-tuple-element.95.k_ref, bf16[2304,384]{1,0:T(8,128)(2,1)} %get-tuple-element.96.v_ref, s32[1,1280]{1,0:T(1,128)} %broadcast_in_dim.11.start_ref), custom_call_target="tpu_custom_call" | custom-call | flops 3636461568 | bytes 7077888 | tf_op jit(solution)/shard_map/attend/pallas_call | solution.py:382
  192.7 19.3 %collective-permute-done.22 = bf16[272,1536]{1,0:T(8,128)(2,1)S(1)} collective-permute-done((bf16[272,1536]{1,0:T(8,128)(2,1)S(1)}, bf16[272,1536]{1,0:T(8,128)(2,1)S(1)}, u32[]{:S(2)}, u32[]{:S(2)}) %collective-permute-start.22) | collective-permute-done | bytes 835616 | tf_op jit(solution)/shard_map/ppermute | solution.py:49
  215.5 17.0 %collective-permute-done.23.refs_1_ = bf16[272,1536]{1,0:T(8,128)(2,1)S(1)} collective-permute-done((bf16[272,1536]{1,0:T(8,128)(2,1)S(1)}, bf16[272,1536]{1,0:T(8,128)(2,1)S(1)}, u32[]{:S(2)}, u32[]{:S(2)}) %collective-permute-start.23) | collective-permute-done | bytes 835616 | tf_op jit(solution)/shard_map/ppermute | solution.py:49
  236.7 30.2 %feed.1 = (bf16[1088,1024]{1,0:T(8,128)(2,1)}, bf16[1088,1024]{1,0:T(8,128)(2,1)}, bf16[1088,1024]{1,0:T(8,128)(2,1)}, f32[544,1536]{1,0:T(8,128)}, bf16[544,1536]{1,0:T(8,128)(2,1)}) custom-call(bf16[272,1536]{1,0:T(8,128)(2,1)} %copy-done.14, bf16[272,1536]{1,0:T(8,128)(2,1)} %copy-done.29, bf16[272,1536]{1,0:T(8,128)(2,1)} %copy-done.30, ...), custom_call_target="tpu_custom_call" | custom-call | flops 17112760320 | bytes 9437184 | tf_op jit(solution)/shard_map/feed/pallas_call | solution.py:535
  270.8 18.9 %feed_weights.1 = bf16[4,2,3,384,512]{4,3,2,1,0:T(8,128)(2,1)} custom-call(bf16[272,1536]{1,0:T(8,128)(2,1)} %copy-done.14, bf16[272,1536]{1,0:T(8,128)(2,1)} %copy-done.29, bf16[272,1536]{1,0:T(8,128)(2,1)} %copy-done.30, bf16[272,1536]{1,0:T(8,128)(2,1)} %collective-permute-done.25.refs_3_, bf16[272,1536]{1,0:T(8,128)(2,1)} %bitcast.76, ...), custom_call_target="tpu_custom_call" | custom-call | flops 10267656192 | bytes 9437184 | tf_op jit(solution)/shard_map/feed_weights/pallas_call | solution.py:574
  289.8 8.7 %feed_out.1 = (f32[544,1536]{1,0:T(8,128)}, bf16[544,1536]{1,0:T(8,128)(2,1)}) custom-call(bf16[1088,1024]{1,0:T(8,128)(2,1)} %get-tuple-element.103.hidden_ref.refs_8_, bf16[4,2,3,384,512]{4,3,2,1,0:T(8,128)(2,1)} %bitcast.92), custom_call_target="tpu_custom_call" | custom-call | flops 3422552064 | bytes 5013504 | tf_op jit(solution)/shard_map/feed_out/pallas_call | solution.py:612
  303.1 18.0 %collective-permute-done.29 = bf16[272,1536]{1,0:T(8,128)(2,1)S(1)} collective-permute-done((bf16[272,1536]{1,0:T(8,128)(2,1)S(1)}, bf16[272,1536]{1,0:T(8,128)(2,1)S(1)}, u32[]{:S(2)}, u32[]{:S(2)}) %collective-permute-start.29) | collective-permute-done | bytes 835616 | tf_op jit(solution)/shard_map/ppermute | solution.py:49
  323.0 16.0 %collective-permute-done.28 = bf16[272,1536]{1,0:T(8,128)(2,1)S(1)} collective-permute-done((bf16[272,1536]{1,0:T(8,128)(2,1)S(1)}, bf16[272,1536]{1,0:T(8,128)(2,1)S(1)}, u32[]{:S(2)}, u32[]{:S(2)}) %collective-permute-start.28) | collective-permute-done | bytes 835616 | tf_op jit(solution)/shard_map/ppermute | solution.py:49
  344.4 17.7 %collective-permute-done.30.refs_1_ = bf16[272,1536]{1,0:T(8,128)(2,1)S(1)} collective-permute-done((bf16[272,1536]{1,0:T(8,128)(2,1)S(1)}, bf16[272,1536]{1,0:T(8,128)(2,1)S(1)}, u32[]{:S(2)}, u32[]{:S(2)}) %collective-permute-start.30) | collective-permute-done | bytes 835616 | tf_op jit(solution)/shard_map/ppermute | solution.py:49
  365.8 8.0 %out_back.1 = (bf16[1088,384]{1,0:T(8,128)(2,1)}, bf16[4,192,384]{2,1,0:T(8,128)(2,1)}, bf16[4,192,384]{2,1,0:T(8,128)(2,1)}) custom-call(bf16[1088,384]{1,0:T(8,128)(2,1)} %get-tuple-element.97.o_ref, bf16[4,384,1536]{2,1,0:T(8,128)(2,1)} %place_weights.1.refs_8_.weight_ref, bf16[272,1536]{1,0:T(8,128)(2,1)} %copy-done.17, bf16[272,1536]{1,0:T(8,128)(2,1)} %copy-done.31, ...), custom_call_target="tpu_custom_call" | custom-call | flops 2566914048 | bytes 5013504 | tf_op jit(solution)/shard_map/out_back/pallas_call | solution.py:243
  373.7 30.8 %attend_back.1 = (bf16[1088,384]{1,0:T(8,128)(2,1)}, bf16[2304,384]{1,0:T(8,128)(2,1)}, bf16[2304,384]{1,0:T(8,128)(2,1)}) custom-call(s32[2,5]{1,0:T(2,128)} %pad_add_fusion.1.bounds, bf16[1088,384]{1,0:T(8,128)(2,1)} %get-tuple-element.91.q_ref, bf16[2304,384]{1,0:T(8,128)(2,1)} %get-tuple-element.95.k_ref, bf16[2304,384]{1,0:T(8,128)(2,1)} %get-tuple-element.96.v_ref, ...), custom_call_target="tpu_custom_call" | custom-call | flops 9091153920 | bytes 14155776 | tf_op jit(solution)/shard_map/attend_back/pallas_call | solution.py:466
  404.5 14.7 %project_weights.1 = (bf16[4,192,384]{2,1,0:T(8,128)(2,1)}, bf16[4,192,384]{2,1,0:T(8,128)(2,1)}, bf16[4,192,384]{2,1,0:T(8,128)(2,1)}, bf16[4,192,384]{2,1,0:T(...) custom-call(bf16[1088,384]{1,0:T(8,128)(2,1)} %get-tuple-element.109.dq_ref, ...), custom_call_target="tpu_custom_call" | custom-call | flops 6794772480 | bytes 7077888 | tf_op jit(solution)/shard_map/project_weights/pallas_call | solution.py:278
  419.2 18.0 %collective-permute-start.38 = (bf16[4,192,384]{2,1,0:T(8,128)(2,1)}, bf16[4,192,384]{2,1,0:T(8,128)(2,1)S(1)}, u32[]{:S(2)}, u32[]{:S(2)}) collective-permute-start(bf16[4,192,384]{2,1,0:T(8,128)(2,1)} %get-tuple-element.117), channel_id=1, source_target_pairs={{0,4},{4,0},{1,5},{5,1},{2,6},{6,2},{3,7},{7,3},{8,12},{12,8},{9,1... | collective-permute-start | bytes 1769480 | tf_op jit(solution)/shard_map/ppermute | solution.py:33
  437.3 13.6 %collective-permute-done.38 = bf16[4,192,384]{2,1,0:T(8,128)(2,1)S(1)} collective-permute-done((bf16[4,192,384]{2,1,0:T(8,128)(2,1)}, bf16[4,192,384]{2,1,0:T(8,128)(2,1)S(1)}, u32[]{:S(2)}, u32[]{:S(2)}) %collective-permute-start.38) | collective-permute-done | bytes 589856 | tf_op jit(solution)/shard_map/ppermute | solution.py:33
  457.9 12.5 %collective-permute-done.39 = bf16[4,192,384]{2,1,0:T(8,128)(2,1)S(1)} collective-permute-done((bf16[4,192,384]{2,1,0:T(8,128)(2,1)S(1)}, bf16[4,192,384]{2,1,0:T(8,128)(2,1)S(1)}, u32[]{:S(2)}, u32[]{:S(2)}) %collective-permute-start.39) | collective-permute-done | bytes 589856 | tf_op jit(solution)/shard_map/ppermute | solution.py:33
  475.9 13.8 %project_back.1 = (f32[544,1536]{1,0:T(8,128)}, bf16[544,1536]{1,0:T(8,128)(2,1)}, f32[544,1536]{1,0:T(8,128)}, bf16[544,1536]{1,0:T(8,128)(2,1)}) custom-call(bf16[1088,384]{1,0:T(8,128)(2,1)} %get-tuple-element.109.dq_ref, bf16[2304,384]{1,0:T(8,128)(2,1)} %get-tuple-element.110.dk_ref, bf16[2304,384]{1,0:T(8,128)(2,1)} %get-tuple-element.111.dv_ref, ...), custom_call_target="tpu_custom_call" | custom-call | flops 6417285120 | bytes 10027008 | tf_op jit(solution)/shard_map/project_back/pallas_call | solution.py:312
  502.6 12.8 %collective-permute-done.41 = bf16[4,192,384]{2,1,0:T(8,128)(2,1)S(1)} collective-permute-done((bf16[4,192,384]{2,1,0:T(8,128)(2,1)}, bf16[4,192,384]{2,1,0:T(8,128)(2,1)S(1)}, u32[]{:S(2)}, u32[]{:S(2)}) %collective-permute-start.41) | collective-permute-done | bytes 589856 | tf_op jit(solution)/shard_map/ppermute | solution.py:33
  525.3 11.8 %all-to-all-done.3 = bf16[4,192,384]{2,1,0:T(8,128)(2,1)} async-done(((bf16[4,192,384]{2,1,0:T(8,128)(2,1)}), bf16[4,192,384]{2,1,0:T(8,128)(2,1)}, u32[]{:S(2)}, u32[]{:S(2)}) %all-to-all-start.3) | async-done | bytes 589856 | tf_op jit(solution)/shard_map/all_to_all | solution.py:716
  552.0 49.8 %collective-permute-done.42.across_ref = bf16[4,192,384]{2,1,0:T(8,128)(2,1)S(1)} collective-permute-done((bf16[4,192,384]{2,1,0:T(8,128)(2,1)S(1)}, bf16[4,192,384]{2,1,0:T(8,128)(2,1)S(1)}, u32[]{:S(2)}, u32[]{:S(2)}) %collective-permute-start.42) | collective-permute-done | bytes 589856 | tf_op jit(solution)/shard_map/ppermute | solution.py:33
  (266 shorter events, 207.1 us)
Async XLA Ops:
  7.2 229.5 %all-gather.3.cloned.1.call-start = ((), (), s32[]{:S(2)}) async-start(), calls=%async_computation.7 | async-start | bytes 10616832 | tf_op jit(solution)/shard_map/all_gather | solution.py:757
  7.2 31.3 %collective-permute-start.3 = (bf16[272,1536]{1,0:T(8,128)(2,1)}, bf16[272,1536]{1,0:T(8,128)(2,1)S(1)}, u32[]{:S(2)}, u32[]{:S(2)}) collective-permute-start(bf16[272,1536]{1,0:T(8,128)(2,1)} %bitcast.64), channel_id=1, source_target_pairs={{0,1},{1,0},{2,3},{3,2},{4,5},{5,4},{6,7},{7,6},{8,9},{9,8},{10,11... | collective-permute-start | bytes 2506760 | tf_op jit(solution)/shard_map/ppermute | solution.py:49
  9.4 29.1 %collective-permute-start.4 = (bf16[272,1536]{1,0:T(8,128)(2,1)}, bf16[272,1536]{1,0:T(8,128)(2,1)}, u32[]{:S(2)}, u32[]{:S(2)}) collective-permute-start(bf16[272,1536]{1,0:T(8,128)(2,1)} %bitcast.65), channel_id=1, source_target_pairs={{0,4},{1,5},{2,6},{3,7},{8,12},{9,13},{10,14},{11,15},{16,20},{17,... | collective-permute-start | bytes 2506760 | tf_op jit(solution)/shard_map/ppermute | solution.py:41
  38.5 21.4 %collective-permute-start.7 = (bf16[272,1536]{1,0:T(8,128)(2,1)}, bf16[272,1536]{1,0:T(8,128)(2,1)}, u32[]{:S(2)}, u32[]{:S(2)}) collective-permute-start(bf16[272,1536]{1,0:T(8,128)(2,1)} %collective-permute-done.4), channel_id=1, source_target_pairs={{0,1},{1,0},{2,3},{3,2},{4,5},{5,4},{6,7},{7,6},{8,9},{9,8},{10,11... | collective-permute-start | bytes 2506760 | tf_op jit(solution)/shard_map/ppermute | solution.py:49
  60.0 487.0 %reduce-scatter.2.cloned.1.call-start = ((), (), s32[]{:S(2)}) async-start(), calls=%async_computation.6 | async-start | bytes 10616832 | tf_op jit(solution)/shard_map/reduce_scatter | solution.py:802
  77.5 43.4 %collective-permute-start.10 = (bf16[4,192,384]{2,1,0:T(8,128)(2,1)}, bf16[4,192,384]{2,1,0:T(8,128)(2,1)S(1)}, u32[]{:S(2)}, u32[]{:S(2)}) collective-permute-start(bf16[4,192,384]{2,1,0:T(8,128)(2,1)} %collective-permute-done.5.refs_2_), channel_id=1, source_target_pairs={{0,24},{8,0},{16,8},{24,16},{1,25},{9,1},{17,9},{25,17},{2,26},{10... | collective-permute-start | bytes 1769480 | tf_op jit(solution)/shard_map/ppermute | solution.py:691
  80.6 40.3 %collective-permute-start.11 = (bf16[4,192,384]{2,1,0:T(8,128)(2,1)}, bf16[4,192,384]{2,1,0:T(8,128)(2,1)S(1)}, u32[]{:S(2)}, u32[]{:S(2)}) collective-permute-start(bf16[4,192,384]{2,1,0:T(8,128)(2,1)} %collective-permute-done.5.refs_2_), channel_id=1, source_target_pairs={{0,4},{4,0},{1,5},{5,1},{2,6},{6,2},{3,7},{7,3},{8,12},{12,8},{9,1... | collective-permute-start | bytes 1769480 | tf_op jit(solution)/shard_map/ppermute | solution.py:33
  82.9 38.0 %collective-permute-start.14 = (bf16[272,1536]{1,0:T(8,128)(2,1)S(1)}, bf16[272,1536]{1,0:T(8,128)(2,1)}, u32[]{:S(2)}, u32[]{:S(2)}) collective-permute-start(bf16[272,1536]{1,0:T(8,128)(2,1)S(1)} %bitcast.77), channel_id=1, source_target_pairs={{0,1},{1,0},{2,3},{3,2},{4,5},{5,4},{6,7},{7,6},{8,9},{9,8},{10,11... | collective-permute-start | bytes 2506760 | tf_op jit(solution)/shard_map/ppermute | solution.py:49
  83.4 37.5 %collective-permute-start.12 = (bf16[272,1536]{1,0:T(8,128)(2,1)}, bf16[272,1536]{1,0:T(8,128)(2,1)S(1)}, u32[]{:S(2)}, u32[]{:S(2)}) collective-permute-start(bf16[272,1536]{1,0:T(8,128)(2,1)} %collective-permute-done.4), channel_id=1, source_target_pairs={{0,2},{2,0},{1,3},{3,1},{4,6},{6,4},{5,7},{7,5},{8,10},{10,8},{9,1... | collective-permute-start | bytes 2506760 | tf_op jit(solution)/shard_map/ppermute | solution.py:37
  84.8 36.2 %collective-permute-start.13 = (bf16[272,1536]{1,0:T(8,128)(2,1)}, bf16[272,1536]{1,0:T(8,128)(2,1)S(1)}, u32[]{:S(2)}, u32[]{:S(2)}) collective-permute-start(bf16[272,1536]{1,0:T(8,128)(2,1)} %collective-permute-done.7), channel_id=1, source_target_pairs={{0,2},{2,0},{1,3},{3,1},{4,6},{6,4},{5,7},{7,5},{8,10},{10,8},{9,1... | collective-permute-start | bytes 2506760 | tf_op jit(solution)/shard_map/ppermute | solution.py:37
  122.6 39.6 %collective-permute-start.19 = (bf16[272,1536]{1,0:T(8,128)(2,1)S(1)}, bf16[272,1536]{1,0:T(8,128)(2,1)}, u32[]{:S(2)}, u32[]{:S(2)}) collective-permute-start(bf16[272,1536]{1,0:T(8,128)(2,1)S(1)} %bitcast.78), channel_id=1, source_target_pairs={{0,2},{2,0},{1,3},{3,1},{4,6},{6,4},{5,7},{7,5},{8,10},{10,8},{9,1... | collective-permute-start | bytes 2506760 | tf_op jit(solution)/shard_map/ppermute | solution.py:37
  123.4 38.9 %collective-permute-start.20 = (bf16[272,1536]{1,0:T(8,128)(2,1)}, bf16[272,1536]{1,0:T(8,128)(2,1)}, u32[]{:S(2)}, u32[]{:S(2)}) collective-permute-start(bf16[272,1536]{1,0:T(8,128)(2,1)} %collective-permute-done.14.refs_5_), channel_id=1, source_target_pairs={{0,2},{2,0},{1,3},{3,1},{4,6},{6,4},{5,7},{7,5},{8,10},{10,8},{9,1... | collective-permute-start | bytes 2506760 | tf_op jit(solution)/shard_map/ppermute | solution.py:37
  302.5 36.5 %collective-permute-start.28 = (bf16[272,1536]{1,0:T(8,128)(2,1)S(1)}, bf16[272,1536]{1,0:T(8,128)(2,1)S(1)}, u32[]{:S(2)}, u32[]{:S(2)}) collective-permute-start(bf16[272,1536]{1,0:T(8,128)(2,1)S(1)} %add_convert_fusion.5), channel_id=1, source_target_pairs={{0,1},{1,0},{2,3},{3,2},{4,5},{5,4},{6,7},{7,6},{8,9},{9,8},{10,11... | collective-permute-start | bytes 2506760 | tf_op jit(solution)/shard_map/ppermute | solution.py:49
  419.2 31.6 %collective-permute-start.38 = (bf16[4,192,384]{2,1,0:T(8,128)(2,1)}, bf16[4,192,384]{2,1,0:T(8,128)(2,1)S(1)}, u32[]{:S(2)}, u32[]{:S(2)}) collective-permute-start(bf16[4,192,384]{2,1,0:T(8,128)(2,1)} %get-tuple-element.117), channel_id=1, source_target_pairs={{0,4},{4,0},{1,5},{5,1},{2,6},{6,2},{3,7},{7,3},{8,12},{12,8},{9,1... | collective-permute-start | bytes 1769480 | tf_op jit(solution)/shard_map/ppermute | solution.py:33
  457.6 36.0 %collective-permute-start.40 = (bf16[4,192,384]{2,1,0:T(8,128)(2,1)}, bf16[4,192,384]{2,1,0:T(8,128)(2,1)}, u32[]{:S(2)}, u32[]{:S(2)}) collective-permute-start(bf16[4,192,384]{2,1,0:T(8,128)(2,1)} %get-tuple-element.121), channel_id=1, source_target_pairs={{0,4},{4,0},{1,5},{5,1},{2,6},{6,2},{3,7},{7,3},{8,12},{12,8},{9,1... | collective-permute-start | bytes 1769480 | tf_op jit(solution)/shard_map/ppermute | solution.py:33
  472.2 23.5 %all-to-all-start.1 = ((bf16[4,192,384]{2,1,0:T(8,128)(2,1)}), bf16[4,192,384]{2,1,0:T(8,128)(2,1)S(1)}, u32[]{:S(2)}, u32[]{:S(2)}) async-start(bf16[4,192,384]{2,1,0:T(8,128)(2,1)} %add_convert_fusion.9), calls=%async_computation.1 | async-start | bytes 1179648 | tf_op jit(solution)/shard_map/all_to_all | solution.py:716
  489.7 31.9 %collective-permute-start.35 = (bf16[544,1536]{1,0:T(8,128)(2,1)}, bf16[544,1536]{1,0:T(8,128)(2,1)}, u32[]{:S(2)}, u32[]{:S(2)}) collective-permute-start(bf16[544,1536]{1,0:T(8,128)(2,1)} %get-tuple-element.115), channel_id=1, source_target_pairs={{0,2},{2,0},{1,3},{3,1},{4,6},{6,4},{5,7},{7,5},{8,10},{10,8},{9,1... | collective-permute-start | bytes 5013512 | tf_op jit(solution)/shard_map/ppermute | solution.py:37
  495.7 21.7 %all-to-all-start.2 = ((bf16[4,192,384]{2,1,0:T(8,128)(2,1)}), bf16[4,192,384]{2,1,0:T(8,128)(2,1)S(1)}, u32[]{:S(2)}, u32[]{:S(2)}) async-start(bf16[4,192,384]{2,1,0:T(8,128)(2,1)} %add_convert_fusion.8), calls=%async_computation.2 | async-start | bytes 1179648 | tf_op jit(solution)/shard_map/all_to_all | solution.py:716
  502.0 37.0 %collective-permute-start.33 = (bf16[544,1536]{1,0:T(8,128)(2,1)}, bf16[544,1536]{1,0:T(8,128)(2,1)}, u32[]{:S(2)}, u32[]{:S(2)}) collective-permute-start(bf16[544,1536]{1,0:T(8,128)(2,1)} %get-tuple-element.113), channel_id=1, source_target_pairs={{0,2},{2,0},{1,3},{3,1},{4,6},{6,4},{5,7},{7,5},{8,10},{10,8},{9,1... | collective-permute-start | bytes 5013512 | tf_op jit(solution)/shard_map/ppermute | solution.py:37
  541.0 66.0 %collective-permute-start.34 = (bf16[272,1536]{1,0:T(8,128)(2,1)S(1)}, bf16[272,1536]{1,0:T(8,128)(2,1)S(1)}, u32[]{:S(2)}, u32[]{:S(2)}) collective-permute-start(bf16[272,1536]{1,0:T(8,128)(2,1)S(1)} %add_convert_fusion.2), channel_id=1, source_target_pairs={{0,1},{1,0},{2,3},{3,2},{4,5},{5,4},{6,7},{7,6},{8,9},{9,8},{10,11... | collective-permute-start | bytes 2506760 | tf_op jit(solution)/shard_map/ppermute | solution.py:49
  545.7 61.2 %collective-permute-start.37 = (bf16[272,1536]{1,0:T(8,128)(2,1)}, bf16[272,1536]{1,0:T(8,128)(2,1)}, u32[]{:S(2)}, u32[]{:S(2)}) collective-permute-start(bf16[272,1536]{1,0:T(8,128)(2,1)} %add_convert_fusion), channel_id=1, source_target_pairs={{4,0},{5,1},{6,2},{7,3},{12,8},{13,9},{14,10},{15,11},{20,16},{21,... | collective-permute-start | bytes 2506760 | tf_op jit(solution)/shard_map/ppermute | solution.py:45
  547.0 63.4 %collective-permute-start.44 = (bf16[3,384,512]{2,1,0:T(8,128)(2,1)}, bf16[3,384,512]{2,1,0:T(8,128)(2,1)S(1)}, u32[]{:S(2)}, u32[]{:S(2)}) collective-permute-start(bf16[3,384,512]{2,1,0:T(8,128)(2,1)} %bitcast.70), channel_id=1, source_target_pairs={{0,4},{4,0},{1,5},{5,1},{2,6},{6,2},{3,7},{7,3},{8,12},{12,8},{9,1... | collective-permute-start | bytes 3538952 | tf_op jit(solution)/shard_map/ppermute | solution.py:33
  551.2 50.6 %collective-permute-start.42 = (bf16[4,192,384]{2,1,0:T(8,128)(2,1)S(1)}, bf16[4,192,384]{2,1,0:T(8,128)(2,1)S(1)}, u32[]{:S(2)}, u32[]{:S(2)}) collective-permute-start(bf16[4,192,384]{2,1,0:T(8,128)(2,1)S(1)} %get-tuple-element.151.own_ref), channel_id=1, source_target_pairs={{0,4},{4,0},{1,5},{5,1},{2,6},{6,2},{3,7},{7,3},{8,12},{12,8},{9,1... | collective-permute-start | bytes 1769480 | tf_op jit(solution)/shard_map/ppermute | solution.py:33
  612.3 21.3 %collective-permute-start.45 = (bf16[2,3,384,512]{3,2,1,0:T(8,128)(2,1)}, bf16[2,3,384,512]{3,2,1,0:T(8,128)(2,1)}, u32[]{:S(2)}, u32[]{:S(2)}) collective-permute-start(bf16[2,3,384,512]{3,2,1,0:T(8,128)(2,1)} %pad_maximum_fusion), channel_id=1, source_target_pairs={{0,2},{2,0},{1,3},{3,1},{4,6},{6,4},{5,7},{7,5},{8,10},{10,8},{9,1... | collective-permute-start | bytes 7077896 | tf_op jit(solution)/shard_map/ppermute | solution.py:37
  (66 other events, 988.5 us)
Sparse Core Ops, SparseCore 0:
  60.1 154.1 all-gather.2
  289.9 165.6 reduce-scatter.1

commit v5 on v4

v5 whole, which is shorter than its diff:
```python
import functools

import jax
import jax.numpy as jnp
from jax import lax
from jax.experimental import pallas as pl
from jax.experimental.pallas import tpu as pltpu
from jax.sharding import PartitionSpec as P

HEAD_DIM = 64
EPSILON = 1e-05
MASKED = -1e30
BF16 = jnp.bfloat16
F32 = jnp.float32
TILE = 256
LANES = 128
VMEM_BYTES = 60 * 1024 * 1024


def dot(left, right):
    return jnp.dot(left, right, preferred_element_type=F32)


def dot_nt(left, right):
    return lax.dot_general(left, right, (((1,), (1,)), ((), ())), preferred_element_type=F32)


def dot_tn(left, right):
    return lax.dot_general(left, right, (((0,), (0,)), ((), ())), preferred_element_type=F32)


def swap_chip(values):
    return lax.ppermute(values, "chip", [(0, 1), (1, 0)])


def swap_core(values):
    return lax.ppermute(values, "core", [(0, 1), (1, 0)])


def swap_tp(values):
    return lax.ppermute(values, "tp", [(0, 1), (1, 0)])


def in_order(mine, other, mine_first):
    return [jnp.where(mine_first, mine, other), jnp.where(mine_first, other, mine)]


def together(*values):
    return lax.optimization_barrier(values)


def after(values, *earlier):
    return lax.optimization_barrier((values, earlier))[0]


def widen_planes(rows, meanwhile=None):
    if lax.axis_size("tp") != 2:
        gathered = lax.all_gather(rows, "tp", axis=0, tiled=True)
        return [gathered, swap_chip(gathered)]
    return far_block(rows, *meet(swap_tp(rows), swap_chip(rows), meanwhile))


def meet(beside, across, meanwhile):
    return (beside, across) if meanwhile is None else after((beside, across), meanwhile)


def far_block(rows, beside, across):
    cut = rows.shape[0] // 32 * 16
    far = jnp.concatenate([swap_tp(across[:cut]), swap_chip(beside[cut:])], axis=0)
    return [rows, beside, across, far]


def widen_core(blocks):
    return blocks + [swap_core(block) for block in blocks]


def widen(rows):
    return widen_core(widen_planes(rows))


def block_offset(index, half):
    chip, core = lax.axis_index("chip"), lax.axis_index("core")
    if lax.axis_size("tp") != 2:
        return (chip ^ index % 2) * 2 * half + (core ^ index // 2) * half
    place = lax.axis_index("tp")
    return (chip ^ index // 2 % 2) * 2 * half + (core ^ index // 4) * half + (place ^ index % 2) * (half // 2)


def narrow_first(kept, sent, meanwhile=None):
    came = swap_core(sent)
    if lax.axis_size("tp") != 2:
        rows = kept.shape[0] // 2
        total = kept.astype(F32) + came.astype(F32)
        return ((total[:rows] + swap_chip(total[rows:].astype(BF16)).astype(F32)).astype(BF16),)
    rows = kept.shape[0] // 4
    cut = rows // 32 * 16

    def block(index, first, last):
        where = slice(index * rows + first, index * rows + last)
        return kept[where].astype(F32) + came[where].astype(F32)

    top, bottom = meet(swap_chip(block(3, 0, cut).astype(BF16)), swap_tp(block(3, cut, rows).astype(BF16)), meanwhile)
    beside = jnp.concatenate([block(1, 0, cut) + top.astype(F32), block(1, cut, rows)], axis=0).astype(BF16)
    across = jnp.concatenate([block(2, 0, cut), block(2, cut, rows) + bottom.astype(F32)], axis=0).astype(BF16)
    return beside, across, block(0, 0, rows)


def narrow_second(leaving, meanwhile=None):
    done = None
    if len(leaving) == 1:
        if meanwhile is not None:
            done = meanwhile(leaving)
        return lax.psum_scatter(leaving[0], "tp", scatter_dimension=0, tiled=True).astype(F32), done
    from_tp, from_chip = swap_tp(leaving[0]), swap_chip(leaving[1])
    if meanwhile is not None:
        (from_tp, from_chip), done = together((from_tp, from_chip), meanwhile(leaving[:2]))
    return leaving[2] + from_tp.astype(F32) + from_chip.astype(F32), done


def narrow(kept, sent, meanwhile=None):
    return narrow_second(narrow_first(kept, sent), meanwhile)


def take_quarter(values, index, axis):
    size = values.shape[axis] // 4
    return lax.dynamic_slice_in_dim(values, index * size, size, axis)


def all_quarters(own):
    across = swap_chip(own)
    return own, across, swap_core(jnp.stack([own, across]))


def call(kernel, name, flops, moved, **rest):
    return pl.pallas_call(
        kernel,
        name=name,
        cost_estimate=pl.CostEstimate(flops=flops, bytes_accessed=moved, transcendentals=0),
        compiler_params=pltpu.CompilerParams(vmem_limit_bytes=VMEM_BYTES),
        **rest,
    )


def whole():
    return pl.BlockSpec(memory_space=pltpu.VMEM)


def turn(values, cos, sin, direction):
    lane = lax.broadcasted_iota(jnp.int32, (1, LANES), 1)
    partner = jnp.where((lane // 32) % 2 == 0, pltpu.roll(values, 96, 1) * -direction, pltpu.roll(values, 32, 1) * direction)
    return values * cos + partner * sin


def block_spans(count, rows):
    block = rows // count
    return [pl.ds(pl.multiple_of(block_offset(i, rows // 4), 16), block) for i in range(count)]


def project_kernel(count, rows, *refs):
    blocks = refs[:count]
    weight_ref, cos_ref, sin_ref, q_ref, k_ref, v_ref = refs[count:]
    width = q_ref.shape[1]
    for ref in (k_ref, v_ref):
        ref[rows:, :] = jnp.zeros((ref.shape[0] - rows, width), BF16)
    for block, span in zip(blocks, block_spans(count, rows)):
        cos, sin = cos_ref[span, :], sin_ref[span, :]
        for kind, out_ref in ((0, q_ref), (1, k_ref)):
            values = dot_nt(block[...], weight_ref[kind])
            for c in range(0, width, LANES):
                out_ref[span, c : c + LANES] = turn(values[:, c : c + LANES], cos, sin, 1.0).astype(BF16)
        v_ref[span, :] = dot_nt(block[...], weight_ref[2]).astype(BF16)


def project(blocks, weights, cos, sin, keys):
    count = len(blocks)
    block, depth = blocks[0].shape
    rows = count * block
    width = weights.shape[1]
    tall = jax.ShapeDtypeStruct((keys, width), BF16)
    return call(
        functools.partial(project_kernel, count, rows),
        "project",
        rows * depth * width * 6,
        rows * depth * 2,
        out_shape=(jax.ShapeDtypeStruct((rows, width), BF16), tall, tall),
        in_specs=[whole()] * (count + 3),
        out_specs=[whole()] * 3,
    )(*blocks, weights, cos, sin)


def cut_kernel(q_ref, k_ref, v_ref, out_ref, piece_ref, buf):
    part = piece_ref.shape[1]
    span = pl.ds(pl.multiple_of(quarter_places()[0] * part, 16), part)
    for kind, ref in enumerate((q_ref, k_ref, v_ref)):
        buf[...] = jnp.transpose(ref[...])
        piece_ref[kind] = buf[span, :]
    piece_ref[3] = out_ref[span, :]


def cut_attention(wq, wk, wv, wo):
    width, columns = wo.shape
    return call(
        cut_kernel,
        "cut_attention",
        0,
        width * columns * 8,
        out_shape=jax.ShapeDtypeStruct((4, width // 4, columns), BF16),
        in_specs=[whole()] * 4,
        out_specs=whole(),
        scratch_shapes=[pltpu.VMEM((width, columns), BF16)],
    )(wq, wk, wv, wo)


def place_kernel(*refs):
    blocks, out_ref = refs[:-1], refs[-1]
    kinds, part, columns = blocks[0].shape
    me = lax.axis_index("fsdp")
    if part < out_ref.shape[1]:
        out_ref[:, part:, :] = jnp.zeros((kinds, out_ref.shape[1] - part, out_ref.shape[2]), BF16)
    for i, block in enumerate(blocks):
        at = pl.multiple_of((me + i) % len(blocks) * columns, LANES)
        out_ref[:, :part, pl.ds(at, columns)] = block[...]


def place_weights(blocks, width):
    kinds, _, columns = blocks[0].shape
    depth = len(blocks) * columns
    return call(
        place_kernel,
        "place_weights",
        0,
        kinds * width * depth * 4,
        out_shape=jax.ShapeDtypeStruct((kinds, width, depth), BF16),
        in_specs=[whole()] * len(blocks),
        out_specs=whole(),
    )(*blocks)


def store_block(kept_ref, sent_ref, i, block, values):
    half = kept_ref.shape[0]
    at = i * block
    if at < half:
        kept_ref[at : at + block, :] = values.astype(BF16)
    else:
        sent_ref[at - half : at - half + block, :] = values.astype(BF16)


def halves(rows, depth):
    return [jax.ShapeDtypeStruct((rows // 2, depth), BF16)] * 2


def out_kernel(count, o_ref, weight_ref, kept_ref, sent_ref):
    rows = o_ref.shape[0]
    for i, span in enumerate(block_spans(count, rows)):
        store_block(kept_ref, sent_ref, i, rows // count, dot(o_ref[span, :], weight_ref[3]))


def out_project(attended, weights, count):
    rows, width = attended.shape
    depth = weights.shape[2]
    return call(
        functools.partial(out_kernel, count),
        "out_project",
        rows * width * depth * 2,
        rows * depth * 2,
        out_shape=halves(rows, depth),
        in_specs=[whole(), whole()],
        out_specs=[whole(), whole()],
    )(attended, weights)


def out_back_kernel(count, o_ref, weight_ref, *refs):
    blocks, (grad_ref, out_ref, all_rows) = refs[:count], refs[count:]
    rows = o_ref.shape[0]
    for block, span in zip(blocks, block_spans(count, rows)):
        grad = block[...]
        grad_ref[span, :] = dot_nt(grad, weight_ref[3]).astype(BF16)
        all_rows[span, :] = grad
    total = dot_tn(o_ref[...], all_rows[...])
    fsdp, _, part, columns = out_ref.shape
    for z in range(fsdp):
        out_ref[z, 0] = total[:part, z * columns : (z + 1) * columns].astype(BF16)


def out_back(attended, weights, blocks, fsdp, part):
    rows, width = attended.shape
    depth = weights.shape[2]
    return call(
        functools.partial(out_back_kernel, len(blocks)),
        "out_back",
        rows * width * depth * 4,
        rows * depth * 2,
        out_shape=(
            jax.ShapeDtypeStruct((rows, width), BF16),
            jax.ShapeDtypeStruct((fsdp, 1, part, depth // fsdp), BF16),
        ),
        in_specs=[whole()] * (2 + len(blocks)),
        out_specs=[whole()] * 2,
        scratch_shapes=[pltpu.VMEM((rows, depth), BF16)],
    )(attended, weights, *blocks)


def project_weights_kernel(count, dq_ref, dk_ref, dv_ref, done_ref, *refs):
    blocks, (out_ref, all_rows) = refs[:count], refs[count:]
    rows = all_rows.shape[0]
    for block, span in zip(blocks, block_spans(count, rows)):
        all_rows[span, :] = block[...]
    part = out_ref.shape[2]
    for kind, grad in enumerate((dq_ref, dk_ref, dv_ref)):
        out_ref[0, kind] = dot_tn(grad[:rows, :], all_rows[...])[:part].astype(BF16)
    out_ref[0, 3] = done_ref[0, 0]


def project_weights(dq, dk, dv, out_grads, blocks):
    rows, width = dq.shape
    fsdp, _, part, _ = out_grads.shape
    block, depth = blocks[0].shape
    columns = depth // fsdp
    fixed = lambda array: pl.BlockSpec(array.shape, lambda z: (0, 0))
    return call(
        functools.partial(project_weights_kernel, len(blocks)),
        "project_weights",
        rows * width * depth * 6,
        rows * depth * 2,
        grid=(fsdp,),
        out_shape=jax.ShapeDtypeStruct((fsdp, 4, part, columns), BF16),
        in_specs=[fixed(dq), fixed(dk), fixed(dv), pl.BlockSpec((1, 1, part, columns), lambda z: (z, 0, 0, 0))]
        + [pl.BlockSpec((block, columns), lambda z: (0, z))] * len(blocks),
        out_specs=pl.BlockSpec((1, 4, part, columns), lambda z: (z, 0, 0, 0)),
        scratch_shapes=[pltpu.VMEM((rows, columns), BF16)],
    )(dq, dk, dv, out_grads, *blocks)


def column_sums(grads, normed):
    product = grads * normed.astype(F32)
    return jnp.sum(product.reshape(product.shape[0] // 8, 8, product.shape[1]), axis=0)


def project_back_kernel(count, dq_ref, dk_ref, dv_ref, weight_ref, *refs):
    blocks, (kept_ref, sent_ref, gain_ref) = refs[:count], refs[count:]
    rows = dq_ref.shape[0]
    sums = 0.0
    for i, (block, span) in enumerate(zip(blocks, block_spans(count, rows))):
        total = dot(dq_ref[span, :], weight_ref[0]) + dot(dk_ref[span, :], weight_ref[1]) + dot(dv_ref[span, :], weight_ref[2])
        sums = sums + column_sums(total, block[...])
        store_block(kept_ref, sent_ref, i, rows // count, total)
    gain_ref[...] = sums


def project_back(dq, dk, dv, weights, blocks):
    rows, width = dq.shape
    depth = weights.shape[2]
    return call(
        functools.partial(project_back_kernel, len(blocks)),
        "project_back",
        rows * width * depth * 6,
        rows * depth * 4,
        out_shape=halves(rows, depth) + [jax.ShapeDtypeStruct((8, depth), F32)],
        in_specs=[whole()] * (4 + len(blocks)),
        out_specs=[whole()] * 3,
    )(dq, dk, dv, weights, *blocks)


def lane_half(head):
    return (lax.broadcasted_iota(jnp.int32, (1, LANES), 1) // HEAD_DIM) == head % 2


def forward_kernel(rows, bounds, q_ref, k_ref, v_ref, start_ref, o_ref, lse_ref, q_buf, s_buf, top_buf, sum_buf, acc_buf):
    heads = q_buf.shape[0]
    zero = jnp.zeros((), BF16)
    for t in range(-(-rows // TILE)):
        low, high = bounds[0, t], bounds[1, t]
        n = min(TILE, rows - t * TILE)
        span = slice(t * TILE, (t + 1) * TILE)
        start = start_ref[:, span]
        row = t * TILE + lax.broadcasted_iota(jnp.int32, (1, TILE), 1)
        for h in range(heads):
            c = (h // 2) * LANES
            scaled = (q_ref[t * TILE : t * TILE + n, c : c + LANES].astype(F32) * HEAD_DIM**-0.5).astype(BF16)
            q_buf[h, :n, :] = jnp.where(lane_half(h), scaled, zero)
            if n < TILE:
                q_buf[h, n:, :] = jnp.zeros((TILE - n, LANES), BF16)
        top_buf[...] = jnp.full_like(top_buf, MASKED)
        sum_buf[...] = jnp.zeros_like(sum_buf)
        acc_buf[...] = jnp.zeros_like(acc_buf)

        @pl.loop(low, high)
        def _(i):
            at = pl.multiple_of(i * TILE, TILE)
            place = at + lax.broadcasted_iota(jnp.int32, (TILE, TILE), 0)
            allowed = (place >= start) & (place <= row)
            for h in range(heads):
                c = (h // 2) * LANES
                s = jnp.where(allowed, dot_nt(k_ref[pl.ds(at, TILE), c : c + LANES], q_buf[h]), MASKED)
                s_buf[h, pl.ds(at, TILE), :] = s
                top_buf[h] = jnp.maximum(top_buf[h], jnp.max(s.reshape(TILE // 8, 8, TILE), axis=0))

        tops = [jnp.max(top_buf[h], axis=0, keepdims=True) for h in range(heads)]

        @pl.loop(low, high)
        def _(i):
            at = pl.multiple_of(i * TILE, TILE)
            for h in range(heads):
                c = (h // 2) * LANES
                p = jnp.exp(s_buf[h, pl.ds(at, TILE), :] - tops[h])
                sum_buf[h] += jnp.sum(p.reshape(TILE // 8, 8, TILE), axis=0)
                both = dot_tn(v_ref[pl.ds(at, TILE), c : c + LANES], p.astype(BF16))
                acc_buf[h] += both[HEAD_DIM * (h % 2) : HEAD_DIM * (h % 2) + HEAD_DIM]

        for h in range(heads):
            total = jnp.sum(sum_buf[h], axis=0, keepdims=True)
            lse_ref[h : h + 1, span] = tops[h] + jnp.log(total)
            acc_buf[h] = acc_buf[h] / total
        for pair in range(o_ref.shape[1] // LANES):
            second = acc_buf[2 * pair + 1] if 2 * pair + 1 < heads else jnp.zeros((HEAD_DIM, TILE), F32)
            o = jnp.transpose(jnp.concatenate([acc_buf[2 * pair], second], axis=0))
            o_ref[t * TILE : t * TILE + n, pair * LANES : (pair + 1) * LANES] = o[:n].astype(BF16)


def attend(bounds, q, k, v, start, heads):
    rows = q.shape[0]
    keys, width = k.shape
    padded = -(-rows // TILE) * TILE
    return call(
        functools.partial(forward_kernel, rows),
        "attend",
        rows * rows * heads * HEAD_DIM * 2,
        keys * width * 8,
        out_shape=(jax.ShapeDtypeStruct((rows, width), BF16), jax.ShapeDtypeStruct((heads, padded), F32)),
        in_specs=[pl.BlockSpec(memory_space=pltpu.SMEM)] + [whole()] * 4,
        out_specs=[whole(), whole()],
        scratch_shapes=[
            pltpu.VMEM((heads, TILE, LANES), BF16),
            pltpu.VMEM((heads, keys, TILE), F32),
            pltpu.VMEM((heads, 8, TILE), F32),
            pltpu.VMEM((heads, 8, TILE), F32),
            pltpu.VMEM((heads, HEAD_DIM, TILE), F32),
        ],
    )(bounds, q, k, v, start)


def backward_kernel(
    rows, bounds, q_ref, k_ref, v_ref, o_ref, g_ref, lse_ref, start_ref, cos_ref, sin_ref,
    dq_ref, dk_ref, dv_ref, q_buf, g_buf, d_buf, dq_acc, dk_acc, dv_acc,
):
    heads = q_buf.shape[0]
    zero = jnp.zeros((), BF16)
    scale = HEAD_DIM**-0.5
    dk_acc[...] = jnp.zeros_like(dk_acc)
    dv_acc[...] = jnp.zeros_like(dv_acc)
    for t in range(-(-rows // TILE)):
        low, high = bounds[0, t], bounds[1, t]
        n = min(TILE, rows - t * TILE)
        span = slice(t * TILE, (t + 1) * TILE)
        here = slice(t * TILE, t * TILE + n)
        start = start_ref[:, span]
        row = t * TILE + lax.broadcasted_iota(jnp.int32, (1, TILE), 1)
        for pair in range(-(-heads // 2)):
            c = pair * LANES
            scaled = (q_ref[here, c : c + LANES].astype(F32) * scale).astype(BF16)
            grad = g_ref[here, c : c + LANES]
            product = grad.astype(F32) * o_ref[here, c : c + LANES].astype(F32)
            if n < TILE:
                product = jnp.concatenate([product, jnp.zeros((TILE - n, LANES), F32)], axis=0)
            product = jnp.transpose(product)
            for h in range(2 * pair, min(heads, 2 * pair + 2)):
                q_buf[h, :n, :] = jnp.where(lane_half(h), scaled, zero)
                g_buf[h, :n, :] = jnp.where(lane_half(h), grad, zero)
                if n < TILE:
                    q_buf[h, n:, :] = jnp.zeros((TILE - n, LANES), BF16)
                    g_buf[h, n:, :] = jnp.zeros((TILE - n, LANES), BF16)
                d_buf[h : h + 1, :] = jnp.sum(product[HEAD_DIM * (h % 2) : HEAD_DIM * (h % 2) + HEAD_DIM], axis=0, keepdims=True)
        dq_acc[...] = jnp.zeros_like(dq_acc)

        @pl.loop(low, high)
        def _(i):
            at = pl.multiple_of(i * TILE, TILE)
            place = at + lax.broadcasted_iota(jnp.int32, (TILE, TILE), 0)
            allowed = (place >= start) & (place <= row)
            for pair in range(-(-heads // 2)):
                c = pair * LANES
                k = k_ref[pl.ds(at, TILE), c : c + LANES]
                v = v_ref[pl.ds(at, TILE), c : c + LANES]
                dq = dk = dv = 0.0
                for h in range(2 * pair, min(heads, 2 * pair + 2)):
                    p = jnp.where(allowed, jnp.exp(dot_nt(k, q_buf[h]) - lse_ref[h : h + 1, span]), 0.0)
                    ds = (p * (dot_nt(v, g_buf[h]) - d_buf[h : h + 1, :])).astype(BF16)
                    dv = dv + dot(p.astype(BF16), g_buf[h])
                    dk = dk + dot(ds, q_buf[h])
                    dq = dq + dot_tn(ds, jnp.where(lane_half(h), k, zero))
                dk_acc[pl.ds(at, TILE), c : c + LANES] += dk
                dv_acc[pl.ds(at, TILE), c : c + LANES] += dv
                dq_acc[:, c : c + LANES] += dq

        for c in range(0, dk_ref.shape[1], LANES):
            dq = dq_acc[:n, c : c + LANES] * scale
            dq_ref[here, c : c + LANES] = turn(dq, cos_ref[here, :], sin_ref[here, :], -1.0).astype(BF16)
    for c in range(0, dk_ref.shape[1], LANES):
        dk_ref[:, c : c + LANES] = turn(dk_acc[:, c : c + LANES], cos_ref[...], sin_ref[...], -1.0).astype(BF16)
    dv_ref[...] = dv_acc[...].astype(BF16)


def attend_back(bounds, q, k, v, o, grad, lse, start, cos, sin, heads):
    rows = q.shape[0]
    keys, width = k.shape
    tall = jax.ShapeDtypeStruct((keys, width), BF16)
    return call(
        functools.partial(backward_kernel, rows),
        "attend_back",
        rows * rows * heads * HEAD_DIM * 5,
        keys * width * 16,
        out_shape=(jax.ShapeDtypeStruct((rows, width), BF16), tall, tall),
        in_specs=[pl.BlockSpec(memory_space=pltpu.SMEM)] + [whole()] * 9,
        out_specs=[whole()] * 3,
        scratch_shapes=[
            pltpu.VMEM((heads, TILE, LANES), BF16),
            pltpu.VMEM((heads, TILE, LANES), BF16),
            pltpu.VMEM((heads, TILE), F32),
            pltpu.VMEM((TILE, width), F32),
            pltpu.VMEM((keys, width), F32),
            pltpu.VMEM((keys, width), F32),
        ],
    )(bounds, q, k, v, o, grad, lse, start, cos, sin)


def joined(ref):
    shape = ref.shape
    return ref[...].reshape(shape[0] * shape[2], shape[3])


def once(shape):
    return pl.BlockSpec(shape, lambda i: (0,) * len(shape), pipeline_mode=pl.Buffered(1))


def feed_kernel(count, *refs):
    n_refs, dy_refs, weights = refs[:count], refs[count : 2 * count], refs[2 * count : 2 * count + 3]
    hidden_ref, gate_ref, up_ref, kept_ref, sent_ref, gain_ref, acc = refs[2 * count + 3 :]
    step = pl.program_id(0)
    block = n_refs[0].shape[0]

    @pl.when(step == 0)
    def _():
        acc[...] = jnp.zeros_like(acc)

    gate_w, up_w, down_w = (joined(ref) for ref in weights)
    for i in range(count):
        rows = slice(i * block, (i + 1) * block)
        normed = n_refs[i][...]
        gate = dot(normed, gate_w)
        up = dot(normed, up_w)
        grad = dot(dy_refs[i][...], down_w)
        sig = 1.0 / (1.0 + jnp.exp(-gate))
        silu = gate * sig
        hidden_ref[rows, :] = (silu * up).astype(BF16)
        gate_grad = (grad * up * sig * (1.0 + gate * (1.0 - sig))).astype(BF16)
        up_grad = (grad * silu).astype(BF16)
        gate_ref[rows, :] = gate_grad
        up_ref[rows, :] = up_grad
        acc[rows, :] += dot_nt(gate_grad, gate_w) + dot_nt(up_grad, up_w)

    @pl.when(step == pl.num_programs(0) - 1)
    def _():
        total = 0.0
        for i in range(count):
            values = acc[i * block : (i + 1) * block, :]
            store_block(kept_ref, sent_ref, i, block, values)
            total = total + column_sums(values, n_refs[i][...])
        gain_ref[...] = total


def feed(normed, dy, weights):
    count = len(normed)
    block, depth = normed[0].shape
    rows = count * block
    fsdp, _, columns, units = weights.shape
    tile = min(TILE, units)
    kind = lambda k: pl.BlockSpec((fsdp, 1, columns, tile), lambda i: (0, k, 0, i))
    out = pl.BlockSpec((rows, tile), lambda i: (0, i))
    wide = jax.ShapeDtypeStruct((rows, units), BF16)
    half = once((rows // 2, depth))
    return call(
        functools.partial(feed_kernel, count),
        "feed",
        rows * depth * units * 10,
        depth * units * 6,
        grid=(units // tile,),
        out_shape=[wide, wide, wide] + halves(rows, depth) + [jax.ShapeDtypeStruct((8, depth), F32)],
        in_specs=[once((block, depth))] * (2 * count) + [kind(0), kind(1), kind(2)],
        out_specs=[out, out, out, half, half, once((8, depth))],
        scratch_shapes=[pltpu.VMEM((rows, depth), F32)],
    )(*normed, *dy, weights, weights, weights)


def feed_weights_kernel(count, *refs):
    blocks = refs[: 2 * count]
    gate_ref, up_ref, hidden_ref, out_ref, normed, dy = refs[2 * count :]
    block = blocks[0].shape[0]
    fsdp, _, columns, tile = out_ref.shape

    @pl.when(pl.program_id(0) == 0)
    def _():
        for i in range(count):
            normed[i * block : (i + 1) * block, :] = blocks[i][...]
            dy[i * block : (i + 1) * block, :] = blocks[count + i][...]

    for kind, (left, right) in enumerate(((normed, gate_ref), (normed, up_ref), (dy, hidden_ref))):
        out_ref[:, kind] = dot_tn(left[...], right[...]).astype(BF16).reshape(fsdp, columns, tile)


def feed_weights(normed, dy, gate_grad, up_grad, hidden, fsdp):
    count = len(normed)
    block, depth = normed[0].shape
    rows, units = hidden.shape
    columns = depth // fsdp
    tile = min(TILE, units)
    return call(
        functools.partial(feed_weights_kernel, count),
        "feed_weights",
        rows * depth * units * 6,
        depth * units * 6,
        grid=(units // tile,),
        out_shape=jax.ShapeDtypeStruct((fsdp, 3, columns, units), BF16),
        in_specs=[once((block, depth))] * (2 * count) + [pl.BlockSpec((rows, tile), lambda i: (0, i))] * 3,
        out_specs=pl.BlockSpec((fsdp, 3, columns, tile), lambda i: (0, 0, 0, i)),
        scratch_shapes=[pltpu.VMEM((rows, depth), BF16)] * 2,
    )(*normed, *dy, gate_grad, up_grad, hidden)


def feed_out_kernel(count, hidden_ref, weight_ref, kept_ref, sent_ref):
    weight = joined(weight_ref)
    block = hidden_ref.shape[0] // count
    for i in range(count):
        values = dot_nt(hidden_ref[i * block : (i + 1) * block, :], weight)
        store_block(kept_ref, sent_ref, i, block, values)


def feed_out(hidden, weights, count):
    rows = hidden.shape[0]
    fsdp, _, columns, units = weights.shape
    depth = fsdp * columns
    return call(
        functools.partial(feed_out_kernel, count),
        "feed_out",
        rows * depth * units * 2,
        rows * depth * 2,
        grid=(1,),
        out_shape=halves(rows, depth),
        in_specs=[once((rows, units)), pl.BlockSpec((fsdp, 1, columns, units), lambda i: (0, 2, 0, 0))],
        out_specs=[once((rows // 2, depth))] * 2,
    )(hidden, weights)


def quarter_places():
    place = 2 * lax.axis_index("chip") + lax.axis_index("core")
    return place, place ^ 2, place ^ 1, place ^ 3


def finish_feed_kernel(own_ref, across_ref, came_ref, gate_ref, up_ref, down_ref):
    units = own_ref.shape[2]
    for place, piece in zip(quarter_places(), (own_ref, across_ref, came_ref.at[0], came_ref.at[1])):
        span = pl.ds(pl.multiple_of(place * units, LANES), units)
        gate_ref[:, span] = piece[0].astype(F32)
        up_ref[:, span] = piece[1].astype(F32)
        down_ref[span, :] = jnp.transpose(piece[2].astype(F32))


def finish_feed(own, across, came):
    _, columns, units = own.shape
    wide = jax.ShapeDtypeStruct((columns, 4 * units), F32)
    return call(
        finish_feed_kernel,
        "finish_feed",
        0,
        own.size * 24,
        out_shape=(wide, wide, jax.ShapeDtypeStruct((4 * units, columns), F32)),
        in_specs=[whole()] * 3,
        out_specs=[whole()] * 3,
    )(own, across, came)


def finish_attention_kernel(real, own_ref, across_ref, came_ref, q_ref, k_ref, v_ref, out_ref, buf):
    part = own_ref.shape[1]
    pieces = (own_ref, across_ref, came_ref.at[0], came_ref.at[1])
    for kind, ref in enumerate((q_ref, k_ref, v_ref, out_ref)):
        for place, piece in zip(quarter_places(), pieces):
            buf[pl.ds(pl.multiple_of(place * part, 16), part), :] = piece[kind].astype(F32)
        ref[...] = buf[:real, :] if kind == 3 else jnp.transpose(buf[...])[:, :real]


def finish_attention(own, across, came, real):
    _, part, columns = own.shape
    into = jax.ShapeDtypeStruct((columns, real), F32)
    return call(
        functools.partial(finish_attention_kernel, real),
        "finish_attention",
        0,
        own.size * 24,
        out_shape=(into, into, into, jax.ShapeDtypeStruct((real, columns), F32)),
        in_specs=[whole()] * 3,
        out_specs=[whole()] * 4,
        scratch_shapes=[pltpu.VMEM((4 * part, columns), F32)],
    )(own, across, came)


def normalize_back(values, inverse, gain, grad_rows):
    scaled = grad_rows * gain
    return inverse * scaled - values * inverse**3 * jnp.mean(scaled * values, axis=-1, keepdims=True)


def inverse_rms(values):
    return lax.rsqrt(jnp.mean(values * values, axis=-1, keepdims=True) + EPSILON)


def pull_fsdp(values, step):
    count = lax.axis_size("fsdp")
    return lax.ppermute(values, "fsdp", [(i, (i - step) % count) for i in range(count)])


def gather_gains(gains):
    count = lax.axis_size("fsdp")
    rolled = jnp.concatenate([gains] + [pull_fsdp(gains, step) for step in range(1, count)], axis=1).astype(F32)
    twice = jnp.concatenate([rolled, rolled], axis=1)
    at = (count - lax.axis_index("fsdp")) % count * gains.shape[1]
    return lax.dynamic_slice_in_dim(twice, at, rolled.shape[1], 1)


def gain_totals(gains):
    if lax.axis_size("tp") == 2:
        gains = gains + swap_tp(gains)
    else:
        gains = lax.psum(gains, "tp")
    gains = gains + swap_core(gains)
    gains = gains + swap_chip(gains)
    count = lax.axis_size("fsdp")
    blocks = jnp.stack(jnp.split(gains, count, axis=1))
    return jnp.sum(lax.all_to_all(blocks, "fsdp", 0, 0, tiled=True), axis=0)


def scatter_fsdp(values):
    shape = values.shape
    flat = values.reshape((shape[0] * shape[1],) + shape[2:])
    return lax.psum_scatter(flat, "fsdp", scatter_dimension=0, tiled=True)


def shards(tokens, segment_ids, wq, wk, wv, wo, w_gate, w_up, w_down, gain_attn, gain_ffn, cotangent):
    tokens, cotangent, segment_ids = tokens[0], cotangent[0], segment_ids[0]
    fsdp = lax.axis_size("fsdp")
    chip, core = lax.axis_index("chip"), lax.axis_index("core")
    place = 2 * chip + core
    rows = 4 * segment_ids.shape[0]
    real_width = wq.shape[1]
    part = -(-real_width // (4 * HEAD_DIM)) * HEAD_DIM
    heads = part // HEAD_DIM
    width = -(-part // LANES) * LANES
    keys = -(-rows // TILE) * TILE
    both_links = lax.axis_size("tp") == 2

    pad = ((0, 0), (0, 4 * part - real_width))
    own_piece = cut_attention(*[jnp.pad(w, pad) for w in (wq, wk, wv)], jnp.pad(wo, pad[::-1]))
    feed_piece = jnp.stack([take_quarter(w_gate, place, 1), take_quarter(w_up, place, 1), jnp.transpose(take_quarter(w_down, place, 0))])

    position = after(jnp.arange(keys, dtype=jnp.int32), own_piece).astype(F32)
    pair_index = (jnp.arange(LANES, dtype=jnp.int32) % (HEAD_DIM // 2)).astype(F32)
    angles = position[:, None] * (10000.0 ** (-pair_index * 2.0 / HEAD_DIM))[None, :]

    def normed(values):
        values = values.astype(F32)
        return (values * inverse_rms(values) * gain_one).astype(BF16)

    if both_links:
        first = lambda values: [values, swap_tp(values), swap_chip(values)]
        second = lambda blocks: widen_core(blocks) + far_block(*blocks)[3:]
        third = lambda blocks: blocks[:3] + blocks[6:] + blocks[3:6] + [swap_core(blocks[6])]
    else:
        first, second, third = widen_planes, widen_core, lambda blocks: blocks
    ring = [own_piece]
    block, own, gains, ids_other, cos, sin = together(
        pull_fsdp(ring[0], 1),
        first(tokens),
        gather_gains(jnp.stack([gain_attn, gain_ffn])),
        swap_core(segment_ids),
        jnp.cos(angles),
        jnp.sin(angles),
    )
    ring.append(block)
    gain_one, gain_two = gains
    ids_chip = jnp.concatenate(in_order(segment_ids, ids_other, core == 0))
    block, own, ids_across = together(pull_fsdp(ring[-1], 1), second(own), swap_chip(ids_chip))
    ring.append(block)
    feed_weight = lax.all_gather(after(feed_piece, block), "fsdp", axis=0, tiled=False)
    ids = jnp.concatenate(in_order(ids_chip, ids_across, chip == 0))
    start = jnp.sum((ids[None, :] < ids[:, None]).astype(jnp.int32), axis=1)
    dy = cotangent
    for step in range(2, fsdp - 1):
        if step == 2:
            early = [normed(values) for values in own[:6]]
            block, own, early, dy = together(pull_fsdp(ring[-1], 1), third(own), early, first(after(cotangent, block)))
        else:
            block = pull_fsdp(ring[-1], 1)
        ring.append(block)
    weights = place_weights(ring, width)
    tiles = -(-rows // TILE)
    ends = [-(-min((t + 1) * TILE, rows) // TILE) for t in range(tiles)]
    bounds = jnp.stack([start[::TILE] // TILE, jnp.array(ends, jnp.int32)])
    start = jnp.pad(start, (0, tiles * TILE - rows), constant_values=2 * keys)[None]

    if both_links:
        blocks = early[:3] + [normed(own[3])] + early[3:] + [normed(own[7])]
    else:
        blocks = early
    count = len(blocks)
    inputs = tokens.astype(F32)
    inv_one = inverse_rms(inputs)
    q, k, v = project(blocks, weights, cos, sin, keys)
    dy = second(after(dy, q))
    attended, lse = attend(bounds, q, k, v, start, heads)
    attended, dy = together(attended, dy)
    dy = third(dy)
    leaving = narrow_first(*out_project(attended, weights, count), feed_weight)
    attention_rows, dy = narrow_second(leaving, lambda rows, dy=dy: dy)
    residual = inputs + attention_rows

    inv_two = inverse_rms(residual)
    normed_two = widen((residual * inv_two * gain_two).astype(BF16))
    hidden, gate_grad, up_grad, kept, sent, gain_two_sums = feed(normed_two, dy, feed_weight)
    normed_two_grad, feed_grads = narrow(
        kept, sent, lambda leaving: feed_weights(normed_two, dy, after(gate_grad, leaving), up_grad, hidden, fsdp)
    )
    feed_sums = scatter_fsdp(feed_grads)
    resid_grad = cotangent.astype(F32) + normalize_back(residual, inv_two, gain_two, normed_two_grad)
    resid_low = resid_grad.astype(BF16)

    out_kept, out_sent = feed_out(after(hidden, resid_low), feed_weight, count)
    grad_blocks = widen_core(widen_planes(resid_low, out_sent))
    out_grad, out_grads = out_back(attended, weights, grad_blocks, fsdp, part)
    leaving = narrow_first(out_kept, out_sent, out_grad)
    dq, dk, dv = attend_back(bounds, q, k, v, attended, after(out_grad, leaving), lse, start, cos, sin, heads)
    layer_out = residual + narrow_second(leaving, lambda rows: dq)[0]
    project_grads = project_weights(dq, dk, after(dv, layer_out), out_grads, blocks)
    sums = scatter_fsdp(project_grads)
    kept, sent, gain_one_sums = project_back(after(dq, project_grads), dk, dv, weights, blocks)
    gate_all, up_all, down_all = finish_feed(*all_quarters(after(feed_sums, dq)))
    gain_sums = jnp.stack([jnp.sum(gain_one_sums, axis=0) / gain_one, jnp.sum(gain_two_sums, axis=0) / gain_two])
    normed_grad, gain_own = narrow(kept, sent, lambda leaving: gain_totals(after(gain_sums, leaving)))
    grad_input = resid_grad + normalize_back(inputs, inv_one, gain_one, normed_grad)

    q_all, k_all, v_all, out_all = finish_attention(*all_quarters(sums), real_width)
    return (
        layer_out.astype(BF16)[None],
        grad_input[None],
        q_all,
        k_all,
        v_all,
        out_all,
        gate_all,
        up_all,
        down_all,
        gain_own[0],
        gain_own[1],
    )


def solution(mesh):
    devices = mesh.devices.reshape(mesh.shape["fsdp"], mesh.shape["ctx"] // 2, 2, mesh.shape["tp"])
    split = jax.sharding.Mesh(devices, ("fsdp", "chip", "core", "tp"))
    rows = P("fsdp", ("chip", "core", "tp"), None)
    into, outof, gain = P("fsdp", "tp"), P("tp", "fsdp"), P("fsdp")
    return jax.shard_map(
        shards,
        mesh=split,
        in_specs=(rows, P("fsdp", ("chip", "core")), into, into, into, outof, into, into, outof, gain, gain, rows),
        out_specs=(rows, rows, into, into, into, outof, into, into, outof, gain, gain),
        check_vma=False,
    )
```

time: 654 us -> 548 us (0.84)
  waiting for transfers between devices: 272 us -> 166 us
  starting transfers between devices: 105 us -> 83.9 us
  other arithmetic: 60.5 us -> 72.5 us
  blocking collectives: 0 us -> 7.81 us
    ppermute x11 -> x17, waiting for transfers between devices: 91.4 us -> 39.2 us  [swap_tp(): return lax.ppermute(values, 'tp', [(0, 1), (1, 0)])]
    ppermute x6, waiting for transfers between devices: 52.4 us -> 1.41 us  [pull_fsdp(): lax.ppermute(values, 'fsdp', [(i, (i - step) % count) for i in range(coun...]
    all_to_all x5 -> x0, starting transfers between devices: 20.5 us -> none  [the longest x4 16.2 us: sum_over_chips_and_fsdp(): lax.all_to_all(mine, 'fsdp', 0, 0, tiled=True).astype(F32)]
    another operation x3 -> x13, other arithmetic: 2.07 us -> 18.6 us  [the longest x2 2.05 us: attention_piece(): return jnp.stack(pieces + [take_quarter(wide[3], index, 0)])]
    all_to_all x5 -> x0, waiting for transfers between devices: 14 us -> none  [the longest x4 12.6 us: sum_over_chips_and_fsdp(): lax.all_to_all(mine, 'fsdp', 0, 0, tiled=True).astype(F32)]
    convert_element_type x12 -> x6, other arithmetic: 18.7 us -> 5.99 us  [the longest x4 5.77 us: narrow_first(): block(3, cut, rows).astype(BF16)]
    ppermute x19 -> x24, starting transfers between devices: 28.1 us -> 40.4 us  [swap_core(): return lax.ppermute(values, 'core', [(0, 1), (1, 0)])]
    ppermute x10 -> x20, starting transfers between devices: 28.1 us -> 18.9 us  [swap_chip(): return lax.ppermute(values, 'chip', [(0, 1), (1, 0)])]
  transfers between devices with their start and end apart: 56 -> 70, of which waited for: 26 -> 26; matrix products, arithmetic and copies ran while one was open for 12% -> 12% of each run, Pallas kernels for 19% -> 24%
where the time goes in v5:
time: 548 us; the launch traced here: 542 us
  Pallas kernels  181 us (33%)
  waiting for transfers between devices  166 us (30%)
  starting transfers between devices  83.9 us (15%)
  other arithmetic  72.5 us (13%)
  local copies, waits for them, and re-layouts  16.7 us (3%)
  between operations  14.6 us (3%)
  blocking collectives  7.81 us (1%)
    ppermute x20, waiting for transfers between devices, swap_chip(): return lax.ppermute(values, 'chip', [(0, 1), (1, 0)])  106 us
    ppermute x24, starting transfers between devices, swap_core(): return lax.ppermute(values, 'core', [(0, 1), (1, 0)])  40.4 us
    ppermute x17, waiting for transfers between devices, swap_tp(): return lax.ppermute(values, 'tp', [(0, 1), (1, 0)])  39.2 us
    pallas_call x1, Pallas kernels, feed(): call(functools.partial(feed_kernel, count), 'feed', rows * depth * units...  34.9 us
    pallas_call x1, Pallas kernels, attend_back(): call(functools.partial(backward_kernel, rows), 'attend_back', rows * rows...  31.8 us
    pallas_call x1, Pallas kernels, feed_weights(): call(functools.partial(feed_weights_kernel, count), 'feed_weights', rows...  20.4 us
    ppermute x24, waiting for transfers between devices, swap_core(): return lax.ppermute(values, 'core', [(0, 1), (1, 0)])  19 us
    ppermute x20, starting transfers between devices, swap_chip(): return lax.ppermute(values, 'chip', [(0, 1), (1, 0)])  18.9 us
  transfers between devices with their start and end apart: 70, of which 26 were waited for; matrix products, arithmetic and copies ran while one was open for 12% of the time, Pallas kernels for 24%

profile of v5, /device:TPU:1, one launch (start us, length us, event | category | flops | bytes accessed | tf_op | source)
XLA Modules:
  0.0 542.2 jit_solution(11375057208562272364)
XLA Ops:
  18.8 6.2 %multiply_sine_fusion = (f32[2304,128]{1,0:T(8,128)}, f32[2304,128]{1,0:T(8,128)}) fusion(f32[128]{0:T(128)S(1)} %fusion.33, f32[2304]{0:T(1024)S(1)} %convert_element_type.326), kind=kLoop, calls=%fused_computation.22 | loop fusion | flops 294912 | bytes 2369024 | tf_op jit(solution)/shard_map/sin | solution.py:783
  35.9 7.2 %collective-permute-done.1 = bf16[272,1536]{1,0:T(8,128)(2,1)S(1)} collective-permute-done((bf16[272,1536]{1,0:T(8,128)(2,1)S(1)}, bf16[272,1536]{1,0:T(8,128)(2,1)S(1)}, u32[]{:S(2)}, u32[]{:S(2)}) %collective-permute-start.1) | collective-permute-done | bytes 835616 | tf_op jit(solution)/shard_map/ppermute | solution.py:41
  55.9 10.3 %collective-permute-done.12 = bf16[144,1536]{1,0:T(8,128)(2,1)S(1)} collective-permute-done((bf16[144,1536]{1,0:T(8,128)(2,1)S(1)}, bf16[144,1536]{1,0:T(8,128)(2,1)S(1)}, u32[]{:S(2)}, u32[]{:S(2)}) %collective-permute-start.12) | collective-permute-done | bytes 442400 | tf_op jit(solution)/shard_map/ppermute | solution.py:33
  96.5 11.8 %project.1 = (bf16[2176,256]{1,0:T(8,128)(2,1)}, bf16[2304,256]{1,0:T(8,128)(2,1)}, bf16[2304,256]{1,0:T(8,128)(2,1)}) custom-call(bf16[272,1536]{1,0:T(8,128)(2,1)} %get-tuple-element.132.refs_0_, bf16[272,1536]{1,0:T(8,128)(2,1)} %get-tuple-element.133.refs_1_, bf16[272,1536]{1,0:T(8,128)(2,1)} %get-tuple-element.134.refs_2_, ...), custom_call_target="tpu_custom_call" | custom-call | flops 5133828096 | bytes 6684672 | tf_op jit(solution)/shard_map/project/pallas_call | solution.py:180
  118.3 16.9 %attend.1 = (bf16[2176,256]{1,0:T(8,128)(2,1)}, f32[3,2304]{1,0:T(4,128)}) custom-call(s32[2,9]{1,0:T(2,128)} %pad_add_fusion.2.bounds, bf16[2176,256]{1,0:T(8,128)(2,1)} %get-tuple-element.143.q_ref, bf16[2304,256]{1,0:T(8,128)(2,1)} %get-tuple-element.144.k_ref, bf16[2304,256]{1,0:T(8,128)(2,1)} %get-tuple-element.145.v_ref, ...), custom_call_target="tpu_custom_call" | custom-call | flops 1818230784 | bytes 4718592 | tf_op jit(solution)/shard_map/attend/pallas_call | solution.py:424
  137.1 6.4 %out_project.1 = (bf16[1088,1536]{1,0:T(8,128)(2,1)}, bf16[1088,1536]{1,0:T(8,128)(2,1)}) custom-call(bf16[2176,256]{1,0:T(8,128)(2,1)} %get-tuple-element.153.o_ref, bf16[4,256,1536]{2,1,0:T(8,128)(2,1)} %place_weights.1.refs_8_.weight_ref), custom_call_target="tpu_custom_call" | custom-call | flops 1711276032 | bytes 6684672 | tf_op jit(solution)/shard_map/out_project/pallas_call | solution.py:261
  156.6 7.6 %collective-permute-done.24 = bf16[128,1536]{1,0:T(8,128)(2,1)S(1)} collective-permute-done((bf16[128,1536]{1,0:T(8,128)(2,1)S(1)}, bf16[128,1536]{1,0:T(8,128)(2,1)S(1)}, u32[]{:S(2)}, u32[]{:S(2)}) %collective-permute-start.24) | collective-permute-done | bytes 393248 | tf_op jit(solution)/shard_map/ppermute | solution.py:33
  168.9 16.9 %collective-permute-done.26 = bf16[272,1536]{1,0:T(8,128)(2,1)S(1)} collective-permute-done((bf16[272,1536]{1,0:T(8,128)(2,1)S(1)}, bf16[272,1536]{1,0:T(8,128)(2,1)S(1)}, u32[]{:S(2)}, u32[]{:S(2)}) %collective-permute-start.26) | collective-permute-done | bytes 835616 | tf_op jit(solution)/shard_map/ppermute | solution.py:41
  191.0 14.7 %collective-permute-done.30.refs_2_ = bf16[272,1536]{1,0:T(8,128)(2,1)S(1)} collective-permute-done((bf16[272,1536]{1,0:T(8,128)(2,1)S(1)}, bf16[272,1536]{1,0:T(8,128)(2,1)S(1)}, u32[]{:S(2)}, u32[]{:S(2)}) %collective-permute-start.30) | collective-permute-done | bytes 835616 | tf_op jit(solution)/shard_map/ppermute | solution.py:33
  223.0 34.9 %feed.1 = (bf16[2176,512]{1,0:T(8,128)(2,1)}, bf16[2176,512]{1,0:T(8,128)(2,1)}, bf16[2176,512]{1,0:T(8,128)(2,1)}, bf16[1088,1536]{1,0:T(8,128)(2,1)}, bf16[1088,1536]{1,0:T(8,128)(2,1)}, /*index=5*/f32[8,1536]{1,0:T(8,128)}) custom-call(bf16[272,1536]{1,0:T(8,128)(2,1)} %copy-done.15, bf16[272,1536]{1,0:T(8,128)(2,1)} %copy-done.17, ...), custom_call_target="tpu_custom_call" | custom-call | flops 17112760320 | bytes 4718592 | tf_op jit(solution)/shard_map/feed/pallas_call | solution.py:581
  268.7 7.7 %collective-permute-done.38 = bf16[128,1536]{1,0:T(8,128)(2,1)S(1)} collective-permute-done((bf16[128,1536]{1,0:T(8,128)(2,1)S(1)}, bf16[128,1536]{1,0:T(8,128)(2,1)S(1)}, u32[]{:S(2)}, u32[]{:S(2)}) %collective-permute-start.38) | collective-permute-done | bytes 393248 | tf_op jit(solution)/shard_map/ppermute | solution.py:33
  284.6 20.4 %feed_weights.1 = bf16[4,3,384,512]{3,2,1,0:T(8,128)(2,1)} custom-call(bf16[272,1536]{1,0:T(8,128)(2,1)} %copy-done.15, bf16[272,1536]{1,0:T(8,128)(2,1)} %copy-done.17, bf16[272,1536]{1,0:T(8,128)(2,1)} %copy-done.19, bf16[272,1536]{1,0:T(8,128)(2,1)} %copy-done.21, bf16[272,1536]{1,0:T(8,128)(2,1)} %copy-done.27, bf16[272,1536]{1,0:T(8,128)(2,1)} %copy-done.29, ...), custom_call_target="tpu_custom_call" | custom-call | flops 10267656192 | bytes 4718592 | tf_op jit(solution)/shard_map/feed_weights/pallas_call | solution.py:616
  311.3 7.4 %feed_out.1 = (bf16[1088,1536]{1,0:T(8,128)(2,1)}, bf16[1088,1536]{1,0:T(8,128)(2,1)}) custom-call(bf16[2176,512]{1,0:T(8,128)(2,1)} %get-tuple-element.184.refs_18_.hidden_ref, bf16[4,3,384,512]{3,2,1,0:T(8,128)(2,1)} %bitcast.58), custom_call_target="tpu_custom_call" | custom-call | flops 3422552064 | bytes 6684672 | tf_op jit(solution)/shard_map/feed_out/pallas_call | solution.py:641
  322.3 19.9 %collective-permute-done.46.refs_2_ = bf16[272,1536]{1,0:T(8,128)(2,1)S(1)} collective-permute-done((bf16[272,1536]{1,0:T(8,128)(2,1)S(1)}, bf16[272,1536]{1,0:T(8,128)(2,1)S(1)}, u32[]{:S(2)}, u32[]{:S(2)}) %collective-permute-start.46) | collective-permute-done | bytes 835616 | tf_op jit(solution)/shard_map/ppermute | solution.py:33
  345.2 7.2 %collective-permute-done.47 = bf16[128,1536]{1,0:T(8,128)(2,1)S(1)} collective-permute-done((bf16[128,1536]{1,0:T(8,128)(2,1)S(1)}, bf16[128,1536]{1,0:T(8,128)(2,1)S(1)}, u32[]{:S(2)}, u32[]{:S(2)}) %collective-permute-start.47) | collective-permute-done | bytes 393248 | tf_op jit(solution)/shard_map/ppermute | solution.py:41
  364.0 9.1 %out_back.1 = (bf16[2176,256]{1,0:T(8,128)(2,1)}, bf16[4,1,192,384]{3,2,1,0:T(8,128)(2,1)}) custom-call(bf16[2176,256]{1,0:T(8,128)(2,1)} %get-tuple-element.153.o_ref, bf16[4,256,1536]{2,1,0:T(8,128)(2,1)} %place_weights.1.refs_8_.weight_ref, bf16[272,1536]{1,0:T(8,128)(2,1)} %get-tuple-element.225.refs_0_, bf16[272,1536]{1,0:T(8,128)(2,1)} %copy-done.18, ...), custom_call_target="tpu_custom_call" | custom-call | flops 3422552064 | bytes 6684672 | tf_op jit(solution)/shard_map/out_back/pallas_call | solution.py:288
  377.8 31.8 %attend_back.1 = (bf16[2176,256]{1,0:T(8,128)(2,1)}, bf16[2304,256]{1,0:T(8,128)(2,1)}, bf16[2304,256]{1,0:T(8,128)(2,1)}) custom-call(s32[2,9]{1,0:T(2,128)} %pad_add_fusion.2.bounds, bf16[2176,256]{1,0:T(8,128)(2,1)} %get-tuple-element.143.q_ref, bf16[2304,256]{1,0:T(8,128)(2,1)} %get-tuple-element.144.k_ref, bf16[2304,256]{1,0:T(8,128)(2,1)} %get-tuple-element.145.v_ref, ...), custom_call_target="tpu_custom_call" | custom-call | flops 4545576960 | bytes 9437184 | tf_op jit(solution)/shard_map/attend_back/pallas_call | solution.py:507
  412.9 12.4 %project_weights.1 = bf16[4,4,192,384]{3,2,1,0:T(8,128)(2,1)} custom-call(bf16[2176,256]{1,0:T(8,128)(2,1)} %get-tuple-element.201.dq_ref, bf16[2304,256]{1,0:T(8,128)(2,1)} %get-tuple-element.197.dk_ref, bf16[2304,256]{1,0:T(8,128)(2,1)} %get-tuple-element.199.dv_ref, bf16[4,1,192,384]{3,2,1,0:T(8,128)(2,1)} %get-tuple-element.200.done_ref, ...), custom_call_target="tpu_custom_call" | custom-call | flops 5133828096 | bytes 6684672 | tf_op jit(solution)/shard_map/project_weights/pallas_call | solution.py:320
  425.3 11.9 %project_back.1 = (bf16[1088,1536]{1,0:T(8,128)(2,1)}, bf16[1088,1536]{1,0:T(8,128)(2,1)}, f32[8,1536]{1,0:T(8,128)}) custom-call(bf16[2176,256]{1,0:T(8,128)(2,1)} %get-tuple-element.201.dq_ref, bf16[2304,256]{1,0:T(8,128)(2,1)} %get-tuple-element.197.dk_ref, bf16[2304,256]{1,0:T(8,128)(2,1)} %get-tuple-element.199.dv_ref, ...), custom_call_target="tpu_custom_call" | custom-call | flops 5133828096 | bytes 13369344 | tf_op jit(solution)/shard_map/project_back/pallas_call | solution.py:353
  450.0 6.6 %collective-permute-done.56 = bf16[128,1536]{1,0:T(8,128)(2,1)S(1)} collective-permute-done((bf16[128,1536]{1,0:T(8,128)(2,1)S(1)}, bf16[128,1536]{1,0:T(8,128)(2,1)S(1)}, u32[]{:S(2)}, u32[]{:S(2)}) %collective-permute-start.56) | collective-permute-done | bytes 393248 | tf_op jit(solution)/shard_map/ppermute | solution.py:33
  465.0 19.6 %collective-permute-done.65.across_ref = bf16[3,384,512]{2,1,0:T(8,128)(2,1)S(1)} collective-permute-done((bf16[3,384,512]{2,1,0:T(8,128)(2,1)}, bf16[3,384,512]{2,1,0:T(8,128)(2,1)S(1)}, u32[]{:S(2)}, u32[]{:S(2)}) %collective-permute-start.65) | collective-permute-done | bytes 1179680 | tf_op jit(solution)/shard_map/ppermute | solution.py:33
  495.8 6.9 %collective-permute-done.62 = f32[2,1536]{1,0:T(2,128)S(1)} collective-permute-done((f32[2,1536]{1,0:T(2,128)S(1)}, f32[2,1536]{1,0:T(2,128)S(1)}, u32[]{:S(2)}, u32[]{:S(2)}) %collective-permute-start.62) | collective-permute-done | bytes 12320 | tf_op jit(solution)/shard_map/ppermute | solution.py:33
  503.9 7.8 %all_to_all.5 = f32[4,2,384]{2,1,0:T(2,128)S(1)} all-to-all(f32[4,2,384]{2,1,0:T(2,128)S(1)} %pad_maximum_fusion.14), channel_id=1, replica_groups=mesh['fsdp'=4,'chip'=2,'core'=2,'tp'=2] {'fsdp'}, dimensions={0} | all-to-all | bytes 24576 | tf_op jit(solution)/shard_map/all_to_all | solution.py:736
  528.6 6.8 %finish_feed.1 = (f32[384,2048]{1,0:T(8,128)}, f32[384,2048]{1,0:T(8,128)}, f32[2048,384]{1,0:T(8,128)}) custom-call(bf16[3,384,512]{2,1,0:T(8,128)(2,1)} %reduce-scatter.5.cloned.1.call-done.own_ref, bf16[3,384,512]{2,1,0:T(8,128)(2,1)} %copy-done.6, bf16[2,3,384,512]{3,2,1,0:T(8,128)(2,1)} %collective-permute-done.66.came_ref), custom_call_target="tpu_custom_call" | custom-call | bytes 14155776 | tf_op jit(solution)/shard_map/finish_feed/pallas_call | solution.py:670
  (308 shorter events, 218.9 us)
Async XLA Ops:
  7.2 157.0 %all-gather.3.cloned.1.call-start = ((), (), s32[]{:S(2)}) async-start(), calls=%async_computation.5 | async-start | bytes 5898240 | tf_op jit(solution)/shard_map/all_gather | solution.py:790
  8.8 20.0 %collective-permute-start.5 = (bf16[2,384]{1,0:T(2,128)(2,1)S(1)}, bf16[2,384]{1,0:T(2,128)(2,1)S(1)}, u32[]{:S(2)}, u32[]{:S(2)}) collective-permute-start(bf16[2,384]{1,0:T(2,128)(2,1)S(1)} %get-tuple-element.230), channel_id=1, source_target_pairs={{0,8},{8,16},{16,24},{24,0},{1,9},{9,17},{17,25},{25,1},{2,10},{10... | collective-permute-start | bytes 4616 | tf_op jit(solution)/shard_map/ppermute | solution.py:716
  17.5 18.4 %collective-permute-start.2 = (bf16[272,1536]{1,0:T(8,128)(2,1)S(1)}, bf16[272,1536]{1,0:T(8,128)(2,1)}, u32[]{:S(2)}, u32[]{:S(2)}) collective-permute-start(bf16[272,1536]{1,0:T(8,128)(2,1)S(1)} %bitcast.38), channel_id=1, source_target_pairs={{0,4},{4,0},{1,5},{5,1},{2,6},{6,2},{3,7},{7,3},{8,12},{12,8},{9,1... | collective-permute-start | bytes 2506760 | tf_op jit(solution)/shard_map/ppermute | solution.py:33
  49.2 19.9 %collective-permute-start.10 = (bf16[272,1536]{1,0:T(8,128)(2,1)}, bf16[272,1536]{1,0:T(8,128)(2,1)S(1)}, u32[]{:S(2)}, u32[]{:S(2)}) collective-permute-start(bf16[272,1536]{1,0:T(8,128)(2,1)} %collective-permute-done.2), channel_id=1, source_target_pairs={{0,2},{2,0},{1,3},{3,1},{4,6},{6,4},{5,7},{7,5},{8,10},{10,8},{9,1... | collective-permute-start | bytes 2506760 | tf_op jit(solution)/shard_map/ppermute | solution.py:37
  72.6 385.3 %reduce-scatter.5.cloned.1.call-start = ((), (), s32[]{:S(2)}) async-start(), calls=%async_computation.4 | async-start | bytes 5898240 | tf_op jit(solution)/shard_map/reduce_scatter | solution.py:742
  108.4 28.7 %collective-permute-start.18 = (bf16[272,1536]{1,0:T(8,128)(2,1)S(1)}, bf16[272,1536]{1,0:T(8,128)(2,1)}, u32[]{:S(2)}, u32[]{:S(2)}) collective-permute-start(bf16[272,1536]{1,0:T(8,128)(2,1)S(1)} %bitcast.53), channel_id=1, source_target_pairs={{0,2},{2,0},{1,3},{3,1},{4,6},{6,4},{5,7},{7,5},{8,10},{10,8},{9,1... | collective-permute-start | bytes 2506760 | tf_op jit(solution)/shard_map/ppermute | solution.py:37
  112.3 24.8 %collective-permute-start.19 = (bf16[272,1536]{1,0:T(8,128)(2,1)}, bf16[272,1536]{1,0:T(8,128)(2,1)}, u32[]{:S(2)}, u32[]{:S(2)}) collective-permute-start(bf16[272,1536]{1,0:T(8,128)(2,1)} %collective-permute-done.16.refs_9_), channel_id=1, source_target_pairs={{0,2},{2,0},{1,3},{3,1},{4,6},{6,4},{5,7},{7,5},{8,10},{10,8},{9,1... | collective-permute-start | bytes 2506760 | tf_op jit(solution)/shard_map/ppermute | solution.py:37
  112.4 24.8 %collective-permute-start.20 = (bf16[272,1536]{1,0:T(8,128)(2,1)}, bf16[272,1536]{1,0:T(8,128)(2,1)}, u32[]{:S(2)}, u32[]{:S(2)}) collective-permute-start(bf16[272,1536]{1,0:T(8,128)(2,1)} %collective-permute-done.17.refs_10_), channel_id=1, source_target_pairs={{0,2},{2,0},{1,3},{3,1},{4,6},{6,4},{5,7},{7,5},{8,10},{10,8},{9,1... | collective-permute-start | bytes 2506760 | tf_op jit(solution)/shard_map/ppermute | solution.py:37
  117.0 18.3 %collective-permute-start.21 = (bf16[128,1536]{1,0:T(8,128)(2,1)S(1)}, bf16[128,1536]{1,0:T(8,128)(2,1)S(1)}, u32[]{:S(2)}, u32[]{:S(2)}) collective-permute-start(bf16[128,1536]{1,0:T(8,128)(2,1)S(1)} %slice.204), channel_id=1, source_target_pairs={{0,1},{1,0},{2,3},{3,2},{4,5},{5,4},{6,7},{7,6},{8,9},{9,8},{10,11... | collective-permute-start | bytes 1179656 | tf_op jit(solution)/shard_map/ppermute | solution.py:41
  117.1 18.9 %collective-permute-start.22 = (bf16[144,1536]{1,0:T(8,128)(2,1)S(1)}, bf16[144,1536]{1,0:T(8,128)(2,1)S(1)}, u32[]{:S(2)}, u32[]{:S(2)}) collective-permute-start(bf16[144,1536]{1,0:T(8,128)(2,1)S(1)} %slice.205), channel_id=1, source_target_pairs={{0,4},{4,0},{1,5},{5,1},{2,6},{6,2},{3,7},{7,3},{8,12},{12,8},{9,1... | collective-permute-start | bytes 1327112 | tf_op jit(solution)/shard_map/ppermute | solution.py:33
  167.2 18.6 %collective-permute-start.26 = (bf16[272,1536]{1,0:T(8,128)(2,1)S(1)}, bf16[272,1536]{1,0:T(8,128)(2,1)S(1)}, u32[]{:S(2)}, u32[]{:S(2)}) collective-permute-start(bf16[272,1536]{1,0:T(8,128)(2,1)S(1)} %pad_maximum_fusion.5), channel_id=1, source_target_pairs={{0,1},{1,0},{2,3},{3,2},{4,5},{5,4},{6,7},{7,6},{8,9},{9,8},{10,11... | collective-permute-start | bytes 2506760 | tf_op jit(solution)/shard_map/ppermute | solution.py:41
  167.5 18.4 %collective-permute-start.27 = (bf16[272,1536]{1,0:T(8,128)(2,1)S(1)}, bf16[272,1536]{1,0:T(8,128)(2,1)S(1)}, u32[]{:S(2)}, u32[]{:S(2)}) collective-permute-start(bf16[272,1536]{1,0:T(8,128)(2,1)S(1)} %pad_maximum_fusion.6), channel_id=1, source_target_pairs={{0,4},{4,0},{1,5},{5,1},{2,6},{6,2},{3,7},{7,3},{8,12},{12,8},{9,1... | collective-permute-start | bytes 2506760 | tf_op jit(solution)/shard_map/ppermute | solution.py:33
  281.1 23.9 %collective-permute-start.39 = (bf16[272,1536]{1,0:T(8,128)(2,1)}, bf16[272,1536]{1,0:T(8,128)(2,1)S(1)}, u32[]{:S(2)}, u32[]{:S(2)}) collective-permute-start(bf16[272,1536]{1,0:T(8,128)(2,1)} %pad_maximum_fusion.7), channel_id=1, source_target_pairs={{0,1},{1,0},{2,3},{3,2},{4,5},{5,4},{6,7},{7,6},{8,9},{9,8},{10,11... | collective-permute-start | bytes 2506760 | tf_op jit(solution)/shard_map/ppermute | solution.py:41
  283.4 21.5 %collective-permute-start.41 = (bf16[272,1536]{1,0:T(8,128)(2,1)}, bf16[272,1536]{1,0:T(8,128)(2,1)}, u32[]{:S(2)}, u32[]{:S(2)}) collective-permute-start(bf16[272,1536]{1,0:T(8,128)(2,1)} %pad_maximum_fusion.8), channel_id=1, source_target_pairs={{0,4},{4,0},{1,5},{5,1},{2,6},{6,2},{3,7},{7,3},{8,12},{12,8},{9,1... | collective-permute-start | bytes 2506760 | tf_op jit(solution)/shard_map/ppermute | solution.py:33
  318.7 36.5 %collective-permute-start.42 = (bf16[1088,1536]{1,0:T(8,128)(2,1)}, bf16[1088,1536]{1,0:T(8,128)(2,1)}, u32[]{:S(2)}, u32[]{:S(2)}) collective-permute-start(bf16[1088,1536]{1,0:T(8,128)(2,1)} %get-tuple-element.186), channel_id=1, source_target_pairs={{0,2},{2,0},{1,3},{3,1},{4,6},{6,4},{5,7},{7,5},{8,10},{10,8},{9,1... | collective-permute-start | bytes 10027016 | tf_op jit(solution)/shard_map/ppermute | solution.py:37
  320.8 182.0 %reduce-scatter.3.cloned.1.call-start = ((), (), s32[]{:S(2)}) async-start(), calls=%async_computation.3 | async-start | bytes 2949120 | tf_op jit(solution)/shard_map/reduce_scatter | solution.py:742
  321.9 20.3 %collective-permute-start.46 = (bf16[272,1536]{1,0:T(8,128)(2,1)S(1)}, bf16[272,1536]{1,0:T(8,128)(2,1)S(1)}, u32[]{:S(2)}, u32[]{:S(2)}) collective-permute-start(bf16[272,1536]{1,0:T(8,128)(2,1)S(1)} %copy-done.13), channel_id=1, source_target_pairs={{0,4},{4,0},{1,5},{5,1},{2,6},{6,2},{3,7},{7,3},{8,12},{12,8},{9,1... | collective-permute-start | bytes 2506760 | tf_op jit(solution)/shard_map/ppermute | solution.py:33
  321.9 20.3 %collective-permute-start.45 = (bf16[272,1536]{1,0:T(8,128)(2,1)S(1)}, bf16[272,1536]{1,0:T(8,128)(2,1)S(1)}, u32[]{:S(2)}, u32[]{:S(2)}) collective-permute-start(bf16[272,1536]{1,0:T(8,128)(2,1)S(1)} %copy-done.13), channel_id=1, source_target_pairs={{0,1},{1,0},{2,3},{3,2},{4,5},{5,4},{6,7},{7,6},{8,9},{9,8},{10,11... | collective-permute-start | bytes 2506760 | tf_op jit(solution)/shard_map/ppermute | solution.py:41
  376.3 33.3 %collective-permute-start.53 = (bf16[272,1536]{1,0:T(8,128)(2,1)S(1)}, bf16[272,1536]{1,0:T(8,128)(2,1)}, u32[]{:S(2)}, u32[]{:S(2)}) collective-permute-start(bf16[272,1536]{1,0:T(8,128)(2,1)S(1)} %pad_maximum_fusion.9), channel_id=1, source_target_pairs={{0,1},{1,0},{2,3},{3,2},{4,5},{5,4},{6,7},{7,6},{8,9},{9,8},{10,11... | collective-permute-start | bytes 2506760 | tf_op jit(solution)/shard_map/ppermute | solution.py:41
  377.3 32.3 %collective-permute-start.54 = (bf16[272,1536]{1,0:T(8,128)(2,1)}, bf16[272,1536]{1,0:T(8,128)(2,1)}, u32[]{:S(2)}, u32[]{:S(2)}) collective-permute-start(bf16[272,1536]{1,0:T(8,128)(2,1)} %pad_maximum_fusion.10), channel_id=1, source_target_pairs={{0,4},{4,0},{1,5},{5,1},{2,6},{6,2},{3,7},{7,3},{8,12},{12,8},{9,1... | collective-permute-start | bytes 2506760 | tf_op jit(solution)/shard_map/ppermute | solution.py:33
  457.9 26.8 %collective-permute-start.65 = (bf16[3,384,512]{2,1,0:T(8,128)(2,1)}, bf16[3,384,512]{2,1,0:T(8,128)(2,1)S(1)}, u32[]{:S(2)}, u32[]{:S(2)}) collective-permute-start(bf16[3,384,512]{2,1,0:T(8,128)(2,1)} %reduce-scatter.5.cloned.1.call-done.own_ref), channel_id=1, source_target_pairs={{0,4},{4,0},{1,5},{5,1},{2,6},{6,2},{3,7},{7,3},{8,12},{12,8},{9,1... | collective-permute-start | bytes 3538952 | tf_op jit(solution)/shard_map/ppermute | solution.py:33
  462.4 49.4 %collective-permute-start.57 = (bf16[272,1536]{1,0:T(8,128)(2,1)}, bf16[272,1536]{1,0:T(8,128)(2,1)S(1)}, u32[]{:S(2)}, u32[]{:S(2)}) collective-permute-start(bf16[272,1536]{1,0:T(8,128)(2,1)} %pad_maximum_fusion.11), channel_id=1, source_target_pairs={{0,1},{1,0},{2,3},{3,2},{4,5},{5,4},{6,7},{7,6},{8,9},{9,8},{10,11... | collective-permute-start | bytes 2506760 | tf_op jit(solution)/shard_map/ppermute | solution.py:41
  464.8 47.0 %collective-permute-start.59 = (bf16[272,1536]{1,0:T(8,128)(2,1)}, bf16[272,1536]{1,0:T(8,128)(2,1)S(1)}, u32[]{:S(2)}, u32[]{:S(2)}) collective-permute-start(bf16[272,1536]{1,0:T(8,128)(2,1)} %pad_maximum_fusion.12), channel_id=1, source_target_pairs={{0,4},{4,0},{1,5},{5,1},{2,6},{6,2},{3,7},{7,3},{8,12},{12,8},{9,1... | collective-permute-start | bytes 2506760 | tf_op jit(solution)/shard_map/ppermute | solution.py:33
  486.5 42.2 %collective-permute-start.66 = (bf16[2,3,384,512]{3,2,1,0:T(8,128)(2,1)}, bf16[2,3,384,512]{3,2,1,0:T(8,128)(2,1)}, u32[]{:S(2)}, u32[]{:S(2)}) collective-permute-start(bf16[2,3,384,512]{3,2,1,0:T(8,128)(2,1)} %pad_maximum_fusion), channel_id=1, source_target_pairs={{0,2},{2,0},{1,3},{3,1},{4,6},{6,4},{5,7},{7,5},{8,10},{10,8},{9,1... | collective-permute-start | bytes 7077896 | tf_op jit(solution)/shard_map/ppermute | solution.py:37
  (79 other events, 797.6 us)
Sparse Core Ops, SparseCore 0:
  72.7 89.5 all-gather.2
  320.9 81.9 reduce-scatter.4
  438.8 46.5 reduce-scatter.2

commit v6 on v5

--- a/solution.py
+++ b/solution.py
@@ -56,8 +56,9 @@
 def widen_planes(rows, meanwhile=None):
     if lax.axis_size("tp") != 2:
         gathered = lax.all_gather(rows, "tp", axis=0, tiled=True)
-        return [gathered, swap_chip(gathered)]
-    return far_block(rows, *meet(swap_tp(rows), swap_chip(rows), meanwhile))
+        return [gathered, swap_chip(gathered)], meanwhile
+    (beside, across), meanwhile = together((swap_tp(rows), swap_chip(rows)), meanwhile)
+    return far_block(rows, beside, across), meanwhile
 
 
 def meet(beside, across, meanwhile):
@@ -75,7 +76,7 @@
 
 
 def widen(rows):
-    return widen_core(widen_planes(rows))
+    return widen_core(widen_planes(rows)[0])
 
 
 def block_offset(index, half):
@@ -124,11 +125,6 @@
 def take_quarter(values, index, axis):
     size = values.shape[axis] // 4
     return lax.dynamic_slice_in_dim(values, index * size, size, axis)
-
-
-def all_quarters(own):
-    across = swap_chip(own)
-    return own, across, swap_core(jnp.stack([own, across]))
 
 
 def call(kernel, name, flops, moved, **rest):
@@ -724,15 +720,14 @@
     return lax.dynamic_slice_in_dim(twice, at, rolled.shape[1], 1)
 
 
-def gain_totals(gains):
+def over_tp(gains):
     if lax.axis_size("tp") == 2:
-        gains = gains + swap_tp(gains)
-    else:
-        gains = lax.psum(gains, "tp")
-    gains = gains + swap_core(gains)
-    gains = gains + swap_chip(gains)
-    count = lax.axis_size("fsdp")
-    blocks = jnp.stack(jnp.split(gains, count, axis=1))
+        return gains + swap_tp(gains)
+    return lax.psum(gains, "tp")
+
+
+def over_fsdp(gains):
+    blocks = jnp.stack(jnp.split(gains, lax.axis_size("fsdp"), axis=1))
     return jnp.sum(lax.all_to_all(blocks, "fsdp", 0, 0, tiled=True), axis=0)
 
 
@@ -772,7 +767,7 @@
         second = lambda blocks: widen_core(blocks) + far_block(*blocks)[3:]
         third = lambda blocks: blocks[:3] + blocks[6:] + blocks[3:6] + [swap_core(blocks[6])]
     else:
-        first, second, third = widen_planes, widen_core, lambda blocks: blocks
+        first, second, third = lambda values: widen_planes(values)[0], widen_core, lambda blocks: blocks
     ring = [own_piece]
     block, own, gains, ids_other, cos, sin = together(
         pull_fsdp(ring[0], 1),
@@ -830,21 +825,35 @@
     resid_grad = cotangent.astype(F32) + normalize_back(residual, inv_two, gain_two, normed_two_grad)
     resid_low = resid_grad.astype(BF16)
 
-    out_kept, out_sent = feed_out(after(hidden, resid_low), feed_weight, count)
-    grad_blocks = widen_core(widen_planes(resid_low, out_sent))
+    out_partial = feed_out(after(hidden, resid_low), feed_weight, count)
+    planes, (out_kept, out_sent) = widen_planes(resid_low, tuple(out_partial))
+    grad_blocks = widen_core(planes)
     out_grad, out_grads = out_back(attended, weights, grad_blocks, fsdp, part)
     leaving = narrow_first(out_kept, out_sent, out_grad)
     dq, dk, dv = attend_back(bounds, q, k, v, attended, after(out_grad, leaving), lse, start, cos, sin, heads)
-    layer_out = residual + narrow_second(leaving, lambda rows: dq)[0]
-    project_grads = project_weights(dq, dk, after(dv, layer_out), out_grads, blocks)
+    layer_rows, (dq, feed_sums) = narrow_second(leaving, lambda rows, dq=dq, sums=feed_sums: (dq, sums))
+    layer_out = residual + layer_rows
+    feed_across = swap_chip(feed_sums)
+    kept, sent, gain_one_sums = project_back(dq, dk, dv, weights, blocks)
+    gains = jnp.stack([jnp.sum(gain_one_sums, axis=0) / gain_one, jnp.sum(gain_two_sums, axis=0) / gain_two])
+    gains_tp = over_tp(gains)
+    project_grads = project_weights(after(dq, sent), dk, dv, out_grads, blocks)
     sums = scatter_fsdp(project_grads)
-    kept, sent, gain_one_sums = project_back(after(dq, project_grads), dk, dv, weights, blocks)
-    gate_all, up_all, down_all = finish_feed(*all_quarters(after(feed_sums, dq)))
-    gain_sums = jnp.stack([jnp.sum(gain_one_sums, axis=0) / gain_one, jnp.sum(gain_two_sums, axis=0) / gain_two])
-    normed_grad, gain_own = narrow(kept, sent, lambda leaving: gain_totals(after(gain_sums, leaving)))
+    (sent, feed_across, gains), _ = together((sent, feed_across, gains_tp), project_grads)
+    gains_core = swap_core(gains)
+    feed_came = swap_core(jnp.stack([feed_sums, feed_across]))
+    leaving, (gains, gains_core, feed_came) = together(narrow_first(kept, sent), (gains, gains_core, feed_came))
+    gains = gains + gains_core
+    gains_chip = swap_chip(gains)
+    normed_grad, gains = narrow_second(leaving, lambda rows: gains + gains_chip)
+    gain_own = over_fsdp(gains)
     grad_input = resid_grad + normalize_back(inputs, inv_one, gain_one, normed_grad)
 
-    q_all, k_all, v_all, out_all = finish_attention(*all_quarters(sums), real_width)
+    sums = after(sums, grad_input, gain_own)
+    across = swap_chip(sums)
+    feed_all = finish_feed(feed_sums, feed_across, after(feed_came, sums))
+    across, (gate_all, up_all, down_all) = together(across, tuple(feed_all))
+    q_all, k_all, v_all, out_all = finish_attention(sums, across, swap_core(jnp.stack([sums, across])), real_width)
     return (
         layer_out.astype(BF16)[None],
         grad_input[None],

time: 548 us -> 524 us (0.956)
  waiting for transfers between devices: 166 us -> 150 us
  blocking collectives: 7.81 us -> 0 us
    ppermute x20, waiting for transfers between devices: 106 us -> 95.3 us  [swap_chip(): return lax.ppermute(values, 'chip', [(0, 1), (1, 0)])]
    all_to_all x1 -> x0, blocking collectives: 7.81 us -> none  [gain_totals(): return jnp.sum(lax.all_to_all(blocks, 'fsdp', 0, 0, tiled=True), axis=0)]
  transfers between devices with their start and end apart: 70 -> 71, of which waited for: 26 -> 28; matrix products, arithmetic and copies ran while one was open for 12% -> 15% of each run, Pallas kernels for 24% -> 27%
where the time goes in v6:
time: 524 us; the launch traced here: 519 us
  Pallas kernels  181 us (35%)
  waiting for transfers between devices  150 us (29%)
  starting transfers between devices  80.7 us (15%)
  other arithmetic  74.4 us (14%)
  local copies, waits for them, and re-layouts  17.6 us (3%)
  between operations  14.7 us (3%)
    ppermute x20, waiting for transfers between devices, swap_chip(): return lax.ppermute(values, 'chip', [(0, 1), (1, 0)])  95.3 us
    ppermute x17, waiting for transfers between devices, swap_tp(): return lax.ppermute(values, 'tp', [(0, 1), (1, 0)])  37.8 us
    ppermute x24, starting transfers between devices, swap_core(): return lax.ppermute(values, 'core', [(0, 1), (1, 0)])  37.2 us
    pallas_call x1, Pallas kernels, feed(): call(functools.partial(feed_kernel, count), 'feed', rows * depth * units...  34.9 us
    pallas_call x1, Pallas kernels, attend_back(): call(functools.partial(backward_kernel, rows), 'attend_back', rows * rows...  31.8 us
    pallas_call x1, Pallas kernels, feed_weights(): call(functools.partial(feed_weights_kernel, count), 'feed_weights', rows...  20.1 us
    another operation x12, other arithmetic  17.8 us
    pallas_call x1, Pallas kernels, attend(): call(functools.partial(forward_kernel, rows), 'attend', rows * rows * hea...  16.9 us
  transfers between devices with their start and end apart: 71, of which 28 were waited for; matrix products, arithmetic and copies ran while one was open for 15% of the time, Pallas kernels for 27%

profile of v6, /device:TPU:1, one launch (start us, length us, event | category | flops | bytes accessed | tf_op | source)
XLA Modules:
  0.0 518.7 jit_solution(7536361248462900871)
XLA Ops:
  18.8 6.2 %multiply_sine_fusion = (f32[2304,128]{1,0:T(8,128)}, f32[2304,128]{1,0:T(8,128)}) fusion(f32[128]{0:T(128)S(1)} %fusion.33, f32[2304]{0:T(1024)S(1)} %convert_element_type.326), kind=kLoop, calls=%fused_computation.22 | loop fusion | flops 294912 | bytes 2369024 | tf_op jit(solution)/shard_map/sin | solution.py:778
  35.9 7.2 %collective-permute-done.1 = bf16[272,1536]{1,0:T(8,128)(2,1)S(1)} collective-permute-done((bf16[272,1536]{1,0:T(8,128)(2,1)S(1)}, bf16[272,1536]{1,0:T(8,128)(2,1)S(1)}, u32[]{:S(2)}, u32[]{:S(2)}) %collective-permute-start.1) | collective-permute-done | bytes 835616 | tf_op jit(solution)/shard_map/ppermute | solution.py:41
  55.9 10.2 %collective-permute-done.12 = bf16[144,1536]{1,0:T(8,128)(2,1)S(1)} collective-permute-done((bf16[144,1536]{1,0:T(8,128)(2,1)S(1)}, bf16[144,1536]{1,0:T(8,128)(2,1)S(1)}, u32[]{:S(2)}, u32[]{:S(2)}) %collective-permute-start.12) | collective-permute-done | bytes 442400 | tf_op jit(solution)/shard_map/ppermute | solution.py:33
  96.4 11.8 %project.1 = (bf16[2176,256]{1,0:T(8,128)(2,1)}, bf16[2304,256]{1,0:T(8,128)(2,1)}, bf16[2304,256]{1,0:T(8,128)(2,1)}) custom-call(bf16[272,1536]{1,0:T(8,128)(2,1)} %get-tuple-element.150.refs_0_, bf16[272,1536]{1,0:T(8,128)(2,1)} %get-tuple-element.151.refs_1_, bf16[272,1536]{1,0:T(8,128)(2,1)} %get-tuple-element.152.refs_2_, ...), custom_call_target="tpu_custom_call" | custom-call | flops 5133828096 | bytes 6684672 | tf_op jit(solution)/shard_map/project/pallas_call | solution.py:176
  118.2 16.9 %attend.1 = (bf16[2176,256]{1,0:T(8,128)(2,1)}, f32[3,2304]{1,0:T(4,128)}) custom-call(s32[2,9]{1,0:T(2,128)} %pad_add_fusion.2.bounds, bf16[2176,256]{1,0:T(8,128)(2,1)} %get-tuple-element.161.q_ref, bf16[2304,256]{1,0:T(8,128)(2,1)} %get-tuple-element.162.k_ref, bf16[2304,256]{1,0:T(8,128)(2,1)} %get-tuple-element.163.v_ref, ...), custom_call_target="tpu_custom_call" | custom-call | flops 1818230784 | bytes 4718592 | tf_op jit(solution)/shard_map/attend/pallas_call | solution.py:420
  135.3 6.3 %out_project.1 = (bf16[1088,1536]{1,0:T(8,128)(2,1)}, bf16[1088,1536]{1,0:T(8,128)(2,1)}) custom-call(bf16[2176,256]{1,0:T(8,128)(2,1)} %get-tuple-element.171.o_ref, bf16[4,256,1536]{2,1,0:T(8,128)(2,1)} %place_weights.1.refs_8_.weight_ref), custom_call_target="tpu_custom_call" | custom-call | flops 1711276032 | bytes 6684672 | tf_op jit(solution)/shard_map/out_project/pallas_call | solution.py:257
  142.1 5.8 %collective-permute-done.23 = bf16[1088,1536]{1,0:T(8,128)(2,1)S(1)} collective-permute-done((bf16[1088,1536]{1,0:T(8,128)(2,1)}, bf16[1088,1536]{1,0:T(8,128)(2,1)S(1)}, u32[]{:S(2)}, u32[]{:S(2)}) %collective-permute-start.23) | collective-permute-done | bytes 3342368 | tf_op jit(solution)/shard_map/ppermute | solution.py:37
  154.6 7.6 %collective-permute-done.24 = bf16[128,1536]{1,0:T(8,128)(2,1)S(1)} collective-permute-done((bf16[128,1536]{1,0:T(8,128)(2,1)S(1)}, bf16[128,1536]{1,0:T(8,128)(2,1)S(1)}, u32[]{:S(2)}, u32[]{:S(2)}) %collective-permute-start.24) | collective-permute-done | bytes 393248 | tf_op jit(solution)/shard_map/ppermute | solution.py:33
  167.8 16.1 %collective-permute-done.26 = bf16[272,1536]{1,0:T(8,128)(2,1)S(1)} collective-permute-done((bf16[272,1536]{1,0:T(8,128)(2,1)S(1)}, bf16[272,1536]{1,0:T(8,128)(2,1)S(1)}, u32[]{:S(2)}, u32[]{:S(2)}) %collective-permute-start.26) | collective-permute-done | bytes 835616 | tf_op jit(solution)/shard_map/ppermute | solution.py:41
  189.5 17.0 %collective-permute-done.30.refs_2_ = bf16[272,1536]{1,0:T(8,128)(2,1)S(1)} collective-permute-done((bf16[272,1536]{1,0:T(8,128)(2,1)S(1)}, bf16[272,1536]{1,0:T(8,128)(2,1)S(1)}, u32[]{:S(2)}, u32[]{:S(2)}) %collective-permute-start.30) | collective-permute-done | bytes 835616 | tf_op jit(solution)/shard_map/ppermute | solution.py:33
  222.3 34.9 %feed.1 = (bf16[2176,512]{1,0:T(8,128)(2,1)}, bf16[2176,512]{1,0:T(8,128)(2,1)}, bf16[2176,512]{1,0:T(8,128)(2,1)}, bf16[1088,1536]{1,0:T(8,128)(2,1)}, bf16[1088,1536]{1,0:T(8,128)(2,1)}, /*index=5*/f32[8,1536]{1,0:T(8,128)}) custom-call(bf16[272,1536]{1,0:T(8,128)(2,1)} %copy-done.17, bf16[272,1536]{1,0:T(8,128)(2,1)} %copy-done.20, ...), custom_call_target="tpu_custom_call" | custom-call | flops 17112760320 | bytes 4718592 | tf_op jit(solution)/shard_map/feed/pallas_call | solution.py:577
  257.6 5.8 %collective-permute-done.37 = bf16[1088,1536]{1,0:T(8,128)(2,1)S(1)} collective-permute-done((bf16[1088,1536]{1,0:T(8,128)(2,1)}, bf16[1088,1536]{1,0:T(8,128)(2,1)S(1)}, u32[]{:S(2)}, u32[]{:S(2)}) %collective-permute-start.37) | collective-permute-done | bytes 3342368 | tf_op jit(solution)/shard_map/ppermute | solution.py:37
  268.4 7.3 %collective-permute-done.38 = bf16[128,1536]{1,0:T(8,128)(2,1)S(1)} collective-permute-done((bf16[128,1536]{1,0:T(8,128)(2,1)S(1)}, bf16[128,1536]{1,0:T(8,128)(2,1)S(1)}, u32[]{:S(2)}, u32[]{:S(2)}) %collective-permute-start.38) | collective-permute-done | bytes 393248 | tf_op jit(solution)/shard_map/ppermute | solution.py:33
  283.9 20.1 %feed_weights.1 = bf16[4,3,384,512]{3,2,1,0:T(8,128)(2,1)} custom-call(bf16[272,1536]{1,0:T(8,128)(2,1)} %copy-done.17, bf16[272,1536]{1,0:T(8,128)(2,1)} %copy-done.20, bf16[272,1536]{1,0:T(8,128)(2,1)} %copy-done.21, bf16[272,1536]{1,0:T(8,128)(2,1)} %copy-done.22, bf16[272,1536]{1,0:T(8,128)(2,1)} %copy-done.27, bf16[272,1536]{1,0:T(8,128)(2,1)} %copy-done.28, ...), custom_call_target="tpu_custom_call" | custom-call | flops 10267656192 | bytes 4718592 | tf_op jit(solution)/shard_map/feed_weights/pallas_call | solution.py:612
  311.7 7.8 %feed_out.1 = (bf16[1088,1536]{1,0:T(8,128)(2,1)}, bf16[1088,1536]{1,0:T(8,128)(2,1)}) custom-call(bf16[2176,512]{1,0:T(8,128)(2,1)} %get-tuple-element.204.refs_18_.hidden_ref, bf16[4,3,384,512]{3,2,1,0:T(8,128)(2,1)} %bitcast.56), custom_call_target="tpu_custom_call" | custom-call | flops 3422552064 | bytes 6684672 | tf_op jit(solution)/shard_map/feed_out/pallas_call | solution.py:637
  319.5 10.0 %collective-permute-done.43.refs_2_ = bf16[272,1536]{1,0:T(8,128)(2,1)} collective-permute-done((bf16[272,1536]{1,0:T(8,128)(2,1)}, bf16[272,1536]{1,0:T(8,128)(2,1)}, u32[]{:S(2)}, u32[]{:S(2)}) %collective-permute-start.43) | collective-permute-done | bytes 835616 | tf_op jit(solution)/shard_map/ppermute | solution.py:33
  336.8 8.2 %collective-permute-done.47 = bf16[128,1536]{1,0:T(8,128)(2,1)S(1)} collective-permute-done((bf16[128,1536]{1,0:T(8,128)(2,1)S(1)}, bf16[128,1536]{1,0:T(8,128)(2,1)S(1)}, u32[]{:S(2)}, u32[]{:S(2)}) %collective-permute-start.47) | collective-permute-done | bytes 393248 | tf_op jit(solution)/shard_map/ppermute | solution.py:41
  355.5 9.2 %out_back.1 = (bf16[2176,256]{1,0:T(8,128)(2,1)}, bf16[4,1,192,384]{3,2,1,0:T(8,128)(2,1)}) custom-call(bf16[2176,256]{1,0:T(8,128)(2,1)} %get-tuple-element.171.o_ref, bf16[4,256,1536]{2,1,0:T(8,128)(2,1)} %place_weights.1.refs_8_.weight_ref, bf16[272,1536]{1,0:T(8,128)(2,1)} %get-tuple-element.261.refs_0_, ...), custom_call_target="tpu_custom_call" | custom-call | flops 3422552064 | bytes 6684672 | tf_op jit(solution)/shard_map/out_back/pallas_call | solution.py:284
  372.1 31.8 %attend_back.1 = (bf16[2176,256]{1,0:T(8,128)(2,1)}, bf16[2304,256]{1,0:T(8,128)(2,1)}, bf16[2304,256]{1,0:T(8,128)(2,1)}) custom-call(s32[2,9]{1,0:T(2,128)} %pad_add_fusion.2.bounds, bf16[2176,256]{1,0:T(8,128)(2,1)} %get-tuple-element.161.q_ref, bf16[2304,256]{1,0:T(8,128)(2,1)} %get-tuple-element.162.k_ref, bf16[2304,256]{1,0:T(8,128)(2,1)} %get-tuple-element.163.v_ref, ...), custom_call_target="tpu_custom_call" | custom-call | flops 4545576960 | bytes 9437184 | tf_op jit(solution)/shard_map/attend_back/pallas_call | solution.py:503
  404.5 11.9 %project_back.1 = (bf16[1088,1536]{1,0:T(8,128)(2,1)}, bf16[1088,1536]{1,0:T(8,128)(2,1)}, f32[8,1536]{1,0:T(8,128)}) custom-call(bf16[2176,256]{1,0:T(8,128)(2,1)} %get-tuple-element.228.dq_ref, bf16[2304,256]{1,0:T(8,128)(2,1)} %get-tuple-element.221.dk_ref, bf16[2304,256]{1,0:T(8,128)(2,1)} %get-tuple-element.222.dv_ref, ...), custom_call_target="tpu_custom_call" | custom-call | flops 5133828096 | bytes 13369344 | tf_op jit(solution)/shard_map/project_back/pallas_call | solution.py:349
  418.8 12.4 %project_weights.1 = bf16[4,4,192,384]{3,2,1,0:T(8,128)(2,1)} custom-call(bf16[2176,256]{1,0:T(8,128)(2,1)} %get-tuple-element.228.dq_ref, bf16[2304,256]{1,0:T(8,128)(2,1)} %get-tuple-element.221.dk_ref, bf16[2304,256]{1,0:T(8,128)(2,1)} %get-tuple-element.222.dv_ref, bf16[4,1,192,384]{3,2,1,0:T(8,128)(2,1)} %get-tuple-element.229.done_ref, ...), custom_call_target="tpu_custom_call" | custom-call | flops 5133828096 | bytes 6684672 | tf_op jit(solution)/shard_map/project_weights/pallas_call | solution.py:316
  445.7 7.0 %collective-permute-done.58 = bf16[128,1536]{1,0:T(8,128)(2,1)S(1)} collective-permute-done((bf16[128,1536]{1,0:T(8,128)(2,1)S(1)}, bf16[128,1536]{1,0:T(8,128)(2,1)S(1)}, u32[]{:S(2)}, u32[]{:S(2)}) %collective-permute-start.58) | collective-permute-done | bytes 393248 | tf_op jit(solution)/shard_map/ppermute | solution.py:33
  458.1 17.3 %collective-permute-done.64 = f32[2,1536]{1,0:T(2,128)S(1)} collective-permute-done((f32[2,1536]{1,0:T(2,128)S(1)}, f32[2,1536]{1,0:T(2,128)S(1)}, u32[]{:S(2)}, u32[]{:S(2)}) %collective-permute-start.64) | collective-permute-done | bytes 12320 | tf_op jit(solution)/shard_map/ppermute | solution.py:33
  487.5 6.7 %finish_feed.1 = (f32[384,2048]{1,0:T(8,128)}, f32[384,2048]{1,0:T(8,128)}, f32[2048,384]{1,0:T(8,128)}) custom-call(bf16[3,384,512]{2,1,0:T(8,128)(2,1)} %reduce-scatter.3.cloned.1.call-done.own_ref, bf16[3,384,512]{2,1,0:T(8,128)(2,1)} %collective-permute-done.55.across_ref, bf16[2,3,384,512]{3,2,1,0:T(8,128)(2,1)} %collective-permute-done.61.came_ref), custom_call_target="tpu_custom_call" | custom-call | bytes 14155776 | tf_op jit(solution)/shard_map/finish_feed/pallas_call | solution.py:666
  (306 shorter events, 208.3 us)
Async XLA Ops:
  7.2 155.1 %all-gather.3.cloned.1.call-start = ((), (), s32[]{:S(2)}) async-start(), calls=%async_computation.5 | async-start | bytes 5898240 | tf_op jit(solution)/shard_map/all_gather | solution.py:785
  8.8 20.0 %collective-permute-start.5 = (bf16[2,384]{1,0:T(2,128)(2,1)S(1)}, bf16[2,384]{1,0:T(2,128)(2,1)S(1)}, u32[]{:S(2)}, u32[]{:S(2)}) collective-permute-start(bf16[2,384]{1,0:T(2,128)(2,1)S(1)} %get-tuple-element.266), channel_id=1, source_target_pairs={{0,8},{8,16},{16,24},{24,0},{1,9},{9,17},{17,25},{25,1},{2,10},{10... | collective-permute-start | bytes 4616 | tf_op jit(solution)/shard_map/ppermute | solution.py:712
  17.5 18.4 %collective-permute-start.2 = (bf16[272,1536]{1,0:T(8,128)(2,1)S(1)}, bf16[272,1536]{1,0:T(8,128)(2,1)}, u32[]{:S(2)}, u32[]{:S(2)}) collective-permute-start(bf16[272,1536]{1,0:T(8,128)(2,1)S(1)} %bitcast.36), channel_id=1, source_target_pairs={{0,4},{4,0},{1,5},{5,1},{2,6},{6,2},{3,7},{7,3},{8,12},{12,8},{9,1... | collective-permute-start | bytes 2506760 | tf_op jit(solution)/shard_map/ppermute | solution.py:33
  49.2 19.7 %collective-permute-start.10 = (bf16[272,1536]{1,0:T(8,128)(2,1)}, bf16[272,1536]{1,0:T(8,128)(2,1)}, u32[]{:S(2)}, u32[]{:S(2)}) collective-permute-start(bf16[272,1536]{1,0:T(8,128)(2,1)} %collective-permute-done.2), channel_id=1, source_target_pairs={{0,2},{2,0},{1,3},{3,1},{4,6},{6,4},{5,7},{7,5},{8,10},{10,8},{9,1... | collective-permute-start | bytes 2506760 | tf_op jit(solution)/shard_map/ppermute | solution.py:37
  72.5 331.4 %reduce-scatter.3.cloned.1.call-start = ((), (), s32[]{:S(2)}) async-start(), calls=%async_computation.3 | async-start | bytes 5898240 | tf_op jit(solution)/shard_map/reduce_scatter | solution.py:737
  108.2 27.0 %collective-permute-start.18 = (bf16[272,1536]{1,0:T(8,128)(2,1)S(1)}, bf16[272,1536]{1,0:T(8,128)(2,1)}, u32[]{:S(2)}, u32[]{:S(2)}) collective-permute-start(bf16[272,1536]{1,0:T(8,128)(2,1)S(1)} %bitcast.52), channel_id=1, source_target_pairs={{0,2},{2,0},{1,3},{3,1},{4,6},{6,4},{5,7},{7,5},{8,10},{10,8},{9,1... | collective-permute-start | bytes 2506760 | tf_op jit(solution)/shard_map/ppermute | solution.py:37
  112.2 23.1 %collective-permute-start.19 = (bf16[272,1536]{1,0:T(8,128)(2,1)}, bf16[272,1536]{1,0:T(8,128)(2,1)}, u32[]{:S(2)}, u32[]{:S(2)}) collective-permute-start(bf16[272,1536]{1,0:T(8,128)(2,1)} %collective-permute-done.16.refs_9_), channel_id=1, source_target_pairs={{0,2},{2,0},{1,3},{3,1},{4,6},{6,4},{5,7},{7,5},{8,10},{10,8},{9,1... | collective-permute-start | bytes 2506760 | tf_op jit(solution)/shard_map/ppermute | solution.py:37
  112.2 23.0 %collective-permute-start.20 = (bf16[272,1536]{1,0:T(8,128)(2,1)}, bf16[272,1536]{1,0:T(8,128)(2,1)}, u32[]{:S(2)}, u32[]{:S(2)}) collective-permute-start(bf16[272,1536]{1,0:T(8,128)(2,1)} %collective-permute-done.17.refs_10_), channel_id=1, source_target_pairs={{0,2},{2,0},{1,3},{3,1},{4,6},{6,4},{5,7},{7,5},{8,10},{10,8},{9,1... | collective-permute-start | bytes 2506760 | tf_op jit(solution)/shard_map/ppermute | solution.py:37
  116.9 18.3 %collective-permute-start.21 = (bf16[128,1536]{1,0:T(8,128)(2,1)S(1)}, bf16[128,1536]{1,0:T(8,128)(2,1)S(1)}, u32[]{:S(2)}, u32[]{:S(2)}) collective-permute-start(bf16[128,1536]{1,0:T(8,128)(2,1)S(1)} %slice.204), channel_id=1, source_target_pairs={{0,1},{1,0},{2,3},{3,2},{4,5},{5,4},{6,7},{7,6},{8,9},{9,8},{10,11... | collective-permute-start | bytes 1179656 | tf_op jit(solution)/shard_map/ppermute | solution.py:41
  165.3 18.6 %collective-permute-start.26 = (bf16[272,1536]{1,0:T(8,128)(2,1)S(1)}, bf16[272,1536]{1,0:T(8,128)(2,1)S(1)}, u32[]{:S(2)}, u32[]{:S(2)}) collective-permute-start(bf16[272,1536]{1,0:T(8,128)(2,1)S(1)} %pad_maximum_fusion.5), channel_id=1, source_target_pairs={{0,1},{1,0},{2,3},{3,2},{4,5},{5,4},{6,7},{7,6},{8,9},{9,8},{10,11... | collective-permute-start | bytes 2506760 | tf_op jit(solution)/shard_map/ppermute | solution.py:41
  166.5 19.3 %collective-permute-start.27 = (bf16[272,1536]{1,0:T(8,128)(2,1)S(1)}, bf16[272,1536]{1,0:T(8,128)(2,1)S(1)}, u32[]{:S(2)}, u32[]{:S(2)}) collective-permute-start(bf16[272,1536]{1,0:T(8,128)(2,1)S(1)} %pad_maximum_fusion.6), channel_id=1, source_target_pairs={{0,4},{4,0},{1,5},{5,1},{2,6},{6,2},{3,7},{7,3},{8,12},{12,8},{9,1... | collective-permute-start | bytes 2506760 | tf_op jit(solution)/shard_map/ppermute | solution.py:33
  188.1 18.3 %collective-permute-start.30 = (bf16[272,1536]{1,0:T(8,128)(2,1)S(1)}, bf16[272,1536]{1,0:T(8,128)(2,1)S(1)}, u32[]{:S(2)}, u32[]{:S(2)}) collective-permute-start(bf16[272,1536]{1,0:T(8,128)(2,1)S(1)} %multiply_convert_fusion.refs_0_), channel_id=1, source_target_pairs={{0,4},{4,0},{1,5},{5,1},{2,6},{6,2},{3,7},{7,3},{8,12},{12,8},{9,1... | collective-permute-start | bytes 2506760 | tf_op jit(solution)/shard_map/ppermute | solution.py:33
  280.5 23.5 %collective-permute-start.39 = (bf16[272,1536]{1,0:T(8,128)(2,1)}, bf16[272,1536]{1,0:T(8,128)(2,1)}, u32[]{:S(2)}, u32[]{:S(2)}) collective-permute-start(bf16[272,1536]{1,0:T(8,128)(2,1)} %pad_maximum_fusion.7), channel_id=1, source_target_pairs={{0,1},{1,0},{2,3},{3,2},{4,5},{5,4},{6,7},{7,6},{8,9},{9,8},{10,11... | collective-permute-start | bytes 2506760 | tf_op jit(solution)/shard_map/ppermute | solution.py:41
  282.9 21.1 %collective-permute-start.41 = (bf16[272,1536]{1,0:T(8,128)(2,1)}, bf16[272,1536]{1,0:T(8,128)(2,1)}, u32[]{:S(2)}, u32[]{:S(2)}) collective-permute-start(bf16[272,1536]{1,0:T(8,128)(2,1)} %pad_maximum_fusion.8), channel_id=1, source_target_pairs={{0,4},{4,0},{1,5},{5,1},{2,6},{6,2},{3,7},{7,3},{8,12},{12,8},{9,1... | collective-permute-start | bytes 2506760 | tf_op jit(solution)/shard_map/ppermute | solution.py:33
  304.1 182.6 %reduce-scatter.5.cloned.1.call-start = ((), (), s32[]{:S(2)}) async-start(), calls=%async_computation.4 | async-start | bytes 2949120 | tf_op jit(solution)/shard_map/reduce_scatter | solution.py:737
  311.2 18.4 %collective-permute-start.43 = (bf16[272,1536]{1,0:T(8,128)(2,1)}, bf16[272,1536]{1,0:T(8,128)(2,1)}, u32[]{:S(2)}, u32[]{:S(2)}) collective-permute-start(bf16[272,1536]{1,0:T(8,128)(2,1)} %get-tuple-element.261.refs_0_), channel_id=1, source_target_pairs={{0,4},{4,0},{1,5},{5,1},{2,6},{6,2},{3,7},{7,3},{8,12},{12,8},{9,1... | collective-permute-start | bytes 2506760 | tf_op jit(solution)/shard_map/ppermute | solution.py:33
  336.8 18.7 %collective-permute-start.50 = (bf16[272,1536]{1,0:T(8,128)(2,1)}, bf16[272,1536]{1,0:T(8,128)(2,1)}, u32[]{:S(2)}, u32[]{:S(2)}) collective-permute-start(bf16[272,1536]{1,0:T(8,128)(2,1)} %collective-permute-done.42.refs_1_), channel_id=1, source_target_pairs={{0,2},{2,0},{1,3},{3,1},{4,6},{6,4},{5,7},{7,5},{8,10},{10,8},{9,1... | collective-permute-start | bytes 2506760 | tf_op jit(solution)/shard_map/ppermute | solution.py:37
  370.1 33.8 %collective-permute-start.53 = (bf16[272,1536]{1,0:T(8,128)(2,1)}, bf16[272,1536]{1,0:T(8,128)(2,1)}, u32[]{:S(2)}, u32[]{:S(2)}) collective-permute-start(bf16[272,1536]{1,0:T(8,128)(2,1)} %pad_maximum_fusion.9), channel_id=1, source_target_pairs={{0,1},{1,0},{2,3},{3,2},{4,5},{5,4},{6,7},{7,6},{8,9},{9,8},{10,11... | collective-permute-start | bytes 2506760 | tf_op jit(solution)/shard_map/ppermute | solution.py:41
  371.1 32.9 %collective-permute-start.54 = (bf16[272,1536]{1,0:T(8,128)(2,1)}, bf16[272,1536]{1,0:T(8,128)(2,1)}, u32[]{:S(2)}, u32[]{:S(2)}) collective-permute-start(bf16[272,1536]{1,0:T(8,128)(2,1)} %pad_maximum_fusion.10), channel_id=1, source_target_pairs={{0,4},{4,0},{1,5},{5,1},{2,6},{6,2},{3,7},{7,3},{8,12},{12,8},{9,1... | collective-permute-start | bytes 2506760 | tf_op jit(solution)/shard_map/ppermute | solution.py:33
  404.0 27.2 %collective-permute-start.55 = (bf16[3,384,512]{2,1,0:T(8,128)(2,1)}, bf16[3,384,512]{2,1,0:T(8,128)(2,1)}, u32[]{:S(2)}, u32[]{:S(2)}) collective-permute-start(bf16[3,384,512]{2,1,0:T(8,128)(2,1)} %reduce-scatter.3.cloned.1.call-done.own_ref), channel_id=1, source_target_pairs={{0,4},{4,0},{1,5},{5,1},{2,6},{6,2},{3,7},{7,3},{8,12},{12,8},{9,1... | collective-permute-start | bytes 3538952 | tf_op jit(solution)/shard_map/ppermute | solution.py:33
  433.6 21.9 %collective-permute-start.60 = (f32[2,1536]{1,0:T(2,128)S(1)}, f32[2,1536]{1,0:T(2,128)S(1)}, u32[]{:S(2)}, u32[]{:S(2)}) collective-permute-start(f32[2,1536]{1,0:T(2,128)S(1)} %fusion.35), channel_id=1, source_target_pairs={{0,2},{2,0},{1,3},{3,1},{4,6},{6,4},{5,7},{7,5},{8,10},{10,8},{9,1... | collective-permute-start | bytes 36872 | tf_op jit(solution)/shard_map/ppermute | solution.py:37
  435.7 19.8 %collective-permute-start.61 = (bf16[2,3,384,512]{3,2,1,0:T(8,128)(2,1)S(1)}, bf16[2,3,384,512]{3,2,1,0:T(8,128)(2,1)}, u32[]{:S(2)}, u32[]{:S(2)}) collective-permute-start(bf16[2,3,384,512]{3,2,1,0:T(8,128)(2,1)S(1)} %pad_maximum_fusion), channel_id=1, source_target_pairs={{0,2},{2,0},{1,3},{3,1},{4,6},{6,4},{5,7},{7,5},{8,10},{10,8},{9,1... | collective-permute-start | bytes 7077896 | tf_op jit(solution)/shard_map/ppermute | solution.py:37
  455.5 19.9 %collective-permute-start.62 = (bf16[272,1536]{1,0:T(8,128)(2,1)S(1)}, bf16[272,1536]{1,0:T(8,128)(2,1)}, u32[]{:S(2)}, u32[]{:S(2)}) collective-permute-start(bf16[272,1536]{1,0:T(8,128)(2,1)S(1)} %pad_maximum_fusion.11), channel_id=1, source_target_pairs={{0,1},{1,0},{2,3},{3,2},{4,5},{5,4},{6,7},{7,6},{8,9},{9,8},{10,11... | collective-permute-start | bytes 2506760 | tf_op jit(solution)/shard_map/ppermute | solution.py:41
  456.6 18.9 %collective-permute-start.63 = (bf16[272,1536]{1,0:T(8,128)(2,1)S(1)}, bf16[272,1536]{1,0:T(8,128)(2,1)}, u32[]{:S(2)}, u32[]{:S(2)}) collective-permute-start(bf16[272,1536]{1,0:T(8,128)(2,1)S(1)} %pad_maximum_fusion.12), channel_id=1, source_target_pairs={{0,4},{4,0},{1,5},{5,1},{2,6},{6,2},{3,7},{7,3},{8,12},{12,8},{9,1... | collective-permute-start | bytes 2506760 | tf_op jit(solution)/shard_map/ppermute | solution.py:33
  (78 other events, 824.4 us)
Sparse Core Ops, SparseCore 0:
  72.7 89.5 all-gather.2
  304.2 86.3 reduce-scatter.2
  433.7 47.4 reduce-scatter.4

commit v7 on v6

--- a/solution.py
+++ b/solution.py
@@ -529,22 +529,43 @@
 
 
 def feed_kernel(count, *refs):
-    n_refs, dy_refs, weights = refs[:count], refs[count : 2 * count], refs[2 * count : 2 * count + 3]
-    hidden_ref, gate_ref, up_ref, kept_ref, sent_ref, gain_ref, acc = refs[2 * count + 3 :]
-    step = pl.program_id(0)
-    block = n_refs[0].shape[0]
-
-    @pl.when(step == 0)
-    def _():
-        acc[...] = jnp.zeros_like(acc)
-
-    gate_w, up_w, down_w = (joined(ref) for ref in weights)
+    sources, weight_ref = refs[: 2 * count], refs[2 * count]
+    hidden_ref, gate_ref, up_ref, kept_ref, sent_ref, gain_ref, rows_buf, weight_buf, sems = refs[2 * count + 1 :]
+    block = sources[0].shape[0]
+    fsdp, _, columns, units = weight_ref.shape
+
+    def weight_copy(k):
+        return pltpu.make_async_copy(weight_ref.at[:, k], weight_buf.at[k], sems.at[2 * count + k])
+
+    def row_copy(i):
+        return pltpu.make_async_copy(sources[i], rows_buf.at[i], sems.at[i])
+
+    order = [i for pair in zip(range(count), range(count, 2 * count)) for i in pair]
+    row_copy(0).start()
+    for k in range(3):
+        weight_copy(k).start()
+    for i in order[1:]:
+        row_copy(i).start()
+    row_copy(0).wait()
+    total = 0.0
     for i in range(count):
         rows = slice(i * block, (i + 1) * block)
-        normed = n_refs[i][...]
+        if i > 0:
+            row_copy(i).wait()
+        normed = rows_buf[i]
+
+        def weight(k):
+            if i == 0:
+                weight_copy(k).wait()
+            return weight_buf[k].reshape(fsdp * columns, units)
+
+        gate_w = weight(0)
         gate = dot(normed, gate_w)
+        up_w = weight(1)
         up = dot(normed, up_w)
-        grad = dot(dy_refs[i][...], down_w)
+        down_w = weight(2)
+        row_copy(count + i).wait()
+        grad = dot(rows_buf[count + i], down_w)
         sig = 1.0 / (1.0 + jnp.exp(-gate))
         silu = gate * sig
         hidden_ref[rows, :] = (silu * up).astype(BF16)
@@ -552,39 +573,32 @@
         up_grad = (grad * silu).astype(BF16)
         gate_ref[rows, :] = gate_grad
         up_ref[rows, :] = up_grad
-        acc[rows, :] += dot_nt(gate_grad, gate_w) + dot_nt(up_grad, up_w)
-
-    @pl.when(step == pl.num_programs(0) - 1)
-    def _():
-        total = 0.0
-        for i in range(count):
-            values = acc[i * block : (i + 1) * block, :]
-            store_block(kept_ref, sent_ref, i, block, values)
-            total = total + column_sums(values, n_refs[i][...])
-        gain_ref[...] = total
+        values = dot_nt(gate_grad, gate_w) + dot_nt(up_grad, up_w)
+        store_block(kept_ref, sent_ref, i, block, values)
+        total = total + column_sums(values, normed)
+    gain_ref[...] = total
 
 
 def feed(normed, dy, weights):
     count = len(normed)
     block, depth = normed[0].shape
     rows = count * block
-    fsdp, _, columns, units = weights.shape
-    tile = min(TILE, units)
-    kind = lambda k: pl.BlockSpec((fsdp, 1, columns, tile), lambda i: (0, k, 0, i))
-    out = pl.BlockSpec((rows, tile), lambda i: (0, i))
+    fsdp, kinds, columns, units = weights.shape
     wide = jax.ShapeDtypeStruct((rows, units), BF16)
-    half = once((rows // 2, depth))
     return call(
         functools.partial(feed_kernel, count),
         "feed",
         rows * depth * units * 10,
         depth * units * 6,
-        grid=(units // tile,),
         out_shape=[wide, wide, wide] + halves(rows, depth) + [jax.ShapeDtypeStruct((8, depth), F32)],
-        in_specs=[once((block, depth))] * (2 * count) + [kind(0), kind(1), kind(2)],
-        out_specs=[out, out, out, half, half, once((8, depth))],
-        scratch_shapes=[pltpu.VMEM((rows, depth), F32)],
-    )(*normed, *dy, weights, weights, weights)
+        in_specs=[pl.BlockSpec(memory_space=pl.ANY)] * (2 * count + 1),
+        out_specs=[whole()] * 6,
+        scratch_shapes=[
+            pltpu.VMEM((2 * count, block, depth), BF16),
+            pltpu.VMEM((kinds, fsdp, columns, units), BF16),
+            pltpu.SemaphoreType.DMA((2 * count + kinds,)),
+        ],
+    )(*normed, *dy, weights)
 
 
 def feed_weights_kernel(count, *refs):
@@ -754,10 +768,6 @@
     own_piece = cut_attention(*[jnp.pad(w, pad) for w in (wq, wk, wv)], jnp.pad(wo, pad[::-1]))
     feed_piece = jnp.stack([take_quarter(w_gate, place, 1), take_quarter(w_up, place, 1), jnp.transpose(take_quarter(w_down, place, 0))])
 
-    position = after(jnp.arange(keys, dtype=jnp.int32), own_piece).astype(F32)
-    pair_index = (jnp.arange(LANES, dtype=jnp.int32) % (HEAD_DIM // 2)).astype(F32)
-    angles = position[:, None] * (10000.0 ** (-pair_index * 2.0 / HEAD_DIM))[None, :]
-
     def normed(values):
         values = values.astype(F32)
         return (values * inverse_rms(values) * gain_one).astype(BF16)
@@ -769,18 +779,21 @@
     else:
         first, second, third = lambda values: widen_planes(values)[0], widen_core, lambda blocks: blocks
     ring = [own_piece]
-    block, own, gains, ids_other, cos, sin = together(
-        pull_fsdp(ring[0], 1),
-        first(tokens),
-        gather_gains(jnp.stack([gain_attn, gain_ffn])),
-        swap_core(segment_ids),
-        jnp.cos(angles),
-        jnp.sin(angles),
+    position = after(jnp.arange(keys, dtype=jnp.int32), own_piece).astype(F32)
+    pair_index = (jnp.arange(LANES, dtype=jnp.int32) % (HEAD_DIM // 2)).astype(F32)
+    angles = position[:, None] * (10000.0 ** (-pair_index * 2.0 / HEAD_DIM))[None, :]
+    block, own, ids_other, cos, sin = together(
+        pull_fsdp(ring[0], 1), first(tokens), swap_core(segment_ids), jnp.cos(angles), jnp.sin(angles)
     )
     ring.append(block)
+    ids_chip = jnp.concatenate(in_order(segment_ids, ids_other, core == 0))
+    block, own, ids_across, gains = together(
+        pull_fsdp(ring[-1], 1),
+        second(own),
+        swap_chip(ids_chip),
+        gather_gains(after(jnp.stack([gain_attn, gain_ffn]), ids_other)),
+    )
     gain_one, gain_two = gains
-    ids_chip = jnp.concatenate(in_order(segment_ids, ids_other, core == 0))
-    block, own, ids_across = together(pull_fsdp(ring[-1], 1), second(own), swap_chip(ids_chip))
     ring.append(block)
     feed_weight = lax.all_gather(after(feed_piece, block), "fsdp", axis=0, tiled=False)
     ids = jnp.concatenate(in_order(ids_chip, ids_across, chip == 0))

time: 524 us -> 513 us (0.979)
  Pallas kernels: 181 us -> 174 us
    ppermute x6, waiting for transfers between devices: 1.41 us -> 17.7 us  [pull_fsdp(): lax.ppermute(values, 'fsdp', [(i, (i - step) % count) for i in range(coun...]
    ppermute x20, waiting for transfers between devices: 95.3 us -> 81.7 us  [swap_chip(): return lax.ppermute(values, 'chip', [(0, 1), (1, 0)])]
    pallas_call x1, Pallas kernels: 34.9 us -> 28.3 us  [feed(): call(functools.partial(feed_kernel, count), 'feed', rows * depth * units...]
    another operation x12 -> x13, other arithmetic: 17.8 us -> 17.9 us
  transfers between devices with their start and end apart: 71 -> 71, of which waited for: 28 -> 27; matrix products, arithmetic and copies ran while one was open for 15% -> 14% of each run, Pallas kernels for 27% -> 28%
where the time goes in v7:
time: 513 us; the launch traced here: 510 us
  Pallas kernels  174 us (34%)
  waiting for transfers between devices  150 us (29%)
  starting transfers between devices  82.1 us (16%)
  other arithmetic  72.4 us (14%)
  local copies, waits for them, and re-layouts  16.2 us (3%)
  between operations  14.8 us (3%)
    ppermute x20, waiting for transfers between devices, swap_chip(): return lax.ppermute(values, 'chip', [(0, 1), (1, 0)])  81.7 us
    ppermute x24, starting transfers between devices, swap_core(): return lax.ppermute(values, 'core', [(0, 1), (1, 0)])  37.4 us
    ppermute x17, waiting for transfers between devices, swap_tp(): return lax.ppermute(values, 'tp', [(0, 1), (1, 0)])  35.2 us
    pallas_call x1, Pallas kernels, attend_back(): call(functools.partial(backward_kernel, rows), 'attend_back', rows * rows...  31.7 us
    pallas_call x1, Pallas kernels, feed(): call(functools.partial(feed_kernel, count), 'feed', rows * depth * units...  28.3 us
    pallas_call x1, Pallas kernels, feed_weights(): call(functools.partial(feed_weights_kernel, count), 'feed_weights', rows...  20.2 us
    another operation x12, other arithmetic  17.9 us
    ppermute x6, waiting for transfers between devices, pull_fsdp(): lax.ppermute(values, 'fsdp', [(i, (i - step) % count) for i in range(coun...  17.7 us
  transfers between devices with their start and end apart: 71, of which 27 were waited for; matrix products, arithmetic and copies ran while one was open for 14% of the time, Pallas kernels for 28%

profile of v7, /device:TPU:1, one launch (start us, length us, event | category | flops | bytes accessed | tf_op | source)
XLA Modules:
  0.0 509.9 jit_solution(16162539289455928014)
XLA Ops:
  21.6 6.2 %multiply_sine_fusion = (f32[2304,128]{1,0:T(8,128)}, f32[2304,128]{1,0:T(8,128)}) fusion(f32[128]{0:T(128)S(1)} %fusion.33, f32[2304]{0:T(1024)S(1)} %convert_element_type.326), kind=kLoop, calls=%fused_computation.22 | loop fusion | flops 294912 | bytes 2369024 | tf_op jit(solution)/shard_map/sin | solution.py:786
  51.5 12.1 %collective-permute-done.4.refs_2_ = bf16[4,192,384]{2,1,0:T(8,128)(2,1)S(1)} collective-permute-done((bf16[4,192,384]{2,1,0:T(8,128)(2,1)}, bf16[4,192,384]{2,1,0:T(8,128)(2,1)S(1)}, u32[]{:S(2)}, u32[]{:S(2)}) %collective-permute-start.4) | collective-permute-done | bytes 589856 | tf_op jit(solution)/shard_map/ppermute | solution.py:726
  88.9 11.8 %project.1 = (bf16[2176,256]{1,0:T(8,128)(2,1)}, bf16[2304,256]{1,0:T(8,128)(2,1)}, bf16[2304,256]{1,0:T(8,128)(2,1)}) custom-call(bf16[272,1536]{1,0:T(8,128)(2,1)} %get-tuple-element.152.refs_0_, bf16[272,1536]{1,0:T(8,128)(2,1)} %get-tuple-element.153.refs_1_, bf16[272,1536]{1,0:T(8,128)(2,1)} %get-tuple-element.154.refs_2_, ...), custom_call_target="tpu_custom_call" | custom-call | flops 5133828096 | bytes 6684672 | tf_op jit(solution)/shard_map/project/pallas_call | solution.py:176
  112.6 17.1 %attend.1 = (bf16[2176,256]{1,0:T(8,128)(2,1)}, f32[3,2304]{1,0:T(4,128)}) custom-call(s32[2,9]{1,0:T(2,128)} %pad_add_fusion.2.bounds, bf16[2176,256]{1,0:T(8,128)(2,1)} %get-tuple-element.163.q_ref, bf16[2304,256]{1,0:T(8,128)(2,1)} %get-tuple-element.164.k_ref, bf16[2304,256]{1,0:T(8,128)(2,1)} %get-tuple-element.165.v_ref, ...), custom_call_target="tpu_custom_call" | custom-call | flops 1818230784 | bytes 4718592 | tf_op jit(solution)/shard_map/attend/pallas_call | solution.py:420
  129.7 6.3 %out_project.1 = (bf16[1088,1536]{1,0:T(8,128)(2,1)}, bf16[1088,1536]{1,0:T(8,128)(2,1)}) custom-call(bf16[2176,256]{1,0:T(8,128)(2,1)} %get-tuple-element.173.o_ref, bf16[4,256,1536]{2,1,0:T(8,128)(2,1)} %place_weights.1.refs_8_.weight_ref), custom_call_target="tpu_custom_call" | custom-call | flops 1711276032 | bytes 6684672 | tf_op jit(solution)/shard_map/out_project/pallas_call | solution.py:257
  136.7 5.8 %collective-permute-done.23 = bf16[1088,1536]{1,0:T(8,128)(2,1)S(1)} collective-permute-done((bf16[1088,1536]{1,0:T(8,128)(2,1)}, bf16[1088,1536]{1,0:T(8,128)(2,1)S(1)}, u32[]{:S(2)}, u32[]{:S(2)}) %collective-permute-start.23) | collective-permute-done | bytes 3342368 | tf_op jit(solution)/shard_map/ppermute | solution.py:37
  147.8 8.9 %collective-permute-done.24 = bf16[128,1536]{1,0:T(8,128)(2,1)S(1)} collective-permute-done((bf16[128,1536]{1,0:T(8,128)(2,1)S(1)}, bf16[128,1536]{1,0:T(8,128)(2,1)S(1)}, u32[]{:S(2)}, u32[]{:S(2)}) %collective-permute-start.24) | collective-permute-done | bytes 393248 | tf_op jit(solution)/shard_map/ppermute | solution.py:33
  164.0 17.0 %collective-permute-done.26 = bf16[272,1536]{1,0:T(8,128)(2,1)S(1)} collective-permute-done((bf16[272,1536]{1,0:T(8,128)(2,1)S(1)}, bf16[272,1536]{1,0:T(8,128)(2,1)S(1)}, u32[]{:S(2)}, u32[]{:S(2)}) %collective-permute-start.26) | collective-permute-done | bytes 835616 | tf_op jit(solution)/shard_map/ppermute | solution.py:41
  185.8 16.8 %collective-permute-done.30.refs_2_ = bf16[272,1536]{1,0:T(8,128)(2,1)S(1)} collective-permute-done((bf16[272,1536]{1,0:T(8,128)(2,1)S(1)}, bf16[272,1536]{1,0:T(8,128)(2,1)S(1)}, u32[]{:S(2)}, u32[]{:S(2)}) %collective-permute-start.30) | collective-permute-done | bytes 835616 | tf_op jit(solution)/shard_map/ppermute | solution.py:33
  218.9 28.3 %feed.1 = (bf16[2176,512]{1,0:T(8,128)(2,1)}, bf16[2176,512]{1,0:T(8,128)(2,1)}, bf16[2176,512]{1,0:T(8,128)(2,1)}, bf16[1088,1536]{1,0:T(8,128)(2,1)}, bf16[1088,1536]{1,0:T(8,128)(2,1)}, /*index=5*/f32[8,1536]{1,0:T(8,128)}) custom-call(bf16[272,1536]{1,0:T(8,128)(2,1)} %copy-done.20, bf16[272,1536]{1,0:T(8,128)(2,1)} %copy-done.24, ...), custom_call_target="tpu_custom_call" | custom-call | flops 17112760320 | bytes 4718592 | tf_op jit(solution)/shard_map/feed/pallas_call | solution.py:588
  247.5 5.8 %collective-permute-done.37 = bf16[1088,1536]{1,0:T(8,128)(2,1)S(1)} collective-permute-done((bf16[1088,1536]{1,0:T(8,128)(2,1)}, bf16[1088,1536]{1,0:T(8,128)(2,1)S(1)}, u32[]{:S(2)}, u32[]{:S(2)}) %collective-permute-start.37) | collective-permute-done | bytes 3342368 | tf_op jit(solution)/shard_map/ppermute | solution.py:37
  257.9 7.7 %collective-permute-done.38 = bf16[128,1536]{1,0:T(8,128)(2,1)S(1)} collective-permute-done((bf16[128,1536]{1,0:T(8,128)(2,1)S(1)}, bf16[128,1536]{1,0:T(8,128)(2,1)S(1)}, u32[]{:S(2)}, u32[]{:S(2)}) %collective-permute-start.38) | collective-permute-done | bytes 393248 | tf_op jit(solution)/shard_map/ppermute | solution.py:33
  273.6 20.2 %feed_weights.1 = bf16[4,3,384,512]{3,2,1,0:T(8,128)(2,1)} custom-call(bf16[272,1536]{1,0:T(8,128)(2,1)} %copy-done.20, bf16[272,1536]{1,0:T(8,128)(2,1)} %copy-done.24, bf16[272,1536]{1,0:T(8,128)(2,1)} %copy-done.25, bf16[272,1536]{1,0:T(8,128)(2,1)} %copy-done.26, bf16[272,1536]{1,0:T(8,128)(2,1)} %copy-done.32, bf16[272,1536]{1,0:T(8,128)(2,1)} %copy-done.33, ...), custom_call_target="tpu_custom_call" | custom-call | flops 10267656192 | bytes 4718592 | tf_op jit(solution)/shard_map/feed_weights/pallas_call | solution.py:626
  301.9 7.4 %feed_out.1 = (bf16[1088,1536]{1,0:T(8,128)(2,1)}, bf16[1088,1536]{1,0:T(8,128)(2,1)}) custom-call(bf16[2176,512]{1,0:T(8,128)(2,1)} %get-tuple-element.206.refs_18_.hidden_ref, bf16[4,3,384,512]{3,2,1,0:T(8,128)(2,1)} %bitcast.49), custom_call_target="tpu_custom_call" | custom-call | flops 3422552064 | bytes 6684672 | tf_op jit(solution)/shard_map/feed_out/pallas_call | solution.py:651
  309.3 9.6 %collective-permute-done.43.refs_2_ = bf16[272,1536]{1,0:T(8,128)(2,1)} collective-permute-done((bf16[272,1536]{1,0:T(8,128)(2,1)}, bf16[272,1536]{1,0:T(8,128)(2,1)}, u32[]{:S(2)}, u32[]{:S(2)}) %collective-permute-start.43) | collective-permute-done | bytes 835616 | tf_op jit(solution)/shard_map/ppermute | solution.py:33
  327.3 7.7 %collective-permute-done.47 = bf16[128,1536]{1,0:T(8,128)(2,1)S(1)} collective-permute-done((bf16[128,1536]{1,0:T(8,128)(2,1)S(1)}, bf16[128,1536]{1,0:T(8,128)(2,1)S(1)}, u32[]{:S(2)}, u32[]{:S(2)}) %collective-permute-start.47) | collective-permute-done | bytes 393248 | tf_op jit(solution)/shard_map/ppermute | solution.py:41
  345.6 9.1 %out_back.1 = (bf16[2176,256]{1,0:T(8,128)(2,1)}, bf16[4,1,192,384]{3,2,1,0:T(8,128)(2,1)}) custom-call(bf16[2176,256]{1,0:T(8,128)(2,1)} %get-tuple-element.173.o_ref, bf16[4,256,1536]{2,1,0:T(8,128)(2,1)} %place_weights.1.refs_8_.weight_ref, bf16[272,1536]{1,0:T(8,128)(2,1)} %get-tuple-element.263.refs_0_, ...), custom_call_target="tpu_custom_call" | custom-call | flops 3422552064 | bytes 6684672 | tf_op jit(solution)/shard_map/out_back/pallas_call | solution.py:284
  362.6 31.7 %attend_back.1 = (bf16[2176,256]{1,0:T(8,128)(2,1)}, bf16[2304,256]{1,0:T(8,128)(2,1)}, bf16[2304,256]{1,0:T(8,128)(2,1)}) custom-call(s32[2,9]{1,0:T(2,128)} %pad_add_fusion.2.bounds, bf16[2176,256]{1,0:T(8,128)(2,1)} %get-tuple-element.163.q_ref, bf16[2304,256]{1,0:T(8,128)(2,1)} %get-tuple-element.164.k_ref, bf16[2304,256]{1,0:T(8,128)(2,1)} %get-tuple-element.165.v_ref, ...), custom_call_target="tpu_custom_call" | custom-call | flops 4545576960 | bytes 9437184 | tf_op jit(solution)/shard_map/attend_back/pallas_call | solution.py:503
  394.5 11.9 %project_back.1 = (bf16[1088,1536]{1,0:T(8,128)(2,1)}, bf16[1088,1536]{1,0:T(8,128)(2,1)}, f32[8,1536]{1,0:T(8,128)}) custom-call(bf16[2176,256]{1,0:T(8,128)(2,1)} %get-tuple-element.230.dq_ref, bf16[2304,256]{1,0:T(8,128)(2,1)} %get-tuple-element.223.dk_ref, bf16[2304,256]{1,0:T(8,128)(2,1)} %get-tuple-element.224.dv_ref, ...), custom_call_target="tpu_custom_call" | custom-call | flops 5133828096 | bytes 13369344 | tf_op jit(solution)/shard_map/project_back/pallas_call | solution.py:349
  408.6 12.4 %project_weights.1 = bf16[4,4,192,384]{3,2,1,0:T(8,128)(2,1)} custom-call(bf16[2176,256]{1,0:T(8,128)(2,1)} %get-tuple-element.230.dq_ref, bf16[2304,256]{1,0:T(8,128)(2,1)} %get-tuple-element.223.dk_ref, bf16[2304,256]{1,0:T(8,128)(2,1)} %get-tuple-element.224.dv_ref, bf16[4,1,192,384]{3,2,1,0:T(8,128)(2,1)} %get-tuple-element.231.done_ref, ...), custom_call_target="tpu_custom_call" | custom-call | flops 5133828096 | bytes 6684672 | tf_op jit(solution)/shard_map/project_weights/pallas_call | solution.py:316
  436.1 6.6 %collective-permute-done.58 = bf16[128,1536]{1,0:T(8,128)(2,1)S(1)} collective-permute-done((bf16[128,1536]{1,0:T(8,128)(2,1)S(1)}, bf16[128,1536]{1,0:T(8,128)(2,1)S(1)}, u32[]{:S(2)}, u32[]{:S(2)}) %collective-permute-start.58) | collective-permute-done | bytes 393248 | tf_op jit(solution)/shard_map/ppermute | solution.py:33
  448.1 17.3 %collective-permute-done.64 = f32[2,1536]{1,0:T(2,128)S(1)} collective-permute-done((f32[2,1536]{1,0:T(2,128)S(1)}, f32[2,1536]{1,0:T(2,128)S(1)}, u32[]{:S(2)}, u32[]{:S(2)}) %collective-permute-start.64) | collective-permute-done | bytes 12320 | tf_op jit(solution)/shard_map/ppermute | solution.py:33
  466.0 5.5 %all-to-all-start = ((f32[4,2,384]{2,1,0:T(2,128)}), f32[4,2,384]{2,1,0:T(2,128)S(1)}, u32[]{:S(2)}, u32[]{:S(2)}) async-start(f32[4,2,384]{2,1,0:T(2,128)} %pad_maximum_fusion.14), calls=%async_computation.2 | async-start | bytes 24576 | tf_op jit(solution)/shard_map/all_to_all | solution.py:745
  478.9 6.7 %finish_feed.1 = (f32[384,2048]{1,0:T(8,128)}, f32[384,2048]{1,0:T(8,128)}, f32[2048,384]{1,0:T(8,128)}) custom-call(bf16[3,384,512]{2,1,0:T(8,128)(2,1)} %reduce-scatter.3.cloned.1.call-done.own_ref, bf16[3,384,512]{2,1,0:T(8,128)(2,1)} %collective-permute-done.55.across_ref, bf16[2,3,384,512]{3,2,1,0:T(8,128)(2,1)} %collective-permute-done.61.came_ref), custom_call_target="tpu_custom_call" | custom-call | bytes 14155776 | tf_op jit(solution)/shard_map/finish_feed/pallas_call | solution.py:680
  (317 shorter events, 205.2 us)
Async XLA Ops:
  7.2 151.0 %all-gather.3.cloned.1.call-start = ((), (), s32[]{:S(2)}) async-start(), calls=%async_computation.5 | async-start | bytes 5898240 | tf_op jit(solution)/shard_map/all_gather | solution.py:798
  7.3 24.7 %collective-permute-start.2 = (bf16[272,1536]{1,0:T(8,128)(2,1)}, bf16[272,1536]{1,0:T(8,128)(2,1)}, u32[]{:S(2)}, u32[]{:S(2)}) collective-permute-start(bf16[272,1536]{1,0:T(8,128)(2,1)} %bitcast.36), channel_id=1, source_target_pairs={{0,4},{4,0},{1,5},{5,1},{2,6},{6,2},{3,7},{7,3},{8,12},{12,8},{9,1... | collective-permute-start | bytes 2506760 | tf_op jit(solution)/shard_map/ppermute | solution.py:33
  9.4 22.6 %collective-permute-start.1 = (bf16[272,1536]{1,0:T(8,128)(2,1)}, bf16[272,1536]{1,0:T(8,128)(2,1)S(1)}, u32[]{:S(2)}, u32[]{:S(2)}) collective-permute-start(bf16[272,1536]{1,0:T(8,128)(2,1)} %bitcast.37), channel_id=1, source_target_pairs={{0,1},{1,0},{2,3},{3,2},{4,5},{5,4},{6,7},{7,6},{8,9},{9,8},{10,11... | collective-permute-start | bytes 2506760 | tf_op jit(solution)/shard_map/ppermute | solution.py:41
  36.4 27.2 %collective-permute-start.6 = (bf16[272,1536]{1,0:T(8,128)(2,1)S(1)}, bf16[272,1536]{1,0:T(8,128)(2,1)S(1)}, u32[]{:S(2)}, u32[]{:S(2)}) collective-permute-start(bf16[272,1536]{1,0:T(8,128)(2,1)S(1)} %collective-permute-done.1), channel_id=1, source_target_pairs={{0,2},{2,0},{1,3},{3,1},{4,6},{6,4},{5,7},{7,5},{8,10},{10,8},{9,1... | collective-permute-start | bytes 2506760 | tf_op jit(solution)/shard_map/ppermute | solution.py:37
  38.9 25.7 %collective-permute-start.7 = (bf16[272,1536]{1,0:T(8,128)(2,1)}, bf16[272,1536]{1,0:T(8,128)(2,1)S(1)}, u32[]{:S(2)}, u32[]{:S(2)}) collective-permute-start(bf16[272,1536]{1,0:T(8,128)(2,1)} %collective-permute-done.2), channel_id=1, source_target_pairs={{0,2},{2,0},{1,3},{3,1},{4,6},{6,4},{5,7},{7,5},{8,10},{10,8},{9,1... | collective-permute-start | bytes 2506760 | tf_op jit(solution)/shard_map/ppermute | solution.py:37
  39.6 24.0 %collective-permute-start.5 = (bf16[272,1536]{1,0:T(8,128)(2,1)S(1)}, bf16[272,1536]{1,0:T(8,128)(2,1)S(1)}, u32[]{:S(2)}, u32[]{:S(2)}) collective-permute-start(bf16[272,1536]{1,0:T(8,128)(2,1)S(1)} %bitcast.38), channel_id=1, source_target_pairs={{0,2},{2,0},{1,3},{3,1},{4,6},{6,4},{5,7},{7,5},{8,10},{10,8},{9,1... | collective-permute-start | bytes 2506760 | tf_op jit(solution)/shard_map/ppermute | solution.py:37
  66.0 328.3 %reduce-scatter.3.cloned.1.call-start = ((), (), s32[]{:S(2)}) async-start(), calls=%async_computation.3 | async-start | bytes 5898240 | tf_op jit(solution)/shard_map/reduce_scatter | solution.py:751
  100.7 29.0 %collective-permute-start.18 = (bf16[272,1536]{1,0:T(8,128)(2,1)}, bf16[272,1536]{1,0:T(8,128)(2,1)}, u32[]{:S(2)}, u32[]{:S(2)}) collective-permute-start(bf16[272,1536]{1,0:T(8,128)(2,1)} %bitcast.2.refs_8_), channel_id=1, source_target_pairs={{0,2},{2,0},{1,3},{3,1},{4,6},{6,4},{5,7},{7,5},{8,10},{10,8},{9,1... | collective-permute-start | bytes 2506760 | tf_op jit(solution)/shard_map/ppermute | solution.py:37
  105.2 24.5 %collective-permute-start.19 = (bf16[272,1536]{1,0:T(8,128)(2,1)}, bf16[272,1536]{1,0:T(8,128)(2,1)}, u32[]{:S(2)}, u32[]{:S(2)}) collective-permute-start(bf16[272,1536]{1,0:T(8,128)(2,1)} %collective-permute-done.16.refs_9_), channel_id=1, source_target_pairs={{0,2},{2,0},{1,3},{3,1},{4,6},{6,4},{5,7},{7,5},{8,10},{10,8},{9,1... | collective-permute-start | bytes 2506760 | tf_op jit(solution)/shard_map/ppermute | solution.py:37
  105.3 24.5 %collective-permute-start.20 = (bf16[272,1536]{1,0:T(8,128)(2,1)}, bf16[272,1536]{1,0:T(8,128)(2,1)}, u32[]{:S(2)}, u32[]{:S(2)}) collective-permute-start(bf16[272,1536]{1,0:T(8,128)(2,1)} %collective-permute-done.17.refs_10_), channel_id=1, source_target_pairs={{0,2},{2,0},{1,3},{3,1},{4,6},{6,4},{5,7},{7,5},{8,10},{10,8},{9,1... | collective-permute-start | bytes 2506760 | tf_op jit(solution)/shard_map/ppermute | solution.py:37
  109.9 19.7 %collective-permute-start.21 = (bf16[128,1536]{1,0:T(8,128)(2,1)S(1)}, bf16[128,1536]{1,0:T(8,128)(2,1)S(1)}, u32[]{:S(2)}, u32[]{:S(2)}) collective-permute-start(bf16[128,1536]{1,0:T(8,128)(2,1)S(1)} %slice.204), channel_id=1, source_target_pairs={{0,1},{1,0},{2,3},{3,2},{4,5},{5,4},{6,7},{7,6},{8,9},{9,8},{10,11... | collective-permute-start | bytes 1179656 | tf_op jit(solution)/shard_map/ppermute | solution.py:41
  110.2 19.5 %collective-permute-start.22 = (bf16[144,1536]{1,0:T(8,128)(2,1)S(1)}, bf16[144,1536]{1,0:T(8,128)(2,1)S(1)}, u32[]{:S(2)}, u32[]{:S(2)}) collective-permute-start(bf16[144,1536]{1,0:T(8,128)(2,1)S(1)} %slice.205), channel_id=1, source_target_pairs={{0,4},{4,0},{1,5},{5,1},{2,6},{6,2},{3,7},{7,3},{8,12},{12,8},{9,1... | collective-permute-start | bytes 1327112 | tf_op jit(solution)/shard_map/ppermute | solution.py:33
  161.4 19.6 %collective-permute-start.26 = (bf16[272,1536]{1,0:T(8,128)(2,1)S(1)}, bf16[272,1536]{1,0:T(8,128)(2,1)S(1)}, u32[]{:S(2)}, u32[]{:S(2)}) collective-permute-start(bf16[272,1536]{1,0:T(8,128)(2,1)S(1)} %pad_maximum_fusion.5), channel_id=1, source_target_pairs={{0,1},{1,0},{2,3},{3,2},{4,5},{5,4},{6,7},{7,6},{8,9},{9,8},{10,11... | collective-permute-start | bytes 2506760 | tf_op jit(solution)/shard_map/ppermute | solution.py:41
  162.7 19.3 %collective-permute-start.27 = (bf16[272,1536]{1,0:T(8,128)(2,1)S(1)}, bf16[272,1536]{1,0:T(8,128)(2,1)S(1)}, u32[]{:S(2)}, u32[]{:S(2)}) collective-permute-start(bf16[272,1536]{1,0:T(8,128)(2,1)S(1)} %pad_maximum_fusion.6), channel_id=1, source_target_pairs={{0,4},{4,0},{1,5},{5,1},{2,6},{6,2},{3,7},{7,3},{8,12},{12,8},{9,1... | collective-permute-start | bytes 2506760 | tf_op jit(solution)/shard_map/ppermute | solution.py:33
  270.3 23.5 %collective-permute-start.39 = (bf16[272,1536]{1,0:T(8,128)(2,1)}, bf16[272,1536]{1,0:T(8,128)(2,1)}, u32[]{:S(2)}, u32[]{:S(2)}) collective-permute-start(bf16[272,1536]{1,0:T(8,128)(2,1)} %pad_maximum_fusion.7), channel_id=1, source_target_pairs={{0,1},{1,0},{2,3},{3,2},{4,5},{5,4},{6,7},{7,6},{8,9},{9,8},{10,11... | collective-permute-start | bytes 2506760 | tf_op jit(solution)/shard_map/ppermute | solution.py:41
  272.5 21.4 %collective-permute-start.41 = (bf16[272,1536]{1,0:T(8,128)(2,1)}, bf16[272,1536]{1,0:T(8,128)(2,1)}, u32[]{:S(2)}, u32[]{:S(2)}) collective-permute-start(bf16[272,1536]{1,0:T(8,128)(2,1)} %pad_maximum_fusion.8), channel_id=1, source_target_pairs={{0,4},{4,0},{1,5},{5,1},{2,6},{6,2},{3,7},{7,3},{8,12},{12,8},{9,1... | collective-permute-start | bytes 2506760 | tf_op jit(solution)/shard_map/ppermute | solution.py:33
  293.8 184.0 %reduce-scatter.5.cloned.1.call-start = ((), (), s32[]{:S(2)}) async-start(), calls=%async_computation.4 | async-start | bytes 2949120 | tf_op jit(solution)/shard_map/reduce_scatter | solution.py:751
  360.2 34.1 %collective-permute-start.53 = (bf16[272,1536]{1,0:T(8,128)(2,1)}, bf16[272,1536]{1,0:T(8,128)(2,1)}, u32[]{:S(2)}, u32[]{:S(2)}) collective-permute-start(bf16[272,1536]{1,0:T(8,128)(2,1)} %pad_maximum_fusion.9), channel_id=1, source_target_pairs={{0,1},{1,0},{2,3},{3,2},{4,5},{5,4},{6,7},{7,6},{8,9},{9,8},{10,11... | collective-permute-start | bytes 2506760 | tf_op jit(solution)/shard_map/ppermute | solution.py:41
  361.3 33.0 %collective-permute-start.54 = (bf16[272,1536]{1,0:T(8,128)(2,1)}, bf16[272,1536]{1,0:T(8,128)(2,1)}, u32[]{:S(2)}, u32[]{:S(2)}) collective-permute-start(bf16[272,1536]{1,0:T(8,128)(2,1)} %pad_maximum_fusion.10), channel_id=1, source_target_pairs={{0,4},{4,0},{1,5},{5,1},{2,6},{6,2},{3,7},{7,3},{8,12},{12,8},{9,1... | collective-permute-start | bytes 2506760 | tf_op jit(solution)/shard_map/ppermute | solution.py:33
  394.3 26.7 %collective-permute-start.55 = (bf16[3,384,512]{2,1,0:T(8,128)(2,1)}, bf16[3,384,512]{2,1,0:T(8,128)(2,1)}, u32[]{:S(2)}, u32[]{:S(2)}) collective-permute-start(bf16[3,384,512]{2,1,0:T(8,128)(2,1)} %reduce-scatter.3.cloned.1.call-done.own_ref), channel_id=1, source_target_pairs={{0,4},{4,0},{1,5},{5,1},{2,6},{6,2},{3,7},{7,3},{8,12},{12,8},{9,1... | collective-permute-start | bytes 3538952 | tf_op jit(solution)/shard_map/ppermute | solution.py:33
  423.5 22.0 %collective-permute-start.60 = (f32[2,1536]{1,0:T(2,128)S(1)}, f32[2,1536]{1,0:T(2,128)S(1)}, u32[]{:S(2)}, u32[]{:S(2)}) collective-permute-start(f32[2,1536]{1,0:T(2,128)S(1)} %fusion.35), channel_id=1, source_target_pairs={{0,2},{2,0},{1,3},{3,1},{4,6},{6,4},{5,7},{7,5},{8,10},{10,8},{9,1... | collective-permute-start | bytes 36872 | tf_op jit(solution)/shard_map/ppermute | solution.py:37
  425.6 19.9 %collective-permute-start.61 = (bf16[2,3,384,512]{3,2,1,0:T(8,128)(2,1)S(1)}, bf16[2,3,384,512]{3,2,1,0:T(8,128)(2,1)}, u32[]{:S(2)}, u32[]{:S(2)}) collective-permute-start(bf16[2,3,384,512]{3,2,1,0:T(8,128)(2,1)S(1)} %pad_maximum_fusion), channel_id=1, source_target_pairs={{0,2},{2,0},{1,3},{3,1},{4,6},{6,4},{5,7},{7,5},{8,10},{10,8},{9,1... | collective-permute-start | bytes 7077896 | tf_op jit(solution)/shard_map/ppermute | solution.py:37
  445.5 19.9 %collective-permute-start.62 = (bf16[272,1536]{1,0:T(8,128)(2,1)S(1)}, bf16[272,1536]{1,0:T(8,128)(2,1)}, u32[]{:S(2)}, u32[]{:S(2)}) collective-permute-start(bf16[272,1536]{1,0:T(8,128)(2,1)S(1)} %pad_maximum_fusion.11), channel_id=1, source_target_pairs={{0,1},{1,0},{2,3},{3,2},{4,5},{5,4},{6,7},{7,6},{8,9},{9,8},{10,11... | collective-permute-start | bytes 2506760 | tf_op jit(solution)/shard_map/ppermute | solution.py:41
  446.5 18.9 %collective-permute-start.63 = (bf16[272,1536]{1,0:T(8,128)(2,1)S(1)}, bf16[272,1536]{1,0:T(8,128)(2,1)}, u32[]{:S(2)}, u32[]{:S(2)}) collective-permute-start(bf16[272,1536]{1,0:T(8,128)(2,1)S(1)} %pad_maximum_fusion.12), channel_id=1, source_target_pairs={{0,4},{4,0},{1,5},{5,1},{2,6},{6,2},{3,7},{7,3},{8,12},{12,8},{9,1... | collective-permute-start | bytes 2506760 | tf_op jit(solution)/shard_map/ppermute | solution.py:33
  (83 other events, 801.9 us)
Sparse Core Ops, SparseCore 0:
  66.1 92.1 all-gather.2
  294.0 84.3 reduce-scatter.2
  423.6 48.6 reduce-scatter.4

commit v8 on v7

--- a/solution.py
+++ b/solution.py
@@ -774,10 +774,11 @@
 
     if both_links:
         first = lambda values: [values, swap_tp(values), swap_chip(values)]
-        second = lambda blocks: widen_core(blocks) + far_block(*blocks)[3:]
+        second = lambda blocks, *earlier: widen_core(after(blocks, *earlier)) + far_block(*blocks)[3:]
         third = lambda blocks: blocks[:3] + blocks[6:] + blocks[3:6] + [swap_core(blocks[6])]
     else:
-        first, second, third = lambda values: widen_planes(values)[0], widen_core, lambda blocks: blocks
+        first, third = lambda values: widen_planes(values)[0], lambda blocks: blocks
+        second = lambda blocks, *earlier: widen_core(after(blocks, *earlier))
     ring = [own_piece]
     position = after(jnp.arange(keys, dtype=jnp.int32), own_piece).astype(F32)
     pair_index = (jnp.arange(LANES, dtype=jnp.int32) % (HEAD_DIM // 2)).astype(F32)
@@ -787,9 +788,10 @@
     )
     ring.append(block)
     ids_chip = jnp.concatenate(in_order(segment_ids, ids_other, core == 0))
+    hop = pull_fsdp(ring[-1], 1)
     block, own, ids_across, gains = together(
-        pull_fsdp(ring[-1], 1),
-        second(own),
+        hop,
+        second(own, hop),
         swap_chip(ids_chip),
         gather_gains(after(jnp.stack([gain_attn, gain_ffn]), ids_other)),
     )

time: 513 us -> 507 us (0.988)
  Pallas kernels: 174 us -> 180 us
  starting transfers between devices: 82.1 us -> 76.7 us
    ppermute x17, waiting for transfers between devices: 35.2 us -> 29.1 us  [swap_tp(): return lax.ppermute(values, 'tp', [(0, 1), (1, 0)])]
  transfers between devices with their start and end apart: 71 -> 71, of which waited for: 27 -> 25; matrix products, arithmetic and copies ran while one was open for 14% -> 15% of each run, Pallas kernels for 28% -> 29%
where the time goes in v8:
time: 507 us; the launch traced here: 505 us
  Pallas kernels  180 us (36%)
  waiting for transfers between devices  146 us (29%)
  starting transfers between devices  76.7 us (15%)
  other arithmetic  72.1 us (14%)
  local copies, waits for them, and re-layouts  15.8 us (3%)
  between operations  14.8 us (3%)
    ppermute x20, waiting for transfers between devices, swap_chip(): return lax.ppermute(values, 'chip', [(0, 1), (1, 0)])  81.8 us
    pallas_call x1, Pallas kernels, attend_back(): call(functools.partial(backward_kernel, rows), 'attend_back', rows * rows...  35.5 us
    ppermute x24, starting transfers between devices, swap_core(): return lax.ppermute(values, 'core', [(0, 1), (1, 0)])  34 us
    ppermute x17, waiting for transfers between devices, swap_tp(): return lax.ppermute(values, 'tp', [(0, 1), (1, 0)])  29.1 us
    pallas_call x1, Pallas kernels, feed(): call(functools.partial(feed_kernel, count), 'feed', rows * depth * units...  28.3 us
    pallas_call x1, Pallas kernels, feed_weights(): call(functools.partial(feed_weights_kernel, count), 'feed_weights', rows...  20.2 us
    pallas_call x1, Pallas kernels, attend(): call(functools.partial(forward_kernel, rows), 'attend', rows * rows * hea...  19.2 us
    ppermute x6, waiting for transfers between devices, pull_fsdp(): lax.ppermute(values, 'fsdp', [(i, (i - step) % count) for i in range(coun...  18.9 us
  transfers between devices with their start and end apart: 71, of which 25 were waited for; matrix products, arithmetic and copies ran while one was open for 15% of the time, Pallas kernels for 29%

profile of v8, /device:TPU:1, one launch (start us, length us, event | category | flops | bytes accessed | tf_op | source)
XLA Modules:
  0.0 505.4 jit_solution(6790174600937463707)
XLA Ops:
  21.6 6.2 %multiply_sine_fusion = (f32[2304,128]{1,0:T(8,128)}, f32[2304,128]{1,0:T(8,128)}) fusion(f32[128]{0:T(128)S(1)} %fusion.33, f32[2304]{0:T(1024)S(1)} %convert_element_type.326), kind=kLoop, calls=%fused_computation.22 | loop fusion | flops 294912 | bytes 2369024 | tf_op jit(solution)/shard_map/sin | solution.py:787
  39.2 10.5 %collective-permute-done.4.refs_2_ = bf16[4,192,384]{2,1,0:T(8,128)(2,1)S(1)} collective-permute-done((bf16[4,192,384]{2,1,0:T(8,128)(2,1)S(1)}, bf16[4,192,384]{2,1,0:T(8,128)(2,1)S(1)}, u32[]{:S(2)}, u32[]{:S(2)}) %collective-permute-start.4) | collective-permute-done | bytes 589856 | tf_op jit(solution)/shard_map/ppermute | solution.py:726
  85.9 11.8 %project.1 = (bf16[2176,256]{1,0:T(8,128)(2,1)}, bf16[2304,256]{1,0:T(8,128)(2,1)}, bf16[2304,256]{1,0:T(8,128)(2,1)}) custom-call(bf16[272,1536]{1,0:T(8,128)(2,1)} %get-tuple-element.161.refs_0_, bf16[272,1536]{1,0:T(8,128)(2,1)} %get-tuple-element.162.refs_1_, bf16[272,1536]{1,0:T(8,128)(2,1)} %get-tuple-element.163.refs_2_, ...), custom_call_target="tpu_custom_call" | custom-call | flops 5133828096 | bytes 6684672 | tf_op jit(solution)/shard_map/project/pallas_call | solution.py:176
  107.5 19.2 %attend.1 = (bf16[2176,256]{1,0:T(8,128)(2,1)}, f32[3,2304]{1,0:T(4,128)}) custom-call(s32[2,9]{1,0:T(2,128)} %pad_add_fusion.2.bounds, bf16[2176,256]{1,0:T(8,128)(2,1)} %get-tuple-element.172.q_ref, bf16[2304,256]{1,0:T(8,128)(2,1)} %get-tuple-element.173.k_ref, bf16[2304,256]{1,0:T(8,128)(2,1)} %get-tuple-element.174.v_ref, ...), custom_call_target="tpu_custom_call" | custom-call | flops 1818230784 | bytes 4718592 | tf_op jit(solution)/shard_map/attend/pallas_call | solution.py:420
  126.8 6.3 %out_project.1 = (bf16[1088,1536]{1,0:T(8,128)(2,1)}, bf16[1088,1536]{1,0:T(8,128)(2,1)}) custom-call(bf16[2176,256]{1,0:T(8,128)(2,1)} %get-tuple-element.185.o_ref, bf16[4,256,1536]{2,1,0:T(8,128)(2,1)} %place_weights.1.refs_8_.weight_ref), custom_call_target="tpu_custom_call" | custom-call | flops 1711276032 | bytes 6684672 | tf_op jit(solution)/shard_map/out_project/pallas_call | solution.py:257
  133.7 5.8 %collective-permute-done.23 = bf16[1088,1536]{1,0:T(8,128)(2,1)S(1)} collective-permute-done((bf16[1088,1536]{1,0:T(8,128)(2,1)}, bf16[1088,1536]{1,0:T(8,128)(2,1)S(1)}, u32[]{:S(2)}, u32[]{:S(2)}) %collective-permute-start.23) | collective-permute-done | bytes 3342368 | tf_op jit(solution)/shard_map/ppermute | solution.py:37
  144.8 8.8 %collective-permute-done.24 = bf16[128,1536]{1,0:T(8,128)(2,1)S(1)} collective-permute-done((bf16[128,1536]{1,0:T(8,128)(2,1)S(1)}, bf16[128,1536]{1,0:T(8,128)(2,1)S(1)}, u32[]{:S(2)}, u32[]{:S(2)}) %collective-permute-start.24) | collective-permute-done | bytes 393248 | tf_op jit(solution)/shard_map/ppermute | solution.py:33
  158.2 17.9 %collective-permute-done.26 = bf16[272,1536]{1,0:T(8,128)(2,1)S(1)} collective-permute-done((bf16[272,1536]{1,0:T(8,128)(2,1)S(1)}, bf16[272,1536]{1,0:T(8,128)(2,1)S(1)}, u32[]{:S(2)}, u32[]{:S(2)}) %collective-permute-start.26) | collective-permute-done | bytes 835616 | tf_op jit(solution)/shard_map/ppermute | solution.py:41
  180.1 15.8 %collective-permute-done.30.refs_2_ = bf16[272,1536]{1,0:T(8,128)(2,1)S(1)} collective-permute-done((bf16[272,1536]{1,0:T(8,128)(2,1)S(1)}, bf16[272,1536]{1,0:T(8,128)(2,1)S(1)}, u32[]{:S(2)}, u32[]{:S(2)}) %collective-permute-start.30) | collective-permute-done | bytes 835616 | tf_op jit(solution)/shard_map/ppermute | solution.py:33
  204.9 5.8 %collective-permute-start.36 = (bf16[272,1536]{1,0:T(8,128)(2,1)S(1)}, bf16[272,1536]{1,0:T(8,128)(2,1)}, u32[]{:S(2)}, u32[]{:S(2)}) collective-permute-start(bf16[272,1536]{1,0:T(8,128)(2,1)S(1)} %constant_dynamic-update-slice_fusion.8.refs_3_), channel_id=1, source_target_pairs={{0,2},{2,0},{1,3},{3,1},{4,6},{6,4},{5,7},{7,5},{8,10},{10,8},{9,1... | collective-permute-start | bytes 2506760 | tf_op jit(solution)/shard_map/ppermute | solution.py:37
  212.8 28.3 %feed.1 = (bf16[2176,512]{1,0:T(8,128)(2,1)}, bf16[2176,512]{1,0:T(8,128)(2,1)}, bf16[2176,512]{1,0:T(8,128)(2,1)}, bf16[1088,1536]{1,0:T(8,128)(2,1)}, bf16[1088,1536]{1,0:T(8,128)(2,1)}, /*index=5*/f32[8,1536]{1,0:T(8,128)}) custom-call(bf16[272,1536]{1,0:T(8,128)(2,1)} %copy-done.20, bf16[272,1536]{1,0:T(8,128)(2,1)} %copy-done.25, ...), custom_call_target="tpu_custom_call" | custom-call | flops 17112760320 | bytes 4718592 | tf_op jit(solution)/shard_map/feed/pallas_call | solution.py:588
  241.5 5.8 %collective-permute-done.37 = bf16[1088,1536]{1,0:T(8,128)(2,1)S(1)} collective-permute-done((bf16[1088,1536]{1,0:T(8,128)(2,1)}, bf16[1088,1536]{1,0:T(8,128)(2,1)S(1)}, u32[]{:S(2)}, u32[]{:S(2)}) %collective-permute-start.37) | collective-permute-done | bytes 3342368 | tf_op jit(solution)/shard_map/ppermute | solution.py:37
  251.9 7.7 %collective-permute-done.38 = bf16[128,1536]{1,0:T(8,128)(2,1)S(1)} collective-permute-done((bf16[128,1536]{1,0:T(8,128)(2,1)S(1)}, bf16[128,1536]{1,0:T(8,128)(2,1)S(1)}, u32[]{:S(2)}, u32[]{:S(2)}) %collective-permute-start.38) | collective-permute-done | bytes 393248 | tf_op jit(solution)/shard_map/ppermute | solution.py:33
  266.7 20.2 %feed_weights.1 = bf16[4,3,384,512]{3,2,1,0:T(8,128)(2,1)} custom-call(bf16[272,1536]{1,0:T(8,128)(2,1)} %copy-done.20, bf16[272,1536]{1,0:T(8,128)(2,1)} %copy-done.25, bf16[272,1536]{1,0:T(8,128)(2,1)} %copy-done.26, bf16[272,1536]{1,0:T(8,128)(2,1)} %copy-done.27, bf16[272,1536]{1,0:T(8,128)(2,1)} %copy-done.33, bf16[272,1536]{1,0:T(8,128)(2,1)} %copy-done.34, ...), custom_call_target="tpu_custom_call" | custom-call | flops 10267656192 | bytes 4718592 | tf_op jit(solution)/shard_map/feed_weights/pallas_call | solution.py:626
  296.9 7.4 %feed_out.1 = (bf16[1088,1536]{1,0:T(8,128)(2,1)}, bf16[1088,1536]{1,0:T(8,128)(2,1)}) custom-call(bf16[2176,512]{1,0:T(8,128)(2,1)} %get-tuple-element.218.refs_18_.hidden_ref, bf16[4,3,384,512]{3,2,1,0:T(8,128)(2,1)} %bitcast.49), custom_call_target="tpu_custom_call" | custom-call | flops 3422552064 | bytes 6684672 | tf_op jit(solution)/shard_map/feed_out/pallas_call | solution.py:651
  304.4 8.1 %collective-permute-done.43.refs_2_ = bf16[272,1536]{1,0:T(8,128)(2,1)} collective-permute-done((bf16[272,1536]{1,0:T(8,128)(2,1)}, bf16[272,1536]{1,0:T(8,128)(2,1)}, u32[]{:S(2)}, u32[]{:S(2)}) %collective-permute-start.43) | collective-permute-done | bytes 835616 | tf_op jit(solution)/shard_map/ppermute | solution.py:33
  321.3 7.7 %collective-permute-done.47 = bf16[128,1536]{1,0:T(8,128)(2,1)S(1)} collective-permute-done((bf16[128,1536]{1,0:T(8,128)(2,1)S(1)}, bf16[128,1536]{1,0:T(8,128)(2,1)S(1)}, u32[]{:S(2)}, u32[]{:S(2)}) %collective-permute-start.47) | collective-permute-done | bytes 393248 | tf_op jit(solution)/shard_map/ppermute | solution.py:41
  338.7 9.1 %out_back.1 = (bf16[2176,256]{1,0:T(8,128)(2,1)}, bf16[4,1,192,384]{3,2,1,0:T(8,128)(2,1)}) custom-call(bf16[2176,256]{1,0:T(8,128)(2,1)} %get-tuple-element.185.o_ref, bf16[4,256,1536]{2,1,0:T(8,128)(2,1)} %place_weights.1.refs_8_.weight_ref, bf16[272,1536]{1,0:T(8,128)(2,1)} %get-tuple-element.275.refs_0_, ...), custom_call_target="tpu_custom_call" | custom-call | flops 3422552064 | bytes 6684672 | tf_op jit(solution)/shard_map/out_back/pallas_call | solution.py:284
  356.6 35.5 %attend_back.1 = (bf16[2176,256]{1,0:T(8,128)(2,1)}, bf16[2304,256]{1,0:T(8,128)(2,1)}, bf16[2304,256]{1,0:T(8,128)(2,1)}) custom-call(s32[2,9]{1,0:T(2,128)} %pad_add_fusion.2.bounds, bf16[2176,256]{1,0:T(8,128)(2,1)} %get-tuple-element.172.q_ref, bf16[2304,256]{1,0:T(8,128)(2,1)} %get-tuple-element.173.k_ref, bf16[2304,256]{1,0:T(8,128)(2,1)} %get-tuple-element.174.v_ref, ...), custom_call_target="tpu_custom_call" | custom-call | flops 4545576960 | bytes 9437184 | tf_op jit(solution)/shard_map/attend_back/pallas_call | solution.py:503
  393.4 11.9 %project_back.1 = (bf16[1088,1536]{1,0:T(8,128)(2,1)}, bf16[1088,1536]{1,0:T(8,128)(2,1)}, f32[8,1536]{1,0:T(8,128)}) custom-call(bf16[2176,256]{1,0:T(8,128)(2,1)} %get-tuple-element.242.dq_ref, bf16[2304,256]{1,0:T(8,128)(2,1)} %get-tuple-element.235.dk_ref, bf16[2304,256]{1,0:T(8,128)(2,1)} %get-tuple-element.236.dv_ref, ...), custom_call_target="tpu_custom_call" | custom-call | flops 5133828096 | bytes 13369344 | tf_op jit(solution)/shard_map/project_back/pallas_call | solution.py:349
  406.5 12.4 %project_weights.1 = bf16[4,4,192,384]{3,2,1,0:T(8,128)(2,1)} custom-call(bf16[2176,256]{1,0:T(8,128)(2,1)} %get-tuple-element.242.dq_ref, bf16[2304,256]{1,0:T(8,128)(2,1)} %get-tuple-element.235.dk_ref, bf16[2304,256]{1,0:T(8,128)(2,1)} %get-tuple-element.236.dv_ref, bf16[4,1,192,384]{3,2,1,0:T(8,128)(2,1)} %get-tuple-element.243.done_ref, ...), custom_call_target="tpu_custom_call" | custom-call | flops 5133828096 | bytes 6684672 | tf_op jit(solution)/shard_map/project_weights/pallas_call | solution.py:316
  433.9 7.3 %collective-permute-done.58 = bf16[128,1536]{1,0:T(8,128)(2,1)S(1)} collective-permute-done((bf16[128,1536]{1,0:T(8,128)(2,1)S(1)}, bf16[128,1536]{1,0:T(8,128)(2,1)S(1)}, u32[]{:S(2)}, u32[]{:S(2)}) %collective-permute-start.58) | collective-permute-done | bytes 393248 | tf_op jit(solution)/shard_map/ppermute | solution.py:33
  445.7 17.2 %collective-permute-done.64 = f32[2,1536]{1,0:T(2,128)S(1)} collective-permute-done((f32[2,1536]{1,0:T(2,128)S(1)}, f32[2,1536]{1,0:T(2,128)S(1)}, u32[]{:S(2)}, u32[]{:S(2)}) %collective-permute-start.64) | collective-permute-done | bytes 12320 | tf_op jit(solution)/shard_map/ppermute | solution.py:33
  474.2 6.7 %finish_feed.1 = (f32[384,2048]{1,0:T(8,128)}, f32[384,2048]{1,0:T(8,128)}, f32[2048,384]{1,0:T(8,128)}) custom-call(bf16[3,384,512]{2,1,0:T(8,128)(2,1)} %reduce-scatter.3.cloned.1.call-done.own_ref, bf16[3,384,512]{2,1,0:T(8,128)(2,1)} %collective-permute-done.55.across_ref, bf16[2,3,384,512]{3,2,1,0:T(8,128)(2,1)} %collective-permute-done.61.came_ref), custom_call_target="tpu_custom_call" | custom-call | bytes 14155776 | tf_op jit(solution)/shard_map/finish_feed/pallas_call | solution.py:680
  (319 shorter events, 197.0 us)
Async XLA Ops:
  7.2 147.2 %all-gather.3.cloned.1.call-start = ((), (), s32[]{:S(2)}) async-start(), calls=%async_computation.5 | async-start | bytes 5898240 | tf_op jit(solution)/shard_map/all_gather | solution.py:800
  7.3 24.7 %collective-permute-start.2 = (bf16[272,1536]{1,0:T(8,128)(2,1)}, bf16[272,1536]{1,0:T(8,128)(2,1)}, u32[]{:S(2)}, u32[]{:S(2)}) collective-permute-start(bf16[272,1536]{1,0:T(8,128)(2,1)} %bitcast.36), channel_id=1, source_target_pairs={{0,4},{4,0},{1,5},{5,1},{2,6},{6,2},{3,7},{7,3},{8,12},{12,8},{9,1... | collective-permute-start | bytes 2506760 | tf_op jit(solution)/shard_map/ppermute | solution.py:33
  9.4 22.6 %collective-permute-start.1 = (bf16[272,1536]{1,0:T(8,128)(2,1)}, bf16[272,1536]{1,0:T(8,128)(2,1)S(1)}, u32[]{:S(2)}, u32[]{:S(2)}) collective-permute-start(bf16[272,1536]{1,0:T(8,128)(2,1)} %bitcast.37), channel_id=1, source_target_pairs={{0,1},{1,0},{2,3},{3,2},{4,5},{5,4},{6,7},{7,6},{8,9},{9,8},{10,11... | collective-permute-start | bytes 2506760 | tf_op jit(solution)/shard_map/ppermute | solution.py:41
  60.3 19.2 %collective-permute-start.17 = (bf16[272,1536]{1,0:T(8,128)(2,1)}, bf16[272,1536]{1,0:T(8,128)(2,1)}, u32[]{:S(2)}, u32[]{:S(2)}) collective-permute-start(bf16[272,1536]{1,0:T(8,128)(2,1)} %bitcast.2.refs_8_), channel_id=1, source_target_pairs={{0,4},{4,0},{1,5},{5,1},{2,6},{6,2},{3,7},{7,3},{8,12},{12,8},{9,1... | collective-permute-start | bytes 2506760 | tf_op jit(solution)/shard_map/ppermute | solution.py:33
  60.5 19.0 %collective-permute-start.16 = (bf16[272,1536]{1,0:T(8,128)(2,1)}, bf16[272,1536]{1,0:T(8,128)(2,1)}, u32[]{:S(2)}, u32[]{:S(2)}) collective-permute-start(bf16[272,1536]{1,0:T(8,128)(2,1)} %bitcast.2.refs_8_), channel_id=1, source_target_pairs={{0,1},{1,0},{2,3},{3,2},{4,5},{5,4},{6,7},{7,6},{8,9},{9,8},{10,11... | collective-permute-start | bytes 2506760 | tf_op jit(solution)/shard_map/ppermute | solution.py:41
  60.8 331.3 %reduce-scatter.3.cloned.1.call-start = ((), (), s32[]{:S(2)}) async-start(), calls=%async_computation.3 | async-start | bytes 5898240 | tf_op jit(solution)/shard_map/reduce_scatter | solution.py:751
  97.7 29.1 %collective-permute-start.18 = (bf16[272,1536]{1,0:T(8,128)(2,1)}, bf16[272,1536]{1,0:T(8,128)(2,1)}, u32[]{:S(2)}, u32[]{:S(2)}) collective-permute-start(bf16[272,1536]{1,0:T(8,128)(2,1)} %bitcast.2.refs_8_), channel_id=1, source_target_pairs={{0,2},{2,0},{1,3},{3,1},{4,6},{6,4},{5,7},{7,5},{8,10},{10,8},{9,1... | collective-permute-start | bytes 2506760 | tf_op jit(solution)/shard_map/ppermute | solution.py:37
  100.1 26.7 %collective-permute-start.19 = (bf16[272,1536]{1,0:T(8,128)(2,1)}, bf16[272,1536]{1,0:T(8,128)(2,1)}, u32[]{:S(2)}, u32[]{:S(2)}) collective-permute-start(bf16[272,1536]{1,0:T(8,128)(2,1)} %collective-permute-done.16.refs_9_), channel_id=1, source_target_pairs={{0,2},{2,0},{1,3},{3,1},{4,6},{6,4},{5,7},{7,5},{8,10},{10,8},{9,1... | collective-permute-start | bytes 2506760 | tf_op jit(solution)/shard_map/ppermute | solution.py:37
  100.1 26.7 %collective-permute-start.20 = (bf16[272,1536]{1,0:T(8,128)(2,1)}, bf16[272,1536]{1,0:T(8,128)(2,1)}, u32[]{:S(2)}, u32[]{:S(2)}) collective-permute-start(bf16[272,1536]{1,0:T(8,128)(2,1)} %collective-permute-done.17.refs_10_), channel_id=1, source_target_pairs={{0,2},{2,0},{1,3},{3,1},{4,6},{6,4},{5,7},{7,5},{8,10},{10,8},{9,1... | collective-permute-start | bytes 2506760 | tf_op jit(solution)/shard_map/ppermute | solution.py:37
  104.7 21.9 %collective-permute-start.21 = (bf16[128,1536]{1,0:T(8,128)(2,1)S(1)}, bf16[128,1536]{1,0:T(8,128)(2,1)S(1)}, u32[]{:S(2)}, u32[]{:S(2)}) collective-permute-start(bf16[128,1536]{1,0:T(8,128)(2,1)S(1)} %slice.204), channel_id=1, source_target_pairs={{0,1},{1,0},{2,3},{3,2},{4,5},{5,4},{6,7},{7,6},{8,9},{9,8},{10,11... | collective-permute-start | bytes 1179656 | tf_op jit(solution)/shard_map/ppermute | solution.py:41
  105.1 21.6 %collective-permute-start.22 = (bf16[144,1536]{1,0:T(8,128)(2,1)S(1)}, bf16[144,1536]{1,0:T(8,128)(2,1)S(1)}, u32[]{:S(2)}, u32[]{:S(2)}) collective-permute-start(bf16[144,1536]{1,0:T(8,128)(2,1)S(1)} %slice.205), channel_id=1, source_target_pairs={{0,4},{4,0},{1,5},{5,1},{2,6},{6,2},{3,7},{7,3},{8,12},{12,8},{9,1... | collective-permute-start | bytes 1327112 | tf_op jit(solution)/shard_map/ppermute | solution.py:33
  157.5 18.6 %collective-permute-start.26 = (bf16[272,1536]{1,0:T(8,128)(2,1)S(1)}, bf16[272,1536]{1,0:T(8,128)(2,1)S(1)}, u32[]{:S(2)}, u32[]{:S(2)}) collective-permute-start(bf16[272,1536]{1,0:T(8,128)(2,1)S(1)} %pad_maximum_fusion.5), channel_id=1, source_target_pairs={{0,1},{1,0},{2,3},{3,2},{4,5},{5,4},{6,7},{7,6},{8,9},{9,8},{10,11... | collective-permute-start | bytes 2506760 | tf_op jit(solution)/shard_map/ppermute | solution.py:41
  157.8 18.3 %collective-permute-start.27 = (bf16[272,1536]{1,0:T(8,128)(2,1)S(1)}, bf16[272,1536]{1,0:T(8,128)(2,1)S(1)}, u32[]{:S(2)}, u32[]{:S(2)}) collective-permute-start(bf16[272,1536]{1,0:T(8,128)(2,1)S(1)} %pad_maximum_fusion.6), channel_id=1, source_target_pairs={{0,4},{4,0},{1,5},{5,1},{2,6},{6,2},{3,7},{7,3},{8,12},{12,8},{9,1... | collective-permute-start | bytes 2506760 | tf_op jit(solution)/shard_map/ppermute | solution.py:33
  265.2 21.7 %collective-permute-start.39 = (bf16[272,1536]{1,0:T(8,128)(2,1)}, bf16[272,1536]{1,0:T(8,128)(2,1)}, u32[]{:S(2)}, u32[]{:S(2)}) collective-permute-start(bf16[272,1536]{1,0:T(8,128)(2,1)} %pad_maximum_fusion.7), channel_id=1, source_target_pairs={{0,1},{1,0},{2,3},{3,2},{4,5},{5,4},{6,7},{7,6},{8,9},{9,8},{10,11... | collective-permute-start | bytes 2506760 | tf_op jit(solution)/shard_map/ppermute | solution.py:41
  266.4 20.5 %collective-permute-start.41 = (bf16[272,1536]{1,0:T(8,128)(2,1)}, bf16[272,1536]{1,0:T(8,128)(2,1)}, u32[]{:S(2)}, u32[]{:S(2)}) collective-permute-start(bf16[272,1536]{1,0:T(8,128)(2,1)} %pad_maximum_fusion.8), channel_id=1, source_target_pairs={{0,4},{4,0},{1,5},{5,1},{2,6},{6,2},{3,7},{7,3},{8,12},{12,8},{9,1... | collective-permute-start | bytes 2506760 | tf_op jit(solution)/shard_map/ppermute | solution.py:33
  286.9 186.4 %reduce-scatter.5.cloned.1.call-start = ((), (), s32[]{:S(2)}) async-start(), calls=%async_computation.4 | async-start | bytes 2949120 | tf_op jit(solution)/shard_map/reduce_scatter | solution.py:751
  313.9 19.3 %collective-permute-start.44 = (bf16[1088,1536]{1,0:T(8,128)(2,1)}, bf16[1088,1536]{1,0:T(8,128)(2,1)S(1)}, u32[]{:S(2)}, u32[]{:S(2)}) collective-permute-start(bf16[1088,1536]{1,0:T(8,128)(2,1)} %get-tuple-element.222), channel_id=1, source_target_pairs={{0,2},{2,0},{1,3},{3,1},{4,6},{6,4},{5,7},{7,5},{8,10},{10,8},{9,1... | collective-permute-start | bytes 10027016 | tf_op jit(solution)/shard_map/ppermute | solution.py:37
  354.1 37.9 %collective-permute-start.53 = (bf16[272,1536]{1,0:T(8,128)(2,1)}, bf16[272,1536]{1,0:T(8,128)(2,1)}, u32[]{:S(2)}, u32[]{:S(2)}) collective-permute-start(bf16[272,1536]{1,0:T(8,128)(2,1)} %pad_maximum_fusion.9), channel_id=1, source_target_pairs={{0,1},{1,0},{2,3},{3,2},{4,5},{5,4},{6,7},{7,6},{8,9},{9,8},{10,11... | collective-permute-start | bytes 2506760 | tf_op jit(solution)/shard_map/ppermute | solution.py:41
  356.3 35.8 %collective-permute-start.54 = (bf16[272,1536]{1,0:T(8,128)(2,1)}, bf16[272,1536]{1,0:T(8,128)(2,1)}, u32[]{:S(2)}, u32[]{:S(2)}) collective-permute-start(bf16[272,1536]{1,0:T(8,128)(2,1)} %pad_maximum_fusion.10), channel_id=1, source_target_pairs={{0,4},{4,0},{1,5},{5,1},{2,6},{6,2},{3,7},{7,3},{8,12},{12,8},{9,1... | collective-permute-start | bytes 2506760 | tf_op jit(solution)/shard_map/ppermute | solution.py:33
  392.1 26.8 %collective-permute-start.55 = (bf16[3,384,512]{2,1,0:T(8,128)(2,1)}, bf16[3,384,512]{2,1,0:T(8,128)(2,1)}, u32[]{:S(2)}, u32[]{:S(2)}) collective-permute-start(bf16[3,384,512]{2,1,0:T(8,128)(2,1)} %reduce-scatter.3.cloned.1.call-done.own_ref), channel_id=1, source_target_pairs={{0,4},{4,0},{1,5},{5,1},{2,6},{6,2},{3,7},{7,3},{8,12},{12,8},{9,1... | collective-permute-start | bytes 3538952 | tf_op jit(solution)/shard_map/ppermute | solution.py:33
  421.3 22.6 %collective-permute-start.60 = (f32[2,1536]{1,0:T(2,128)S(1)}, f32[2,1536]{1,0:T(2,128)S(1)}, u32[]{:S(2)}, u32[]{:S(2)}) collective-permute-start(f32[2,1536]{1,0:T(2,128)S(1)} %fusion.35), channel_id=1, source_target_pairs={{0,2},{2,0},{1,3},{3,1},{4,6},{6,4},{5,7},{7,5},{8,10},{10,8},{9,1... | collective-permute-start | bytes 36872 | tf_op jit(solution)/shard_map/ppermute | solution.py:37
  423.4 20.5 %collective-permute-start.61 = (bf16[2,3,384,512]{3,2,1,0:T(8,128)(2,1)S(1)}, bf16[2,3,384,512]{3,2,1,0:T(8,128)(2,1)}, u32[]{:S(2)}, u32[]{:S(2)}) collective-permute-start(bf16[2,3,384,512]{3,2,1,0:T(8,128)(2,1)S(1)} %pad_maximum_fusion), channel_id=1, source_target_pairs={{0,2},{2,0},{1,3},{3,1},{4,6},{6,4},{5,7},{7,5},{8,10},{10,8},{9,1... | collective-permute-start | bytes 7077896 | tf_op jit(solution)/shard_map/ppermute | solution.py:37
  443.9 19.0 %collective-permute-start.62 = (bf16[272,1536]{1,0:T(8,128)(2,1)S(1)}, bf16[272,1536]{1,0:T(8,128)(2,1)}, u32[]{:S(2)}, u32[]{:S(2)}) collective-permute-start(bf16[272,1536]{1,0:T(8,128)(2,1)S(1)} %pad_maximum_fusion.11), channel_id=1, source_target_pairs={{0,1},{1,0},{2,3},{3,2},{4,5},{5,4},{6,7},{7,6},{8,9},{9,8},{10,11... | collective-permute-start | bytes 2506760 | tf_op jit(solution)/shard_map/ppermute | solution.py:41
  444.1 18.8 %collective-permute-start.63 = (bf16[272,1536]{1,0:T(8,128)(2,1)S(1)}, bf16[272,1536]{1,0:T(8,128)(2,1)}, u32[]{:S(2)}, u32[]{:S(2)}) collective-permute-start(bf16[272,1536]{1,0:T(8,128)(2,1)S(1)} %pad_maximum_fusion.12), channel_id=1, source_target_pairs={{0,4},{4,0},{1,5},{5,1},{2,6},{6,2},{3,7},{7,3},{8,12},{12,8},{9,1... | collective-permute-start | bytes 2506760 | tf_op jit(solution)/shard_map/ppermute | solution.py:33
  (84 other events, 784.4 us)
Sparse Core Ops, SparseCore 0:
  60.9 89.4 all-gather.2
  287.0 85.3 reduce-scatter.2
  421.4 44.6 reduce-scatter.4
